TPU v7x, 32 devices: a whole 2x2x4 slice. The times are simulated.
32 devices in a mesh: grp: 2 (over x), site: 16 (over z, y, core).
Axes of the slice: x: 2, y: 2, z: 4, core: 2. Of those that a mesh axis runs over, the one named last changes fastest.
Arguments:
- vectors: float32 [4, 3, 16, 288, 256], P('grp', None, 'site'), parts along dimension 0, may hold values from -6 to 6
- links: float32 [6, 2, 3, 3, 16, 288], P('grp', None, None, None, 'site'), parts along dimension 0, may hold values from -1 to 1, as said below
- momenta: int32 [4, 3], replicated, may hold values from -2 to 2
- directions: int32 [256], replicated, may hold values from 0 to 2
Outputs:
- meson: float32 [256, 8, 2, 256], P('site', 'grp'), parts along dimension 1
There are 2 independent parts, one for each index of `grp`. A program takes and returns all parts, laid end to end along the dimension named above; an argument that names none is the same for every part. Nothing has to cross between parts.
Inputs may be any that keep to these rules, and one draw needn't show every extreme that they name: Each links[k, :, :, :, t, s] holds the real and imaginary parts of a unitary 3 x 3 matrix.
All inputs are finite; a program needn't handle non-finite values.
Results may differ from a plain program's by a relative error of at most 0.0001.
Values sent between devices are 32-bit elements; how exact they have to be, the bound alone decides.
No kernel may reach another device: no remote copies, remote signals or barrier semaphores. Data moves between devices by JAX's collectives and lax.ppermute only.
A program may use at most 128 MiB of HBM per device.

v0:
```python
import math

import jax
import jax.numpy as jnp
from jax import lax
from jax.sharding import PartitionSpec as P

TLX = 12
TLY = 12
LZ = 2


kappa = 0.08


def passed_along(block, axis, distance):
    devices = range(lax.axis_size(axis))
    route = [((i - distance) % len(devices), i) for i in devices]
    return lax.ppermute(block, axis, route)


def mat_apply(link_k, field):
    real_part = 0.0
    imag_part = 0.0
    for colour in range(3):
        u_real = link_k[0, :, colour][..., None]
        u_imag = link_k[1, :, colour][..., None]
        f_real = field[0, colour][None]
        f_imag = field[1, colour][None]
        real_part = real_part + u_real * f_real - u_imag * f_imag
        imag_part = imag_part + u_real * f_imag + u_imag * f_real
    return jnp.stack([real_part, imag_part])


def adj_apply(link_k, field):
    real_part = 0.0
    imag_part = 0.0
    for colour in range(3):
        u_real = link_k[0, colour][..., None]
        u_imag = link_k[1, colour][..., None]
        f_real = field[0, colour][None]
        f_imag = field[1, colour][None]
        real_part = real_part + u_real * f_real + u_imag * f_imag
        imag_part = imag_part + u_real * f_imag - u_imag * f_real
    return jnp.stack([real_part, imag_part])


def hop_terms(field, links, sign, tiles):
    link_x = links[0]
    back_x = adj_apply(link_x, field)
    above_x = passed_along(field[:, :, :, 0], "site", -tiles)
    below_x = passed_along(back_x[:, :, :, -1], "site", tiles)
    forward = mat_apply(
        link_x, jnp.concatenate([field[:, :, :, 1:], above_x[:, :, :, None]], axis=3)
    )
    backward = jnp.concatenate([below_x[:, :, :, None], back_x[:, :, :, :-1]], axis=3)
    terms = [forward + sign * backward]
    link_y = links[1]
    back_y = adj_apply(link_y, field)
    above_y = passed_along(field[:, :, :, :, 0], "site", -1)
    below_y = passed_along(back_y[:, :, :, :, -1], "site", 1)
    forward = mat_apply(
        link_y, jnp.concatenate([field[:, :, :, :, 1:], above_y[:, :, :, :, None]], axis=4)
    )
    backward = jnp.concatenate([below_y[:, :, :, :, None], back_y[:, :, :, :, :-1]], axis=4)
    terms.append(forward + sign * backward)
    link_z = links[2]
    forward = mat_apply(link_z, jnp.roll(field, -1, 2))
    backward = jnp.roll(adj_apply(link_z, field), 1, 2)
    terms.append(forward + sign * backward)
    return terms


def meson_fields(left_field, shifted, momenta, xs, ys, zs, lx, ly, planes, scale):
    nev = left_field.shape[-1]
    flat_v = left_field.reshape((2, 3, -1, nev))
    flat_s = shifted.reshape((2, 3, -1, nev))
    blocks = []
    for moment in range(momenta.shape[0]):
        frac = (momenta[moment, 0] * xs % lx).astype(jnp.float32) / lx
        frac = frac + (momenta[moment, 1] * ys % ly).astype(jnp.float32) / ly
        frac = frac + (momenta[moment, 2] * zs % planes).astype(jnp.float32) / planes
        theta = (2.0 * math.pi * frac).reshape(-1)
        cosine = jnp.cos(theta)[:, None]
        sine = jnp.sin(theta)[:, None]
        a_real = cosine * flat_v[0] - sine * flat_v[1]
        a_imag = -(sine * flat_v[0] + cosine * flat_v[1])
        left = jnp.stack([a_real, a_imag])
        prods = jnp.einsum("acsn,bcsm->anbm", left, flat_s, precision=lax.Precision.HIGHEST)
        re_block = prods[0, :, 0] - prods[1, :, 1]
        im_block = prods[0, :, 1] + prods[1, :, 0]
        blocks.append(jnp.stack([re_block, im_block], axis=1))
    return jnp.stack(blocks, axis=1) * scale


def on_device(vectors, links, momenta, directions):
    devices = lax.axis_size("site")
    tiles = math.isqrt(devices)
    position = lax.axis_index("site")
    tile_row = position // tiles
    tile_col = position % tiles
    nev = vectors.shape[-1]
    field = vectors[:, :, 0].reshape((2, 3, LZ, TLX, TLY, nev))
    local_links = links[:, :, :, :, 0].reshape((3, 2, 3, 3, LZ, TLX, TLY))
    masks = (directions[None, :] == jnp.arange(3, dtype=jnp.int32)[:, None]).astype(jnp.float32)
    current = field
    for repeat in range(2):
        terms = hop_terms(current, local_links, 1.0, tiles)
        current = current + kappa * (terms[0] + terms[1] + terms[2] - 6.0 * current)
    terms = hop_terms(current, local_links, -1.0, tiles)
    shifted = 0.0
    for which in range(3):
        shifted = shifted + masks[which][None, None, None, None, None, :] * terms[which]
    lx = TLX * tiles
    ly = TLY * tiles
    zs = jnp.arange(LZ, dtype=jnp.int32)[:, None, None]
    xs = (tile_row * TLX + jnp.arange(TLX, dtype=jnp.int32))[None, :, None]
    ys = (tile_col * TLY + jnp.arange(TLY, dtype=jnp.int32))[None, None, :]
    scale = 1.0 / math.sqrt(3.0 * lx * ly * LZ)
    partial_sums = meson_fields(field, shifted, momenta, xs, ys, zs, lx, ly, LZ, scale)
    return lax.psum_scatter(partial_sums, "site", scatter_dimension=0, tiled=True)


def solution(mesh):
    placed = (
        P("grp", None, "site", None, None),
        P("grp", None, None, None, "site", None),
        P(),
        P(),
    )
    return jax.shard_map(
        on_device,
        mesh=mesh,
        in_specs=placed,
        out_specs=P("site", "grp", None, None),
        check_vma=False,
    )
```

profile of v0, /device:TPU:0, one launch (start us, length us, event | category | flops | bytes accessed | tf_op | source)
XLA Modules:
  0.0 473.8 jit_solution(14543858174275118778)
XLA Ops:
  6.5 2.8 copy.52
  18.0 14.0 %multiply_add_fusion.18 = (f32[1,3,2,12,12,256]{5,0,4,3,2,1:T(1,128)S(1)}, f32[1,3,2,12,12,256]{5,0,4,3,2,1:T(1,128)S(1)}, f32[1,3,2,12,12,256]{5,0,4,3,2,1:T(1,128)S(1)}, f32[1,3,2,12,12,256]{5,0,4,3,2,1:T(1,128)S(1)}) fusion(f32[2,12,12,256]{3,2,1,0:T(8,128)} %copy.77, f32[3,2,12,12]{3,2,1,0:T(8,128)S(1)} %get-tuple-element.241, ...), kind=kLoop, calls=%fused_computation.182 | loop fusion | flops 9732096 | bytes 5349888 | tf_op jit(solution)/shard_map/add | solution.py:43
  33.1 3.1 collective-permute-start.1
  37.7 2.2 collective-permute-start
  40.6 2.3 collective-permute-start.2
  47.7 1.8 fusion.182
  49.4 1.7 fusion.184
  52.0 2.0 fusion.105
  62.0 1.8 fusion.147
  63.8 1.9 fusion.145
  72.1 1.9 fusion.159
  74.0 2.0 fusion.157
  86.0 2.3 multiply_subtract_fusion
  88.5 8.4 %multiply_add_fusion.14 = (f32[1,3,2,12,12,256]{5,0,4,3,2,1:T(1,128)}, f32[1,3,2,12,12,256]{5,0,4,3,2,1:T(1,128)}) fusion(f32[3,2,12,12]{3,2,1,0:T(8,128)S(1)} %copy-done.93, f32[3,2,12,12]{3,2,1,0:T(8,128)S(1)} %copy-done.95, f32[3,2,12,12]{3,2,1,0:T(8,128)S(1)} %copy-done.97, f32[3,2,12,12]{3,2,1,0:T(8,128)S(1)} %copy-done.99, ...), kind=kLoop, calls=%fused_computation.174 | loop fusion | flops 4866048 | bytes 3559680 | tf_op jit(solution)/shard_map/add | solution.py:43
  97.0 3.0 multiply_subtract_fusion.21
  100.1 8.3 %multiply_subtract_fusion.16 = (f32[1,3,2,12,12,256]{5,0,4,3,2,1:T(1,128)}, f32[1,3,2,12,12,256]{5,0,4,3,2,1:T(1,128)}) fusion(f32[2,12,12,256]{3,2,1,0:T(8,128)S(1)} %copy-done.48, f32[3,2,12,12]{3,2,1,0:T(8,128)S(1)} %copy-done.125, f32[2,12,12,256]{3,2,1,0:T(8,128)S(1)} %copy-done.47, f32[3,2,12,12]{3,2,1,0:T(8,128)S(1)} %copy-done.123, ...), kind=kLoop, calls=%fused_computation.176 | loop fusion | flops 4866048 | bytes 3559680 | tf_op jit(solution)/shard_map/sub | solution.py:30
  109.1 1.9 slice.861
  110.9 1.7 slice.891
  139.7 2.7 fusion.90
  144.9 2.8 fusion.85
  149.8 7.2 %multiply_subtract_fusion.20 = (f32[1,3,2,12,12,256]{5,0,4,3,2,1:T(1,128)S(1)}, f32[1,3,2,12,12,256]{5,0,4,3,2,1:T(1,128)S(1)}) fusion(f32[2,12,12,256]{3,2,1,0:T(8,128)S(1)} %copy.65, f32[3,2,12,12]{3,2,1,0:T(8,128)S(1)} %copy-done.114, f32[2,12,12,256]{3,2,1,0:T(8,128)S(1)} %copy.63, f32[3,2,12,12]{3,2,1,0:T(8,128)S(1)} %copy-done.113, ...), kind=kLoop, calls=%fused_computation.184 | loop fusion | flops 4866048 | bytes 3559680 | tf_op jit(solution)/shard_map/sub | solution.py:30
  157.2 7.2 %multiply_subtract_fusion.18 = (f32[1,3,2,12,12,256]{5,0,4,3,2,1:T(1,128)S(1)}, f32[1,3,2,12,12,256]{5,0,4,3,2,1:T(1,128)S(1)}) fusion(f32[2,12,12,256]{3,2,1,0:T(8,128)S(1)} %copy.93, f32[3,2,12,12]{3,2,1,0:T(8,128)S(1)} %copy-done.108, f32[2,12,12,256]{3,2,1,0:T(8,128)S(1)} %copy.91, f32[3,2,12,12]{3,2,1,0:T(8,128)S(1)} %copy-done.107, ...), kind=kLoop, calls=%fused_computation.180 | loop fusion | flops 4866048 | bytes 3559680 | tf_op jit(solution)/shard_map/sub | solution.py:30
  164.5 10.6 %multiply_add_fusion.1 = f32[2,3,2,12,12,256]{5,0,4,3,2,1:T(2,128)S(1)} fusion(f32[2,3,2,12,12,256]{5,0,4,3,2,1:T(2,128)S(1)} %bitcast.451, f32[1,3,2,12,12,256]{5,0,4,3,2,1:T(1,128)S(1)} %copy-done.13, f32[1,3,2,12,12,256]{5,0,4,3,2,1:T(1,128)S(1)} %copy-done.11, f32[2,3,1,12,12,256]{5,0,4,3,2,1:T(2,128)S(1)} %fusion.63, ...), kind=kLoop, calls=%fused_computation.129 | loop fusion | flops 7962624 | bytes 15335424 | tf_op jit(solution)/shard_map/add | solution.py:109
  179.4 12.7 %multiply_add_fusion.12 = (f32[1,3,2,12,12,256]{5,0,4,3,2,1:T(1,128)S(1)}, f32[1,3,2,12,12,256]{5,0,4,3,2,1:T(1,128)S(1)}, f32[1,3,2,12,12,256]{5,0,4,3,2,1:T(1,128)S(1)}, f32[1,3,2,12,12,256]{5,0,4,3,2,1:T(1,128)S(1)}) fusion(f32[2,12,12,256]{3,2,1,0:T(8,128)S(1)} %copy.133, f32[2,12,12,256]{3,2,1,0:T(8,128)S(1)} %copy.131, ...), kind=kLoop, calls=%fused_computation.170 | loop fusion | flops 9732096 | bytes 5349888 | tf_op jit(solution)/shard_map/add | solution.py:43
  192.2 7.2 %multiply_add_fusion.8 = (f32[1,3,2,12,12,256]{5,0,4,3,2,1:T(1,128)S(1)}, f32[1,3,2,12,12,256]{5,0,4,3,2,1:T(1,128)S(1)}) fusion(f32[2,12,12,256]{3,2,1,0:T(8,128)S(1)} %copy.133, f32[2,12,12,256]{3,2,1,0:T(8,128)S(1)} %copy.131, f32[2,12,12,256]{3,2,1,0:T(8,128)S(1)} %copy.129, f32[2,12,12,256]{3,2,1,0:T(8,128)S(1)} %copy.127, ...), kind=kLoop, calls=%fused_computation.162 | loop fusion | flops 4866048 | bytes 3559680 | tf_op jit(solution)/shard_map/add | solution.py:43
  199.5 1.9 collective-permute-start.4
  201.7 1.8 collective-permute-start.6
  207.4 7.2 %multiply_subtract_fusion.10 = (f32[1,3,2,12,12,256]{5,0,4,3,2,1:T(1,128)S(1)}, f32[1,3,2,12,12,256]{5,0,4,3,2,1:T(1,128)S(1)}) fusion(f32[2,12,12,256]{3,2,1,0:T(8,128)S(1)} %copy.162, f32[2,12,12,256]{3,2,1,0:T(8,128)S(1)} %copy.160, f32[2,12,12,256]{3,2,1,0:T(8,128)S(1)} %copy.158, f32[2,12,12,256]{3,2,1,0:T(8,128)S(1)} %copy.156, ...), kind=kLoop, calls=%fused_computation.164 | loop fusion | flops 4866048 | bytes 3559680 | tf_op jit(solution)/shard_map/sub | solution.py:30
  223.2 7.2 %multiply_subtract_fusion.14 = (f32[1,3,2,12,12,256]{5,0,4,3,2,1:T(1,128)S(1)}, f32[1,3,2,12,12,256]{5,0,4,3,2,1:T(1,128)S(1)}) fusion(f32[2,12,12,256]{3,2,1,0:T(8,128)S(1)} %copy.121, f32[2,12,12,256]{3,2,1,0:T(8,128)S(1)} %copy.119, f32[2,12,12,256]{3,2,1,0:T(8,128)S(1)} %copy.117, f32[2,12,12,256]{3,2,1,0:T(8,128)S(1)} %copy.115, ...), kind=kLoop, calls=%fused_computation.172 | loop fusion | flops 4866048 | bytes 3559680 | tf_op jit(solution)/shard_map/sub | solution.py:30
  230.5 7.2 %multiply_subtract_fusion.12 = (f32[1,3,2,12,12,256]{5,0,4,3,2,1:T(1,128)S(1)}, f32[1,3,2,12,12,256]{5,0,4,3,2,1:T(1,128)S(1)}) fusion(f32[2,12,12,256]{3,2,1,0:T(8,128)S(1)} %copy.148, f32[2,12,12,256]{3,2,1,0:T(8,128)S(1)} %copy.146, f32[2,12,12,256]{3,2,1,0:T(8,128)S(1)} %copy.144, f32[2,12,12,256]{3,2,1,0:T(8,128)S(1)} %copy.142, ...), kind=kLoop, calls=%fused_computation.168 | loop fusion | flops 4866048 | bytes 3559680 | tf_op jit(solution)/shard_map/sub | solution.py:30
  237.8 20.9 %multiply_add_fusion = f32[2,3,2,12,12,256]{5,0,4,3,2,1:T(2,128)S(1)} fusion(f32[1,3,2,12,12,256]{5,0,4,3,2,1:T(1,128)S(1)} %get-tuple-element.40, f32[1,3,2,12,12,256]{5,0,4,3,2,1:T(1,128)S(1)} %get-tuple-element.39, f32[2,3,1,12,12,256]{5,0,4,3,2,1:T(2,128)S(1)} %fusion.62, f32[1,3,2,12,12,256]{5,0,4,3,2,1:T(1,128)S(1)} %get-tuple-element.38, ...), kind=kLoop, calls=%fused_computation.128 | loop fusion | flops 15925248 | bytes 27131904 | tf_op jit(solution)/shard_map/add | solution.py:109
  263.8 14.0 %multiply_add_fusion.2 = (f32[1,3,2,12,12,256]{5,0,4,3,2,1:T(1,128)}, f32[1,3,2,12,12,256]{5,0,4,3,2,1:T(1,128)}, f32[1,3,2,12,12,256]{5,0,4,3,2,1:T(1,128)S(1)}, f32[1,3,2,12,12,256]{5,0,4,3,2,1:T(1,128)S(1)}) fusion(f32[2,12,12,256]{3,2,1,0:T(8,128)S(1)} %copy.175, f32[2,12,12,256]{3,2,1,0:T(8,128)S(1)} %copy.173, f32[2,12,12,256]{3,2,1,0:T(8,128)S(1)} %copy.171, ...), kind=kLoop, calls=%fused_computation.150 | loop fusion | flops 9732096 | bytes 5349888 | tf_op jit(solution)/shard_map/add | solution.py:43
  277.7 7.1 %multiply_add_fusion.6 = (f32[1,3,2,12,12,256]{5,0,4,3,2,1:T(1,128)S(1)}, f32[1,3,2,12,12,256]{5,0,4,3,2,1:T(1,128)S(1)}) fusion(f32[2,12,12,256]{3,2,1,0:T(8,128)S(1)} %copy.175, f32[2,12,12,256]{3,2,1,0:T(8,128)S(1)} %copy.173, f32[2,12,12,256]{3,2,1,0:T(8,128)S(1)} %copy.171, f32[2,12,12,256]{3,2,1,0:T(8,128)S(1)} %copy.169, ...), kind=kLoop, calls=%fused_computation.158 | loop fusion | flops 4866048 | bytes 3559680 | tf_op jit(solution)/shard_map/add | solution.py:43
  284.8 6.3 %fusion.115 = (f32[2,12,12,256]{3,2,1,0:T(8,128)}, f32[2,12,12,256]{3,2,1,0:T(8,128)}, f32[2,12,12,256]{3,2,1,0:T(8,128)}, f32[2,12,12,256]{3,2,1,0:T(8,128)}, f...) fusion(f32[2,3,1,12,12,256]{5,0,4,3,2,1:T(2,128)S(1)} %get-tuple-element.78, ...), kind=kLoop, calls=%fused_computation.335 | loop fusion | flops 442368 | bytes 3538944 | tf_op jit(solution)/shard_map/slice | solution.py:28
  292.8 1.7 mul.4936
  294.6 1.7 mul.4941
  296.3 1.7 mul.4946
  298.0 1.7 mul.4951
  301.5 4.4 collective-permute-start.10
  307.7 2.0 collective-permute-start.9
  310.6 8.1 %multiply_subtract_fusion.4 = (f32[1,3,288,256]{3,0,2,1:T(1,128)}, f32[1,3,288,256]{3,0,2,1:T(1,128)}) fusion(f32[288,256]{1,0:T(8,128)S(1)} %copy-done.66, f32[3,288]{1,0:T(4,128)S(1)} %copy-done.145, f32[288,256]{1,0:T(8,128)S(1)} %copy-done.65, f32[3,288]{1,0:T(4,128)S(1)} %copy-done.144, f32[288,256]{1,0:T(8,128)S(1)} %copy-done.64, ...), kind=kLoop, calls=%fused_computation.152 | loop fusion | flops 4866048 | bytes 3559680 | tf_op jit(solution)/shard_map/sub | solution.py:30
  318.7 2.3 fusion.1
  321.0 6.3 %fusion.125 = (f32[2,12,12,256]{3,2,1,0:T(8,128)}, f32[2,12,12,256]{3,2,1,0:T(8,128)}, f32[2,12,12,256]{3,2,1,0:T(8,128)}, f32[2,12,12,256]{3,2,1,0:T(8,128)}, f...) fusion(f32[2,3,2,12,1,256]{5,0,4,3,2,1:T(2,128)S(1)} %bitcast.493, f32[2,3,2,12,11,256]{5,0,4,3,2,1:T(2,128)S(1)} %slice-done), kind=kLoop, calls=%fused_computation.345 | loop fusion | flops 442368 | bytes 3538944 | tf_op jit(solution)/shard_map/slice | solution.py:28
  327.3 6.6 %fusion.120 = (f32[2,12,12,256]{3,2,1,0:T(8,128)}, f32[2,12,12,256]{3,2,1,0:T(8,128)}, f32[2,12,12,256]{3,2,1,0:T(8,128)}, f32[2,12,12,256]{3,2,1,0:T(8,128)}, f...) fusion(f32[2,3,2,1,12,256]{5,0,4,3,2,1:T(2,128)S(1)} %bitcast.492, f32[2,3,2,11,12,256]{5,0,4,3,2,1:T(2,128)S(1)} %slice-done.1), kind=kLoop, calls=%fused_computation.340 | loop fusion | flops 442368 | bytes 3538944 | tf_op jit(solution)/shard_map/slice | solution.py:28
  333.9 1.7 mul.4878
  335.6 1.8 mul.4883
  339.1 1.7 mul.4893
  342.6 1.7 mul.4903
  344.3 1.7 mul.4813
  346.1 1.8 mul.4818
  347.8 1.8 mul.4823
  349.6 1.8 mul.4828
  351.4 1.7 mul.4833
  353.1 1.8 mul.4838
  354.9 2.7 fusion.3
  357.7 2.8 fusion.5
  360.7 7.0 %multiply_subtract_fusion.6 = (f32[1,3,288,256]{3,0,2,1:T(1,128)S(1)}, f32[1,3,288,256]{3,0,2,1:T(1,128)S(1)}) fusion(f32[288,256]{1,0:T(8,128)S(1)} %copy-done.60, f32[3,288]{1,0:T(4,128)S(1)} %copy-done.139, f32[288,256]{1,0:T(8,128)S(1)} %copy-done.58, f32[3,288]{1,0:T(4,128)S(1)} %copy-done.138, f32[288,256]{1,0:T(8,128)S(1)} %copy-done.57, ...), kind=kLoop, calls=%fused_computation.156 | loop fusion | flops 4866048 | bytes 3559680 | tf_op jit(solution)/shard_map/sub | solution.py:30
  367.9 7.0 %multiply_subtract_fusion.8 = (f32[1,3,288,256]{3,0,2,1:T(1,128)S(1)}, f32[1,3,288,256]{3,0,2,1:T(1,128)S(1)}) fusion(f32[288,256]{1,0:T(8,128)S(1)} %copy-done.59, f32[3,288]{1,0:T(4,128)S(1)} %copy-done.136, f32[288,256]{1,0:T(8,128)S(1)} %copy-done.56, f32[3,288]{1,0:T(4,128)S(1)} %copy-done.134, f32[288,256]{1,0:T(8,128)S(1)} %copy-done.54, ...), kind=kLoop, calls=%fused_computation.160 | loop fusion | flops 4866048 | bytes 3559680 | tf_op jit(solution)/shard_map/sub | solution.py:30
  374.9 5.8 %fusion.29 = f32[2,3,288,256]{3,0,2,1:T(2,128)S(1)} fusion(f32[2,3,288,256]{3,0,2,1:T(2,128)S(1)} %bitcast.456, f32[1,3,288,256]{3,0,2,1:T(1,128)S(1)} %get-tuple-element.64, f32[1,3,288,256]{3,0,2,1:T(1,128)S(1)} %get-tuple-element.63, f32[2,3,288,256]{3,0,2,1:T(2,128)S(1)} %bitcast.455, f32[1,3,288,256]{3,0,2,1:T(1,128)S(1)} %get-tuple-element.62, ...), kind=kLoop, calls=%fused_computation.105 | loop fusion | flops 4866048 | bytes 12389376 | tf_op jit(solution)/shard_map/add | solution.py:113
  380.7 3.6 fusion.58
  385.5 3.6 fusion.55
  390.3 3.6 fusion.52
  395.0 3.9 fusion.49
  400.7 64.3 %reduce-scatter.2.cloned.1.call-done = f32[16,4,2,256]{3,0,2,1:T(8,128)} async-done(((f32[256,4,2,256]{3,0,2,1:T(8,128)}), f32[16,4,2,256]{3,0,2,1:T(8,128)}) %reduce-scatter.2.cloned.1.call-update) | async-done | bytes 131088 | tf_op jit(solution)/shard_map/reduce_scatter | solution.py:121
  (528 shorter events, 111.5 us)
Async XLA Ops:
  6.5 458.5 %reduce-scatter.2.cloned.1.call-start = ((), (), s32[]{:S(2)}) async-start(), calls=%async_computation.1 | async-start | bytes 2228224 | tf_op jit(solution)/shard_map/reduce_scatter | solution.py:121
  17.8 14.2 %copy-start.67 = (f32[3,2,12,12]{3,2,1,0:T(8,128)}, f32[3,2,12,12]{3,2,1,0:T(8,128)S(1)}, u32[]{:S(2)}) copy-start(f32[3,2,12,12]{3,2,1,0:T(8,128)S(1)} %get-tuple-element.237) | copy-start | bytes 10372
  17.8 14.2 %copy-start.69 = (f32[3,2,12,12]{3,2,1,0:T(8,128)}, f32[3,2,12,12]{3,2,1,0:T(8,128)S(1)}, u32[]{:S(2)}) copy-start(f32[3,2,12,12]{3,2,1,0:T(8,128)S(1)} %get-tuple-element.238) | copy-start | bytes 10372
  17.8 14.2 %copy-start.71 = (f32[3,2,12,12]{3,2,1,0:T(8,128)}, f32[3,2,12,12]{3,2,1,0:T(8,128)S(1)}, u32[]{:S(2)}) copy-start(f32[3,2,12,12]{3,2,1,0:T(8,128)S(1)} %get-tuple-element.239) | copy-start | bytes 10372
  17.8 14.2 %copy-start.73 = (f32[3,2,12,12]{3,2,1,0:T(8,128)}, f32[3,2,12,12]{3,2,1,0:T(8,128)S(1)}, u32[]{:S(2)}) copy-start(f32[3,2,12,12]{3,2,1,0:T(8,128)S(1)} %get-tuple-element.240) | copy-start | bytes 10372
  17.8 14.2 %copy-start.75 = (f32[3,2,12,12]{3,2,1,0:T(8,128)}, f32[3,2,12,12]{3,2,1,0:T(8,128)S(1)}, u32[]{:S(2)}) copy-start(f32[3,2,12,12]{3,2,1,0:T(8,128)S(1)} %get-tuple-element.241) | copy-start | bytes 10372
  17.9 14.2 %copy-start.77 = (f32[3,2,12,12]{3,2,1,0:T(8,128)}, f32[3,2,12,12]{3,2,1,0:T(8,128)S(1)}, u32[]{:S(2)}) copy-start(f32[3,2,12,12]{3,2,1,0:T(8,128)S(1)} %get-tuple-element.242) | copy-start | bytes 10372
  17.9 14.2 %copy-start.79 = (f32[3,2,12,12]{3,2,1,0:T(8,128)}, f32[3,2,12,12]{3,2,1,0:T(8,128)S(1)}, u32[]{:S(2)}) copy-start(f32[3,2,12,12]{3,2,1,0:T(8,128)S(1)} %get-tuple-element.187) | copy-start | bytes 10372
  17.9 14.2 %copy-start.81 = (f32[3,2,12,12]{3,2,1,0:T(8,128)}, f32[3,2,12,12]{3,2,1,0:T(8,128)S(1)}, u32[]{:S(2)}) copy-start(f32[3,2,12,12]{3,2,1,0:T(8,128)S(1)} %get-tuple-element.188) | copy-start | bytes 10372
  17.9 14.2 %copy-start.83 = (f32[3,2,12,12]{3,2,1,0:T(8,128)}, f32[3,2,12,12]{3,2,1,0:T(8,128)S(1)}, u32[]{:S(2)}) copy-start(f32[3,2,12,12]{3,2,1,0:T(8,128)S(1)} %get-tuple-element.189) | copy-start | bytes 10372
  17.9 14.2 %copy-start.85 = (f32[3,2,12,12]{3,2,1,0:T(8,128)}, f32[3,2,12,12]{3,2,1,0:T(8,128)S(1)}, u32[]{:S(2)}) copy-start(f32[3,2,12,12]{3,2,1,0:T(8,128)S(1)} %get-tuple-element.190) | copy-start | bytes 10372
  17.9 14.2 %copy-start.87 = (f32[3,2,12,12]{3,2,1,0:T(8,128)}, f32[3,2,12,12]{3,2,1,0:T(8,128)S(1)}, u32[]{:S(2)}) copy-start(f32[3,2,12,12]{3,2,1,0:T(8,128)S(1)} %get-tuple-element.191) | copy-start | bytes 10372
  17.9 14.2 %copy-start.89 = (f32[3,2,12,12]{3,2,1,0:T(8,128)}, f32[3,2,12,12]{3,2,1,0:T(8,128)S(1)}, u32[]{:S(2)}) copy-start(f32[3,2,12,12]{3,2,1,0:T(8,128)S(1)} %get-tuple-element.192) | copy-start | bytes 10372
  33.1 131.3 %collective-permute-start.1 = (f32[2,3,2,12,256]{4,0,3,2,1:T(2,128)}, f32[2,3,2,12,256]{4,0,3,2,1:T(2,128)}, u32[]{:S(2)}, u32[]{:S(2)}) collective-permute-start(f32[2,3,2,12,256]{4,0,3,2,1:T(2,128)} %maximum_bitcast_fusion.25), channel_id=1, source_target_pairs={{12,0},{13,1},{14,2},{15,3},{0,4},{1,5},{2,6},{3,7},{4,8},{5,9},{6... | collective-permute-start | bytes 442376 | tf_op jit(solution)/shard_map/ppermute | solution.py:19
  37.0 127.5 %collective-permute-start.3 = (f32[2,3,2,12,256]{4,0,3,2,1:T(2,128)}, f32[2,3,2,12,256]{4,0,3,2,1:T(2,128)}, u32[]{:S(2)}, u32[]{:S(2)}) collective-permute-start(f32[2,3,2,12,256]{4,0,3,2,1:T(2,128)} %maximum_bitcast_fusion.24), channel_id=1, source_target_pairs={{15,0},{0,1},{1,2},{2,3},{3,4},{4,5},{5,6},{6,7},{7,8},{8,9},{9,10... | collective-permute-start | bytes 442376 | tf_op jit(solution)/shard_map/ppermute | solution.py:19
  37.7 101.4 %collective-permute-start = (f32[2,3,2,12,256]{4,0,3,2,1:T(2,128)}, f32[2,3,2,12,256]{4,0,3,2,1:T(2,128)}, u32[]{:S(2)}, u32[]{:S(2)}) collective-permute-start(f32[2,3,2,12,256]{4,0,3,2,1:T(2,128)} %slice_bitcast_fusion.7), channel_id=1, source_target_pairs={{4,0},{5,1},{6,2},{7,3},{8,4},{9,5},{10,6},{11,7},{12,8},{13,9},{1... | collective-permute-start | bytes 442376 | tf_op jit(solution)/shard_map/ppermute | solution.py:19
  40.6 103.5 %collective-permute-start.2 = (f32[2,3,2,12,256]{4,0,3,2,1:T(2,128)}, f32[2,3,2,12,256]{4,0,3,2,1:T(2,128)}, u32[]{:S(2)}, u32[]{:S(2)}) collective-permute-start(f32[2,3,2,12,256]{4,0,3,2,1:T(2,128)} %slice_bitcast_fusion.6), channel_id=1, source_target_pairs={{1,0},{2,1},{3,2},{4,3},{5,4},{6,5},{7,6},{8,7},{9,8},{10,9},{11,1... | collective-permute-start | bytes 442376 | tf_op jit(solution)/shard_map/ppermute | solution.py:19
  57.3 28.6 %copy-start.2 = (f32[2,3,1,288,256]{4,3,2,1,0:T(8,128)S(1)}, f32[2,3,1,288,256]{4,3,2,1,0:T(8,128)}, u32[]{:S(2)}) copy-start(f32[2,3,1,288,256]{4,3,2,1,0:T(8,128)} %param.4) | copy-start | bytes 5308420
  88.5 8.4 %copy-start.148 = (f32[288]{0:T(512)S(1)}, f32[288]{0:T(512)}, u32[]{:S(2)}) copy-start(f32[288]{0:T(512)} %cos.41) | copy-start | bytes 3460
  88.5 8.4 %copy-start.149 = (f32[288]{0:T(512)S(1)}, f32[288]{0:T(512)}, u32[]{:S(2)}) copy-start(f32[288]{0:T(512)} %cos.43) | copy-start | bytes 3460
  88.5 8.4 %copy-start.150 = (f32[288]{0:T(512)S(1)}, f32[288]{0:T(512)}, u32[]{:S(2)}) copy-start(f32[288]{0:T(512)} %cos.45) | copy-start | bytes 3460
  88.5 8.4 %copy-start.151 = (f32[288]{0:T(512)S(1)}, f32[288]{0:T(512)}, u32[]{:S(2)}) copy-start(f32[288]{0:T(512)} %sin.41) | copy-start | bytes 3460
  88.5 8.4 %copy-start.152 = (f32[288]{0:T(512)S(1)}, f32[288]{0:T(512)}, u32[]{:S(2)}) copy-start(f32[288]{0:T(512)} %sin.43) | copy-start | bytes 3460
  88.5 8.4 %copy-start.153 = (f32[288]{0:T(512)S(1)}, f32[288]{0:T(512)}, u32[]{:S(2)}) copy-start(f32[288]{0:T(512)} %sin.45) | copy-start | bytes 3460
  100.1 8.4 %copy-start.147 = (f32[3,256]{1,0:T(4,128)S(1)}, f32[3,256]{1,0:T(4,128)}, u32[]{:S(2)}) copy-start(f32[3,256]{1,0:T(4,128)} %fusion.143) | copy-start | bytes 9220
  110.9 27.4 %copy-start.11 = (f32[1,3,2,12,12,256]{5,0,4,3,2,1:T(1,128)S(1)}, f32[1,3,2,12,12,256]{5,0,4,3,2,1:T(1,128)}, u32[]{:S(2)}) copy-start(f32[1,3,2,12,12,256]{5,0,4,3,2,1:T(1,128)} %get-tuple-element.51) | copy-start | bytes 2654212
  110.9 27.4 %copy-start.13 = (f32[1,3,2,12,12,256]{5,0,4,3,2,1:T(1,128)S(1)}, f32[1,3,2,12,12,256]{5,0,4,3,2,1:T(1,128)}, u32[]{:S(2)}) copy-start(f32[1,3,2,12,12,256]{5,0,4,3,2,1:T(1,128)} %get-tuple-element.52) | copy-start | bytes 2654212
  149.8 7.3 %copy-start.103 = (f32[3,2,12,12]{3,2,1,0:T(8,128)S(1)}, f32[3,2,12,12]{3,2,1,0:T(8,128)}, u32[]{:S(2)}) copy-start(f32[3,2,12,12]{3,2,1,0:T(8,128)} %get-tuple-element.158) | copy-start | bytes 10372
  149.8 7.3 %copy-start.104 = (f32[3,2,12,12]{3,2,1,0:T(8,128)S(1)}, f32[3,2,12,12]{3,2,1,0:T(8,128)}, u32[]{:S(2)}) copy-start(f32[3,2,12,12]{3,2,1,0:T(8,128)} %get-tuple-element.159) | copy-start | bytes 10372
  149.8 7.3 %copy-start.105 = (f32[3,2,12,12]{3,2,1,0:T(8,128)S(1)}, f32[3,2,12,12]{3,2,1,0:T(8,128)}, u32[]{:S(2)}) copy-start(f32[3,2,12,12]{3,2,1,0:T(8,128)} %get-tuple-element.160) | copy-start | bytes 10372
  149.8 7.3 %copy-start.106 = (f32[3,2,12,12]{3,2,1,0:T(8,128)S(1)}, f32[3,2,12,12]{3,2,1,0:T(8,128)}, u32[]{:S(2)}) copy-start(f32[3,2,12,12]{3,2,1,0:T(8,128)} %get-tuple-element.161) | copy-start | bytes 10372
  149.8 7.3 %copy-start.107 = (f32[3,2,12,12]{3,2,1,0:T(8,128)S(1)}, f32[3,2,12,12]{3,2,1,0:T(8,128)}, u32[]{:S(2)}) copy-start(f32[3,2,12,12]{3,2,1,0:T(8,128)} %get-tuple-element.162) | copy-start | bytes 10372
  149.8 7.3 %copy-start.108 = (f32[3,2,12,12]{3,2,1,0:T(8,128)S(1)}, f32[3,2,12,12]{3,2,1,0:T(8,128)}, u32[]{:S(2)}) copy-start(f32[3,2,12,12]{3,2,1,0:T(8,128)} %get-tuple-element.163) | copy-start | bytes 10372
  149.8 14.6 %copy-start.18 = (f32[1,3,2,12,12,256]{5,0,4,3,2,1:T(1,128)S(1)}, f32[1,3,2,12,12,256]{5,0,4,3,2,1:T(1,128)}, u32[]{:S(2)}) copy-start(f32[1,3,2,12,12,256]{5,0,4,3,2,1:T(1,128)} %get-tuple-element.50) | copy-start | bytes 2654212
  157.1 7.3 %copy-start.4 = (f32[1,3,2,12,12,256]{5,0,4,3,2,1:T(1,128)S(1)}, f32[1,3,2,12,12,256]{5,0,4,3,2,1:T(1,128)}, u32[]{:S(2)}) copy-start(f32[1,3,2,12,12,256]{5,0,4,3,2,1:T(1,128)} %copy-done.3) | copy-start | bytes 2654212
  157.1 7.3 %copy-start.6 = (f32[1,3,2,12,12,256]{5,0,4,3,2,1:T(1,128)S(1)}, f32[1,3,2,12,12,256]{5,0,4,3,2,1:T(1,128)}, u32[]{:S(2)}) copy-start(f32[1,3,2,12,12,256]{5,0,4,3,2,1:T(1,128)} %copy-done.5) | copy-start | bytes 2654212
  157.1 7.3 %copy-start.8 = (f32[1,3,2,12,12,256]{5,0,4,3,2,1:T(1,128)S(1)}, f32[1,3,2,12,12,256]{5,0,4,3,2,1:T(1,128)}, u32[]{:S(2)}) copy-start(f32[1,3,2,12,12,256]{5,0,4,3,2,1:T(1,128)} %copy-done.7) | copy-start | bytes 2654212
  157.1 7.3 %copy-start.10 = (f32[1,3,2,12,12,256]{5,0,4,3,2,1:T(1,128)S(1)}, f32[1,3,2,12,12,256]{5,0,4,3,2,1:T(1,128)}, u32[]{:S(2)}) copy-start(f32[1,3,2,12,12,256]{5,0,4,3,2,1:T(1,128)} %copy-done.9) | copy-start | bytes 2654212
  157.1 7.3 %copy-start.17 = (f32[1,3,2,12,12,256]{5,0,4,3,2,1:T(1,128)S(1)}, f32[1,3,2,12,12,256]{5,0,4,3,2,1:T(1,128)}, u32[]{:S(2)}) copy-start(f32[1,3,2,12,12,256]{5,0,4,3,2,1:T(1,128)} %get-tuple-element.49) | copy-start | bytes 2654212
  175.1 39.5 %copy-start.1 = (f32[2,3,2,12,12,256]{5,0,4,3,2,1:T(2,128)}, f32[2,3,2,12,12,256]{5,0,4,3,2,1:T(2,128)S(1)}, u32[]{:S(2)}) copy-start(f32[2,3,2,12,12,256]{5,0,4,3,2,1:T(2,128)S(1)} %multiply_add_fusion.1) | copy-start | bytes 5308420
  179.4 12.8 %copy-start.92 = (f32[3,2,12,12]{3,2,1,0:T(8,128)S(1)}, f32[3,2,12,12]{3,2,1,0:T(8,128)}, u32[]{:S(2)}) copy-start(f32[3,2,12,12]{3,2,1,0:T(8,128)} %get-tuple-element.193) | copy-start | bytes 10372
  179.4 12.8 %copy-start.94 = (f32[3,2,12,12]{3,2,1,0:T(8,128)S(1)}, f32[3,2,12,12]{3,2,1,0:T(8,128)}, u32[]{:S(2)}) copy-start(f32[3,2,12,12]{3,2,1,0:T(8,128)} %get-tuple-element.194) | copy-start | bytes 10372
  179.4 12.8 %copy-start.96 = (f32[3,2,12,12]{3,2,1,0:T(8,128)S(1)}, f32[3,2,12,12]{3,2,1,0:T(8,128)}, u32[]{:S(2)}) copy-start(f32[3,2,12,12]{3,2,1,0:T(8,128)} %get-tuple-element.195) | copy-start | bytes 10372
  179.4 12.8 %copy-start.98 = (f32[3,2,12,12]{3,2,1,0:T(8,128)S(1)}, f32[3,2,12,12]{3,2,1,0:T(8,128)}, u32[]{:S(2)}) copy-start(f32[3,2,12,12]{3,2,1,0:T(8,128)} %get-tuple-element.196) | copy-start | bytes 10372
  179.4 12.8 %copy-start.100 = (f32[3,2,12,12]{3,2,1,0:T(8,128)S(1)}, f32[3,2,12,12]{3,2,1,0:T(8,128)}, u32[]{:S(2)}) copy-start(f32[3,2,12,12]{3,2,1,0:T(8,128)} %get-tuple-element.197) | copy-start | bytes 10372
  179.4 12.8 %copy-start.102 = (f32[3,2,12,12]{3,2,1,0:T(8,128)S(1)}, f32[3,2,12,12]{3,2,1,0:T(8,128)}, u32[]{:S(2)}) copy-start(f32[3,2,12,12]{3,2,1,0:T(8,128)} %get-tuple-element.198) | copy-start | bytes 10372
  199.5 16.0 %collective-permute-start.4 = (f32[2,3,2,12,256]{4,0,3,2,1:T(2,128)S(1)}, f32[2,3,2,12,256]{4,0,3,2,1:T(2,128)S(1)}, u32[]{:S(2)}, u32[]{:S(2)}) collective-permute-start(f32[2,3,2,12,256]{4,0,3,2,1:T(2,128)S(1)} %slice_bitcast_fusion.5), channel_id=1, source_target_pairs={{4,0},{5,1},{6,2},{7,3},{8,4},{9,5},{10,6},{11,7},{12,8},{13,9},{1... | collective-permute-start | bytes 442376 | tf_op jit(solution)/shard_map/ppermute | solution.py:19
  201.5 36.3 %collective-permute-start.5 = (f32[2,3,2,12,256]{4,0,3,2,1:T(2,128)S(1)}, f32[2,3,2,12,256]{4,0,3,2,1:T(2,128)S(1)}, u32[]{:S(2)}, u32[]{:S(2)}) collective-permute-start(f32[2,3,2,12,256]{4,0,3,2,1:T(2,128)S(1)} %maximum_bitcast_fusion.23), channel_id=1, source_target_pairs={{12,0},{13,1},{14,2},{15,3},{0,4},{1,5},{2,6},{3,7},{4,8},{5,9},{6... | collective-permute-start | bytes 442376 | tf_op jit(solution)/shard_map/ppermute | solution.py:19
  201.7 17.5 %collective-permute-start.6 = (f32[2,3,2,12,256]{4,0,3,2,1:T(2,128)S(1)}, f32[2,3,2,12,256]{4,0,3,2,1:T(2,128)S(1)}, u32[]{:S(2)}, u32[]{:S(2)}) collective-permute-start(f32[2,3,2,12,256]{4,0,3,2,1:T(2,128)S(1)} %slice_bitcast_fusion.4), channel_id=1, source_target_pairs={{1,0},{2,1},{3,2},{4,3},{5,4},{6,5},{7,6},{8,7},{9,8},{10,9},{11,1... | collective-permute-start | bytes 442376 | tf_op jit(solution)/shard_map/ppermute | solution.py:19
  203.6 34.1 %collective-permute-start.7 = (f32[2,3,2,12,256]{4,0,3,2,1:T(2,128)S(1)}, f32[2,3,2,12,256]{4,0,3,2,1:T(2,128)S(1)}, u32[]{:S(2)}, u32[]{:S(2)}) collective-permute-start(f32[2,3,2,12,256]{4,0,3,2,1:T(2,128)S(1)} %maximum_bitcast_fusion.22), channel_id=1, source_target_pairs={{15,0},{0,1},{1,2},{2,3},{3,4},{4,5},{5,6},{6,7},{7,8},{8,9},{9,10... | collective-permute-start | bytes 442376 | tf_op jit(solution)/shard_map/ppermute | solution.py:19
  230.5 7.3 %copy-start.12 = (f32[1,3,2,12,12,256]{5,0,4,3,2,1:T(1,128)S(1)}, f32[1,3,2,12,12,256]{5,0,4,3,2,1:T(1,128)}, u32[]{:S(2)}) copy-start(f32[1,3,2,12,12,256]{5,0,4,3,2,1:T(1,128)} %get-tuple-element.51) | copy-start | bytes 2654212
  230.5 7.3 %copy-start.14 = (f32[1,3,2,12,12,256]{5,0,4,3,2,1:T(1,128)S(1)}, f32[1,3,2,12,12,256]{5,0,4,3,2,1:T(1,128)}, u32[]{:S(2)}) copy-start(f32[1,3,2,12,12,256]{5,0,4,3,2,1:T(1,128)} %get-tuple-element.52) | copy-start | bytes 2654212
  301.5 19.5 %collective-permute-start.10 = (f32[2,3,2,12,256]{4,0,3,2,1:T(2,128)}, f32[2,3,2,12,256]{4,0,3,2,1:T(2,128)S(1)}, u32[]{:S(2)}, u32[]{:S(2)}) collective-permute-start(f32[2,3,2,12,256]{4,0,3,2,1:T(2,128)} %slice_bitcast_fusion.2), channel_id=1, source_target_pairs={{1,0},{2,1},{3,2},{4,3},{5,4},{6,5},{7,6},{8,7},{9,8},{10,9},{11,1... | collective-permute-start | bytes 442376 | tf_op jit(solution)/shard_map/ppermute | solution.py:19
  306.7 48.2 %collective-permute-start.11 = (f32[2,3,2,12,256]{4,0,3,2,1:T(2,128)}, f32[2,3,2,12,256]{4,0,3,2,1:T(2,128)}, u32[]{:S(2)}, u32[]{:S(2)}) collective-permute-start(f32[2,3,2,12,256]{4,0,3,2,1:T(2,128)} %maximum_bitcast_fusion.20), channel_id=1, source_target_pairs={{15,0},{0,1},{1,2},{2,3},{3,4},{4,5},{5,6},{6,7},{7,8},{8,9},{9,10... | collective-permute-start | bytes 442376 | tf_op jit(solution)/shard_map/ppermute | solution.py:19
  306.7 20.6 %collective-permute-start.8 = (f32[2,3,2,12,256]{4,0,3,2,1:T(2,128)S(1)}, f32[2,3,2,12,256]{4,0,3,2,1:T(2,128)S(1)}, u32[]{:S(2)}, u32[]{:S(2)}) collective-permute-start(f32[2,3,2,12,256]{4,0,3,2,1:T(2,128)S(1)} %copy-done.127), channel_id=1, source_target_pairs={{4,0},{5,1},{6,2},{7,3},{8,4},{9,5},{10,6},{11,7},{12,8},{13,9},{1... | collective-permute-start | bytes 442376 | tf_op jit(solution)/shard_map/ppermute | solution.py:19
  307.7 49.9 %collective-permute-start.9 = (f32[2,3,2,12,256]{4,0,3,2,1:T(2,128)}, f32[2,3,2,12,256]{4,0,3,2,1:T(2,128)}, u32[]{:S(2)}, u32[]{:S(2)}) collective-permute-start(f32[2,3,2,12,256]{4,0,3,2,1:T(2,128)} %maximum_bitcast_fusion.21), channel_id=1, source_target_pairs={{12,0},{13,1},{14,2},{15,3},{0,4},{1,5},{2,6},{3,7},{4,8},{5,9},{6... | collective-permute-start | bytes 442376 | tf_op jit(solution)/shard_map/ppermute | solution.py:19
  360.6 7.1 %copy-start.49 = (f32[288,256]{1,0:T(8,128)S(1)}, f32[288,256]{1,0:T(8,128)}, u32[]{:S(2)}) copy-start(f32[288,256]{1,0:T(8,128)} %mul.4813) | copy-start | bytes 884740
  360.6 7.1 %copy-start.50 = (f32[288,256]{1,0:T(8,128)S(1)}, f32[288,256]{1,0:T(8,128)}, u32[]{:S(2)}) copy-start(f32[288,256]{1,0:T(8,128)} %mul.4818) | copy-start | bytes 884740
  360.6 7.1 %copy-start.52 = (f32[288,256]{1,0:T(8,128)S(1)}, f32[288,256]{1,0:T(8,128)}, u32[]{:S(2)}) copy-start(f32[288,256]{1,0:T(8,128)} %mul.4823) | copy-start | bytes 884740
  360.6 7.1 %copy-start.54 = (f32[288,256]{1,0:T(8,128)S(1)}, f32[288,256]{1,0:T(8,128)}, u32[]{:S(2)}) copy-start(f32[288,256]{1,0:T(8,128)} %mul.4828) | copy-start | bytes 884740
  360.6 7.1 %copy-start.56 = (f32[288,256]{1,0:T(8,128)S(1)}, f32[288,256]{1,0:T(8,128)}, u32[]{:S(2)}) copy-start(f32[288,256]{1,0:T(8,128)} %mul.4833) | copy-start | bytes 884740
  360.6 7.1 %copy-start.59 = (f32[288,256]{1,0:T(8,128)S(1)}, f32[288,256]{1,0:T(8,128)}, u32[]{:S(2)}) copy-start(f32[288,256]{1,0:T(8,128)} %mul.4838) | copy-start | bytes 884740
  360.7 7.1 %copy-start.130 = (f32[3,288]{1,0:T(4,128)S(1)}, f32[3,288]{1,0:T(4,128)}, u32[]{:S(2)}) copy-start(f32[3,288]{1,0:T(4,128)} %mul.4821) | copy-start | bytes 10372
  360.7 7.1 %copy-start.132 = (f32[3,288]{1,0:T(4,128)S(1)}, f32[3,288]{1,0:T(4,128)}, u32[]{:S(2)}) copy-start(f32[3,288]{1,0:T(4,128)} %mul.4826) | copy-start | bytes 10372
  (111 other events, 331.0 us)
Sparse Core Ops, SparseCore 0:
  400.9 64.1 reduce-scatter.1
where the time goes:
time: 484 us; the launch traced here: 474 us
  other arithmetic  235 us (49%)
  local copies, waits for them, and re-layouts  125 us (26%)
  waiting for transfers between devices  64.4 us (13%)
  starting transfers between devices  18.1 us (4%)
  between operations  16.8 us (3%)
  matrix products  14.6 us (3%)
    mul x81, local copies, waits for them, and re-layouts, mat_apply(): real_part = real_part + u_real * f_real - u_imag * f_imag  67.1 us
    sub x9, other arithmetic, mat_apply(): real_part = real_part + u_real * f_real - u_imag * f_imag  66.6 us
    reduce_scatter x1, waiting for transfers between devices, on_device(): lax.psum_scatter(partial_sums, 'site', scatter_dimension=0, tiled=True)  64.3 us
    add x6, other arithmetic, adj_apply(): real_part = real_part + u_real * f_real + u_imag * f_imag  63.4 us
    add x2, other arithmetic, on_device(): current = current + kappa * (terms[0] + terms[1] + terms[2] - 6.0 * current)  31.5 us
    slice x3, other arithmetic, mat_apply(): f_real = field[0, colour][None]  19.1 us
    ppermute x12, starting transfers between devices, passed_along(): return lax.ppermute(block, axis, route)  18.1 us
    dot_general x4, matrix products, meson_fields(): jnp.einsum('acsn,bcsm->anbm', left, flat_s, precision=lax.Precision.HIGHEST)  14.6 us
  transfers between devices with their start and end apart: 13, of which 1 were waited for; matrix products, arithmetic and copies ran while one was open for 43% of the time, Pallas kernels for 0%

commit v1 on v0

v1 whole, which is shorter than its diff:
```python
import functools
import math

import jax
import jax.numpy as jnp
import numpy as np
from jax import lax
from jax.experimental import pallas as pl
from jax.experimental.pallas import tpu as pltpu
from jax.sharding import PartitionSpec as P

TLX = 12
TLY = 12
LZ = 2
KAPPA = 0.08

LAYER = LZ * TLY
SITES = TLX * LAYER
XROWS = 3 * LAYER
MAIN = TLX * XROWS
PADDED = (TLX + 2) * XROWS
EDGE = 4 * XROWS
HEAD = MAIN // 128 * 128
TAIL = MAIN - HEAD + EDGE
LANES = 128
CX, CY, CZ = 0, 18, 36
CYF, CYB, CZS, CZD = 54, 72, 90, 108
VMEM_LIMIT = 60 * 2**20


def call(kernel, outs, scratch=(), flops=0, moved=0, **kwargs):
    return pl.pallas_call(
        kernel,
        out_shape=outs,
        scratch_shapes=list(scratch),
        compiler_params=pltpu.CompilerParams(vmem_limit_bytes=VMEM_LIMIT),
        cost_estimate=pl.CostEstimate(flops=flops, bytes_accessed=moved, transcendentals=0),
        **kwargs,
    )


def f32(*shape):
    return jax.ShapeDtypeStruct(shape, jnp.float32)


def bf16(*shape):
    return jax.ShapeDtypeStruct(shape, jnp.bfloat16)


def spread(table, column, lanes=LANES):
    return jnp.broadcast_to(table[:, column : column + 1], (table.shape[0], lanes))


def matvec(table, first, field, adjoint=False, acc=None, minus=False):
    out = [[None] * 3, [None] * 3] if acc is None else [list(acc[0]), list(acc[1])]
    lanes = field[0][0].shape[-1]

    def put(part, row, value, negative):
        if negative != minus:
            out[part][row] = -value if out[part][row] is None else out[part][row] - value
        else:
            out[part][row] = value if out[part][row] is None else out[part][row] + value

    for row in range(3):
        for col in range(3):
            at = first + (3 * col + row if adjoint else 3 * row + col)
            real = spread(table, at, lanes)
            imag = spread(table, at + 9, lanes)
            put(0, row, real * field[0][col], False)
            put(0, row, imag * field[1][col], not adjoint)
            put(1, row, real * field[1][col], False)
            put(1, row, imag * field[0][col], adjoint)
    return out


def layer_rows(ref, part, half, first, size=LAYER):
    return ref[part, half, first : first + size, :]


def grid2(load):
    return [[load(part, colour) for colour in range(3)] for part in range(2)]


def y_rows(colour, z, y):
    return pl.ds(XROWS + colour * LAYER + z * TLY + y, TLX, stride=XROWS)


def send_layers(f_ref, wc_ref, xlo_ref, xhi_ref, ylo_ref, yhi_ref):
    last = TLX * XROWS
    for half in range(f_ref.shape[1]):
        for part in range(2):
            xlo_ref[part, half] = f_ref[part, half, XROWS : 2 * XROWS, :]
            for colour in range(3):
                for z in range(LZ):
                    to = colour * LAYER + z * TLX
                    ylo_ref[part, half, to : to + TLX, :] = f_ref[part, half, y_rows(colour, z, 0), :]
        table = wc_ref[TLX * LAYER : (TLX + 1) * LAYER, :]
        hop = matvec(table, CX, grid2(lambda p, c: layer_rows(f_ref, p, half, last + c * LAYER)), adjoint=True)
        for part in range(2):
            for colour in range(3):
                xhi_ref[part, half, colour * LAYER : (colour + 1) * LAYER, :] = hop[part][colour]
        for z in range(LZ):
            table = wc_ref[pl.ds(LAYER + z * TLY + TLY - 1, TLX, stride=LAYER), :]
            hop = matvec(table, CY, grid2(lambda p, c: f_ref[p, half, y_rows(c, z, TLY - 1), :]), adjoint=True)
            for part in range(2):
                for colour in range(3):
                    to = colour * LAYER + z * TLX
                    yhi_ref[part, half, to : to + TLX, :] = hop[part][colour]


def clear_ends(ref):
    for part in range(2):
        for half in range(ref.shape[1]):
            ref[part, half, 0:XROWS, :] = jnp.zeros((XROWS, LANES), jnp.float32)
            ref[part, half, PADDED - XROWS : PADDED, :] = jnp.zeros((XROWS, LANES), jnp.float32)


def pack_kernel(v_ref, l_ref, fr_ref, wc_ref, xlo_ref, xhi_ref, ylo_ref, yhi_ref, la, lb, ta, tb):
    la[...] = jnp.zeros_like(la)
    lb[...] = jnp.zeros_like(lb)
    plane = SITES // LZ
    la[0:54, 0:SITES] = l_ref[...]
    la[CYF : CYF + 18, 0:SITES] = l_ref[CY : CY + 18, :]
    la[CYB : CYB + 18, 0:SITES] = l_ref[CY : CY + 18, :]
    la[CZS : CZS + 18, 0:SITES] = l_ref[CZ : CZ + 18, :]
    la[CZD : CZD + 18, 0:SITES] = l_ref[CZ : CZ + 18, :]
    for part in range(2):
        for row in range(3):
            for col in range(3):
                k = 9 * part + 3 * row + col
                kt = CZ + 9 * part + 3 * col + row
                value = l_ref[kt : kt + 1, :]
                sign = 1.0 if part == 0 else -1.0
                lb[CZS + k : CZS + k + 1, 0:SITES] = sign * value
                lb[CZD + k : CZD + k + 1, 0:SITES] = -sign * value
    ta[...] = jnp.transpose(la[...])
    tb[...] = jnp.transpose(lb[...])
    raw = ta[0:SITES, :]
    other = jnp.concatenate([tb[plane:SITES, :], tb[0:plane, :]], axis=0)
    y = lax.broadcasted_iota(jnp.int32, (SITES, LANES), 0) % TLY
    column = lax.broadcasted_iota(jnp.int32, (SITES, LANES), 1)
    back = pltpu.roll(raw, 1, 0)
    is_yf = (column >= CYF) & (column < CYB)
    is_yb = (column >= CYB) & (column < CZS)
    table = jnp.where(is_yb, back, raw)
    gone = (is_yf & (y == TLY - 1)) | (is_yb & (y == 0))
    ta[0:SITES, :] = jnp.where(gone, 0.0, table) + other
    wc_ref[0:LAYER, :] = jnp.zeros((LAYER, LANES), jnp.float32)
    clear_ends(fr_ref)
    for x in range(TLX):
        for z in range(LZ):
            src = z * plane + x * TLY
            dst = (x + 1) * LAYER + z * TLY
            wc_ref[dst : dst + TLY, :] = ta[src : src + TLY, :]
            for half in range(fr_ref.shape[1]):
                for part in range(2):
                    for colour in range(3):
                        dst = (x + 1) * XROWS + colour * LAYER + z * TLY
                        fr_ref[part, half, dst : dst + TLY, :] = v_ref[
                            3 * part + colour, src : src + TLY, half * LANES : (half + 1) * LANES
                        ]
    send_layers(fr_ref, wc_ref, xlo_ref, xhi_ref, ylo_ref, yhi_ref)


def roll_layer(f_ref, half, base, rolled):
    for part in range(2):
        for colour in range(3):
            rows = f_ref[part, half, pl.ds(base + colour * LAYER, LAYER), :]
            at = colour * LAYER
            rolled[0, half, part, at : at + LAYER, :] = pltpu.roll(rows, LAYER - 1, 0)
            rolled[1, half, part, at : at + LAYER, :] = pltpu.roll(rows, 1, 0)
            rolled[2, half, part, at : at + LAYER, :] = pltpu.roll(rows, TLY, 0)


def layer_hops(f_ref, wc_ref, rolled, half, x, tile, z_column):
    base = pl.multiple_of((x + 1) * XROWS, 8)
    table = wc_ref[pl.ds(pl.multiple_of((x + 1) * LAYER, 8) + 8 * tile, 8), :]
    below = wc_ref[pl.ds(pl.multiple_of(x * LAYER, 8) + 8 * tile, 8), :]

    def straight(shift):
        return lambda p, c: f_ref[p, half, pl.ds(base + shift + c * LAYER + 8 * tile, 8), :]

    def turned(which):
        return lambda p, c: rolled[which, half, p, c * LAYER + 8 * tile : c * LAYER + 8 * tile + 8, :]

    return (
        (table, CX, straight(XROWS), False, 0),
        (below, CX, straight(-XROWS), True, 0),
        (table, CYF, turned(0), False, 1),
        (table, CYB, turned(1), True, 1),
        (table, z_column, turned(2), False, 2),
    ), straight(0)


def smear_kernel(f_ref, wc_ref, out_ref, rolled):
    clear_ends(out_ref)

    def layer(x, carry):
        base = pl.multiple_of((x + 1) * XROWS, 8)
        for half in range(f_ref.shape[1]):
            roll_layer(f_ref, half, base, rolled)
        for tile in range(LAYER // 8):
            for half in range(f_ref.shape[1]):
                hops, here = layer_hops(f_ref, wc_ref, rolled, half, x, tile, CZS)
                acc = None
                for weights, column, load, adjoint, _ in hops:
                    acc = matvec(weights, column, grid2(load), adjoint, acc)
                for part in range(2):
                    for colour in range(3):
                        value = (1.0 - 6.0 * KAPPA) * here(part, colour) + KAPPA * acc[part][colour]
                        out_ref[part, half, pl.ds(base + colour * LAYER + 8 * tile, 8), :] = value
        return carry

    lax.fori_loop(0, TLX, layer, 0)


def cross(once_ref, wc_ref, rxlo, rxhi, rylo, ryhi, save=None):
    last = TLX * XROWS
    for half in range(once_ref.shape[1]):
        table = wc_ref[TLX * LAYER : (TLX + 1) * LAYER, :]
        hop_x = matvec(table, CX, grid2(lambda p, c: layer_rows(rxhi, p, half, c * LAYER)))
        hop_y = []
        for z in range(LZ):
            table = wc_ref[pl.ds(LAYER + z * TLY + TLY - 1, TLX, stride=LAYER), :]
            hop_y.append(matvec(table, CY, grid2(lambda p, c: layer_rows(ryhi, p, half, c * LAYER + z * TLX, TLX))))
        for part in range(2):
            for colour in range(3):
                at = colour * LAYER
                low = layer_rows(rxlo, part, half, at)
                once_ref[part, half, XROWS + at : XROWS + at + LAYER, :] += KAPPA * low
                once_ref[part, half, last + at : last + at + LAYER, :] += KAPPA * hop_x[part][colour]
                if save is not None:
                    save[part, half, at : at + LAYER, :] = low
                    save[part, half, XROWS + at : XROWS + at + LAYER, :] = hop_x[part][colour]
                for z in range(LZ):
                    low = layer_rows(rylo, part, half, at + z * TLX, TLX)
                    rows = y_rows(colour, z, 0)
                    once_ref[part, half, rows, :] = once_ref[part, half, rows, :] + KAPPA * low
                    rows = y_rows(colour, z, TLY - 1)
                    once_ref[part, half, rows, :] = once_ref[part, half, rows, :] + KAPPA * hop_y[z][part][colour]
                    if save is not None:
                        to = 2 * XROWS + at + z * TLX
                        save[part, half, to : to + TLX, :] = low
                        save[part, half, to + XROWS : to + XROWS + TLX, :] = hop_y[z][part][colour]


def edge_kernel(part_ref, wc_ref, rxlo, rxhi, rylo, ryhi, once_ref, save, xlo_ref, xhi_ref, ylo_ref, yhi_ref):
    once_ref[...] = part_ref[...]
    cross(once_ref, wc_ref, rxlo, rxhi, rylo, ryhi, save)
    send_layers(once_ref, wc_ref, xlo_ref, xhi_ref, ylo_ref, yhi_ref)


def split(value):
    high = value.astype(jnp.bfloat16)
    return high, (value - high.astype(jnp.float32)).astype(jnp.bfloat16)


def phased(real, imag, half, lane, at, size, cos_ref, sin_ref, ah_ref, al_ref):
    real, imag = jnp.transpose(real), jnp.transpose(imag)
    halves = ah_ref.shape[0] // cos_ref.shape[0] // LANES
    for m in range(cos_ref.shape[0]):
        cosine = jnp.broadcast_to(cos_ref[m : m + 1, lane : lane + LANES], (LANES, LANES))
        sine = jnp.broadcast_to(sin_ref[m : m + 1, lane : lane + LANES], (LANES, LANES))
        row = (m * halves + half) * LANES
        high, low = split(cosine * real - sine * imag)
        ah_ref[row : row + LANES, at : at + LANES] = high
        al_ref[row : row + LANES, at : at + LANES] = low
        high, low = split(sine * real + cosine * imag)
        ah_ref[row : row + LANES, size + at : size + at + LANES] = high
        al_ref[row : row + LANES, size + at : size + at + LANES] = low


def head_kernel(fr_ref, cos_ref, sin_ref, ah_ref, al_ref):
    for half in range(fr_ref.shape[1]):
        for at in range(0, HEAD, LANES):
            real, imag = (fr_ref[p, half, XROWS + at : XROWS + at + LANES, :] for p in range(2))
            phased(real, imag, half, at, at, HEAD, cos_ref, sin_ref, ah_ref, al_ref)


def tail_kernel(fr_ref, save, cos_ref, sin_ref, ah_ref, al_ref, rows):
    for half in range(fr_ref.shape[1]):
        for part in range(2):
            rows[part, 0 : MAIN - HEAD, :] = fr_ref[part, half, XROWS + HEAD : XROWS + MAIN, :]
            rows[part, MAIN - HEAD : TAIL, :] = save[part, half]
        for at in range(0, TAIL, LANES):
            real, imag = (rows[p, at : at + LANES, :] for p in range(2))
            phased(real, imag, half, HEAD + at, at, TAIL, cos_ref, sin_ref, ah_ref, al_ref)


def displace_kernel(part_ref, wc_ref, rxlo, rxhi, rylo, ryhi, mask_ref, sh_ref, sl_ref, th_ref, tl_ref, twice, shift, rolled):
    twice[...] = part_ref[...]
    cross(twice, wc_ref, rxlo, rxhi, rylo, ryhi)
    halves = range(twice.shape[1])

    def layer(x, carry):
        into = pl.multiple_of(x * XROWS, 8)
        for half in halves:
            roll_layer(twice, half, pl.multiple_of((x + 1) * XROWS, 8), rolled)
        for tile in range(LAYER // 8):
            for half in halves:
                hops, _ = layer_hops(twice, wc_ref, rolled, half, x, tile, CZD)
                total = None
                for which in range(3):
                    acc = None
                    for weights, column, load, adjoint, direction in hops:
                        if direction == which:
                            acc = matvec(weights, column, grid2(load), adjoint, acc, adjoint)
                    lanes = slice(half * LANES, (half + 1) * LANES)
                    mask = jnp.broadcast_to(mask_ref[which : which + 1, lanes], (8, LANES))
                    acc = [[mask * a for a in row] for row in acc]
                    total = acc if total is None else [[t + a for t, a in zip(*rows)] for rows in zip(total, acc)]
                for part in range(2):
                    for colour in range(3):
                        shift[part, half, pl.ds(into + colour * LAYER + 8 * tile, 8), :] = total[part][colour]
        return carry

    lax.fori_loop(0, TLX, layer, 0)
    last = TLX * XROWS
    for half in halves:
        lanes = slice(half * LANES, (half + 1) * LANES)
        mask_x = jnp.broadcast_to(mask_ref[0:1, lanes], (XROWS, LANES))
        mask_y = jnp.broadcast_to(mask_ref[1:2, lanes], (TLX, LANES))
        for part in range(2):
            shift[part, half, MAIN : MAIN + XROWS, :] = mask_x * twice[part, half, XROWS : 2 * XROWS, :]
            shift[part, half, MAIN + XROWS : MAIN + 2 * XROWS, :] = -mask_x * twice[part, half, last : last + XROWS, :]
            for colour in range(3):
                for z in range(LZ):
                    to = MAIN + 2 * XROWS + colour * LAYER + z * TLX
                    shift[part, half, to : to + TLX, :] = mask_y * twice[part, half, y_rows(colour, z, 0), :]
                    to += XROWS
                    shift[part, half, to : to + TLX, :] = -mask_y * twice[part, half, y_rows(colour, z, TLY - 1), :]
    width = len(halves) * LANES
    for high_ref, low_ref, first, size in ((sh_ref, sl_ref, 0, HEAD), (th_ref, tl_ref, HEAD, TAIL)):
        for half in halves:
            real = slice(half * LANES, (half + 1) * LANES)
            imag = slice(width + half * LANES, width + (half + 1) * LANES)
            for row in range(0, size, 128):
                top = slice(row, row + 128)
                bottom = slice(size + row, size + row + 128)
                high, low = split(shift[0, half, first + row : first + row + 128, :])
                high_ref[top, real] = high
                low_ref[top, real] = low
                high_ref[bottom, imag] = -high
                low_ref[bottom, imag] = -low
                high, low = split(shift[1, half, first + row : first + row + 128, :])
                high_ref[bottom, real] = high
                low_ref[bottom, real] = low
                high_ref[top, imag] = high
                low_ref[top, imag] = low


def dot(a, b):
    return jnp.dot(a, b, preferred_element_type=jnp.float32)


def meson_kernel(ah, al, bh, bl, sh, sl, th, tl, out_ref):
    total = dot(ah[...], sh[...]) + dot(ah[...], sl[...]) + dot(al[...], sh[...])
    out_ref[...] = total + dot(bh[...], th[...]) + dot(bh[...], tl[...]) + dot(bl[...], th[...])


def phases(momenta, position, devices, tiles):
    site = np.arange(SITES)
    x, zy = site // LAYER, site % LAYER
    own = [np.repeat(a.reshape(TLX, 1, LAYER), 3, 1).reshape(-1) for a in (x, zy % TLY, zy // TLY)]
    edge = np.arange(LAYER)
    full = np.full(LAYER, 0)
    edges = (
        (full + TLX - 1, edge % TLY, edge // TLY),
        (full, edge % TLY, edge // TLY),
        (edge % TLX, full + TLY - 1, edge // TLX),
        (edge % TLX, full, edge // TLX),
    )
    steps = (-tiles, tiles, -1, 1)
    xs, ys, zs, move = own[0], own[1], own[2], np.zeros(MAIN, np.int64)
    for step, (ex, ey, ez) in zip(steps, edges):
        xs = np.concatenate([xs] + [ex] * 3)
        ys = np.concatenate([ys] + [ey] * 3)
        zs = np.concatenate([zs] + [ez] * 3)
        move = np.concatenate([move, np.full(XROWS, step)])
    tile = (position + jnp.asarray(move, jnp.int32) + devices) % devices
    lx, ly = TLX * tiles, TLY * tiles
    sx = (tile // tiles) * TLX + jnp.asarray(xs, jnp.int32)
    sy = (tile % tiles) * TLY + jnp.asarray(ys, jnp.int32)
    sz = jnp.asarray(zs, jnp.int32)
    frac = (momenta[:, 0:1] * sx % lx).astype(jnp.float32) / lx
    frac = frac + (momenta[:, 1:2] * sy % ly).astype(jnp.float32) / ly
    frac = frac + (momenta[:, 2:3] * sz % LZ).astype(jnp.float32) / LZ
    theta = 2.0 * math.pi * frac
    return jnp.cos(theta), jnp.sin(theta)


def send(block, devices, distance):
    return lax.ppermute(block, "site", [(i, (i + distance) % devices) for i in range(devices)])


def halo(sends, devices, tiles):
    xlo, xhi, ylo, yhi = sends
    return (
        send(xhi, devices, tiles),
        send(xlo, devices, -tiles),
        send(yhi, devices, 1),
        send(ylo, devices, -1),
    )


def stages(devices):
    found, stride = [], 1
    while stride < devices:
        left = devices // stride
        size = 2 if stride < 4 else 4 if left % 4 == 0 else 2
        found.append((stride, size))
        stride *= size
    return found


def scatter_sum(block, position, devices):
    shape = block.shape[1:]
    for stride, size in stages(devices):
        left = block.shape[0] // size
        block = block.reshape((left, size) + shape)
        mine = (position // stride) % size
        total = lax.dynamic_index_in_dim(block, mine, 1, keepdims=False)
        for step in range(1, size):
            other = (mine + step) % size
            out = lax.dynamic_index_in_dim(block, other, 1, keepdims=False)
            route = []
            for i in range(devices):
                digit = (i // stride) % size
                route.append((i, i + ((digit + step) % size - digit) * stride))
            total = total + lax.ppermute(out, "site", route)
        block = total
    return block[0]


def on_device(vectors, links, momenta, directions):
    devices = lax.axis_size("site")
    tiles = math.isqrt(devices)
    position = lax.axis_index("site")
    nev = vectors.shape[-1]
    moments = momenta.shape[0]
    field = vectors.reshape(6, SITES, nev)
    table = links.reshape(54, SITES)
    halves = nev // LANES
    layer = f32(2, halves, XROWS, LANES)
    padded = f32(2, halves, PADDED, LANES)
    fr, wc, *sends = call(
        pack_kernel,
        (padded, f32((TLX + 1) * LAYER, LANES), layer, layer, layer, layer),
        [pltpu.VMEM((128, 384), jnp.float32)] * 2 + [pltpu.VMEM((384, 128), jnp.float32)] * 2,
    )(field, table)
    received = halo(sends, devices, tiles)
    rolled = pltpu.VMEM((3, halves, 2, XROWS, LANES), jnp.float32)
    flops = 2 * 180 * 2 * SITES * nev
    once = call(smear_kernel, padded, [rolled], flops, 3 << 20)(fr, wc)
    cosine, sine = phases(momenta, position, devices, tiles)
    head = bf16(moments * nev, 2 * HEAD)
    tail = bf16(moments * nev, 2 * TAIL)
    ah, al = call(head_kernel, (head, head), flops=flops, moved=8 << 20)(fr, cosine, sine)
    once, save, *sends = call(edge_kernel, (padded, f32(2, halves, EDGE, LANES), layer, layer, layer, layer))(
        once, wc, *received
    )
    received = halo(sends, devices, tiles)
    twice = call(smear_kernel, padded, [rolled], flops, 3 << 20)(once, wc)
    rows = pltpu.VMEM((2, TAIL, LANES), jnp.float32)
    bh, bl = call(tail_kernel, (tail, tail), [rows], flops=flops, moved=4 << 20)(fr, save, cosine, sine)
    scale = 1.0 / math.sqrt(3.0 * TLX * tiles * TLY * tiles * LZ)
    which = jnp.arange(3, dtype=jnp.int32)[:, None]
    masks = jnp.where(directions[None, :] == which, jnp.float32(scale), jnp.float32(0.0))
    sh, sl, th, tl = call(
        displace_kernel,
        (bf16(2 * HEAD, 2 * nev), bf16(2 * HEAD, 2 * nev), bf16(2 * TAIL, 2 * nev), bf16(2 * TAIL, 2 * nev)),
        [
            pltpu.VMEM((2, halves, PADDED, LANES), jnp.float32),
            pltpu.VMEM((2, halves, HEAD + TAIL, LANES), jnp.float32),
            rolled,
        ],
    )(twice, wc, *received, masks)
    whole = lambda a: pl.BlockSpec(a.shape, lambda m: (0, 0))
    partial = pl.pallas_call(
        meson_kernel,
        out_shape=f32(nev, moments * 2 * nev),
        grid=(moments,),
        in_specs=[pl.BlockSpec((nev, 2 * HEAD), lambda m: (m, 0))] * 2
        + [pl.BlockSpec((nev, 2 * TAIL), lambda m: (m, 0))] * 2
        + [whole(sh), whole(sl), whole(th), whole(tl)],
        out_specs=pl.BlockSpec((nev, 2 * nev), lambda m: (0, m)),
        compiler_params=pltpu.CompilerParams(vmem_limit_bytes=VMEM_LIMIT),
    )(ah, al, bh, bl, sh, sl, th, tl)
    total = scatter_sum(partial.reshape(devices, nev // devices, moments * 2 * nev), position, devices)
    return total.reshape(nev // devices, moments, 2, nev)


def solution(mesh):
    placed = (
        P("grp", None, "site", None, None),
        P("grp", None, None, None, "site", None),
        P(),
        P(),
    )
    return jax.shard_map(
        on_device,
        mesh=mesh,
        in_specs=placed,
        out_specs=P("site", "grp", None, None),
        check_vma=False,
    )
```

time: 484 us -> 137 us (0.28); the launches traced: 474 us -> 136 us
  other arithmetic: 235 us -> 4.08 us
  local copies, waits for them, and re-layouts: 125 us -> 5.97 us
  Pallas kernels: 0 us -> 78.7 us
  waiting for transfers between devices: 64.4 us -> 25.5 us
  between operations: 16.8 us -> 0.34 us
  matrix products: 14.6 us -> 0 us
    add x13 -> x4, other arithmetic: 102 us -> 1.44 us  [the longest x3 1.42 us: scatter_sum(): total = total + lax.ppermute(out, 'site', route)]
    pallas_call x0 -> x8, Pallas kernels: none -> 78.6 us  [the longest x1 17.2 us: on_device(): call(displace_kernel, (bf16(2 * HEAD, 2 * nev), bf16(2 * HEAD, 2 * nev),...]
    mul x104 -> x0, local copies, waits for them, and re-layouts: 73.5 us -> none  [the longest x81 67.1 us: mat_apply(): real_part = real_part + u_real * f_real - u_imag * f_imag]
    sub x15 -> x0, other arithmetic: 72.2 us -> none  [the longest x9 66.6 us: mat_apply(): real_part = real_part + u_real * f_real - u_imag * f_imag]
    reduce_scatter x1 -> x0, waiting for transfers between devices: 64.3 us -> none  [on_device(): lax.psum_scatter(partial_sums, 'site', scatter_dimension=0, tiled=True)]
    ppermute x12 -> x13, waiting for transfers between devices: 0.03 us -> 25.5 us  [the longest x5 25.5 us: scatter_sum(): total = total + lax.ppermute(out, 'site', route)]
    slice x55 -> x1, local copies, waits for them, and re-layouts: 24.9 us -> 0.18 us  [phases(): frac = (momenta[:, 0:1] * sx % lx).astype(jnp.float32) / lx]
    slice x3 -> x0, other arithmetic: 19.1 us -> none  [mat_apply(): f_real = field[0, colour][None]]
  transfers between devices with their start and end apart: 13 -> 13, of which waited for: 1 -> 5; matrix products, arithmetic and copies ran while one was open for 43% -> 1% of each run, Pallas kernels for 0% -> 30%
where the time goes in v1:
time: 137 us; the launch traced here: 136 us
  Pallas kernels  78.7 us (57%)
  waiting for transfers between devices  25.5 us (19%)
  starting transfers between devices  21.8 us (16%)
  local copies, waits for them, and re-layouts  5.97 us (4%)
  other arithmetic  4.08 us (3%)
    ppermute x5, waiting for transfers between devices, scatter_sum(): total = total + lax.ppermute(out, 'site', route)  25.5 us
    ppermute x8, starting transfers between devices, send(): lax.ppermute(block, 'site', [(i, (i + distance) % devices) for i in range...  17.8 us
    pallas_call x1, Pallas kernels, on_device(): call(displace_kernel, (bf16(2 * HEAD, 2 * nev), bf16(2 * HEAD, 2 * nev),...  17.2 us
    pallas_call x1, Pallas kernels, on_device(): once = call(smear_kernel, padded, [rolled], flops, 3 << 20)(fr, wc)  15.4 us
    pallas_call x1, Pallas kernels, on_device(): twice = call(smear_kernel, padded, [rolled], flops, 3 << 20)(once, wc)  15.4 us
    pallas_call x1, Pallas kernels, on_device(): pl.pallas_call(meson_kernel, out_shape=f32(nev, moments * 2 * nev), grid=...  12.2 us
    pallas_call x1, Pallas kernels, on_device(): call(head_kernel, (head, head), flops=flops, moved=8 << 20)  5.99 us
    pallas_call x1, Pallas kernels, on_device(): call(tail_kernel, (tail, tail), [rows], flops=flops, moved=4 << 20)  4.46 us
  transfers between devices with their start and end apart: 13, of which 5 were waited for; matrix products, arithmetic and copies ran while one was open for 1% of the time, Pallas kernels for 30%

profile of v1, /device:TPU:0, one launch (start us, length us, event | category | flops | bytes accessed | tf_op | source)
XLA Modules:
  0.0 136.3 jit_solution(16093522955221168205)
XLA Ops:
  0.0 0.0 copy-start.11
  0.0 0.0 copy-start.12
  0.0 1.2 reduce
  1.2 0.7 reshape.23.l_ref
  1.9 3.7 %shard_map.82 = (f32[2,2,1008,128]{3,2,1,0:T(8,128)}, f32[312,128]{1,0:T(8,128)}, f32[2,2,72,128]{3,2,1,0:T(8,128)}, f32[2,2,72,128]{3,2,1,0:T(8,128)}, f32[2,2,...) custom-call(f32[6,288,256]{2,1,0:T(8,128)} %bitcast.15, f32[54,288]{1,0:T(8,128)} %reshape.23.l_ref), custom_call_target="tpu_custom_call" | custom-call | tf_op jit(solution)/shard_map/pallas_call | solution.py:446
  5.5 3.1 %collective-permute-start = (f32[2,2,72,128]{3,2,1,0:T(8,128)}, f32[2,2,72,128]{3,2,1,0:T(8,128)S(1)}, u32[]{:S(2)}, u32[]{:S(2)}) collective-permute-start(f32[2,2,72,128]{3,2,1,0:T(8,128)} %get-tuple-element.29), channel_id=1, source_target_pairs={{0,4},{1,5},{2,6},{3,7},{4,8},{5,9},{6,10},{7,11},{8,12},{9,13},{1... | collective-permute-start | bytes 442376 | tf_op jit(solution)/shard_map/ppermute | solution.py:393
  8.6 2.0 %collective-permute-start.1 = (f32[2,2,72,128]{3,2,1,0:T(8,128)}, f32[2,2,72,128]{3,2,1,0:T(8,128)S(1)}, u32[]{:S(2)}, u32[]{:S(2)}) collective-permute-start(f32[2,2,72,128]{3,2,1,0:T(8,128)} %get-tuple-element.30), channel_id=1, source_target_pairs={{0,12},{1,13},{2,14},{3,15},{4,0},{5,1},{6,2},{7,3},{8,4},{9,5},{1... | collective-permute-start | bytes 442376 | tf_op jit(solution)/shard_map/ppermute | solution.py:393
  10.6 0.0 collective-permute-start.2
  10.6 4.4 %collective-permute-start.3 = (f32[2,2,72,128]{3,2,1,0:T(8,128)}, f32[2,2,72,128]{3,2,1,0:T(8,128)S(1)}, u32[]{:S(2)}, u32[]{:S(2)}) collective-permute-start(f32[2,2,72,128]{3,2,1,0:T(8,128)} %get-tuple-element.32), channel_id=1, source_target_pairs={{0,15},{1,0},{2,1},{3,2},{4,3},{5,4},{6,5},{7,6},{8,7},{9,8},{10,9... | collective-permute-start | bytes 442376 | tf_op jit(solution)/shard_map/ppermute | solution.py:393
  15.0 0.0 copy-done.9
  15.0 0.2 slice_reduce_fusion.2
  15.2 0.0 copy-done.11
  15.2 0.0 copy-done.12
  15.2 0.0 copy-done.13
  15.3 0.0 copy-done.10
  15.3 0.9 fusion.22
  16.2 15.4 %shard_map.84.part_ref = f32[2,2,1008,128]{3,2,1,0:T(8,128)} custom-call(f32[2,2,1008,128]{3,2,1,0:T(8,128)} %get-tuple-element.25.fr_ref.f_ref, f32[312,128]{1,0:T(8,128)} %get-tuple-element.28.wc_ref), custom_call_target="tpu_custom_call" | custom-call | flops 53084160 | bytes 3145728 | tf_op jit(solution)/shard_map/pallas_call | solution.py:454
  31.6 6.0 %shard_map.83 = (bf16[1024,1536]{1,0:T(8,128)(2,1)}, bf16[1024,1536]{1,0:T(8,128)(2,1)}) custom-call(f32[2,2,1008,128]{3,2,1,0:T(8,128)} %get-tuple-element.25.fr_ref.f_ref, f32[4,1152]{1,0:T(4,128)} %get-tuple-element.52.cos_ref, f32[4,1152]{1,0:T(4,128)} %get-tuple-element.51.sin_ref), custom_call_target="tpu_custom_call" | custom-call | flops 53084160 | bytes 8388608 | tf_op jit(solution)/shard_map/pallas_call | solution.py:458
  37.6 0.0 collective-permute-done.rxlo
  37.6 0.0 collective-permute-done.1.rxhi
  37.6 0.0 copy-start.2
  37.6 0.0 collective-permute-done.2.rylo
  37.6 0.0 copy-start.3
  37.6 0.0 collective-permute-done.3.ryhi
  37.6 0.6 copy-done.1
  38.2 0.1 copy-done.2
  38.3 0.0 copy-done.3
  38.4 0.7 copy-done.4
  39.0 4.4 %shard_map.85 = (f32[2,2,1008,128]{3,2,1,0:T(8,128)}, f32[2,2,288,128]{3,2,1,0:T(8,128)}, f32[2,2,72,128]{3,2,1,0:T(8,128)}, f32[2,2,72,128]{3,2,1,0:T(8,128)}, ...) custom-call(f32[2,2,1008,128]{3,2,1,0:T(8,128)} %shard_map.84.part_ref, f32[312,128]{1,0:T(8,128)} %get-tuple-element.28.wc_ref, ...), custom_call_target="tpu_custom_call" | custom-call | tf_op jit(solution)/shard_map/pallas_call | solution.py:459
  43.5 0.0 collective-permute-start.4
  43.5 3.8 %collective-permute-start.5 = (f32[2,2,72,128]{3,2,1,0:T(8,128)}, f32[2,2,72,128]{3,2,1,0:T(8,128)S(1)}, u32[]{:S(2)}, u32[]{:S(2)}) collective-permute-start(f32[2,2,72,128]{3,2,1,0:T(8,128)} %get-tuple-element.38), channel_id=1, source_target_pairs={{0,12},{1,13},{2,14},{3,15},{4,0},{5,1},{6,2},{7,3},{8,4},{9,5},{1... | collective-permute-start | bytes 442376 | tf_op jit(solution)/shard_map/ppermute | solution.py:393
  47.3 0.0 collective-permute-start.6
  47.3 4.4 %collective-permute-start.7 = (f32[2,2,72,128]{3,2,1,0:T(8,128)}, f32[2,2,72,128]{3,2,1,0:T(8,128)S(1)}, u32[]{:S(2)}, u32[]{:S(2)}) collective-permute-start(f32[2,2,72,128]{3,2,1,0:T(8,128)} %get-tuple-element.40), channel_id=1, source_target_pairs={{0,15},{1,0},{2,1},{3,2},{4,3},{5,4},{6,5},{7,6},{8,7},{9,8},{10,9... | collective-permute-start | bytes 442376 | tf_op jit(solution)/shard_map/ppermute | solution.py:393
  51.7 0.0 copy-done.14
  51.7 0.6 fusion.21.mask_ref
  52.3 15.4 %shard_map.87.part_ref = f32[2,2,1008,128]{3,2,1,0:T(8,128)} custom-call(f32[2,2,1008,128]{3,2,1,0:T(8,128)} %get-tuple-element.36.f_ref, f32[312,128]{1,0:T(8,128)} %get-tuple-element.28.wc_ref), custom_call_target="tpu_custom_call" | custom-call | flops 53084160 | bytes 3145728 | tf_op jit(solution)/shard_map/pallas_call | solution.py:463
  67.7 4.5 %shard_map.86 = (bf16[1024,768]{1,0:T(8,128)(2,1)}, bf16[1024,768]{1,0:T(8,128)(2,1)}) custom-call(f32[2,2,1008,128]{3,2,1,0:T(8,128)} %get-tuple-element.25.fr_ref.f_ref, f32[2,2,288,128]{3,2,1,0:T(8,128)} %get-tuple-element.33.save, f32[4,1152]{1,0:T(4,128)} %get-tuple-element.52.cos_ref, f32[4,1152]{1,0:T(4,128)} %get-tuple-element.51.sin_ref), custom_call_target="tpu_custom_call" | custom-call | flops 53084160 | bytes 4194304 | tf_op jit(solution)/shard_map/pallas_call | solution.py:465
  72.2 0.0 collective-permute-done.4.rxlo
  72.2 0.0 collective-permute-done.5.rxhi
  72.2 0.0 copy-start.6
  72.2 0.0 collective-permute-done.6.rylo
  72.2 0.0 copy-start.7
  72.2 0.0 collective-permute-done.7.ryhi
  72.2 0.6 copy-done.5
  72.9 0.1 copy-done.6
  72.9 0.1 copy-done.7
  73.0 0.7 copy-done.8
  73.6 17.2 %shard_map.88 = (bf16[1536,512]{1,0:T(8,128)(2,1)}, bf16[1536,512]{1,0:T(8,128)(2,1)}, bf16[768,512]{1,0:T(8,128)(2,1)}, bf16[768,512]{1,0:T(8,128)(2,1)}) custom-call(f32[2,2,1008,128]{3,2,1,0:T(8,128)} %shard_map.87.part_ref, f32[312,128]{1,0:T(8,128)} %get-tuple-element.28.wc_ref, f32[2,2,72,128]{3,2,1,0:T(8,128)} %copy-done.5, ...), custom_call_target="tpu_custom_call" | custom-call | tf_op jit(solution)/shard_map/pallas_call | solution.py:469
  90.8 12.2 %shard_map.89 = f32[256,2048]{1,0:T(8,128)} custom-call(bf16[1024,1536]{1,0:T(8,128)(2,1)} %get-tuple-element.26.ah, bf16[1024,1536]{1,0:T(8,128)(2,1)} %get-tuple-element.27.al, bf16[1024,768]{1,0:T(8,128)(2,1)} %get-tuple-element.34.bh, bf16[1024,768]{1,0:T(8,128)(2,1)} %get-tuple-element.35.bl, bf16[1536,512]{1,0:T(8,128)(2,1)} %get-tuple-element.41.sh, ...), custom_call_target="tpu_custom_call" | custom-call | tf_op jit(solution)/shard_map/pallas_call | solution.py:479
  102.9 1.4 %dynamic-slice_bitcast_fusion = f32[8,16,2048]{2,1,0:T(8,128)S(1)} fusion(f32[8,2,16,2048]{3,2,1,0:T(8,128)} %bitcast.11, s32[]{:T(128)S(6)} %select_n.113), kind=kLoop, calls=%fused_computation.1 | loop fusion | bytes 2097156 | tf_op jit(solution)/shard_map/jit(dynamic_index_in_dim)/squeeze | solution.py:425
  104.4 0.1 collective-permute-start.8
  104.5 2.7 %collective-permute-done.8 = f32[8,16,2048]{2,1,0:T(8,128)} collective-permute-done((f32[8,16,2048]{2,1,0:T(8,128)S(1)}, f32[8,16,2048]{2,1,0:T(8,128)}, u32[]{:S(2)}, u32[]{:S(2)}) %collective-permute-start.8) | collective-permute-done | bytes 1048608 | tf_op jit(solution)/shard_map/ppermute | solution.py:430
  107.2 0.0 copy-done
  107.2 1.3 bitcast_add_fusion
  108.6 0.1 collective-permute-start.9
  108.8 13.9 %collective-permute-done.9 = f32[4,16,2048]{2,1,0:T(8,128)S(1)} collective-permute-done((f32[4,16,2048]{2,1,0:T(8,128)S(1)}, f32[4,16,2048]{2,1,0:T(8,128)S(1)}, u32[]{:S(2)}, u32[]{:S(2)}) %collective-permute-start.9) | collective-permute-done | bytes 524320 | tf_op jit(solution)/shard_map/ppermute | solution.py:430
  122.7 0.1 bitcast_add_fusion.1
  122.8 0.1 collective-permute-start.10
  122.8 3.8 %collective-permute-start.12 = (f32[1,16,2048]{2,1,0:T(8,128)S(1)}, f32[1,16,2048]{2,1,0:T(8,128)S(1)}, u32[]{:S(2)}, u32[]{:S(2)}) collective-permute-start(f32[1,16,2048]{2,1,0:T(8,128)S(1)} %get-tuple-element.49), channel_id=1, source_target_pairs={{0,12},{1,13},{2,14},{3,15},{4,0},{5,1},{6,2},{7,3},{8,4},{9,5},{1... | collective-permute-start | bytes 393224 | tf_op jit(solution)/shard_map/ppermute | solution.py:430
  126.7 0.0 collective-permute-start.11
  126.7 4.4 %collective-permute-done.10 = f32[1,16,2048]{2,1,0:T(8,128)S(1)} collective-permute-done((f32[1,16,2048]{2,1,0:T(8,128)S(1)}, f32[1,16,2048]{2,1,0:T(8,128)S(1)}, u32[]{:S(2)}, u32[]{:S(2)}) %collective-permute-start.10) | collective-permute-done | bytes 131104 | tf_op jit(solution)/shard_map/ppermute | solution.py:430
  131.1 0.8 collective-permute-done.12
  131.9 3.6 %collective-permute-done.11 = f32[1,16,2048]{2,1,0:T(8,128)S(1)} collective-permute-done((f32[1,16,2048]{2,1,0:T(8,128)S(1)}, f32[1,16,2048]{2,1,0:T(8,128)S(1)}, u32[]{:S(2)}, u32[]{:S(2)}) %collective-permute-start.11) | collective-permute-done | bytes 131104 | tf_op jit(solution)/shard_map/ppermute | solution.py:430
  135.6 0.8 reshape_squeeze.3
  (13 shorter events, 0.1 us)
Async XLA Ops:
  0.0 15.2 %copy-start.11 = (s32[1152]{0:T(1024)S(1)}, s32[1152]{0:T(1024)}, u32[]{:S(2)}) copy-start(s32[1152]{0:T(1024)} %constant.175.clone) | copy-start | bytes 13828
  0.0 15.2 %copy-start.12 = (s32[1152]{0:T(1024)S(1)}, s32[1152]{0:T(1024)}, u32[]{:S(2)}) copy-start(s32[1152]{0:T(1024)} %constant.174.clone) | copy-start | bytes 13828
  0.0 15.2 %copy-start.13 = (s32[1152]{0:T(1024)S(1)}, s32[1152]{0:T(1024)}, u32[]{:S(2)}) copy-start(s32[1152]{0:T(1024)} %constant.173.clone) | copy-start | bytes 13828
  0.0 15.3 %copy-start.10 = (s32[1152]{0:T(1024)S(1)}, s32[1152]{0:T(1024)}, u32[]{:S(2)}) copy-start(s32[1152]{0:T(1024)} %constant.176.clone) | copy-start | bytes 13828
  0.0 15.0 %copy-start.9 = (s32[4,3]{1,0:T(4,128)S(1)}, s32[4,3]{1,0:T(4,128)}, u32[]{:S(2)}) copy-start(s32[4,3]{1,0:T(4,128)} %param.10) | copy-start | bytes 148
  5.5 32.1 %collective-permute-start = (f32[2,2,72,128]{3,2,1,0:T(8,128)}, f32[2,2,72,128]{3,2,1,0:T(8,128)S(1)}, u32[]{:S(2)}, u32[]{:S(2)}) collective-permute-start(f32[2,2,72,128]{3,2,1,0:T(8,128)} %get-tuple-element.29), channel_id=1, source_target_pairs={{0,4},{1,5},{2,6},{3,7},{4,8},{5,9},{6,10},{7,11},{8,12},{9,13},{1... | collective-permute-start | bytes 442376 | tf_op jit(solution)/shard_map/ppermute | solution.py:393
  8.6 29.0 %collective-permute-start.1 = (f32[2,2,72,128]{3,2,1,0:T(8,128)}, f32[2,2,72,128]{3,2,1,0:T(8,128)S(1)}, u32[]{:S(2)}, u32[]{:S(2)}) collective-permute-start(f32[2,2,72,128]{3,2,1,0:T(8,128)} %get-tuple-element.30), channel_id=1, source_target_pairs={{0,12},{1,13},{2,14},{3,15},{4,0},{5,1},{6,2},{7,3},{8,4},{9,5},{1... | collective-permute-start | bytes 442376 | tf_op jit(solution)/shard_map/ppermute | solution.py:393
  10.6 27.0 %collective-permute-start.2 = (f32[2,2,72,128]{3,2,1,0:T(8,128)}, f32[2,2,72,128]{3,2,1,0:T(8,128)S(1)}, u32[]{:S(2)}, u32[]{:S(2)}) collective-permute-start(f32[2,2,72,128]{3,2,1,0:T(8,128)} %get-tuple-element.31), channel_id=1, source_target_pairs={{0,1},{1,2},{2,3},{3,4},{4,5},{5,6},{6,7},{7,8},{8,9},{9,10},{10,1... | collective-permute-start | bytes 442376 | tf_op jit(solution)/shard_map/ppermute | solution.py:393
  10.6 27.0 %collective-permute-start.3 = (f32[2,2,72,128]{3,2,1,0:T(8,128)}, f32[2,2,72,128]{3,2,1,0:T(8,128)S(1)}, u32[]{:S(2)}, u32[]{:S(2)}) collective-permute-start(f32[2,2,72,128]{3,2,1,0:T(8,128)} %get-tuple-element.32), channel_id=1, source_target_pairs={{0,15},{1,0},{2,1},{3,2},{4,3},{5,4},{6,5},{7,6},{8,7},{9,8},{10,9... | collective-permute-start | bytes 442376 | tf_op jit(solution)/shard_map/ppermute | solution.py:393
  31.6 20.2 %copy-start.14 = (s32[256]{0:T(256)S(1)}, s32[256]{0:T(256)}, u32[]{:S(2)}) copy-start(s32[256]{0:T(256)} %param.11) | copy-start | bytes 3076
  37.6 0.7 copy-start.1
  37.6 0.7 copy-start.2
  37.6 0.8 copy-start.3
  38.4 0.7 copy-start.4
  43.5 28.7 %collective-permute-start.4 = (f32[2,2,72,128]{3,2,1,0:T(8,128)}, f32[2,2,72,128]{3,2,1,0:T(8,128)S(1)}, u32[]{:S(2)}, u32[]{:S(2)}) collective-permute-start(f32[2,2,72,128]{3,2,1,0:T(8,128)} %get-tuple-element.37), channel_id=1, source_target_pairs={{0,4},{1,5},{2,6},{3,7},{4,8},{5,9},{6,10},{7,11},{8,12},{9,13},{1... | collective-permute-start | bytes 442376 | tf_op jit(solution)/shard_map/ppermute | solution.py:393
  43.5 28.7 %collective-permute-start.5 = (f32[2,2,72,128]{3,2,1,0:T(8,128)}, f32[2,2,72,128]{3,2,1,0:T(8,128)S(1)}, u32[]{:S(2)}, u32[]{:S(2)}) collective-permute-start(f32[2,2,72,128]{3,2,1,0:T(8,128)} %get-tuple-element.38), channel_id=1, source_target_pairs={{0,12},{1,13},{2,14},{3,15},{4,0},{5,1},{6,2},{7,3},{8,4},{9,5},{1... | collective-permute-start | bytes 442376 | tf_op jit(solution)/shard_map/ppermute | solution.py:393
  47.3 24.9 %collective-permute-start.6 = (f32[2,2,72,128]{3,2,1,0:T(8,128)}, f32[2,2,72,128]{3,2,1,0:T(8,128)S(1)}, u32[]{:S(2)}, u32[]{:S(2)}) collective-permute-start(f32[2,2,72,128]{3,2,1,0:T(8,128)} %get-tuple-element.39), channel_id=1, source_target_pairs={{0,1},{1,2},{2,3},{3,4},{4,5},{5,6},{6,7},{7,8},{8,9},{9,10},{10,1... | collective-permute-start | bytes 442376 | tf_op jit(solution)/shard_map/ppermute | solution.py:393
  47.3 24.9 %collective-permute-start.7 = (f32[2,2,72,128]{3,2,1,0:T(8,128)}, f32[2,2,72,128]{3,2,1,0:T(8,128)S(1)}, u32[]{:S(2)}, u32[]{:S(2)}) collective-permute-start(f32[2,2,72,128]{3,2,1,0:T(8,128)} %get-tuple-element.40), channel_id=1, source_target_pairs={{0,15},{1,0},{2,1},{3,2},{4,3},{5,4},{6,5},{7,6},{8,7},{9,8},{10,9... | collective-permute-start | bytes 442376 | tf_op jit(solution)/shard_map/ppermute | solution.py:393
  72.2 0.7 copy-start.5
  72.2 0.7 copy-start.6
  72.2 0.7 copy-start.7
  73.0 0.7 copy-start.8
  102.9 4.3 %copy-start = (f32[256,2048]{1,0:T(8,128)S(1)}, f32[256,2048]{1,0:T(8,128)}, u32[]{:S(2)}) copy-start(f32[256,2048]{1,0:T(8,128)} %shard_map.89) | copy-start | bytes 6291460
  104.4 2.9 %collective-permute-start.8 = (f32[8,16,2048]{2,1,0:T(8,128)S(1)}, f32[8,16,2048]{2,1,0:T(8,128)}, u32[]{:S(2)}, u32[]{:S(2)}) collective-permute-start(f32[8,16,2048]{2,1,0:T(8,128)S(1)} %dynamic-slice_bitcast_fusion), channel_id=1, source_target_pairs={{0,1},{1,0},{2,3},{3,2},{4,5},{5,4},{6,7},{7,6},{8,9},{9,8},{10,11... | collective-permute-start | bytes 3145736 | tf_op jit(solution)/shard_map/ppermute | solution.py:430
  108.6 14.0 %collective-permute-start.9 = (f32[4,16,2048]{2,1,0:T(8,128)S(1)}, f32[4,16,2048]{2,1,0:T(8,128)S(1)}, u32[]{:S(2)}, u32[]{:S(2)}) collective-permute-start(f32[4,16,2048]{2,1,0:T(8,128)S(1)} %dynamic-slice_bitcast_fusion.1), channel_id=1, source_target_pairs={{0,2},{1,3},{2,0},{3,1},{4,6},{5,7},{6,4},{7,5},{8,10},{9,11},{10,... | collective-permute-start | bytes 1572872 | tf_op jit(solution)/shard_map/ppermute | solution.py:430
  122.8 8.3 %collective-permute-start.10 = (f32[1,16,2048]{2,1,0:T(8,128)S(1)}, f32[1,16,2048]{2,1,0:T(8,128)S(1)}, u32[]{:S(2)}, u32[]{:S(2)}) collective-permute-start(f32[1,16,2048]{2,1,0:T(8,128)S(1)} %get-tuple-element.48), channel_id=1, source_target_pairs={{0,4},{1,5},{2,6},{3,7},{4,8},{5,9},{6,10},{7,11},{8,12},{9,13},{1... | collective-permute-start | bytes 393224 | tf_op jit(solution)/shard_map/ppermute | solution.py:430
  122.8 9.1 %collective-permute-start.12 = (f32[1,16,2048]{2,1,0:T(8,128)S(1)}, f32[1,16,2048]{2,1,0:T(8,128)S(1)}, u32[]{:S(2)}, u32[]{:S(2)}) collective-permute-start(f32[1,16,2048]{2,1,0:T(8,128)S(1)} %get-tuple-element.49), channel_id=1, source_target_pairs={{0,12},{1,13},{2,14},{3,15},{4,0},{5,1},{6,2},{7,3},{8,4},{9,5},{1... | collective-permute-start | bytes 393224 | tf_op jit(solution)/shard_map/ppermute | solution.py:430
  126.7 8.9 %collective-permute-start.11 = (f32[1,16,2048]{2,1,0:T(8,128)S(1)}, f32[1,16,2048]{2,1,0:T(8,128)S(1)}, u32[]{:S(2)}, u32[]{:S(2)}) collective-permute-start(f32[1,16,2048]{2,1,0:T(8,128)S(1)} %get-tuple-element.50), channel_id=1, source_target_pairs={{0,8},{1,9},{2,10},{3,11},{4,12},{5,13},{6,14},{7,15},{8,0},{9,1},... | collective-permute-start | bytes 393224 | tf_op jit(solution)/shard_map/ppermute | solution.py:430

commit v2 on v1

--- a/solution.py
+++ b/solution.py
@@ -23,15 +23,19 @@
 HEAD = MAIN // 128 * 128
 TAIL = MAIN - HEAD + EDGE
 LANES = 128
+BX, BYF, BYB, BZS, BZD, WIDE = 0, 18, 36, 54, 72, 90
 CX, CY, CZ = 0, 18, 36
 CYF, CYB, CZS, CZD = 54, 72, 90, 108
-VMEM_LIMIT = 60 * 2**20
-
-
-def call(kernel, outs, scratch=(), flops=0, moved=0, **kwargs):
+VMEM_LIMIT = 12 * 2**20
+
+
+def call(kernel, outs, scratch=(), flops=0, moved=0, inputs=1, **kwargs):
+    on_chip = pl.BlockSpec(memory_space=pltpu.VMEM)
     return pl.pallas_call(
         kernel,
         out_shape=outs,
+        in_specs=[on_chip] * inputs,
+        out_specs=jax.tree.map(lambda _: on_chip, outs),
         scratch_shapes=list(scratch),
         compiler_params=pltpu.CompilerParams(vmem_limit_bytes=VMEM_LIMIT),
         cost_estimate=pl.CostEstimate(flops=flops, bytes_accessed=moved, transcendentals=0),
@@ -172,44 +176,91 @@
             rolled[2, half, part, at : at + LAYER, :] = pltpu.roll(rows, TLY, 0)
 
 
-def layer_hops(f_ref, wc_ref, rolled, half, x, tile, z_column):
-    base = pl.multiple_of((x + 1) * XROWS, 8)
-    table = wc_ref[pl.ds(pl.multiple_of((x + 1) * LAYER, 8) + 8 * tile, 8), :]
-    below = wc_ref[pl.ds(pl.multiple_of(x * LAYER, 8) + 8 * tile, 8), :]
+def layer_hops(f_ref, wb_ref, rolled, x, tile, z_column):
+    step = 8 * tile
+    base = (x + 1) * XROWS
+
+    def table(column):
+        return wb_ref[x + 1, column, pl.ds(pl.multiple_of(step, 8), 8), :]
+
+    def below(column):
+        return wb_ref[x, column, pl.ds(pl.multiple_of(step, 8), 8), :]
 
     def straight(shift):
-        return lambda p, c: f_ref[p, half, pl.ds(base + shift + c * LAYER + 8 * tile, 8), :]
+        return lambda p, c, half: f_ref[p, half, pl.ds(pl.multiple_of(base + shift + c * LAYER + step, 8), 8), :]
 
     def turned(which):
-        return lambda p, c: rolled[which, half, p, c * LAYER + 8 * tile : c * LAYER + 8 * tile + 8, :]
+        return lambda p, c, half: rolled[which, half, p, pl.ds(pl.multiple_of(c * LAYER + step, 8), 8), :]
 
     return (
-        (table, CX, straight(XROWS), False, 0),
-        (below, CX, straight(-XROWS), True, 0),
-        (table, CYF, turned(0), False, 1),
-        (table, CYB, turned(1), True, 1),
+        (table, BX, straight(XROWS), False, 0),
+        (below, BX, straight(-XROWS), True, 0),
+        (table, BYF, turned(0), False, 1),
+        (table, BYB, turned(1), True, 1),
         (table, z_column, turned(2), False, 2),
     ), straight(0)
 
 
-def smear_kernel(f_ref, wc_ref, out_ref, rolled):
+def hop_all(weights, column, load, adjoint, halves, acc, minus=False):
+    for col in range(3):
+        field = [[load(p, col, half) for half in halves] for p in range(2)]
+        for row in range(3):
+            at = column + (3 * col + row if adjoint else 3 * row + col)
+            real = weights(at)
+            imag = weights(at + 9)
+            for half in halves:
+                terms = (
+                    (0, real * field[0][half], False),
+                    (0, imag * field[1][half], not adjoint),
+                    (1, real * field[1][half], False),
+                    (1, imag * field[0][half], adjoint),
+                )
+                for part, value, negative in terms:
+                    before = acc[part][row][half]
+                    if before is None:
+                        acc[part][row][half] = -value if negative != minus else value
+                    else:
+                        acc[part][row][half] = before - value if negative != minus else before + value
+    return acc
+
+
+def spread_kernel(wc_ref, wb_ref):
+    def layer(x, carry):
+        table = wc_ref[pl.ds(pl.multiple_of(x * LAYER, 8), LAYER), :]
+        for column in range(WIDE):
+            source = column if column < 18 else column + CYF - 18
+            wb_ref[x, column] = spread(table, source)
+        return carry
+
+    lax.fori_loop(0, TLX + 1, layer, 0)
+
+
+def empty_acc(halves):
+    return [[[None for _ in halves] for _ in range(3)] for _ in range(2)]
+
+
+def smear_kernel(f_ref, wb_ref, out_ref, rolled):
     clear_ends(out_ref)
+    halves = range(f_ref.shape[1])
 
     def layer(x, carry):
         base = pl.multiple_of((x + 1) * XROWS, 8)
-        for half in range(f_ref.shape[1]):
+        for half in halves:
             roll_layer(f_ref, half, base, rolled)
-        for tile in range(LAYER // 8):
-            for half in range(f_ref.shape[1]):
-                hops, here = layer_hops(f_ref, wc_ref, rolled, half, x, tile, CZS)
-                acc = None
-                for weights, column, load, adjoint, _ in hops:
-                    acc = matvec(weights, column, grid2(load), adjoint, acc)
-                for part in range(2):
-                    for colour in range(3):
-                        value = (1.0 - 6.0 * KAPPA) * here(part, colour) + KAPPA * acc[part][colour]
+
+        def tiles(tile, carry):
+            hops, here = layer_hops(f_ref, wb_ref, rolled, x, tile, BZS)
+            acc = empty_acc(halves)
+            for weights, column, load, adjoint, _ in hops:
+                hop_all(weights, column, load, adjoint, halves, acc)
+            for part in range(2):
+                for colour in range(3):
+                    for half in halves:
+                        value = (1.0 - 6.0 * KAPPA) * here(part, colour, half) + KAPPA * acc[part][colour][half]
                         out_ref[part, half, pl.ds(base + colour * LAYER + 8 * tile, 8), :] = value
-        return carry
+            return carry
+
+        return lax.fori_loop(0, LAYER // 8, tiles, carry, unroll=True)
 
     lax.fori_loop(0, TLX, layer, 0)
 
@@ -287,7 +338,7 @@
             phased(real, imag, half, HEAD + at, at, TAIL, cos_ref, sin_ref, ah_ref, al_ref)
 
 
-def displace_kernel(part_ref, wc_ref, rxlo, rxhi, rylo, ryhi, mask_ref, sh_ref, sl_ref, th_ref, tl_ref, twice, shift, rolled):
+def displace_kernel(part_ref, wc_ref, wb_ref, rxlo, rxhi, rylo, ryhi, mask_ref, sh_ref, sl_ref, th_ref, tl_ref, twice, shift, rolled):
     twice[...] = part_ref[...]
     cross(twice, wc_ref, rxlo, rxhi, rylo, ryhi)
     halves = range(twice.shape[1])
@@ -296,23 +347,31 @@
         into = pl.multiple_of(x * XROWS, 8)
         for half in halves:
             roll_layer(twice, half, pl.multiple_of((x + 1) * XROWS, 8), rolled)
-        for tile in range(LAYER // 8):
-            for half in halves:
-                hops, _ = layer_hops(twice, wc_ref, rolled, half, x, tile, CZD)
-                total = None
-                for which in range(3):
-                    acc = None
-                    for weights, column, load, adjoint, direction in hops:
-                        if direction == which:
-                            acc = matvec(weights, column, grid2(load), adjoint, acc, adjoint)
+
+        def tiles(tile, carry):
+            hops, _ = layer_hops(twice, wb_ref, rolled, x, tile, BZD)
+            total = empty_acc(halves)
+            for which in range(3):
+                acc = empty_acc(halves)
+                for weights, column, load, adjoint, direction in hops:
+                    if direction == which:
+                        hop_all(weights, column, load, adjoint, halves, acc, adjoint)
+                for half in halves:
                     lanes = slice(half * LANES, (half + 1) * LANES)
                     mask = jnp.broadcast_to(mask_ref[which : which + 1, lanes], (8, LANES))
-                    acc = [[mask * a for a in row] for row in acc]
-                    total = acc if total is None else [[t + a for t, a in zip(*rows)] for rows in zip(total, acc)]
-                for part in range(2):
-                    for colour in range(3):
-                        shift[part, half, pl.ds(into + colour * LAYER + 8 * tile, 8), :] = total[part][colour]
-        return carry
+                    for part in range(2):
+                        for row in range(3):
+                            value = mask * acc[part][row][half]
+                            before = total[part][row][half]
+                            total[part][row][half] = value if before is None else before + value
+            for part in range(2):
+                for colour in range(3):
+                    for half in halves:
+                        at = pl.ds(pl.multiple_of(into + colour * LAYER + 8 * tile, 8), 8)
+                        shift[part, half, at, :] = total[part][colour][half]
+            return carry
+
+        return lax.fori_loop(0, LAYER // 8, tiles, carry, unroll=True)
 
     lax.fori_loop(0, TLX, layer, 0)
     last = TLX * XROWS
@@ -447,22 +506,24 @@
         pack_kernel,
         (padded, f32((TLX + 1) * LAYER, LANES), layer, layer, layer, layer),
         [pltpu.VMEM((128, 384), jnp.float32)] * 2 + [pltpu.VMEM((384, 128), jnp.float32)] * 2,
+        inputs=2,
     )(field, table)
     received = halo(sends, devices, tiles)
+    flops = 2 * 180 * 2 * SITES * nev
+    wb = call(spread_kernel, f32(TLX + 1, WIDE, LAYER, LANES), (), flops >> 4, 1 << 20)(wc)
     rolled = pltpu.VMEM((3, halves, 2, XROWS, LANES), jnp.float32)
-    flops = 2 * 180 * 2 * SITES * nev
-    once = call(smear_kernel, padded, [rolled], flops, 3 << 20)(fr, wc)
+    once = call(smear_kernel, padded, [rolled], flops, 3 << 20, 2)(fr, wb)
     cosine, sine = phases(momenta, position, devices, tiles)
     head = bf16(moments * nev, 2 * HEAD)
     tail = bf16(moments * nev, 2 * TAIL)
-    ah, al = call(head_kernel, (head, head), flops=flops, moved=8 << 20)(fr, cosine, sine)
-    once, save, *sends = call(edge_kernel, (padded, f32(2, halves, EDGE, LANES), layer, layer, layer, layer))(
+    ah, al = call(head_kernel, (head, head), (), flops, 8 << 20, 3)(fr, cosine, sine)
+    once, save, *sends = call(edge_kernel, (padded, f32(2, halves, EDGE, LANES), layer, layer, layer, layer), inputs=6)(
         once, wc, *received
     )
     received = halo(sends, devices, tiles)
-    twice = call(smear_kernel, padded, [rolled], flops, 3 << 20)(once, wc)
+    twice = call(smear_kernel, padded, [rolled], flops, 3 << 20, 2)(once, wb)
     rows = pltpu.VMEM((2, TAIL, LANES), jnp.float32)
-    bh, bl = call(tail_kernel, (tail, tail), [rows], flops=flops, moved=4 << 20)(fr, save, cosine, sine)
+    bh, bl = call(tail_kernel, (tail, tail), [rows], flops, 4 << 20, 4)(fr, save, cosine, sine)
     scale = 1.0 / math.sqrt(3.0 * TLX * tiles * TLY * tiles * LZ)
     which = jnp.arange(3, dtype=jnp.int32)[:, None]
     masks = jnp.where(directions[None, :] == which, jnp.float32(scale), jnp.float32(0.0))
@@ -474,7 +535,8 @@
             pltpu.VMEM((2, halves, HEAD + TAIL, LANES), jnp.float32),
             rolled,
         ],
-    )(twice, wc, *received, masks)
+        inputs=8,
+    )(twice, wc, wb, *received, masks)
     whole = lambda a: pl.BlockSpec(a.shape, lambda m: (0, 0))
     partial = pl.pallas_call(
         meson_kernel,

time: 137 us -> 88.7 us (0.65)
  Pallas kernels: 78.7 us -> 35.6 us
  local copies, waits for them, and re-layouts: 5.97 us -> 2.67 us
    pallas_call x4 -> x5, Pallas kernels: 41.2 us -> 19.2 us  [the longest x1 6.39 us: on_device(): call(spread_kernel, f32(TLX + 1, WIDE, LAYER, LANES), (), flops >> 4, 1 <...]
    pallas_call x1, Pallas kernels: 17.2 us -> 6.41 us  [on_device(): call(displace_kernel, (bf16(2 * HEAD, 2 * nev), bf16(2 * HEAD, 2 * nev),...]
    pallas_call x1, Pallas kernels: 12.2 us -> 8.12 us  [on_device(): pl.pallas_call(meson_kernel, out_shape=f32(nev, moments * 2 * nev), grid=...]
    pallas_call x1, Pallas kernels: 4.44 us -> 1.07 us  [on_device(): call(edge_kernel, (padded, f32(2, halves, EDGE, LANES), layer, layer, lay...]
    pallas_call x1, Pallas kernels: 3.65 us -> 0.75 us  [on_device(): call(pack_kernel, (padded, f32((TLX + 1) * LAYER, LANES), layer, layer, l...]
    unnamed x30 -> x14, local copies, waits for them, and re-layouts: 2.82 us -> 1.5 us
  transfers between devices with their start and end apart: 13 -> 13, of which waited for: 5 -> 4; matrix products, arithmetic and copies ran while one was open for 1% -> 1% of each run, Pallas kernels for 30% -> 22%
where the time goes in v2:
time: 88.7 us; the launch traced here: 88.5 us
  Pallas kernels  35.6 us (40%)
  waiting for transfers between devices  25 us (28%)
  starting transfers between devices  22 us (25%)
  other arithmetic  2.89 us (3%)
  local copies, waits for them, and re-layouts  2.67 us (3%)
    ppermute x5, waiting for transfers between devices, scatter_sum(): total = total + lax.ppermute(out, 'site', route)  25 us
    ppermute x8, starting transfers between devices, send(): lax.ppermute(block, 'site', [(i, (i + distance) % devices) for i in range...  18 us
    pallas_call x1, Pallas kernels, on_device(): pl.pallas_call(meson_kernel, out_shape=f32(nev, moments * 2 * nev), grid=...  8.12 us
    pallas_call x1, Pallas kernels, on_device(): call(displace_kernel, (bf16(2 * HEAD, 2 * nev), bf16(2 * HEAD, 2 * nev),...  6.41 us
    pallas_call x1, Pallas kernels, on_device(): call(spread_kernel, f32(TLX + 1, WIDE, LAYER, LANES), (), flops >> 4, 1 <...  6.39 us
    pallas_call x1, Pallas kernels, on_device(): once = call(smear_kernel, padded, [rolled], flops, 3 << 20, 2)(fr, wb)  5.13 us
    pallas_call x1, Pallas kernels, on_device(): twice = call(smear_kernel, padded, [rolled], flops, 3 << 20, 2)(once, wb)  5.11 us
    ppermute x5, starting transfers between devices, scatter_sum(): total = total + lax.ppermute(out, 'site', route)  4.01 us
  transfers between devices with their start and end apart: 13, of which 4 were waited for; matrix products, arithmetic and copies ran while one was open for 1% of the time, Pallas kernels for 22%

profile of v2, /device:TPU:0, one launch (start us, length us, event | category | flops | bytes accessed | tf_op | source)
XLA Modules:
  0.0 88.5 jit_solution(15472983860080224374)
XLA Ops:
  0.0 0.0 copy-start.3
  0.0 0.0 copy-start.4
  0.0 0.0 copy-start.5
  0.0 0.0 copy-start.2
  0.0 0.0 copy-start.1
  0.0 1.2 %reduce = f32[3,2,3,3,288]{4,3,2,1,0:T(4,128)S(1)} reduce(f32[3,2,3,3,1,288]{5,4,3,2,1,0:T(1,128)} %param.9, f32[]{:T(128)} %constant.179), dimensions={4}, to_apply=%param.9.reduce_sub_computation | reduce | bytes 124420 | tf_op args[1]
  1.2 0.0 copy-start
  1.2 1.5 %copy-done = f32[2,3,1,288,256]{4,3,2,1,0:T(8,128)S(1)} copy-done((f32[2,3,1,288,256]{4,3,2,1,0:T(8,128)S(1)}, f32[2,3,1,288,256]{4,3,2,1,0:T(8,128)}, u32[]{:S(2)}) %copy-start) | copy-done | bytes 1769496
  2.7 0.8 shard_map.82
  3.5 3.1 %collective-permute-start = (f32[2,2,72,128]{3,2,1,0:T(8,128)S(1)}, f32[2,2,72,128]{3,2,1,0:T(8,128)S(1)}, u32[]{:S(2)}, u32[]{:S(2)}) collective-permute-start(f32[2,2,72,128]{3,2,1,0:T(8,128)S(1)} %get-tuple-element.29), channel_id=1, source_target_pairs={{0,4},{1,5},{2,6},{3,7},{4,8},{5,9},{6,10},{7,11},{8,12},{9,13},{1... | collective-permute-start | bytes 442376 | tf_op jit(solution)/shard_map/ppermute | solution.py:452
  6.6 2.1 %collective-permute-start.1 = (f32[2,2,72,128]{3,2,1,0:T(8,128)S(1)}, f32[2,2,72,128]{3,2,1,0:T(8,128)S(1)}, u32[]{:S(2)}, u32[]{:S(2)}) collective-permute-start(f32[2,2,72,128]{3,2,1,0:T(8,128)S(1)} %get-tuple-element.30), channel_id=1, source_target_pairs={{0,12},{1,13},{2,14},{3,15},{4,0},{5,1},{6,2},{7,3},{8,4},{9,5},{1... | collective-permute-start | bytes 442376 | tf_op jit(solution)/shard_map/ppermute | solution.py:452
  8.7 0.0 collective-permute-start.2
  8.7 4.4 %collective-permute-start.3 = (f32[2,2,72,128]{3,2,1,0:T(8,128)S(1)}, f32[2,2,72,128]{3,2,1,0:T(8,128)S(1)}, u32[]{:S(2)}, u32[]{:S(2)}) collective-permute-start(f32[2,2,72,128]{3,2,1,0:T(8,128)S(1)} %get-tuple-element.32), channel_id=1, source_target_pairs={{0,15},{1,0},{2,1},{3,2},{4,3},{5,4},{6,5},{7,6},{8,7},{9,8},{10,9... | collective-permute-start | bytes 442376 | tf_op jit(solution)/shard_map/ppermute | solution.py:452
  13.1 0.0 copy-done.1
  13.1 0.2 slice_reduce_fusion.2
  13.3 0.0 copy-done.3
  13.3 0.0 copy-done.4
  13.3 0.0 copy-done.5
  13.4 0.0 copy-done.2
  13.4 0.3 fusion.22
  13.7 6.4 %shard_map.84.wb_ref = f32[13,90,24,128]{3,2,1,0:T(8,128)S(1)} custom-call(f32[312,128]{1,0:T(8,128)S(1)} %get-tuple-element.28.wc_ref), custom_call_target="tpu_custom_call" | custom-call | flops 3317760 | bytes 1048576 | tf_op jit(solution)/shard_map/pallas_call | solution.py:513
  20.1 5.1 %shard_map.85.part_ref = f32[2,2,1008,128]{3,2,1,0:T(8,128)S(1)} custom-call(f32[2,2,1008,128]{3,2,1,0:T(8,128)S(1)} %get-tuple-element.25.fr_ref.f_ref, f32[13,90,24,128]{3,2,1,0:T(8,128)S(1)} %shard_map.84.wb_ref), custom_call_target="tpu_custom_call" | custom-call | flops 53084160 | bytes 3145728 | tf_op jit(solution)/shard_map/pallas_call | solution.py:515
  25.2 0.0 copy-start.6
  25.2 1.7 %shard_map.83 = (bf16[1024,1536]{1,0:T(8,128)(2,1)S(1)}, bf16[1024,1536]{1,0:T(8,128)(2,1)S(1)}) custom-call(f32[2,2,1008,128]{3,2,1,0:T(8,128)S(1)} %get-tuple-element.25.fr_ref.f_ref, f32[4,1152]{1,0:T(4,128)S(1)} %get-tuple-element.52.cos_ref, f32[4,1152]{1,0:T(4,128)S(1)} %get-tuple-element.51.sin_ref), custom_call_target="tpu_custom_call" | custom-call | flops 53084160 | bytes 8388608 | tf_op jit(solution)/shard_map/pallas_call | solution.py:519
  26.9 0.0 collective-permute-done.rxlo
  26.9 0.0 collective-permute-done.1.rxhi
  26.9 0.0 collective-permute-done.2.rylo
  27.0 0.0 collective-permute-done.3.ryhi
  27.0 1.1 %shard_map.86 = (f32[2,2,1008,128]{3,2,1,0:T(8,128)S(1)}, f32[2,2,288,128]{3,2,1,0:T(8,128)S(1)}, f32[2,2,72,128]{3,2,1,0:T(8,128)S(1)}, f32[2,2,72,128]{3,2,1,0...) custom-call(f32[2,2,1008,128]{3,2,1,0:T(8,128)S(1)} %shard_map.85.part_ref, ...), custom_call_target="tpu_custom_call" | custom-call | tf_op jit(solution)/shard_map/pallas_call | solution.py:520
  28.0 0.1 collective-permute-start.4
  28.1 3.8 %collective-permute-start.5 = (f32[2,2,72,128]{3,2,1,0:T(8,128)S(1)}, f32[2,2,72,128]{3,2,1,0:T(8,128)S(1)}, u32[]{:S(2)}, u32[]{:S(2)}) collective-permute-start(f32[2,2,72,128]{3,2,1,0:T(8,128)S(1)} %get-tuple-element.38), channel_id=1, source_target_pairs={{0,12},{1,13},{2,14},{3,15},{4,0},{5,1},{6,2},{7,3},{8,4},{9,5},{1... | collective-permute-start | bytes 442376 | tf_op jit(solution)/shard_map/ppermute | solution.py:452
  31.9 0.0 collective-permute-start.6
  31.9 4.4 %collective-permute-start.7 = (f32[2,2,72,128]{3,2,1,0:T(8,128)S(1)}, f32[2,2,72,128]{3,2,1,0:T(8,128)S(1)}, u32[]{:S(2)}, u32[]{:S(2)}) collective-permute-start(f32[2,2,72,128]{3,2,1,0:T(8,128)S(1)} %get-tuple-element.40), channel_id=1, source_target_pairs={{0,15},{1,0},{2,1},{3,2},{4,3},{5,4},{6,5},{7,6},{8,7},{9,8},{10,9... | collective-permute-start | bytes 442376 | tf_op jit(solution)/shard_map/ppermute | solution.py:452
  36.4 0.0 copy-done.6
  36.4 5.1 %shard_map.88.part_ref = f32[2,2,1008,128]{3,2,1,0:T(8,128)S(1)} custom-call(f32[2,2,1008,128]{3,2,1,0:T(8,128)S(1)} %get-tuple-element.36.f_ref, f32[13,90,24,128]{3,2,1,0:T(8,128)S(1)} %shard_map.84.wb_ref), custom_call_target="tpu_custom_call" | custom-call | flops 53084160 | bytes 3145728 | tf_op jit(solution)/shard_map/pallas_call | solution.py:524
  41.5 0.9 %shard_map.87 = (bf16[1024,768]{1,0:T(8,128)(2,1)S(1)}, bf16[1024,768]{1,0:T(8,128)(2,1)S(1)}) custom-call(f32[2,2,1008,128]{3,2,1,0:T(8,128)S(1)} %get-tuple-element.25.fr_ref.f_ref, f32[2,2,288,128]{3,2,1,0:T(8,128)S(1)} %get-tuple-element.33.save, f32[4,1152]{1,0:T(4,128)S(1)} %get-tuple-element.52.cos_ref, f32[4,1152]{1,0:T(4,128)S(1)} %get-tuple-element.51.sin_ref), custom_call_target="tpu_custom_call" | custom-call | flops 53084160 | bytes 4194304 | tf_op jit(solution)/shard_map/pallas_call | solution.py:526
  42.4 0.0 collective-permute-done.4.rxlo
  42.4 0.0 collective-permute-done.5.rxhi
  42.4 0.0 collective-permute-done.6.rylo
  42.4 0.0 collective-permute-done.7.ryhi
  42.4 6.4 %shard_map.89 = (bf16[1536,512]{1,0:T(8,128)(2,1)S(1)}, bf16[1536,512]{1,0:T(8,128)(2,1)S(1)}, bf16[768,512]{1,0:T(8,128)(2,1)S(1)}, bf16[768,512]{1,0:T(8,128)(2,1)S(1)}) custom-call(f32[2,2,1008,128]{3,2,1,0:T(8,128)S(1)} %shard_map.88.part_ref, f32[312,128]{1,0:T(8,128)S(1)} %get-tuple-element.28.wc_ref, f32[13,90,24,128]{3,2,1,0:T(8,128)S(1)} %shard_map.84.wb_ref, ...), custom_call_target="tpu_custom_call" | custom-call | tf_op jit(solution)/shard_map/pallas_call | solution.py:530
  48.8 8.1 %shard_map.90 = f32[256,2048]{1,0:T(8,128)S(1)} custom-call(bf16[1024,1536]{1,0:T(8,128)(2,1)S(1)} %get-tuple-element.26.ah, bf16[1024,1536]{1,0:T(8,128)(2,1)S(1)} %get-tuple-element.27.al, bf16[1024,768]{1,0:T(8,128)(2,1)S(1)} %get-tuple-element.34.bh, bf16[1024,768]{1,0:T(8,128)(2,1)S(1)} %get-tuple-element.35.bl, ...), custom_call_target="tpu_custom_call" | custom-call | tf_op jit(solution)/shard_map/pallas_call | solution.py:541
  57.0 0.1 dynamic-slice_bitcast_fusion
  57.1 0.1 collective-permute-start.8
  57.2 2.7 %collective-permute-done.8 = f32[8,16,2048]{2,1,0:T(8,128)} collective-permute-done((f32[8,16,2048]{2,1,0:T(8,128)S(1)}, f32[8,16,2048]{2,1,0:T(8,128)}, u32[]{:S(2)}, u32[]{:S(2)}) %collective-permute-start.8) | collective-permute-done | bytes 1048608 | tf_op jit(solution)/shard_map/ppermute | solution.py:489
  59.9 1.3 %bitcast_add_fusion = f32[8,16,2048]{2,1,0:T(8,128)S(1)} fusion(f32[8,16,2048]{2,1,0:T(8,128)} %collective-permute-done.8, f32[8,2,16,2048]{3,2,1,0:T(8,128)S(1)} %bitcast.12, s32[]{:T(128)S(6)} %select_n.111), kind=kLoop, calls=%fused_computation | loop fusion | flops 262144 | bytes 3145732 | tf_op jit(solution)/shard_map/add | solution.py:489
  61.3 0.1 collective-permute-start.9
  61.5 13.9 %collective-permute-done.9 = f32[4,16,2048]{2,1,0:T(8,128)S(1)} collective-permute-done((f32[4,16,2048]{2,1,0:T(8,128)S(1)}, f32[4,16,2048]{2,1,0:T(8,128)S(1)}, u32[]{:S(2)}, u32[]{:S(2)}) %collective-permute-start.9) | collective-permute-done | bytes 524320 | tf_op jit(solution)/shard_map/ppermute | solution.py:489
  75.3 0.1 bitcast_add_fusion.1
  75.5 0.1 collective-permute-start.10
  75.5 0.8 collective-permute-start.11
  76.4 3.0 %collective-permute-start.12 = (f32[1,16,2048]{2,1,0:T(8,128)S(1)}, f32[1,16,2048]{2,1,0:T(8,128)S(1)}, u32[]{:S(2)}, u32[]{:S(2)}) collective-permute-start(f32[1,16,2048]{2,1,0:T(8,128)S(1)} %get-tuple-element.49), channel_id=1, source_target_pairs={{0,12},{1,13},{2,14},{3,15},{4,0},{5,1},{6,2},{7,3},{8,4},{9,5},{1... | collective-permute-start | bytes 393224 | tf_op jit(solution)/shard_map/ppermute | solution.py:489
  79.3 4.3 %collective-permute-done.10 = f32[1,16,2048]{2,1,0:T(8,128)S(1)} collective-permute-done((f32[1,16,2048]{2,1,0:T(8,128)S(1)}, f32[1,16,2048]{2,1,0:T(8,128)S(1)}, u32[]{:S(2)}, u32[]{:S(2)}) %collective-permute-start.10) | collective-permute-done | bytes 131104 | tf_op jit(solution)/shard_map/ppermute | solution.py:489
  83.7 4.0 %collective-permute-done.11 = f32[1,16,2048]{2,1,0:T(8,128)S(1)} collective-permute-done((f32[1,16,2048]{2,1,0:T(8,128)S(1)}, f32[1,16,2048]{2,1,0:T(8,128)S(1)}, u32[]{:S(2)}, u32[]{:S(2)}) %collective-permute-start.11) | collective-permute-done | bytes 131104 | tf_op jit(solution)/shard_map/ppermute | solution.py:489
  87.7 0.0 collective-permute-done.12
  87.7 0.8 reshape_squeeze.3
  (6 shorter events, 0.2 us)
Async XLA Ops:
  0.0 13.3 %copy-start.3 = (s32[1152]{0:T(1024)S(1)}, s32[1152]{0:T(1024)}, u32[]{:S(2)}) copy-start(s32[1152]{0:T(1024)} %constant.173.clone) | copy-start | bytes 13828
  0.0 13.3 %copy-start.4 = (s32[1152]{0:T(1024)S(1)}, s32[1152]{0:T(1024)}, u32[]{:S(2)}) copy-start(s32[1152]{0:T(1024)} %constant.174.clone) | copy-start | bytes 13828
  0.0 13.3 %copy-start.5 = (s32[1152]{0:T(1024)S(1)}, s32[1152]{0:T(1024)}, u32[]{:S(2)}) copy-start(s32[1152]{0:T(1024)} %constant.175.clone) | copy-start | bytes 13828
  0.0 13.4 %copy-start.2 = (s32[1152]{0:T(1024)S(1)}, s32[1152]{0:T(1024)}, u32[]{:S(2)}) copy-start(s32[1152]{0:T(1024)} %constant.176.clone) | copy-start | bytes 13828
  0.0 13.1 %copy-start.1 = (s32[4,3]{1,0:T(4,128)S(1)}, s32[4,3]{1,0:T(4,128)}, u32[]{:S(2)}) copy-start(s32[4,3]{1,0:T(4,128)} %param.10) | copy-start | bytes 148
  1.2 1.5 %copy-start = (f32[2,3,1,288,256]{4,3,2,1,0:T(8,128)S(1)}, f32[2,3,1,288,256]{4,3,2,1,0:T(8,128)}, u32[]{:S(2)}) copy-start(f32[2,3,1,288,256]{4,3,2,1,0:T(8,128)} %param.8) | copy-start | bytes 5308420
  3.5 23.5 %collective-permute-start = (f32[2,2,72,128]{3,2,1,0:T(8,128)S(1)}, f32[2,2,72,128]{3,2,1,0:T(8,128)S(1)}, u32[]{:S(2)}, u32[]{:S(2)}) collective-permute-start(f32[2,2,72,128]{3,2,1,0:T(8,128)S(1)} %get-tuple-element.29), channel_id=1, source_target_pairs={{0,4},{1,5},{2,6},{3,7},{4,8},{5,9},{6,10},{7,11},{8,12},{9,13},{1... | collective-permute-start | bytes 442376 | tf_op jit(solution)/shard_map/ppermute | solution.py:452
  6.6 20.4 %collective-permute-start.1 = (f32[2,2,72,128]{3,2,1,0:T(8,128)S(1)}, f32[2,2,72,128]{3,2,1,0:T(8,128)S(1)}, u32[]{:S(2)}, u32[]{:S(2)}) collective-permute-start(f32[2,2,72,128]{3,2,1,0:T(8,128)S(1)} %get-tuple-element.30), channel_id=1, source_target_pairs={{0,12},{1,13},{2,14},{3,15},{4,0},{5,1},{6,2},{7,3},{8,4},{9,5},{1... | collective-permute-start | bytes 442376 | tf_op jit(solution)/shard_map/ppermute | solution.py:452
  8.7 18.3 %collective-permute-start.2 = (f32[2,2,72,128]{3,2,1,0:T(8,128)S(1)}, f32[2,2,72,128]{3,2,1,0:T(8,128)S(1)}, u32[]{:S(2)}, u32[]{:S(2)}) collective-permute-start(f32[2,2,72,128]{3,2,1,0:T(8,128)S(1)} %get-tuple-element.31), channel_id=1, source_target_pairs={{0,1},{1,2},{2,3},{3,4},{4,5},{5,6},{6,7},{7,8},{8,9},{9,10},{10,1... | collective-permute-start | bytes 442376 | tf_op jit(solution)/shard_map/ppermute | solution.py:452
  8.7 18.3 %collective-permute-start.3 = (f32[2,2,72,128]{3,2,1,0:T(8,128)S(1)}, f32[2,2,72,128]{3,2,1,0:T(8,128)S(1)}, u32[]{:S(2)}, u32[]{:S(2)}) collective-permute-start(f32[2,2,72,128]{3,2,1,0:T(8,128)S(1)} %get-tuple-element.32), channel_id=1, source_target_pairs={{0,15},{1,0},{2,1},{3,2},{4,3},{5,4},{6,5},{7,6},{8,7},{9,8},{10,9... | collective-permute-start | bytes 442376 | tf_op jit(solution)/shard_map/ppermute | solution.py:452
  25.2 11.2 %copy-start.6 = (s32[256]{0:T(256)S(1)}, s32[256]{0:T(256)}, u32[]{:S(2)}) copy-start(s32[256]{0:T(256)} %param.11) | copy-start | bytes 3076
  28.0 14.3 %collective-permute-start.4 = (f32[2,2,72,128]{3,2,1,0:T(8,128)S(1)}, f32[2,2,72,128]{3,2,1,0:T(8,128)S(1)}, u32[]{:S(2)}, u32[]{:S(2)}) collective-permute-start(f32[2,2,72,128]{3,2,1,0:T(8,128)S(1)} %get-tuple-element.37), channel_id=1, source_target_pairs={{0,4},{1,5},{2,6},{3,7},{4,8},{5,9},{6,10},{7,11},{8,12},{9,13},{1... | collective-permute-start | bytes 442376 | tf_op jit(solution)/shard_map/ppermute | solution.py:452
  28.1 14.3 %collective-permute-start.5 = (f32[2,2,72,128]{3,2,1,0:T(8,128)S(1)}, f32[2,2,72,128]{3,2,1,0:T(8,128)S(1)}, u32[]{:S(2)}, u32[]{:S(2)}) collective-permute-start(f32[2,2,72,128]{3,2,1,0:T(8,128)S(1)} %get-tuple-element.38), channel_id=1, source_target_pairs={{0,12},{1,13},{2,14},{3,15},{4,0},{5,1},{6,2},{7,3},{8,4},{9,5},{1... | collective-permute-start | bytes 442376 | tf_op jit(solution)/shard_map/ppermute | solution.py:452
  31.9 10.5 %collective-permute-start.6 = (f32[2,2,72,128]{3,2,1,0:T(8,128)S(1)}, f32[2,2,72,128]{3,2,1,0:T(8,128)S(1)}, u32[]{:S(2)}, u32[]{:S(2)}) collective-permute-start(f32[2,2,72,128]{3,2,1,0:T(8,128)S(1)} %get-tuple-element.39), channel_id=1, source_target_pairs={{0,1},{1,2},{2,3},{3,4},{4,5},{5,6},{6,7},{7,8},{8,9},{9,10},{10,1... | collective-permute-start | bytes 442376 | tf_op jit(solution)/shard_map/ppermute | solution.py:452
  31.9 10.5 %collective-permute-start.7 = (f32[2,2,72,128]{3,2,1,0:T(8,128)S(1)}, f32[2,2,72,128]{3,2,1,0:T(8,128)S(1)}, u32[]{:S(2)}, u32[]{:S(2)}) collective-permute-start(f32[2,2,72,128]{3,2,1,0:T(8,128)S(1)} %get-tuple-element.40), channel_id=1, source_target_pairs={{0,15},{1,0},{2,1},{3,2},{4,3},{5,4},{6,5},{7,6},{8,7},{9,8},{10,9... | collective-permute-start | bytes 442376 | tf_op jit(solution)/shard_map/ppermute | solution.py:452
  57.1 2.9 %collective-permute-start.8 = (f32[8,16,2048]{2,1,0:T(8,128)S(1)}, f32[8,16,2048]{2,1,0:T(8,128)}, u32[]{:S(2)}, u32[]{:S(2)}) collective-permute-start(f32[8,16,2048]{2,1,0:T(8,128)S(1)} %dynamic-slice_bitcast_fusion), channel_id=1, source_target_pairs={{0,1},{1,0},{2,3},{3,2},{4,5},{5,4},{6,7},{7,6},{8,9},{9,8},{10,11... | collective-permute-start | bytes 3145736 | tf_op jit(solution)/shard_map/ppermute | solution.py:489
  61.3 14.0 %collective-permute-start.9 = (f32[4,16,2048]{2,1,0:T(8,128)S(1)}, f32[4,16,2048]{2,1,0:T(8,128)S(1)}, u32[]{:S(2)}, u32[]{:S(2)}) collective-permute-start(f32[4,16,2048]{2,1,0:T(8,128)S(1)} %dynamic-slice_bitcast_fusion.1), channel_id=1, source_target_pairs={{0,2},{1,3},{2,0},{3,1},{4,6},{5,7},{6,4},{7,5},{8,10},{9,11},{10,... | collective-permute-start | bytes 1572872 | tf_op jit(solution)/shard_map/ppermute | solution.py:489
  75.5 8.2 %collective-permute-start.10 = (f32[1,16,2048]{2,1,0:T(8,128)S(1)}, f32[1,16,2048]{2,1,0:T(8,128)S(1)}, u32[]{:S(2)}, u32[]{:S(2)}) collective-permute-start(f32[1,16,2048]{2,1,0:T(8,128)S(1)} %get-tuple-element.48), channel_id=1, source_target_pairs={{0,4},{1,5},{2,6},{3,7},{4,8},{5,9},{6,10},{7,11},{8,12},{9,13},{1... | collective-permute-start | bytes 393224 | tf_op jit(solution)/shard_map/ppermute | solution.py:489
  75.5 12.2 %collective-permute-start.11 = (f32[1,16,2048]{2,1,0:T(8,128)S(1)}, f32[1,16,2048]{2,1,0:T(8,128)S(1)}, u32[]{:S(2)}, u32[]{:S(2)}) collective-permute-start(f32[1,16,2048]{2,1,0:T(8,128)S(1)} %get-tuple-element.50), channel_id=1, source_target_pairs={{0,8},{1,9},{2,10},{3,11},{4,12},{5,13},{6,14},{7,15},{8,0},{9,1},... | collective-permute-start | bytes 393224 | tf_op jit(solution)/shard_map/ppermute | solution.py:489
  76.4 11.3 %collective-permute-start.12 = (f32[1,16,2048]{2,1,0:T(8,128)S(1)}, f32[1,16,2048]{2,1,0:T(8,128)S(1)}, u32[]{:S(2)}, u32[]{:S(2)}) collective-permute-start(f32[1,16,2048]{2,1,0:T(8,128)S(1)} %get-tuple-element.49), channel_id=1, source_target_pairs={{0,12},{1,13},{2,14},{3,15},{4,0},{5,1},{6,2},{7,3},{8,4},{9,5},{1... | collective-permute-start | bytes 393224 | tf_op jit(solution)/shard_map/ppermute | solution.py:489

commit v3 on v2

--- a/solution.py
+++ b/solution.py
@@ -29,12 +29,13 @@
 VMEM_LIMIT = 12 * 2**20
 
 
-def call(kernel, outs, scratch=(), flops=0, moved=0, inputs=1, **kwargs):
+def call(kernel, outs, scratch=(), flops=0, moved=0, inputs=1, scalars=0, off_chip=0, **kwargs):
     on_chip = pl.BlockSpec(memory_space=pltpu.VMEM)
+    first = [pl.BlockSpec(memory_space=pltpu.SMEM)] * scalars + [pl.BlockSpec(memory_space=pltpu.HBM)] * off_chip
     return pl.pallas_call(
         kernel,
         out_shape=outs,
-        in_specs=[on_chip] * inputs,
+        in_specs=first + [on_chip] * inputs,
         out_specs=jax.tree.map(lambda _: on_chip, outs),
         scratch_shapes=list(scratch),
         compiler_params=pltpu.CompilerParams(vmem_limit_bytes=VMEM_LIMIT),
@@ -224,15 +225,39 @@
     return acc
 
 
+def hop_column(weights, col, field, adjoint, acc, minus):
+    for row in range(3):
+        at = 3 * col + row if adjoint else 3 * row + col
+        real, imag = weights(at), weights(at + 9)
+        terms = (
+            (0, real * field[0], False),
+            (0, imag * field[1], not adjoint),
+            (1, real * field[1], False),
+            (1, imag * field[0], adjoint),
+        )
+        for part, value, negative in terms:
+            before = acc[part][row][0]
+            if before is None:
+                acc[part][row][0] = -value if negative != minus else value
+            else:
+                acc[part][row][0] = before - value if negative != minus else before + value
+
+
 def spread_kernel(wc_ref, wb_ref):
-    def layer(x, carry):
-        table = wc_ref[pl.ds(pl.multiple_of(x * LAYER, 8), LAYER), :]
-        for column in range(WIDE):
-            source = column if column < 18 else column + CYF - 18
-            wb_ref[x, column] = spread(table, source)
-        return carry
-
-    lax.fori_loop(0, TLX + 1, layer, 0)
+    rest = wc_ref[...]
+    terms = []
+    for _ in range(2):
+        terms.append(rest.astype(jnp.bfloat16))
+        rest = rest - terms[-1].astype(jnp.float32)
+    terms = jnp.concatenate(terms, axis=1)
+    row = lax.broadcasted_iota(jnp.int32, (LANES, 2 * LANES), 0)
+    right = lax.broadcasted_iota(jnp.int32, (LANES, 2 * LANES), 1) // LANES
+    for column in range(0, WIDE, 2):
+        source = column if column < 18 else column + CYF - 18
+        ones = jnp.where(row == source + right, 1.0, 0.0).astype(jnp.bfloat16)
+        copies = dot(terms, jnp.concatenate([ones] * 2, axis=0))
+        for k in range(2):
+            wb_ref[:, column + k] = copies[:, k * LANES : (k + 1) * LANES].reshape(TLX + 1, LAYER, LANES)
 
 
 def empty_acc(halves):
@@ -338,47 +363,54 @@
             phased(real, imag, half, HEAD + at, at, TAIL, cos_ref, sin_ref, ah_ref, al_ref)
 
 
-def displace_kernel(part_ref, wc_ref, wb_ref, rxlo, rxhi, rylo, ryhi, mask_ref, sh_ref, sl_ref, th_ref, tl_ref, twice, shift, rolled):
+def displace_kernel(part_ref, wc_ref, wb_ref, rxlo, rxhi, rylo, ryhi, dir_ref, sh_ref, sl_ref, th_ref, tl_ref, twice, shift, rolled, *, scale):
     twice[...] = part_ref[...]
     cross(twice, wc_ref, rxlo, rxhi, rylo, ryhi)
     halves = range(twice.shape[1])
+
+    def along(which, half, rows=8):
+        return jnp.broadcast_to(dir_ref[0:1, half * LANES : (half + 1) * LANES], (rows, LANES)) == which
 
     def layer(x, carry):
         into = pl.multiple_of(x * XROWS, 8)
         for half in halves:
             roll_layer(twice, half, pl.multiple_of((x + 1) * XROWS, 8), rolled)
-
-        def tiles(tile, carry):
+        for tile in range(LAYER // 8):
             hops, _ = layer_hops(twice, wb_ref, rolled, x, tile, BZD)
-            total = empty_acc(halves)
-            for which in range(3):
-                acc = empty_acc(halves)
-                for weights, column, load, adjoint, direction in hops:
-                    if direction == which:
-                        hop_all(weights, column, load, adjoint, halves, acc, adjoint)
-                for half in halves:
-                    lanes = slice(half * LANES, (half + 1) * LANES)
-                    mask = jnp.broadcast_to(mask_ref[which : which + 1, lanes], (8, LANES))
-                    for part in range(2):
-                        for row in range(3):
-                            value = mask * acc[part][row][half]
-                            before = total[part][row][half]
-                            total[part][row][half] = value if before is None else before + value
-            for part in range(2):
-                for colour in range(3):
-                    for half in halves:
+            (ahead_x, bx, load_xf, _, _), (below, _, load_xb, _, _) = hops[0], hops[1]
+            (table, byf, load_yf, _, _), (_, byb, load_yb, _, _), (_, bz, load_z, _, _) = hops[2:]
+            for half in halves:
+                is_x, is_y = along(0, half), along(1, half)
+                acc = empty_acc([0])
+                for col in range(3):
+                    ahead = [
+                        jnp.where(is_x, load_xf(p, col, half), jnp.where(is_y, load_yf(p, col, half), load_z(p, col, half)))
+                        for p in range(2)
+                    ]
+                    behind = [
+                        jnp.where(is_x, load_xb(p, col, half), jnp.where(is_y, load_yb(p, col, half), 0.0))
+                        for p in range(2)
+                    ]
+
+                    def forward(at):
+                        return jnp.where(is_x, ahead_x(bx + at), jnp.where(is_y, table(byf + at), table(bz + at)))
+
+                    def backward(at):
+                        return jnp.where(is_x, below(bx + at), table(byb + at))
+
+                    hop_column(forward, col, ahead, False, acc, False)
+                    hop_column(backward, col, behind, True, acc, True)
+                for part in range(2):
+                    for colour in range(3):
                         at = pl.ds(pl.multiple_of(into + colour * LAYER + 8 * tile, 8), 8)
-                        shift[part, half, at, :] = total[part][colour][half]
-            return carry
-
-        return lax.fori_loop(0, LAYER // 8, tiles, carry, unroll=True)
+                        shift[part, half, at, :] = scale * acc[part][colour][0]
+        return carry
 
     lax.fori_loop(0, TLX, layer, 0)
     last = TLX * XROWS
     for half in halves:
-        lanes = slice(half * LANES, (half + 1) * LANES)
-        mask_x = jnp.broadcast_to(mask_ref[0:1, lanes], (XROWS, LANES))
-        mask_y = jnp.broadcast_to(mask_ref[1:2, lanes], (TLX, LANES))
+        mask_x = jnp.where(along(0, half, XROWS), scale, 0.0)
+        mask_y = jnp.where(along(1, half, TLX), scale, 0.0)
         for part in range(2):
             shift[part, half, MAIN : MAIN + XROWS, :] = mask_x * twice[part, half, XROWS : 2 * XROWS, :]
             shift[part, half, MAIN + XROWS : MAIN + 2 * XROWS, :] = -mask_x * twice[part, half, last : last + XROWS, :]
@@ -415,6 +447,51 @@
 def meson_kernel(ah, al, bh, bl, sh, sl, th, tl, out_ref):
     total = dot(ah[...], sh[...]) + dot(ah[...], sl[...]) + dot(al[...], sh[...])
     out_ref[...] = total + dot(bh[...], th[...]) + dot(bh[...], tl[...]) + dot(bl[...], th[...])
+
+
+def product(blocks, moments, refs):
+    ah, al, bh, bl, sh, sl, th, tl = refs
+    nev = ah.shape[0] // moments
+    size = blocks[1]
+
+    def rows(ref):
+        picked = [ref[pl.ds(pl.multiple_of(m * nev + b, size), size), :] for m in range(moments) for b in blocks[0]]
+        return jnp.concatenate(picked, axis=0)
+
+    ahv, alv, bhv, blv = rows(ah), rows(al), rows(bh), rows(bl)
+    total = dot(ahv, sh[...]) + dot(ahv, sl[...]) + dot(alv, sh[...])
+    return total + dot(bhv, th[...]) + dot(bhv, tl[...]) + dot(blv, th[...])
+
+
+def put(out_ref, value, count, moments, added=None):
+    size, width = out_ref.shape[1], value.shape[-1]
+    for m in range(moments):
+        for k in range(count):
+            block = value[(m * count + k) * size : (m * count + k + 1) * size]
+            lanes = slice(m * width, (m + 1) * width)
+            if added is not None:
+                block = block + added(k, lanes)
+            out_ref[k, :, lanes] = block
+
+
+def owners(groups, size, cores, turns):
+    position = lax.axis_index("site")
+    core, y, z = position % 2, position // 2 % 2, position // 4
+    core = (core + cores) % 2
+    return [((z + g) % groups * 4 + (y + turn) % 2 * 2 + core) * size for g in range(groups) for turn in turns]
+
+
+def piece_kernel(*refs, moments, groups, cores, turns):
+    out_ref = refs[-1]
+    size = out_ref.shape[1]
+    blocks = owners(groups, size, cores, turns)
+    put(out_ref, product((blocks, size), moments, refs[:-1]), len(blocks), moments)
+
+
+def merge_kernel(mine, theirs, *outs, picks):
+    for out_ref, pairs in zip(outs, picks):
+        for k, (a, b) in enumerate(pairs):
+            out_ref[k] = mine[a] + theirs[b]
 
 
 def phases(momenta, position, devices, tiles):
@@ -525,10 +602,8 @@
     rows = pltpu.VMEM((2, TAIL, LANES), jnp.float32)
     bh, bl = call(tail_kernel, (tail, tail), [rows], flops, 4 << 20, 4)(fr, save, cosine, sine)
     scale = 1.0 / math.sqrt(3.0 * TLX * tiles * TLY * tiles * LZ)
-    which = jnp.arange(3, dtype=jnp.int32)[:, None]
-    masks = jnp.where(directions[None, :] == which, jnp.float32(scale), jnp.float32(0.0))
-    sh, sl, th, tl = call(
-        displace_kernel,
+    operands = call(
+        functools.partial(displace_kernel, scale=scale),
         (bf16(2 * HEAD, 2 * nev), bf16(2 * HEAD, 2 * nev), bf16(2 * TAIL, 2 * nev), bf16(2 * TAIL, 2 * nev)),
         [
             pltpu.VMEM((2, halves, PADDED, LANES), jnp.float32),
@@ -536,20 +611,74 @@
             rolled,
         ],
         inputs=8,
-    )(twice, wc, wb, *received, masks)
+    )(twice, wc, wb, *received, directions[None, :])
+    operands = (ah, al, bh, bl) + tuple(operands)
+    size, columns = nev // devices, moments * 2 * nev
+    if size % 16 == 0 and devices % 8 == 0:
+        total = pieces(operands, position, devices, moments, size, columns)
+    else:
+        total = whole_product(operands, position, devices, moments, nev)
+    return total.reshape(size, moments, 2, nev)
+
+
+def whole_product(operands, position, devices, moments, nev):
     whole = lambda a: pl.BlockSpec(a.shape, lambda m: (0, 0))
     partial = pl.pallas_call(
         meson_kernel,
         out_shape=f32(nev, moments * 2 * nev),
         grid=(moments,),
-        in_specs=[pl.BlockSpec((nev, 2 * HEAD), lambda m: (m, 0))] * 2
-        + [pl.BlockSpec((nev, 2 * TAIL), lambda m: (m, 0))] * 2
-        + [whole(sh), whole(sl), whole(th), whole(tl)],
+        in_specs=[pl.BlockSpec((nev, a.shape[1]), lambda m: (m, 0)) for a in operands[:4]]
+        + [whole(a) for a in operands[4:]],
         out_specs=pl.BlockSpec((nev, 2 * nev), lambda m: (0, m)),
-        compiler_params=pltpu.CompilerParams(vmem_limit_bytes=VMEM_LIMIT),
-    )(ah, al, bh, bl, sh, sl, th, tl)
-    total = scatter_sum(partial.reshape(devices, nev // devices, moments * 2 * nev), position, devices)
-    return total.reshape(nev // devices, moments, 2, nev)
+        compiler_params=pltpu.CompilerParams(vmem_limit_bytes=40 * 2**20),
+    )(*operands)
+    return scatter_sum(partial.reshape(devices, nev // devices, moments * 2 * nev), position, devices)
+
+
+def pieces(operands, position, devices, moments, size, columns):
+    groups = devices // 4
+    shared = dict(moments=moments, groups=groups)
+    cost = dict(flops=2 * 3 * size * groups * moments * 4 * (HEAD + TAIL) * 256, moved=1 << 20)
+    block = lambda count: f32(count, size, columns)
+    out = call(
+        functools.partial(piece_kernel, cores=1, turns=(0, 1), **shared), block(2 * groups), (), inputs=8, **cost
+    )(*operands)
+    swapped = lax.ppermute(out, "site", [(i, i ^ 1) for i in range(devices)])
+    far = call(
+        functools.partial(piece_kernel, cores=0, turns=(1,), **shared), block(groups), (), inputs=8, **cost
+    )(*operands)
+    early = list(range(1, groups // 2 + 1))
+    late = list(range(groups // 2 + 1, groups)) + [0]
+    first, second = call(
+        functools.partial(merge_kernel, picks=[[(g, 2 * g + 1) for g in early], [(g, 2 * g + 1) for g in late]]),
+        (block(len(early)), block(len(late))),
+        inputs=2,
+    )(far, swapped)
+    flip = [(i, i ^ 2) for i in range(devices)]
+    first = lax.ppermute(first, "site", flip)
+    second = lax.ppermute(second, "site", flip)
+    near = call(
+        functools.partial(piece_kernel, cores=0, turns=(0,), **shared), block(groups), (), inputs=8, **cost
+    )(*operands)
+    near = call(
+        functools.partial(merge_kernel, picks=[[(g, 2 * g) for g in range(groups)]]), (block(groups),), inputs=2
+    )(near, swapped)[0]
+    total = None
+    arrived = []
+    for steps, got in ((early, first), (late, second)):
+        sums = call(
+            functools.partial(merge_kernel, picks=[[(g, k)] for k, g in enumerate(steps)]),
+            tuple(block(1) for _ in steps),
+            inputs=2,
+        )(near, got)
+        for step, value in zip(steps, sums):
+            if step == 0:
+                total = value
+            else:
+                arrived.append(lax.ppermute(value, "site", [(i, (i + 4 * step) % devices) for i in range(devices)]))
+    for value in arrived:
+        total = total + value
+    return total[0]
 
 
 def solution(mesh):

time: 88.7 us -> 71.1 us (0.80)
  waiting for transfers between devices: 25 us -> 17.4 us
  Pallas kernels: 35.6 us -> 29 us
  starting transfers between devices: 22 us -> 20.3 us
  other arithmetic: 2.89 us -> 1.47 us
    ppermute x5 -> x6, waiting for transfers between devices: 25 us -> 17.4 us  [the longest x3 7.05 us: pieces(): lax.ppermute(value, 'site', [(i, (i + 4 * step) % devices) for i in range...]
    pallas_call x1, Pallas kernels: 6.39 us -> 2.11 us  [on_device(): call(spread_kernel, f32(TLX + 1, WIDE, LAYER, LANES), (), flops >> 4, 1 <...]
    pallas_call x2 -> x8, Pallas kernels: 14.5 us -> 12.2 us  [the longest x1 4.27 us: on_device(): call(functools.partial(displace_kernel, scale=scale), (bf16(2 * HEAD, 2 *...]
    ppermute x5 -> x6, starting transfers between devices: 4.01 us -> 2.34 us  [the longest x1 2.01 us: pieces(): second = lax.ppermute(second, 'site', flip)]
    add x3 -> x1, other arithmetic: 1.42 us -> 0.03 us  [pieces(): total = total + value]
  transfers between devices with their start and end apart: 13 -> 14, of which waited for: 4 -> 6; matrix products, arithmetic and copies ran while one was open for 1% -> 1% of each run, Pallas kernels for 22% -> 27%
where the time goes in v3:
time: 71.1 us; the launch traced here: 71 us
  Pallas kernels  29 us (41%)
  starting transfers between devices  20.3 us (29%)
  waiting for transfers between devices  17.4 us (24%)
  local copies, waits for them, and re-layouts  2.5 us (4%)
  other arithmetic  1.47 us (2%)
    ppermute x8, starting transfers between devices, send(): lax.ppermute(block, 'site', [(i, (i + distance) % devices) for i in range...  18 us
    ppermute x3, waiting for transfers between devices, pieces(): lax.ppermute(value, 'site', [(i, (i + 4 * step) % devices) for i in range...  7.05 us
    pallas_call x1, Pallas kernels, on_device(): once = call(smear_kernel, padded, [rolled], flops, 3 << 20, 2)(fr, wb)  5.12 us
    pallas_call x1, Pallas kernels, on_device(): twice = call(smear_kernel, padded, [rolled], flops, 3 << 20, 2)(once, wb)  5.11 us
    ppermute x1, waiting for transfers between devices, pieces(): first = lax.ppermute(first, 'site', flip)  5.1 us
    ppermute x1, waiting for transfers between devices, pieces(): second = lax.ppermute(second, 'site', flip)  4.61 us
    pallas_call x1, Pallas kernels, on_device(): call(functools.partial(displace_kernel, scale=scale), (bf16(2 * HEAD, 2 *...  4.27 us
    pallas_call x1, Pallas kernels, pieces(): call(functools.partial(piece_kernel, cores=1, turns=(0, 1), **shared), bl...  3.81 us
  transfers between devices with their start and end apart: 14, of which 6 were waited for; matrix products, arithmetic and copies ran while one was open for 1% of the time, Pallas kernels for 27%

profile of v3, /device:TPU:0, one launch (start us, length us, event | category | flops | bytes accessed | tf_op | source)
XLA Modules:
  0.0 71.0 jit_solution(10106542434924548064)
XLA Ops:
  0.0 0.0 copy-start.4
  0.0 0.0 copy-start.5
  0.0 0.0 copy-start.6
  0.0 1.1 %reduce = f32[3,2,3,3,288]{4,3,2,1,0:T(4,128)S(1)} reduce(f32[3,2,3,3,1,288]{5,4,3,2,1,0:T(1,128)} %param.9, f32[]{:T(128)} %constant.92), dimensions={4}, to_apply=%param.9.reduce_sub_computation | reduce | bytes 124420 | tf_op args[1]
  1.2 0.0 copy-start
  1.2 1.5 %copy-done = f32[2,3,1,288,256]{4,3,2,1,0:T(8,128)S(1)} copy-done((f32[2,3,1,288,256]{4,3,2,1,0:T(8,128)S(1)}, f32[2,3,1,288,256]{4,3,2,1,0:T(8,128)}, u32[]{:S(2)}) %copy-start) | copy-done | bytes 1769496
  2.7 0.8 %shard_map.82 = (f32[2,2,1008,128]{3,2,1,0:T(8,128)S(1)}, f32[312,128]{1,0:T(8,128)S(1)}, f32[2,2,72,128]{3,2,1,0:T(8,128)S(1)}, f32[2,2,72,128]{3,2,1,0:T(8,128...) custom-call(f32[6,288,256]{2,1,0:T(8,128)S(1)} %bitcast.2, f32[54,288]{1,0:T(8,128)S(1)} %reshape.10.l_ref), custom_call_target="tpu_custom_call" | custom-call | tf_op jit(solution)/shard_map/pallas_call | solution.py:582
  3.4 3.1 %collective-permute-start = (f32[2,2,72,128]{3,2,1,0:T(8,128)S(1)}, f32[2,2,72,128]{3,2,1,0:T(8,128)S(1)}, u32[]{:S(2)}, u32[]{:S(2)}) collective-permute-start(f32[2,2,72,128]{3,2,1,0:T(8,128)S(1)} %get-tuple-element.35), channel_id=1, source_target_pairs={{0,4},{1,5},{2,6},{3,7},{4,8},{5,9},{6,10},{7,11},{8,12},{9,13},{1... | collective-permute-start | bytes 442376 | tf_op jit(solution)/shard_map/ppermute | solution.py:529
  6.5 2.1 %collective-permute-start.1 = (f32[2,2,72,128]{3,2,1,0:T(8,128)S(1)}, f32[2,2,72,128]{3,2,1,0:T(8,128)S(1)}, u32[]{:S(2)}, u32[]{:S(2)}) collective-permute-start(f32[2,2,72,128]{3,2,1,0:T(8,128)S(1)} %get-tuple-element.36), channel_id=1, source_target_pairs={{0,12},{1,13},{2,14},{3,15},{4,0},{5,1},{6,2},{7,3},{8,4},{9,5},{1... | collective-permute-start | bytes 442376 | tf_op jit(solution)/shard_map/ppermute | solution.py:529
  8.6 0.0 collective-permute-start.2
  8.6 4.4 %collective-permute-start.3 = (f32[2,2,72,128]{3,2,1,0:T(8,128)S(1)}, f32[2,2,72,128]{3,2,1,0:T(8,128)S(1)}, u32[]{:S(2)}, u32[]{:S(2)}) collective-permute-start(f32[2,2,72,128]{3,2,1,0:T(8,128)S(1)} %get-tuple-element.38), channel_id=1, source_target_pairs={{0,15},{1,0},{2,1},{3,2},{4,3},{5,4},{6,5},{7,6},{8,7},{9,8},{10,9... | collective-permute-start | bytes 442376 | tf_op jit(solution)/shard_map/ppermute | solution.py:529
  13.1 0.0 copy-done.4
  13.1 0.0 copy-done.5
  13.1 0.0 copy-done.6
  13.1 2.1 %shard_map.84.wb_ref = f32[13,90,24,128]{3,2,1,0:T(8,128)S(1)} custom-call(f32[312,128]{1,0:T(8,128)S(1)} %get-tuple-element.34.wc_ref), custom_call_target="tpu_custom_call" | custom-call | flops 3317760 | bytes 1048576 | tf_op jit(solution)/shard_map/pallas_call | solution.py:590
  15.2 0.0 copy-start.2
  15.2 5.1 %shard_map.85.part_ref = f32[2,2,1008,128]{3,2,1,0:T(8,128)S(1)} custom-call(f32[2,2,1008,128]{3,2,1,0:T(8,128)S(1)} %get-tuple-element.31.fr_ref.f_ref, f32[13,90,24,128]{3,2,1,0:T(8,128)S(1)} %shard_map.84.wb_ref), custom_call_target="tpu_custom_call" | custom-call | flops 53084160 | bytes 3145728 | tf_op jit(solution)/shard_map/pallas_call | solution.py:592
  20.4 0.0 copy-done.2
  20.4 0.0 copy-start.3
  20.4 0.2 slice_reduce_fusion.2
  20.6 0.0 collective-permute-done.rxlo
  20.6 0.0 collective-permute-done.1.rxhi
  20.6 0.0 collective-permute-done.2.rylo
  20.6 0.0 collective-permute-done.3.ryhi
  20.6 1.1 %shard_map.86 = (f32[2,2,1008,128]{3,2,1,0:T(8,128)S(1)}, f32[2,2,288,128]{3,2,1,0:T(8,128)S(1)}, f32[2,2,72,128]{3,2,1,0:T(8,128)S(1)}, f32[2,2,72,128]{3,2,1,0...) custom-call(f32[2,2,1008,128]{3,2,1,0:T(8,128)S(1)} %shard_map.85.part_ref, ...), custom_call_target="tpu_custom_call" | custom-call | tf_op jit(solution)/shard_map/pallas_call | solution.py:597
  21.7 0.1 collective-permute-start.4
  21.8 3.8 %collective-permute-start.5 = (f32[2,2,72,128]{3,2,1,0:T(8,128)S(1)}, f32[2,2,72,128]{3,2,1,0:T(8,128)S(1)}, u32[]{:S(2)}, u32[]{:S(2)}) collective-permute-start(f32[2,2,72,128]{3,2,1,0:T(8,128)S(1)} %get-tuple-element.44), channel_id=1, source_target_pairs={{0,12},{1,13},{2,14},{3,15},{4,0},{5,1},{6,2},{7,3},{8,4},{9,5},{1... | collective-permute-start | bytes 442376 | tf_op jit(solution)/shard_map/ppermute | solution.py:529
  25.6 0.0 collective-permute-start.6
  25.6 4.4 %collective-permute-start.7 = (f32[2,2,72,128]{3,2,1,0:T(8,128)S(1)}, f32[2,2,72,128]{3,2,1,0:T(8,128)S(1)}, u32[]{:S(2)}, u32[]{:S(2)}) collective-permute-start(f32[2,2,72,128]{3,2,1,0:T(8,128)S(1)} %get-tuple-element.46), channel_id=1, source_target_pairs={{0,15},{1,0},{2,1},{3,2},{4,3},{5,4},{6,5},{7,6},{8,7},{9,8},{10,9... | collective-permute-start | bytes 442376 | tf_op jit(solution)/shard_map/ppermute | solution.py:529
  30.0 0.0 copy-done.3
  30.0 0.3 fusion.21
  30.3 1.7 %shard_map.83 = (bf16[1024,1536]{1,0:T(8,128)(2,1)S(1)}, bf16[1024,1536]{1,0:T(8,128)(2,1)S(1)}) custom-call(f32[2,2,1008,128]{3,2,1,0:T(8,128)S(1)} %get-tuple-element.31.fr_ref.f_ref, f32[4,1152]{1,0:T(4,128)S(1)} %get-tuple-element.61.cos_ref, f32[4,1152]{1,0:T(4,128)S(1)} %get-tuple-element.60.sin_ref), custom_call_target="tpu_custom_call" | custom-call | flops 53084160 | bytes 8388608 | tf_op jit(solution)/shard_map/pallas_call | solution.py:596
  32.0 5.1 %shard_map.88.part_ref = f32[2,2,1008,128]{3,2,1,0:T(8,128)S(1)} custom-call(f32[2,2,1008,128]{3,2,1,0:T(8,128)S(1)} %get-tuple-element.42.f_ref, f32[13,90,24,128]{3,2,1,0:T(8,128)S(1)} %shard_map.84.wb_ref), custom_call_target="tpu_custom_call" | custom-call | flops 53084160 | bytes 3145728 | tf_op jit(solution)/shard_map/pallas_call | solution.py:601
  37.1 0.0 copy-start.1
  37.1 0.9 %shard_map.87 = (bf16[1024,768]{1,0:T(8,128)(2,1)S(1)}, bf16[1024,768]{1,0:T(8,128)(2,1)S(1)}) custom-call(f32[2,2,1008,128]{3,2,1,0:T(8,128)S(1)} %get-tuple-element.31.fr_ref.f_ref, f32[2,2,288,128]{3,2,1,0:T(8,128)S(1)} %get-tuple-element.39.save, f32[4,1152]{1,0:T(4,128)S(1)} %get-tuple-element.61.cos_ref, f32[4,1152]{1,0:T(4,128)S(1)} %get-tuple-element.60.sin_ref), custom_call_target="tpu_custom_call" | custom-call | flops 53084160 | bytes 4194304 | tf_op jit(solution)/shard_map/pallas_call | solution.py:603
  38.0 0.0 collective-permute-done.4.rxlo
  38.1 0.0 collective-permute-done.5.rxhi
  38.1 0.0 collective-permute-done.6.rylo
  38.1 0.0 collective-permute-done.7.ryhi
  38.1 0.0 copy-done.1
  38.1 4.3 %shard_map.89 = (bf16[1536,512]{1,0:T(8,128)(2,1)S(1)}, bf16[1536,512]{1,0:T(8,128)(2,1)S(1)}, bf16[768,512]{1,0:T(8,128)(2,1)S(1)}, bf16[768,512]{1,0:T(8,128)(2,1)S(1)}) custom-call(f32[2,2,1008,128]{3,2,1,0:T(8,128)S(1)} %shard_map.88.part_ref, f32[312,128]{1,0:T(8,128)S(1)} %get-tuple-element.34.wc_ref, f32[13,90,24,128]{3,2,1,0:T(8,128)S(1)} %shard_map.84.wb_ref, ...), custom_call_target="tpu_custom_call" | custom-call | tf_op jit(solution)/shard_map/pallas_call | solution.py:605
  42.4 3.8 %shard_map.91 = f32[8,16,2048]{2,1,0:T(8,128)S(1)} custom-call(bf16[1024,1536]{1,0:T(8,128)(2,1)S(1)} %get-tuple-element.32.refs_0_, bf16[1024,1536]{1,0:T(8,128)(2,1)S(1)} %get-tuple-element.33.refs_1_, bf16[1024,768]{1,0:T(8,128)(2,1)S(1)} %get-tuple-element.40.refs_2_, bf16[1024,768]{1,0:T(8,128)(2,1)S(1)} %get-tuple-element.41.refs_3_, ...), custom_call_target="tpu_custom_call" | custom-call | flops 1811939328 | bytes 1048576 | tf_op jit(solution)/shard_map/pallas_call | solution.py:643
  46.2 0.1 collective-permute-start.8
  46.3 2.0 %shard_map.93.mine = f32[4,16,2048]{2,1,0:T(8,128)S(1)} custom-call(bf16[1024,1536]{1,0:T(8,128)(2,1)S(1)} %get-tuple-element.32.refs_0_, bf16[1024,1536]{1,0:T(8,128)(2,1)S(1)} %get-tuple-element.33.refs_1_, bf16[1024,768]{1,0:T(8,128)(2,1)S(1)} %get-tuple-element.40.refs_2_, bf16[1024,768]{1,0:T(8,128)(2,1)S(1)} %get-tuple-element.41.refs_3_, ...), custom_call_target="tpu_custom_call" | custom-call | flops 1811939328 | bytes 1048576 | tf_op jit(solution)/shard_map/pallas_call | solution.py:647
  48.2 0.7 collective-permute-done.8.theirs
  48.9 0.1 shard_map.94
  49.0 0.1 collective-permute-start.10
  49.0 2.0 %collective-permute-start.9 = (f32[2,16,2048]{2,1,0:T(8,128)S(1)}, f32[2,16,2048]{2,1,0:T(8,128)S(1)}, u32[]{:S(2)}, u32[]{:S(2)}) collective-permute-start(f32[2,16,2048]{2,1,0:T(8,128)S(1)} %get-tuple-element.51), channel_id=1, source_target_pairs={{0,2},{1,3},{2,0},{3,1},{4,6},{5,7},{6,4},{7,5},{8,10},{9,11},{10,... | collective-permute-start | bytes 786440 | tf_op jit(solution)/shard_map/ppermute | solution.py:659
  51.1 2.0 %shard_map.90.mine = f32[4,16,2048]{2,1,0:T(8,128)S(1)} custom-call(bf16[1024,1536]{1,0:T(8,128)(2,1)S(1)} %get-tuple-element.32.refs_0_, bf16[1024,1536]{1,0:T(8,128)(2,1)S(1)} %get-tuple-element.33.refs_1_, bf16[1024,768]{1,0:T(8,128)(2,1)S(1)} %get-tuple-element.40.refs_2_, bf16[1024,768]{1,0:T(8,128)(2,1)S(1)} %get-tuple-element.41.refs_3_, ...), custom_call_target="tpu_custom_call" | custom-call | flops 1811939328 | bytes 1048576 | tf_op jit(solution)/shard_map/pallas_call | solution.py:660
  53.0 0.1 shard_map.92.mine
  53.1 5.1 %collective-permute-done.10.theirs = f32[2,16,2048]{2,1,0:T(8,128)S(1)} collective-permute-done((f32[2,16,2048]{2,1,0:T(8,128)S(1)}, f32[2,16,2048]{2,1,0:T(8,128)S(1)}, u32[]{:S(2)}, u32[]{:S(2)}) %collective-permute-start.10) | collective-permute-done | bytes 262176 | tf_op jit(solution)/shard_map/ppermute | solution.py:658
  58.2 0.1 collective-permute-start.11
  58.3 0.1 collective-permute-start.12
  58.4 4.6 %collective-permute-done.9.theirs = f32[2,16,2048]{2,1,0:T(8,128)S(1)} collective-permute-done((f32[2,16,2048]{2,1,0:T(8,128)S(1)}, f32[2,16,2048]{2,1,0:T(8,128)S(1)}, u32[]{:S(2)}, u32[]{:S(2)}) %collective-permute-start.9) | collective-permute-done | bytes 262176 | tf_op jit(solution)/shard_map/ppermute | solution.py:659
  63.0 0.1 collective-permute-start.13
  63.1 3.4 %collective-permute-done.11 = f32[1,16,2048]{2,1,0:T(8,128)S(1)} collective-permute-done((f32[1,16,2048]{2,1,0:T(8,128)S(1)}, f32[1,16,2048]{2,1,0:T(8,128)S(1)}, u32[]{:S(2)}, u32[]{:S(2)}) %collective-permute-start.11) | collective-permute-done | bytes 131104 | tf_op jit(solution)/shard_map/ppermute | solution.py:678
  66.5 3.1 %collective-permute-done.12 = f32[1,16,2048]{2,1,0:T(8,128)S(1)} collective-permute-done((f32[1,16,2048]{2,1,0:T(8,128)S(1)}, f32[1,16,2048]{2,1,0:T(8,128)S(1)}, u32[]{:S(2)}, u32[]{:S(2)}) %collective-permute-start.12) | collective-permute-done | bytes 131104 | tf_op jit(solution)/shard_map/ppermute | solution.py:678
  69.7 0.5 collective-permute-done.13
  70.2 0.8 %reshape_squeeze.3 = f32[16,4,2,256]{3,2,1,0:T(2,128)} reshape(f32[1,16,2048]{2,1,0:T(8,128)S(1)} %add_add_fusion) | data formatting | bytes 262144 | tf_op jit(solution)/shard_map/reshape;squeeze | solution.py:621
  (5 shorter events, 0.2 us)
Async XLA Ops:
  0.0 13.1 %copy-start.4 = (s32[1152]{0:T(1024)S(1)}, s32[1152]{0:T(1024)}, u32[]{:S(2)}) copy-start(s32[1152]{0:T(1024)} %constant.86.clone) | copy-start | bytes 13828
  0.0 13.1 %copy-start.5 = (s32[1152]{0:T(1024)S(1)}, s32[1152]{0:T(1024)}, u32[]{:S(2)}) copy-start(s32[1152]{0:T(1024)} %constant.87.clone) | copy-start | bytes 13828
  0.0 13.1 %copy-start.6 = (s32[1152]{0:T(1024)S(1)}, s32[1152]{0:T(1024)}, u32[]{:S(2)}) copy-start(s32[1152]{0:T(1024)} %constant.88.clone) | copy-start | bytes 13828
  1.2 1.5 %copy-start = (f32[2,3,1,288,256]{4,3,2,1,0:T(8,128)S(1)}, f32[2,3,1,288,256]{4,3,2,1,0:T(8,128)}, u32[]{:S(2)}) copy-start(f32[2,3,1,288,256]{4,3,2,1,0:T(8,128)} %param.8) | copy-start | bytes 5308420
  3.4 17.1 %collective-permute-start = (f32[2,2,72,128]{3,2,1,0:T(8,128)S(1)}, f32[2,2,72,128]{3,2,1,0:T(8,128)S(1)}, u32[]{:S(2)}, u32[]{:S(2)}) collective-permute-start(f32[2,2,72,128]{3,2,1,0:T(8,128)S(1)} %get-tuple-element.35), channel_id=1, source_target_pairs={{0,4},{1,5},{2,6},{3,7},{4,8},{5,9},{6,10},{7,11},{8,12},{9,13},{1... | collective-permute-start | bytes 442376 | tf_op jit(solution)/shard_map/ppermute | solution.py:529
  6.5 14.0 %collective-permute-start.1 = (f32[2,2,72,128]{3,2,1,0:T(8,128)S(1)}, f32[2,2,72,128]{3,2,1,0:T(8,128)S(1)}, u32[]{:S(2)}, u32[]{:S(2)}) collective-permute-start(f32[2,2,72,128]{3,2,1,0:T(8,128)S(1)} %get-tuple-element.36), channel_id=1, source_target_pairs={{0,12},{1,13},{2,14},{3,15},{4,0},{5,1},{6,2},{7,3},{8,4},{9,5},{1... | collective-permute-start | bytes 442376 | tf_op jit(solution)/shard_map/ppermute | solution.py:529
  8.6 12.0 %collective-permute-start.2 = (f32[2,2,72,128]{3,2,1,0:T(8,128)S(1)}, f32[2,2,72,128]{3,2,1,0:T(8,128)S(1)}, u32[]{:S(2)}, u32[]{:S(2)}) collective-permute-start(f32[2,2,72,128]{3,2,1,0:T(8,128)S(1)} %get-tuple-element.37), channel_id=1, source_target_pairs={{0,1},{1,2},{2,3},{3,4},{4,5},{5,6},{6,7},{7,8},{8,9},{9,10},{10,1... | collective-permute-start | bytes 442376 | tf_op jit(solution)/shard_map/ppermute | solution.py:529
  8.6 12.0 %collective-permute-start.3 = (f32[2,2,72,128]{3,2,1,0:T(8,128)S(1)}, f32[2,2,72,128]{3,2,1,0:T(8,128)S(1)}, u32[]{:S(2)}, u32[]{:S(2)}) collective-permute-start(f32[2,2,72,128]{3,2,1,0:T(8,128)S(1)} %get-tuple-element.38), channel_id=1, source_target_pairs={{0,15},{1,0},{2,1},{3,2},{4,3},{5,4},{6,5},{7,6},{8,7},{9,8},{10,9... | collective-permute-start | bytes 442376 | tf_op jit(solution)/shard_map/ppermute | solution.py:529
  15.2 5.1 %copy-start.2 = (s32[4,3]{1,0:T(4,128)S(1)}, s32[4,3]{1,0:T(4,128)}, u32[]{:S(2)}) copy-start(s32[4,3]{1,0:T(4,128)} %param.10) | copy-start | bytes 148
  20.4 9.6 %copy-start.3 = (s32[1152]{0:T(1024)S(1)}, s32[1152]{0:T(1024)}, u32[]{:S(2)}) copy-start(s32[1152]{0:T(1024)} %constant.89.clone) | copy-start | bytes 13828
  21.7 16.4 %collective-permute-start.4 = (f32[2,2,72,128]{3,2,1,0:T(8,128)S(1)}, f32[2,2,72,128]{3,2,1,0:T(8,128)S(1)}, u32[]{:S(2)}, u32[]{:S(2)}) collective-permute-start(f32[2,2,72,128]{3,2,1,0:T(8,128)S(1)} %get-tuple-element.43), channel_id=1, source_target_pairs={{0,4},{1,5},{2,6},{3,7},{4,8},{5,9},{6,10},{7,11},{8,12},{9,13},{1... | collective-permute-start | bytes 442376 | tf_op jit(solution)/shard_map/ppermute | solution.py:529
  21.8 16.3 %collective-permute-start.5 = (f32[2,2,72,128]{3,2,1,0:T(8,128)S(1)}, f32[2,2,72,128]{3,2,1,0:T(8,128)S(1)}, u32[]{:S(2)}, u32[]{:S(2)}) collective-permute-start(f32[2,2,72,128]{3,2,1,0:T(8,128)S(1)} %get-tuple-element.44), channel_id=1, source_target_pairs={{0,12},{1,13},{2,14},{3,15},{4,0},{5,1},{6,2},{7,3},{8,4},{9,5},{1... | collective-permute-start | bytes 442376 | tf_op jit(solution)/shard_map/ppermute | solution.py:529
  25.6 12.5 %collective-permute-start.6 = (f32[2,2,72,128]{3,2,1,0:T(8,128)S(1)}, f32[2,2,72,128]{3,2,1,0:T(8,128)S(1)}, u32[]{:S(2)}, u32[]{:S(2)}) collective-permute-start(f32[2,2,72,128]{3,2,1,0:T(8,128)S(1)} %get-tuple-element.45), channel_id=1, source_target_pairs={{0,1},{1,2},{2,3},{3,4},{4,5},{5,6},{6,7},{7,8},{8,9},{9,10},{10,1... | collective-permute-start | bytes 442376 | tf_op jit(solution)/shard_map/ppermute | solution.py:529
  25.6 12.5 %collective-permute-start.7 = (f32[2,2,72,128]{3,2,1,0:T(8,128)S(1)}, f32[2,2,72,128]{3,2,1,0:T(8,128)S(1)}, u32[]{:S(2)}, u32[]{:S(2)}) collective-permute-start(f32[2,2,72,128]{3,2,1,0:T(8,128)S(1)} %get-tuple-element.46), channel_id=1, source_target_pairs={{0,15},{1,0},{2,1},{3,2},{4,3},{5,4},{6,5},{7,6},{8,7},{9,8},{10,9... | collective-permute-start | bytes 442376 | tf_op jit(solution)/shard_map/ppermute | solution.py:529
  37.1 1.0 %copy-start.1 = (s32[256]{0:T(256)S(1)}, s32[256]{0:T(256)}, u32[]{:S(2)}) copy-start(s32[256]{0:T(256)} %param.11) | copy-start | bytes 3076
  46.2 2.7 %collective-permute-start.8 = (f32[8,16,2048]{2,1,0:T(8,128)S(1)}, f32[8,16,2048]{2,1,0:T(8,128)S(1)}, u32[]{:S(2)}, u32[]{:S(2)}) collective-permute-start(f32[8,16,2048]{2,1,0:T(8,128)S(1)} %shard_map.91), channel_id=1, source_target_pairs={{0,1},{1,0},{2,3},{3,2},{4,5},{5,4},{6,7},{7,6},{8,9},{9,8},{10,11... | collective-permute-start | bytes 3145736 | tf_op jit(solution)/shard_map/ppermute | solution.py:646
  49.0 9.2 %collective-permute-start.10 = (f32[2,16,2048]{2,1,0:T(8,128)S(1)}, f32[2,16,2048]{2,1,0:T(8,128)S(1)}, u32[]{:S(2)}, u32[]{:S(2)}) collective-permute-start(f32[2,16,2048]{2,1,0:T(8,128)S(1)} %get-tuple-element.53), channel_id=1, source_target_pairs={{0,2},{1,3},{2,0},{3,1},{4,6},{5,7},{6,4},{7,5},{8,10},{9,11},{10,... | collective-permute-start | bytes 786440 | tf_op jit(solution)/shard_map/ppermute | solution.py:658
  49.0 14.0 %collective-permute-start.9 = (f32[2,16,2048]{2,1,0:T(8,128)S(1)}, f32[2,16,2048]{2,1,0:T(8,128)S(1)}, u32[]{:S(2)}, u32[]{:S(2)}) collective-permute-start(f32[2,16,2048]{2,1,0:T(8,128)S(1)} %get-tuple-element.51), channel_id=1, source_target_pairs={{0,2},{1,3},{2,0},{3,1},{4,6},{5,7},{6,4},{7,5},{8,10},{9,11},{10,... | collective-permute-start | bytes 786440 | tf_op jit(solution)/shard_map/ppermute | solution.py:659
  58.2 8.3 %collective-permute-start.11 = (f32[1,16,2048]{2,1,0:T(8,128)S(1)}, f32[1,16,2048]{2,1,0:T(8,128)S(1)}, u32[]{:S(2)}, u32[]{:S(2)}) collective-permute-start(f32[1,16,2048]{2,1,0:T(8,128)S(1)} %get-tuple-element.54), channel_id=1, source_target_pairs={{0,4},{1,5},{2,6},{3,7},{4,8},{5,9},{6,10},{7,11},{8,12},{9,13},{1... | collective-permute-start | bytes 393224 | tf_op jit(solution)/shard_map/ppermute | solution.py:678
  58.3 11.4 %collective-permute-start.12 = (f32[1,16,2048]{2,1,0:T(8,128)S(1)}, f32[1,16,2048]{2,1,0:T(8,128)S(1)}, u32[]{:S(2)}, u32[]{:S(2)}) collective-permute-start(f32[1,16,2048]{2,1,0:T(8,128)S(1)} %get-tuple-element.55), channel_id=1, source_target_pairs={{0,8},{1,9},{2,10},{3,11},{4,12},{5,13},{6,14},{7,15},{8,0},{9,1},... | collective-permute-start | bytes 393224 | tf_op jit(solution)/shard_map/ppermute | solution.py:678
  63.0 7.1 %collective-permute-start.13 = (f32[1,16,2048]{2,1,0:T(8,128)S(1)}, f32[1,16,2048]{2,1,0:T(8,128)S(1)}, u32[]{:S(2)}, u32[]{:S(2)}) collective-permute-start(f32[1,16,2048]{2,1,0:T(8,128)S(1)} %get-tuple-element.56), channel_id=1, source_target_pairs={{0,12},{1,13},{2,14},{3,15},{4,0},{5,1},{6,2},{7,3},{8,4},{9,5},{1... | collective-permute-start | bytes 393224 | tf_op jit(solution)/shard_map/ppermute | solution.py:678

commit v4 on v3

--- a/solution.py
+++ b/solution.py
@@ -18,12 +18,14 @@
 SITES = TLX * LAYER
 XROWS = 3 * LAYER
 MAIN = TLX * XROWS
-PADDED = (TLX + 2) * XROWS
+BOTH = 2 * XROWS
+PADDED = (TLX + 2) * BOTH
+WINDOW = 3 * BOTH
+SPLIT = 4 * BOTH
 EDGE = 4 * XROWS
 HEAD = MAIN // 128 * 128
 TAIL = MAIN - HEAD + EDGE
 LANES = 128
-BX, BYF, BYB, BZS, BZD, WIDE = 0, 18, 36, 54, 72, 90
 CX, CY, CZ = 0, 18, 36
 CYF, CYB, CZS, CZD = 54, 72, 90, 108
 VMEM_LIMIT = 12 * 2**20
@@ -79,45 +81,46 @@
 
 
 def layer_rows(ref, part, half, first, size=LAYER):
-    return ref[part, half, first : first + size, :]
+    at = part * XROWS + first
+    return ref[half, at : at + size, :]
 
 
 def grid2(load):
     return [[load(part, colour) for colour in range(3)] for part in range(2)]
 
 
-def y_rows(colour, z, y):
-    return pl.ds(XROWS + colour * LAYER + z * TLY + y, TLX, stride=XROWS)
+def y_rows(part, colour, z, y):
+    return pl.ds(BOTH + part * XROWS + colour * LAYER + z * TLY + y, TLX, stride=BOTH)
 
 
 def send_layers(f_ref, wc_ref, xlo_ref, xhi_ref, ylo_ref, yhi_ref):
-    last = TLX * XROWS
-    for half in range(f_ref.shape[1]):
+    last = TLX * BOTH
+    for half in range(f_ref.shape[0]):
+        xlo_ref[half] = f_ref[half, BOTH : 2 * BOTH, :]
         for part in range(2):
-            xlo_ref[part, half] = f_ref[part, half, XROWS : 2 * XROWS, :]
             for colour in range(3):
                 for z in range(LZ):
-                    to = colour * LAYER + z * TLX
-                    ylo_ref[part, half, to : to + TLX, :] = f_ref[part, half, y_rows(colour, z, 0), :]
+                    to = part * XROWS + colour * LAYER + z * TLX
+                    ylo_ref[half, to : to + TLX, :] = f_ref[half, y_rows(part, colour, z, 0), :]
         table = wc_ref[TLX * LAYER : (TLX + 1) * LAYER, :]
         hop = matvec(table, CX, grid2(lambda p, c: layer_rows(f_ref, p, half, last + c * LAYER)), adjoint=True)
         for part in range(2):
             for colour in range(3):
-                xhi_ref[part, half, colour * LAYER : (colour + 1) * LAYER, :] = hop[part][colour]
+                to = part * XROWS + colour * LAYER
+                xhi_ref[half, to : to + LAYER, :] = hop[part][colour]
         for z in range(LZ):
             table = wc_ref[pl.ds(LAYER + z * TLY + TLY - 1, TLX, stride=LAYER), :]
-            hop = matvec(table, CY, grid2(lambda p, c: f_ref[p, half, y_rows(c, z, TLY - 1), :]), adjoint=True)
+            hop = matvec(table, CY, grid2(lambda p, c: f_ref[half, y_rows(p, c, z, TLY - 1), :]), adjoint=True)
             for part in range(2):
                 for colour in range(3):
-                    to = colour * LAYER + z * TLX
-                    yhi_ref[part, half, to : to + TLX, :] = hop[part][colour]
+                    to = part * XROWS + colour * LAYER + z * TLX
+                    yhi_ref[half, to : to + TLX, :] = hop[part][colour]
 
 
 def clear_ends(ref):
-    for part in range(2):
-        for half in range(ref.shape[1]):
-            ref[part, half, 0:XROWS, :] = jnp.zeros((XROWS, LANES), jnp.float32)
-            ref[part, half, PADDED - XROWS : PADDED, :] = jnp.zeros((XROWS, LANES), jnp.float32)
+    for half in range(ref.shape[0]):
+        ref[half, 0:BOTH, :] = jnp.zeros((BOTH, LANES), jnp.float32)
+        ref[half, PADDED - BOTH : PADDED, :] = jnp.zeros((BOTH, LANES), jnp.float32)
 
 
 def pack_kernel(v_ref, l_ref, fr_ref, wc_ref, xlo_ref, xhi_ref, ylo_ref, yhi_ref, la, lb, ta, tb):
@@ -157,142 +160,125 @@
             src = z * plane + x * TLY
             dst = (x + 1) * LAYER + z * TLY
             wc_ref[dst : dst + TLY, :] = ta[src : src + TLY, :]
-            for half in range(fr_ref.shape[1]):
+            for half in range(fr_ref.shape[0]):
                 for part in range(2):
                     for colour in range(3):
-                        dst = (x + 1) * XROWS + colour * LAYER + z * TLY
-                        fr_ref[part, half, dst : dst + TLY, :] = v_ref[
+                        dst = (x + 1) * BOTH + part * XROWS + colour * LAYER + z * TLY
+                        fr_ref[half, dst : dst + TLY, :] = v_ref[
                             3 * part + colour, src : src + TLY, half * LANES : (half + 1) * LANES
                         ]
     send_layers(fr_ref, wc_ref, xlo_ref, xhi_ref, ylo_ref, yhi_ref)
 
 
-def roll_layer(f_ref, half, base, rolled):
-    for part in range(2):
-        for colour in range(3):
-            rows = f_ref[part, half, pl.ds(base + colour * LAYER, LAYER), :]
-            at = colour * LAYER
-            rolled[0, half, part, at : at + LAYER, :] = pltpu.roll(rows, LAYER - 1, 0)
-            rolled[1, half, part, at : at + LAYER, :] = pltpu.roll(rows, 1, 0)
-            rolled[2, half, part, at : at + LAYER, :] = pltpu.roll(rows, TLY, 0)
-
-
-def layer_hops(f_ref, wb_ref, rolled, x, tile, z_column):
-    step = 8 * tile
-    base = (x + 1) * XROWS
-
-    def table(column):
-        return wb_ref[x + 1, column, pl.ds(pl.multiple_of(step, 8), 8), :]
-
-    def below(column):
-        return wb_ref[x, column, pl.ds(pl.multiple_of(step, 8), 8), :]
-
-    def straight(shift):
-        return lambda p, c, half: f_ref[p, half, pl.ds(pl.multiple_of(base + shift + c * LAYER + step, 8), 8), :]
-
-    def turned(which):
-        return lambda p, c, half: rolled[which, half, p, pl.ds(pl.multiple_of(c * LAYER + step, 8), 8), :]
-
-    return (
-        (table, BX, straight(XROWS), False, 0),
-        (below, BX, straight(-XROWS), True, 0),
-        (table, BYF, turned(0), False, 1),
-        (table, BYB, turned(1), True, 1),
-        (table, z_column, turned(2), False, 2),
-    ), straight(0)
-
-
-def hop_all(weights, column, load, adjoint, halves, acc, minus=False):
-    for col in range(3):
-        field = [[load(p, col, half) for half in halves] for p in range(2)]
-        for row in range(3):
-            at = column + (3 * col + row if adjoint else 3 * row + col)
-            real = weights(at)
-            imag = weights(at + 9)
-            for half in halves:
-                terms = (
-                    (0, real * field[0][half], False),
-                    (0, imag * field[1][half], not adjoint),
-                    (1, real * field[1][half], False),
-                    (1, imag * field[0][half], adjoint),
-                )
-                for part, value, negative in terms:
-                    before = acc[part][row][half]
-                    if before is None:
-                        acc[part][row][half] = -value if negative != minus else value
-                    else:
-                        acc[part][row][half] = before - value if negative != minus else before + value
-    return acc
-
-
-def hop_column(weights, col, field, adjoint, acc, minus):
-    for row in range(3):
-        at = 3 * col + row if adjoint else 3 * row + col
-        real, imag = weights(at), weights(at + 9)
-        terms = (
-            (0, real * field[0], False),
-            (0, imag * field[1], not adjoint),
-            (1, real * field[1], False),
-            (1, imag * field[0], adjoint),
-        )
-        for part, value, negative in terms:
-            before = acc[part][row][0]
-            if before is None:
-                acc[part][row][0] = -value if negative != minus else value
-            else:
-                acc[part][row][0] = before - value if negative != minus else before + value
-
-
-def spread_kernel(wc_ref, wb_ref):
-    rest = wc_ref[...]
-    terms = []
-    for _ in range(2):
-        terms.append(rest.astype(jnp.bfloat16))
-        rest = rest - terms[-1].astype(jnp.float32)
-    terms = jnp.concatenate(terms, axis=1)
-    row = lax.broadcasted_iota(jnp.int32, (LANES, 2 * LANES), 0)
-    right = lax.broadcasted_iota(jnp.int32, (LANES, 2 * LANES), 1) // LANES
-    for column in range(0, WIDE, 2):
-        source = column if column < 18 else column + CYF - 18
-        ones = jnp.where(row == source + right, 1.0, 0.0).astype(jnp.bfloat16)
-        copies = dot(terms, jnp.concatenate([ones] * 2, axis=0))
-        for k in range(2):
-            wb_ref[:, column + k] = copies[:, k * LANES : (k + 1) * LANES].reshape(TLX + 1, LAYER, LANES)
-
-
-def empty_acc(halves):
-    return [[[None for _ in halves] for _ in range(3)] for _ in range(2)]
-
-
-def smear_kernel(f_ref, wb_ref, out_ref, rolled):
+def split(value):
+    high = value.astype(jnp.bfloat16)
+    return high, (value - high.astype(jnp.float32)).astype(jnp.bfloat16)
+
+
+def sources(kinds):
+    column = np.full((6, len(kinds) * BOTH), -1, np.int32)
+    sign = np.zeros((6, len(kinds) * BOTH), np.float32)
+    for k, kind in enumerate(kinds):
+        if kind is None:
+            continue
+        first, adjoint, factor, below = kind
+        for ri in range(2):
+            for row in range(3):
+                for rj in range(2):
+                    for col in range(3):
+                        at = first + (3 * col + row if adjoint else 3 * row + col)
+                        weight = 1.0
+                        if ri != rj:
+                            at += 9
+                            weight = -1.0 if (ri == 0) != adjoint else 1.0
+                        lanes = slice(k * BOTH + rj * XROWS + col * LAYER, k * BOTH + rj * XROWS + (col + 1) * LAYER)
+                        column[3 * ri + row, lanes] = at + (2 * LANES if below else 0)
+                        sign[3 * ri + row, lanes] = factor * weight
+    return column, sign
+
+
+def expand(terms, column_ref, sign_ref, block, first, width):
+    deep = terms.shape[1] // (2 * LANES)
+    row = lax.broadcasted_iota(jnp.int32, (LANES, width), 0)
+    column = jnp.broadcast_to(column_ref[block : block + 1, first : first + width], (LANES, width))
+    sign = jnp.broadcast_to(sign_ref[block : block + 1, first : first + width], (LANES, width))
+    ones = []
+    for k in range(deep):
+        ones += [jnp.where(row + 2 * k * LANES == column, sign, 0.0).astype(jnp.bfloat16)] * 2
+    return dot(terms, jnp.concatenate(ones, axis=0))
+
+
+def operator_kernel(wc_ref, column_ref, sign_ref, more_ref, moresign_ref, high_ref, low_ref, *, middle, kinds, extra):
+    high, low = split(wc_ref[...])
+    own, below = slice(LAYER, (TLX + 1) * LAYER), slice(0, TLX * LAYER)
+    deep = jnp.concatenate([high[own], low[own], high[below], low[below]], axis=1)
+    single = jnp.concatenate([high[own], low[own]], axis=1)
+    width = -(-len(kinds) * BOTH // LANES) * LANES
+    wide = 2 * LANES
+
+    def mask(first, size, shifts):
+        p = lax.broadcasted_iota(jnp.int32, (LAYER, size), 0)
+        lane = lax.broadcasted_iota(jnp.int32, (LAYER, size), 1) + first
+        q = lane % LAYER
+        block = lane // BOTH
+        found = None
+        for k, shift in enumerate(shifts):
+            if shift is not None:
+                here = (block == k) & (q == (p + shift if shift != TLY else (p + TLY) % LAYER))
+                found = here if found is None else found | here
+        return found
+
+    keep = mask(0, width, kinds)
+    keeps = [mask(middle, wide, [shift if k == place else None for k in range(len(kinds))]) for place, shift in extra]
+    for block in range(6):
+        value = expand(deep, column_ref, sign_ref, block, 0, width).reshape(TLX, LAYER, width)
+        value = jnp.where(keep[None], value, 0.0)
+        center = value[:, :, middle : middle + wide]
+        for k in range(len(extra)):
+            other = expand(single, more_ref, moresign_ref, block, k * wide, wide).reshape(TLX, LAYER, wide)
+            center = center + jnp.where(keeps[k][None], other, 0.0)
+        pieces = [value[:, :, :middle], center]
+        if middle + wide < width:
+            pieces.append(value[:, :, middle + wide :])
+        at = 0
+        for piece in pieces:
+            size = min(piece.shape[2], len(kinds) * BOTH - at)
+            if size > 0:
+                high, low = split(piece)
+                for x in range(TLX):
+                    rows = slice(x * BOTH + block * LAYER, x * BOTH + (block + 1) * LAYER)
+                    high_ref[rows, at : at + size] = high[x, :, :size]
+                    low_ref[rows, at : at + size] = low[x, :, :size]
+            at += piece.shape[2]
+
+
+def split_field(f_ref, high_ref, low_ref, scale=None):
+    for half in range(f_ref.shape[0]):
+        lanes = slice(half * LANES, (half + 1) * LANES)
+        for row in range(0, PADDED, BOTH):
+            value = f_ref[half, row : row + BOTH, :]
+            high, low = split(value if scale is None else scale * value)
+            high_ref[row : row + BOTH, lanes] = high
+            low_ref[row : row + BOTH, lanes] = low
+
+
+def smear_kernel(f_ref, oh_ref, ol_ref, out_ref, fh, fl):
     clear_ends(out_ref)
-    halves = range(f_ref.shape[1])
-
-    def layer(x, carry):
-        base = pl.multiple_of((x + 1) * XROWS, 8)
-        for half in halves:
-            roll_layer(f_ref, half, base, rolled)
-
-        def tiles(tile, carry):
-            hops, here = layer_hops(f_ref, wb_ref, rolled, x, tile, BZS)
-            acc = empty_acc(halves)
-            for weights, column, load, adjoint, _ in hops:
-                hop_all(weights, column, load, adjoint, halves, acc)
-            for part in range(2):
-                for colour in range(3):
-                    for half in halves:
-                        value = (1.0 - 6.0 * KAPPA) * here(part, colour, half) + KAPPA * acc[part][colour][half]
-                        out_ref[part, half, pl.ds(base + colour * LAYER + 8 * tile, 8), :] = value
-            return carry
-
-        return lax.fori_loop(0, LAYER // 8, tiles, carry, unroll=True)
-
-    lax.fori_loop(0, TLX, layer, 0)
+    split_field(f_ref, fh, fl)
+    for x in range(TLX):
+        rows = slice(x * BOTH, (x + 1) * BOTH)
+        high, low = oh_ref[rows, :], ol_ref[rows, :]
+        window = slice(x * BOTH, x * BOTH + WINDOW)
+        hops = dot(high, fh[window, :]) + dot(high, fl[window, :]) + dot(low, fh[window, :])
+        at = slice((x + 1) * BOTH, (x + 2) * BOTH)
+        for half in range(f_ref.shape[0]):
+            lanes = slice(half * LANES, (half + 1) * LANES)
+            out_ref[half, at, :] = (1.0 - 6.0 * KAPPA) * f_ref[half, at, :] + KAPPA * hops[:, lanes]
 
 
 def cross(once_ref, wc_ref, rxlo, rxhi, rylo, ryhi, save=None):
-    last = TLX * XROWS
-    for half in range(once_ref.shape[1]):
+    last = TLX * BOTH
+    for half in range(once_ref.shape[0]):
         table = wc_ref[TLX * LAYER : (TLX + 1) * LAYER, :]
         hop_x = matvec(table, CX, grid2(lambda p, c: layer_rows(rxhi, p, half, c * LAYER)))
         hop_y = []
@@ -303,17 +289,18 @@
             for colour in range(3):
                 at = colour * LAYER
                 low = layer_rows(rxlo, part, half, at)
-                once_ref[part, half, XROWS + at : XROWS + at + LAYER, :] += KAPPA * low
-                once_ref[part, half, last + at : last + at + LAYER, :] += KAPPA * hop_x[part][colour]
+                to = part * XROWS + at
+                once_ref[half, BOTH + to : BOTH + to + LAYER, :] += KAPPA * low
+                once_ref[half, last + to : last + to + LAYER, :] += KAPPA * hop_x[part][colour]
                 if save is not None:
                     save[part, half, at : at + LAYER, :] = low
                     save[part, half, XROWS + at : XROWS + at + LAYER, :] = hop_x[part][colour]
                 for z in range(LZ):
                     low = layer_rows(rylo, part, half, at + z * TLX, TLX)
-                    rows = y_rows(colour, z, 0)
-                    once_ref[part, half, rows, :] = once_ref[part, half, rows, :] + KAPPA * low
-                    rows = y_rows(colour, z, TLY - 1)
-                    once_ref[part, half, rows, :] = once_ref[part, half, rows, :] + KAPPA * hop_y[z][part][colour]
+                    rows = y_rows(part, colour, z, 0)
+                    once_ref[half, rows, :] = once_ref[half, rows, :] + KAPPA * low
+                    rows = y_rows(part, colour, z, TLY - 1)
+                    once_ref[half, rows, :] = once_ref[half, rows, :] + KAPPA * hop_y[z][part][colour]
                     if save is not None:
                         to = 2 * XROWS + at + z * TLX
                         save[part, half, to : to + TLX, :] = low
@@ -324,11 +311,6 @@
     once_ref[...] = part_ref[...]
     cross(once_ref, wc_ref, rxlo, rxhi, rylo, ryhi, save)
     send_layers(once_ref, wc_ref, xlo_ref, xhi_ref, ylo_ref, yhi_ref)
-
-
-def split(value):
-    high = value.astype(jnp.bfloat16)
-    return high, (value - high.astype(jnp.float32)).astype(jnp.bfloat16)
 
 
 def phased(real, imag, half, lane, at, size, cos_ref, sin_ref, ah_ref, al_ref):
@@ -346,98 +328,91 @@
         al_ref[row : row + LANES, size + at : size + at + LANES] = low
 
 
-def head_kernel(fr_ref, cos_ref, sin_ref, ah_ref, al_ref):
-    for half in range(fr_ref.shape[1]):
+def own_rows(fr_ref, rows, half, first, stop):
+    for part in range(2):
+        for x in range(first // XROWS, -(-stop // XROWS)):
+            low, high = max(first, x * XROWS), min(stop, (x + 1) * XROWS)
+            at = (x + 1) * BOTH + part * XROWS + low - x * XROWS
+            rows[part, low - first : high - first, :] = fr_ref[half, at : at + high - low, :]
+
+
+def head_kernel(fr_ref, cos_ref, sin_ref, ah_ref, al_ref, rows):
+    for half in range(fr_ref.shape[0]):
+        own_rows(fr_ref, rows, half, 0, HEAD)
         for at in range(0, HEAD, LANES):
-            real, imag = (fr_ref[p, half, XROWS + at : XROWS + at + LANES, :] for p in range(2))
+            real, imag = (rows[p, at : at + LANES, :] for p in range(2))
             phased(real, imag, half, at, at, HEAD, cos_ref, sin_ref, ah_ref, al_ref)
 
 
 def tail_kernel(fr_ref, save, cos_ref, sin_ref, ah_ref, al_ref, rows):
-    for half in range(fr_ref.shape[1]):
+    for half in range(fr_ref.shape[0]):
+        own_rows(fr_ref, rows, half, HEAD, MAIN)
         for part in range(2):
-            rows[part, 0 : MAIN - HEAD, :] = fr_ref[part, half, XROWS + HEAD : XROWS + MAIN, :]
             rows[part, MAIN - HEAD : TAIL, :] = save[part, half]
         for at in range(0, TAIL, LANES):
             real, imag = (rows[p, at : at + LANES, :] for p in range(2))
             phased(real, imag, half, HEAD + at, at, TAIL, cos_ref, sin_ref, ah_ref, al_ref)
 
 
-def displace_kernel(part_ref, wc_ref, wb_ref, rxlo, rxhi, rylo, ryhi, dir_ref, sh_ref, sl_ref, th_ref, tl_ref, twice, shift, rolled, *, scale):
+def displace_kernel(part_ref, wc_ref, oh_ref, ol_ref, rxlo, rxhi, rylo, ryhi, dir_ref, sh_ref, sl_ref, th_ref, tl_ref, twice, shift, fh, fl, *, scale):
     twice[...] = part_ref[...]
     cross(twice, wc_ref, rxlo, rxhi, rylo, ryhi)
-    halves = range(twice.shape[1])
-
-    def along(which, half, rows=8):
-        return jnp.broadcast_to(dir_ref[0:1, half * LANES : (half + 1) * LANES], (rows, LANES)) == which
-
-    def layer(x, carry):
-        into = pl.multiple_of(x * XROWS, 8)
-        for half in halves:
-            roll_layer(twice, half, pl.multiple_of((x + 1) * XROWS, 8), rolled)
-        for tile in range(LAYER // 8):
-            hops, _ = layer_hops(twice, wb_ref, rolled, x, tile, BZD)
-            (ahead_x, bx, load_xf, _, _), (below, _, load_xb, _, _) = hops[0], hops[1]
-            (table, byf, load_yf, _, _), (_, byb, load_yb, _, _), (_, bz, load_z, _, _) = hops[2:]
-            for half in halves:
-                is_x, is_y = along(0, half), along(1, half)
-                acc = empty_acc([0])
-                for col in range(3):
-                    ahead = [
-                        jnp.where(is_x, load_xf(p, col, half), jnp.where(is_y, load_yf(p, col, half), load_z(p, col, half)))
-                        for p in range(2)
-                    ]
-                    behind = [
-                        jnp.where(is_x, load_xb(p, col, half), jnp.where(is_y, load_yb(p, col, half), 0.0))
-                        for p in range(2)
-                    ]
-
-                    def forward(at):
-                        return jnp.where(is_x, ahead_x(bx + at), jnp.where(is_y, table(byf + at), table(bz + at)))
-
-                    def backward(at):
-                        return jnp.where(is_x, below(bx + at), table(byb + at))
-
-                    hop_column(forward, col, ahead, False, acc, False)
-                    hop_column(backward, col, behind, True, acc, True)
-                for part in range(2):
-                    for colour in range(3):
-                        at = pl.ds(pl.multiple_of(into + colour * LAYER + 8 * tile, 8), 8)
-                        shift[part, half, at, :] = scale * acc[part][colour][0]
-        return carry
-
-    lax.fori_loop(0, TLX, layer, 0)
-    last = TLX * XROWS
+    halves = range(twice.shape[0])
+    width = len(halves) * LANES
+
+    def along(which, lanes, rows):
+        return jnp.broadcast_to(dir_ref[0:1, lanes], (rows, lanes.stop - lanes.start)) == which
+
     for half in halves:
-        mask_x = jnp.where(along(0, half, XROWS), scale, 0.0)
-        mask_y = jnp.where(along(1, half, TLX), scale, 0.0)
+        lanes = slice(half * LANES, (half + 1) * LANES)
+        for row in range(0, PADDED, BOTH):
+            value = scale * twice[half, row : row + BOTH, :]
+            for which in range(3):
+                high, low = split(jnp.where(along(which, lanes, BOTH), value, 0.0))
+                fh[which, row : row + BOTH, lanes] = high
+                fl[which, row : row + BOTH, lanes] = low
+    for x in range(TLX):
+        rows = slice(x * BOTH, (x + 1) * BOTH)
+        low, mid, top = (slice((x + k) * BOTH, (x + k + 1) * BOTH) for k in range(3))
+
+        def columns(ref):
+            return jnp.concatenate([ref[0, low, :], ref[0, top, :], ref[1, mid, :], ref[2, mid, :]], axis=0)
+
+        fields, rest = columns(fh), columns(fl)
+        weights = oh_ref[rows, :]
+        value = dot(weights, fields) + dot(weights, rest) + dot(ol_ref[rows, :], fields)
         for part in range(2):
-            shift[part, half, MAIN : MAIN + XROWS, :] = mask_x * twice[part, half, XROWS : 2 * XROWS, :]
-            shift[part, half, MAIN + XROWS : MAIN + 2 * XROWS, :] = -mask_x * twice[part, half, last : last + XROWS, :]
+            shift[part, x * XROWS : (x + 1) * XROWS, :] = value[part * XROWS : (part + 1) * XROWS]
+    last = TLX * BOTH
+    for half in halves:
+        lanes = slice(half * LANES, (half + 1) * LANES)
+        mask_x = jnp.where(along(0, lanes, XROWS), scale, 0.0)
+        mask_y = jnp.where(along(1, lanes, TLX), scale, 0.0)
+        for part in range(2):
+            at = part * XROWS
+            shift[part, MAIN : MAIN + XROWS, lanes] = mask_x * twice[half, BOTH + at : BOTH + at + XROWS, :]
+            shift[part, MAIN + XROWS : MAIN + 2 * XROWS, lanes] = -mask_x * twice[half, last + at : last + at + XROWS, :]
             for colour in range(3):
                 for z in range(LZ):
                     to = MAIN + 2 * XROWS + colour * LAYER + z * TLX
-                    shift[part, half, to : to + TLX, :] = mask_y * twice[part, half, y_rows(colour, z, 0), :]
+                    shift[part, to : to + TLX, lanes] = mask_y * twice[half, y_rows(part, colour, z, 0), :]
                     to += XROWS
-                    shift[part, half, to : to + TLX, :] = -mask_y * twice[part, half, y_rows(colour, z, TLY - 1), :]
-    width = len(halves) * LANES
+                    shift[part, to : to + TLX, lanes] = -mask_y * twice[half, y_rows(part, colour, z, TLY - 1), :]
     for high_ref, low_ref, first, size in ((sh_ref, sl_ref, 0, HEAD), (th_ref, tl_ref, HEAD, TAIL)):
-        for half in halves:
-            real = slice(half * LANES, (half + 1) * LANES)
-            imag = slice(width + half * LANES, width + (half + 1) * LANES)
-            for row in range(0, size, 128):
-                top = slice(row, row + 128)
-                bottom = slice(size + row, size + row + 128)
-                high, low = split(shift[0, half, first + row : first + row + 128, :])
-                high_ref[top, real] = high
-                low_ref[top, real] = low
-                high_ref[bottom, imag] = -high
-                low_ref[bottom, imag] = -low
-                high, low = split(shift[1, half, first + row : first + row + 128, :])
-                high_ref[bottom, real] = high
-                low_ref[bottom, real] = low
-                high_ref[top, imag] = high
-                low_ref[top, imag] = low
+        real, imag = slice(0, width), slice(width, 2 * width)
+        for row in range(0, size, 128):
+            top = slice(row, row + 128)
+            bottom = slice(size + row, size + row + 128)
+            high, low = split(shift[0, first + row : first + row + 128, :])
+            high_ref[top, real] = high
+            low_ref[top, real] = low
+            high_ref[bottom, imag] = -high
+            low_ref[bottom, imag] = -low
+            high, low = split(shift[1, first + row : first + row + 128, :])
+            high_ref[bottom, real] = high
+            low_ref[bottom, real] = low
+            high_ref[top, imag] = high
+            low_ref[top, imag] = low
 
 
 def dot(a, b):
@@ -577,8 +552,8 @@
     field = vectors.reshape(6, SITES, nev)
     table = links.reshape(54, SITES)
     halves = nev // LANES
-    layer = f32(2, halves, XROWS, LANES)
-    padded = f32(2, halves, PADDED, LANES)
+    layer = f32(halves, BOTH, LANES)
+    padded = f32(halves, PADDED, LANES)
     fr, wc, *sends = call(
         pack_kernel,
         (padded, f32((TLX + 1) * LAYER, LANES), layer, layer, layer, layer),
@@ -587,18 +562,31 @@
     )(field, table)
     received = halo(sends, devices, tiles)
     flops = 2 * 180 * 2 * SITES * nev
-    wb = call(spread_kernel, f32(TLX + 1, WIDE, LAYER, LANES), (), flops >> 4, 1 << 20)(wc)
-    rolled = pltpu.VMEM((3, halves, 2, XROWS, LANES), jnp.float32)
-    once = call(smear_kernel, padded, [rolled], flops, 3 << 20, 2)(fr, wb)
+    smear = operator(
+        wc,
+        kinds=((CX, True, 1.0, True), (CYF, False, 1.0, False), (CX, False, 1.0, False)),
+        shifts=(0, 1, 0),
+        extra=((1, CYB, True, 1.0, -1), (1, CZS, False, 1.0, TLY)),
+        middle=LANES,
+    )
+    pair = [pltpu.VMEM((PADDED, nev), jnp.bfloat16)] * 2
+    once = call(smear_kernel, padded, pair, flops, 3 << 20, 3)(fr, *smear)
     cosine, sine = phases(momenta, position, devices, tiles)
     head = bf16(moments * nev, 2 * HEAD)
     tail = bf16(moments * nev, 2 * TAIL)
-    ah, al = call(head_kernel, (head, head), (), flops, 8 << 20, 3)(fr, cosine, sine)
-    once, save, *sends = call(edge_kernel, (padded, f32(2, halves, EDGE, LANES), layer, layer, layer, layer), inputs=6)(
-        once, wc, *received
+    rows = pltpu.VMEM((2, HEAD, LANES), jnp.float32)
+    ah, al = call(head_kernel, (head, head), [rows], flops, 8 << 20, 3)(fr, cosine, sine)
+    displace = operator(
+        wc,
+        kinds=((CX, True, -1.0, True), (CX, False, 1.0, False), (CYF, False, 1.0, False), (CZD, False, 1.0, False)),
+        shifts=(0, 0, 1, TLY),
+        extra=((2, CYB, True, -1.0, -1),),
+        middle=2 * LANES,
     )
+    edges = f32(2, halves, EDGE, LANES)
+    once, save, *sends = call(edge_kernel, (padded, edges, layer, layer, layer, layer), inputs=6)(once, wc, *received)
     received = halo(sends, devices, tiles)
-    twice = call(smear_kernel, padded, [rolled], flops, 3 << 20, 2)(once, wb)
+    twice = call(smear_kernel, padded, pair, flops, 3 << 20, 3)(once, *smear)
     rows = pltpu.VMEM((2, TAIL, LANES), jnp.float32)
     bh, bl = call(tail_kernel, (tail, tail), [rows], flops, 4 << 20, 4)(fr, save, cosine, sine)
     scale = 1.0 / math.sqrt(3.0 * TLX * tiles * TLY * tiles * LZ)
@@ -606,12 +594,12 @@
         functools.partial(displace_kernel, scale=scale),
         (bf16(2 * HEAD, 2 * nev), bf16(2 * HEAD, 2 * nev), bf16(2 * TAIL, 2 * nev), bf16(2 * TAIL, 2 * nev)),
         [
-            pltpu.VMEM((2, halves, PADDED, LANES), jnp.float32),
-            pltpu.VMEM((2, halves, HEAD + TAIL, LANES), jnp.float32),
-            rolled,
-        ],
-        inputs=8,
-    )(twice, wc, wb, *received, directions[None, :])
+            pltpu.VMEM((halves, PADDED, LANES), jnp.float32),
+            pltpu.VMEM((2, HEAD + TAIL, nev), jnp.float32),
+        ]
+        + [pltpu.VMEM((3, PADDED, nev), jnp.bfloat16)] * 2,
+        inputs=9,
+    )(twice, wc, *displace, *received, directions[None, :])
     operands = (ah, al, bh, bl) + tuple(operands)
     size, columns = nev // devices, moments * 2 * nev
     if size % 16 == 0 and devices % 8 == 0:
@@ -619,6 +607,27 @@
     else:
         total = whole_product(operands, position, devices, moments, nev)
     return total.reshape(size, moments, 2, nev)
+
+
+def operator(wc, kinds, shifts, extra, middle):
+    lanes = len(kinds) * BOTH
+    width = -(-lanes // LANES) * LANES
+    column, sign = sources(kinds)
+    column = np.pad(column, ((0, 0), (0, width - lanes)), constant_values=-1)
+    sign = np.pad(sign, ((0, 0), (0, width - lanes)))
+    more, moresign = [], []
+    for place, first, adjoint, factor, _ in extra:
+        c, w = sources([(first, adjoint, factor, False) if k == place else None for k in range(len(kinds))])
+        c = np.pad(c, ((0, 0), (0, width - lanes)), constant_values=-1)
+        w = np.pad(w, ((0, 0), (0, width - lanes)))
+        more.append(c[:, middle : middle + 2 * LANES])
+        moresign.append(w[:, middle : middle + 2 * LANES])
+    kernel = functools.partial(
+        operator_kernel, middle=middle, kinds=shifts, extra=[(place, shift) for place, _, _, _, shift in extra]
+    )
+    out = bf16(TLX * BOTH, lanes)
+    tables = (column, sign, np.concatenate(more, 1), np.concatenate(moresign, 1))
+    return call(kernel, (out, out), (), 1 << 30, 4 << 20, 5)(wc, *map(jnp.asarray, tables))
 
 
 def whole_product(operands, position, devices, moments, nev):

time: 71.1 us -> 66.8 us (0.940)
  Pallas kernels: 29 us -> 23.7 us
    pallas_call x5 -> x6, Pallas kernels: 15.1 us -> 10.5 us  [the longest x2 4.17 us: operator(): call(kernel, (out, out), (), 1 << 30, 4 << 20, 5)]
    ppermute x8, waiting for transfers between devices: 0.02 us -> 0.94 us  [send(): lax.ppermute(block, 'site', [(i, (i + distance) % devices) for i in range...]
    pallas_call x1, Pallas kernels: 4.27 us -> 3.49 us  [on_device(): call(functools.partial(displace_kernel, scale=scale), (bf16(2 * HEAD, 2 *...]
    unnamed x14 -> x30, local copies, waits for them, and re-layouts: 1.5 us -> 1.55 us
  transfers between devices with their start and end apart: 14 -> 14, of which waited for: 6 -> 7; matrix products, arithmetic and copies ran while one was open for 1% -> 1% of each run, Pallas kernels for 27% -> 22%
where the time goes in v4:
time: 66.8 us; the launch traced here: 66.6 us
  Pallas kernels  23.7 us (35%)
  starting transfers between devices  20.3 us (30%)
  waiting for transfers between devices  18.1 us (27%)
  local copies, waits for them, and re-layouts  2.54 us (4%)
  other arithmetic  1.5 us (2%)
    ppermute x8, starting transfers between devices, send(): lax.ppermute(block, 'site', [(i, (i + distance) % devices) for i in range...  18 us
    ppermute x3, waiting for transfers between devices, pieces(): lax.ppermute(value, 'site', [(i, (i + 4 * step) % devices) for i in range...  7.05 us
    ppermute x1, waiting for transfers between devices, pieces(): first = lax.ppermute(first, 'site', flip)  5.1 us
    ppermute x1, waiting for transfers between devices, pieces(): second = lax.ppermute(second, 'site', flip)  4.61 us
    pallas_call x2, Pallas kernels, operator(): call(kernel, (out, out), (), 1 << 30, 4 << 20, 5)  4.17 us
    pallas_call x1, Pallas kernels, pieces(): call(functools.partial(piece_kernel, cores=1, turns=(0, 1), **shared), bl...  3.81 us
    pallas_call x1, Pallas kernels, on_device(): call(functools.partial(displace_kernel, scale=scale), (bf16(2 * HEAD, 2 *...  3.49 us
    pallas_call x1, Pallas kernels, pieces(): call(functools.partial(piece_kernel, cores=0, turns=(1,), **shared), bloc...  2.19 us
  transfers between devices with their start and end apart: 14, of which 7 were waited for; matrix products, arithmetic and copies ran while one was open for 1% of the time, Pallas kernels for 22%

profile of v4, /device:TPU:0, one launch (start us, length us, event | category | flops | bytes accessed | tf_op | source)
XLA Modules:
  0.0 66.6 jit_solution(12066457400706278356)
XLA Ops:
  0.0 0.0 copy-start.6
  0.0 0.0 copy-start.7
  0.0 1.2 %reduce = f32[3,2,3,3,288]{4,3,2,1,0:T(4,128)S(1)} reduce(f32[3,2,3,3,1,288]{5,4,3,2,1,0:T(1,128)} %param.17, f32[]{:T(128)} %constant.116), dimensions={4}, to_apply=%param.17.reduce_sub_computation | reduce | bytes 124420 | tf_op args[1]
  1.3 0.0 copy-start
  1.3 1.5 %copy-done = f32[2,3,1,288,256]{4,3,2,1,0:T(8,128)S(1)} copy-done((f32[2,3,1,288,256]{4,3,2,1,0:T(8,128)S(1)}, f32[2,3,1,288,256]{4,3,2,1,0:T(8,128)}, u32[]{:S(2)}) %copy-start) | copy-done | bytes 1769496
  2.7 0.8 %shard_map.154 = (f32[2,2016,128]{2,1,0:T(8,128)S(1)}, f32[312,128]{1,0:T(8,128)S(1)}, f32[2,144,128]{2,1,0:T(8,128)S(1)}, f32[2,144,128]{2,1,0:T(8,128)S(1)}, f...) custom-call(f32[6,288,256]{2,1,0:T(8,128)S(1)} %bitcast.2, f32[54,288]{1,0:T(8,128)S(1)} %reshape.10.l_ref), custom_call_target="tpu_custom_call" | custom-call | tf_op jit(solution)/shard_map/pallas_call | solution.py:557
  3.5 3.1 %collective-permute-start = (f32[2,144,128]{2,1,0:T(8,128)S(1)}, f32[2,144,128]{2,1,0:T(8,128)S(1)}, u32[]{:S(2)}, u32[]{:S(2)}) collective-permute-start(f32[2,144,128]{2,1,0:T(8,128)S(1)} %get-tuple-element.41), channel_id=1, source_target_pairs={{0,4},{1,5},{2,6},{3,7},{4,8},{5,9},{6,10},{7,11},{8,12},{9,13},{1... | collective-permute-start | bytes 442376 | tf_op jit(solution)/shard_map/ppermute | solution.py:504
  6.6 2.1 %collective-permute-start.1 = (f32[2,144,128]{2,1,0:T(8,128)S(1)}, f32[2,144,128]{2,1,0:T(8,128)S(1)}, u32[]{:S(2)}, u32[]{:S(2)}) collective-permute-start(f32[2,144,128]{2,1,0:T(8,128)S(1)} %get-tuple-element.42), channel_id=1, source_target_pairs={{0,12},{1,13},{2,14},{3,15},{4,0},{5,1},{6,2},{7,3},{8,4},{9,5},{1... | collective-permute-start | bytes 442376 | tf_op jit(solution)/shard_map/ppermute | solution.py:504
  8.7 0.0 collective-permute-start.2
  8.7 4.4 %collective-permute-start.3 = (f32[2,144,128]{2,1,0:T(8,128)S(1)}, f32[2,144,128]{2,1,0:T(8,128)S(1)}, u32[]{:S(2)}, u32[]{:S(2)}) collective-permute-start(f32[2,144,128]{2,1,0:T(8,128)S(1)} %get-tuple-element.44), channel_id=1, source_target_pairs={{0,15},{1,0},{2,1},{3,2},{4,3},{5,4},{6,5},{7,6},{8,7},{9,8},{10,9... | collective-permute-start | bytes 442376 | tf_op jit(solution)/shard_map/ppermute | solution.py:504
  13.1 0.0 copy-done.12
  13.2 0.0 copy-done.13
  13.2 0.0 copy-done.14
  13.2 0.0 copy-done.4
  13.2 0.0 copy-done.5
  13.2 0.0 copy-done.6
  13.2 0.0 copy-done.7
  13.2 2.0 %shard_map.156 = (bf16[1728,432]{1,0:T(8,128)(2,1)S(1)}, bf16[1728,432]{1,0:T(8,128)(2,1)S(1)}) custom-call(f32[312,128]{1,0:T(8,128)S(1)} %get-tuple-element.38.wc_ref, s32[6,512]{1,0:T(8,128)S(1)} %copy-done.4, f32[6,512]{1,0:T(8,128)S(1)} %copy-done.5, s32[6,512]{1,0:T(8,128)S(1)} %copy-done.6, f32[6,512]{1,0:T(8,128)S(1)} %copy-done.7), custom_call_target="tpu_custom_call" | custom-call | flops 1073741824 | bytes 4194304 | tf_op jit(solution)/shard_map/pallas_call | solution.py:630
  15.2 0.0 copy-start.10
  15.2 1.8 %shard_map.157.part_ref = f32[2,2016,128]{2,1,0:T(8,128)S(1)} custom-call(f32[2,2016,128]{2,1,0:T(8,128)S(1)} %get-tuple-element.35.fr_ref.f_ref, bf16[1728,432]{1,0:T(8,128)(2,1)S(1)} %get-tuple-element.39.oh_ref, bf16[1728,432]{1,0:T(8,128)(2,1)S(1)} %get-tuple-element.40.ol_ref), custom_call_target="tpu_custom_call" | custom-call | flops 53084160 | bytes 3145728 | tf_op jit(solution)/shard_map/pallas_call | solution.py:573
  17.0 0.0 copy-done.10
  17.0 0.0 copy-start.11
  17.0 0.2 slice_reduce_fusion.2
  17.2 0.0 copy-start.3
  17.2 0.0 copy-start.8
  17.2 0.0 copy-start.9
  17.3 0.0 collective-permute-done.rxlo
  17.3 0.0 collective-permute-done.1.rxhi
  17.3 0.9 %collective-permute-done.2.rylo = f32[2,144,128]{2,1,0:T(8,128)S(1)} collective-permute-done((f32[2,144,128]{2,1,0:T(8,128)S(1)}, f32[2,144,128]{2,1,0:T(8,128)S(1)}, u32[]{:S(2)}, u32[]{:S(2)}) %collective-permute-start.2) | collective-permute-done | bytes 147488 | tf_op jit(solution)/shard_map/ppermute | solution.py:504
  18.2 0.0 collective-permute-done.3.ryhi
  18.2 1.1 %shard_map.158 = (f32[2,2016,128]{2,1,0:T(8,128)S(1)}, f32[2,2,288,128]{3,2,1,0:T(8,128)S(1)}, f32[2,144,128]{2,1,0:T(8,128)S(1)}, f32[2,144,128]{2,1,0:T(8,128)...) custom-call(f32[2,2016,128]{2,1,0:T(8,128)S(1)} %shard_map.157.part_ref, ...), custom_call_target="tpu_custom_call" | custom-call | tf_op jit(solution)/shard_map/pallas_call | solution.py:587
  19.3 0.1 collective-permute-start.4
  19.4 3.8 %collective-permute-start.5 = (f32[2,144,128]{2,1,0:T(8,128)S(1)}, f32[2,144,128]{2,1,0:T(8,128)S(1)}, u32[]{:S(2)}, u32[]{:S(2)}) collective-permute-start(f32[2,144,128]{2,1,0:T(8,128)S(1)} %get-tuple-element.52), channel_id=1, source_target_pairs={{0,12},{1,13},{2,14},{3,15},{4,0},{5,1},{6,2},{7,3},{8,4},{9,5},{1... | collective-permute-start | bytes 442376 | tf_op jit(solution)/shard_map/ppermute | solution.py:504
  23.2 0.0 collective-permute-start.6
  23.2 4.4 %collective-permute-start.7 = (f32[2,144,128]{2,1,0:T(8,128)S(1)}, f32[2,144,128]{2,1,0:T(8,128)S(1)}, u32[]{:S(2)}, u32[]{:S(2)}) collective-permute-start(f32[2,144,128]{2,1,0:T(8,128)S(1)} %get-tuple-element.54), channel_id=1, source_target_pairs={{0,15},{1,0},{2,1},{3,2},{4,3},{5,4},{6,5},{7,6},{8,7},{9,8},{10,9... | collective-permute-start | bytes 442376 | tf_op jit(solution)/shard_map/ppermute | solution.py:504
  27.6 0.3 fusion.21
  27.9 1.7 %shard_map.155 = (bf16[1024,1536]{1,0:T(8,128)(2,1)S(1)}, bf16[1024,1536]{1,0:T(8,128)(2,1)S(1)}) custom-call(f32[2,2016,128]{2,1,0:T(8,128)S(1)} %get-tuple-element.35.fr_ref.f_ref, f32[4,1152]{1,0:T(4,128)S(1)} %get-tuple-element.69.cos_ref, f32[4,1152]{1,0:T(4,128)S(1)} %get-tuple-element.68.sin_ref), custom_call_target="tpu_custom_call" | custom-call | flops 53084160 | bytes 8388608 | tf_op jit(solution)/shard_map/pallas_call | solution.py:578
  29.7 2.2 %shard_map.161 = (bf16[1728,576]{1,0:T(8,128)(2,1)S(1)}, bf16[1728,576]{1,0:T(8,128)(2,1)S(1)}) custom-call(f32[312,128]{1,0:T(8,128)S(1)} %get-tuple-element.38.wc_ref, s32[6,640]{1,0:T(8,128)S(1)} %copy-done.2, f32[6,640]{1,0:T(8,128)S(1)} %copy-done.3, s32[6,256]{1,0:T(8,128)S(1)} %copy-done.8, f32[6,256]{1,0:T(8,128)S(1)} %copy-done.9), custom_call_target="tpu_custom_call" | custom-call | flops 1073741824 | bytes 4194304 | tf_op jit(solution)/shard_map/pallas_call | solution.py:630
  31.9 1.7 %shard_map.160.part_ref = f32[2,2016,128]{2,1,0:T(8,128)S(1)} custom-call(f32[2,2016,128]{2,1,0:T(8,128)S(1)} %get-tuple-element.48.f_ref, bf16[1728,432]{1,0:T(8,128)(2,1)S(1)} %get-tuple-element.39.oh_ref, bf16[1728,432]{1,0:T(8,128)(2,1)S(1)} %get-tuple-element.40.ol_ref), custom_call_target="tpu_custom_call" | custom-call | flops 53084160 | bytes 3145728 | tf_op jit(solution)/shard_map/pallas_call | solution.py:589
  33.6 0.0 copy-start.1
  33.6 0.9 %shard_map.159 = (bf16[1024,768]{1,0:T(8,128)(2,1)S(1)}, bf16[1024,768]{1,0:T(8,128)(2,1)S(1)}) custom-call(f32[2,2016,128]{2,1,0:T(8,128)S(1)} %get-tuple-element.35.fr_ref.f_ref, f32[2,2,288,128]{3,2,1,0:T(8,128)S(1)} %get-tuple-element.45.save, f32[4,1152]{1,0:T(4,128)S(1)} %get-tuple-element.69.cos_ref, f32[4,1152]{1,0:T(4,128)S(1)} %get-tuple-element.68.sin_ref), custom_call_target="tpu_custom_call" | custom-call | flops 53084160 | bytes 4194304 | tf_op jit(solution)/shard_map/pallas_call | solution.py:591
  34.5 0.0 collective-permute-done.4.rxlo
  34.5 0.0 collective-permute-done.5.rxhi
  34.5 0.0 collective-permute-done.6.rylo
  34.5 0.0 collective-permute-done.7.ryhi
  34.5 3.5 %shard_map.162 = (bf16[1536,512]{1,0:T(8,128)(2,1)S(1)}, bf16[1536,512]{1,0:T(8,128)(2,1)S(1)}, bf16[768,512]{1,0:T(8,128)(2,1)S(1)}, bf16[768,512]{1,0:T(8,128)(2,1)S(1)}) custom-call(f32[2,2016,128]{2,1,0:T(8,128)S(1)} %shard_map.160.part_ref, f32[312,128]{1,0:T(8,128)S(1)} %get-tuple-element.38.wc_ref, bf16[1728,576]{1,0:T(8,128)(2,1)S(1)} %get-tuple-element.49.oh_ref, ...), custom_call_target="tpu_custom_call" | custom-call | tf_op jit(solution)/shard_map/pallas_call | solution.py:593
  38.0 3.8 %shard_map.164 = f32[8,16,2048]{2,1,0:T(8,128)S(1)} custom-call(bf16[1024,1536]{1,0:T(8,128)(2,1)S(1)} %get-tuple-element.36.refs_0_, bf16[1024,1536]{1,0:T(8,128)(2,1)S(1)} %get-tuple-element.37.refs_1_, bf16[1024,768]{1,0:T(8,128)(2,1)S(1)} %get-tuple-element.46.refs_2_, bf16[1024,768]{1,0:T(8,128)(2,1)S(1)} %get-tuple-element.47.refs_3_, ...), custom_call_target="tpu_custom_call" | custom-call | flops 1811939328 | bytes 1048576 | tf_op jit(solution)/shard_map/pallas_call | solution.py:652
  41.8 0.1 collective-permute-start.8
  41.9 2.2 %shard_map.166.mine = f32[4,16,2048]{2,1,0:T(8,128)S(1)} custom-call(bf16[1024,1536]{1,0:T(8,128)(2,1)S(1)} %get-tuple-element.36.refs_0_, bf16[1024,1536]{1,0:T(8,128)(2,1)S(1)} %get-tuple-element.37.refs_1_, bf16[1024,768]{1,0:T(8,128)(2,1)S(1)} %get-tuple-element.46.refs_2_, bf16[1024,768]{1,0:T(8,128)(2,1)S(1)} %get-tuple-element.47.refs_3_, ...), custom_call_target="tpu_custom_call" | custom-call | flops 1811939328 | bytes 1048576 | tf_op jit(solution)/shard_map/pallas_call | solution.py:656
  44.1 0.4 collective-permute-done.8.theirs
  44.6 0.1 shard_map.167
  44.6 0.1 collective-permute-start.10
  44.7 2.0 %collective-permute-start.9 = (f32[2,16,2048]{2,1,0:T(8,128)S(1)}, f32[2,16,2048]{2,1,0:T(8,128)S(1)}, u32[]{:S(2)}, u32[]{:S(2)}) collective-permute-start(f32[2,16,2048]{2,1,0:T(8,128)S(1)} %get-tuple-element.59), channel_id=1, source_target_pairs={{0,2},{1,3},{2,0},{3,1},{4,6},{5,7},{6,4},{7,5},{8,10},{9,11},{10,... | collective-permute-start | bytes 786440 | tf_op jit(solution)/shard_map/ppermute | solution.py:668
  46.7 2.0 %shard_map.163.mine = f32[4,16,2048]{2,1,0:T(8,128)S(1)} custom-call(bf16[1024,1536]{1,0:T(8,128)(2,1)S(1)} %get-tuple-element.36.refs_0_, bf16[1024,1536]{1,0:T(8,128)(2,1)S(1)} %get-tuple-element.37.refs_1_, bf16[1024,768]{1,0:T(8,128)(2,1)S(1)} %get-tuple-element.46.refs_2_, bf16[1024,768]{1,0:T(8,128)(2,1)S(1)} %get-tuple-element.47.refs_3_, ...), custom_call_target="tpu_custom_call" | custom-call | flops 1811939328 | bytes 1048576 | tf_op jit(solution)/shard_map/pallas_call | solution.py:669
  48.7 0.1 shard_map.165.mine
  48.8 5.1 %collective-permute-done.10.theirs = f32[2,16,2048]{2,1,0:T(8,128)S(1)} collective-permute-done((f32[2,16,2048]{2,1,0:T(8,128)S(1)}, f32[2,16,2048]{2,1,0:T(8,128)S(1)}, u32[]{:S(2)}, u32[]{:S(2)}) %collective-permute-start.10) | collective-permute-done | bytes 262176 | tf_op jit(solution)/shard_map/ppermute | solution.py:667
  53.9 0.1 collective-permute-start.11
  54.0 0.1 collective-permute-start.12
  54.1 4.6 %collective-permute-done.9.theirs = f32[2,16,2048]{2,1,0:T(8,128)S(1)} collective-permute-done((f32[2,16,2048]{2,1,0:T(8,128)S(1)}, f32[2,16,2048]{2,1,0:T(8,128)S(1)}, u32[]{:S(2)}, u32[]{:S(2)}) %collective-permute-start.9) | collective-permute-done | bytes 262176 | tf_op jit(solution)/shard_map/ppermute | solution.py:668
  58.7 0.1 collective-permute-start.13
  58.8 3.4 %collective-permute-done.11 = f32[1,16,2048]{2,1,0:T(8,128)S(1)} collective-permute-done((f32[1,16,2048]{2,1,0:T(8,128)S(1)}, f32[1,16,2048]{2,1,0:T(8,128)S(1)}, u32[]{:S(2)}, u32[]{:S(2)}) %collective-permute-start.11) | collective-permute-done | bytes 131104 | tf_op jit(solution)/shard_map/ppermute | solution.py:687
  62.2 3.1 %collective-permute-done.12 = f32[1,16,2048]{2,1,0:T(8,128)S(1)} collective-permute-done((f32[1,16,2048]{2,1,0:T(8,128)S(1)}, f32[1,16,2048]{2,1,0:T(8,128)S(1)}, u32[]{:S(2)}, u32[]{:S(2)}) %collective-permute-start.12) | collective-permute-done | bytes 131104 | tf_op jit(solution)/shard_map/ppermute | solution.py:687
  65.3 0.5 collective-permute-done.13
  65.8 0.8 %reshape_squeeze.3 = f32[16,4,2,256]{3,2,1,0:T(2,128)} reshape(f32[1,16,2048]{2,1,0:T(8,128)S(1)} %add_add_fusion) | data formatting | bytes 262144 | tf_op jit(solution)/shard_map/reshape;squeeze | solution.py:609
  (17 shorter events, 0.2 us)
Async XLA Ops:
  0.0 13.2 %copy-start.12 = (s32[1152]{0:T(1024)S(1)}, s32[1152]{0:T(1024)}, u32[]{:S(2)}) copy-start(s32[1152]{0:T(1024)} %constant.106.clone) | copy-start | bytes 13828
  0.0 13.2 %copy-start.13 = (s32[1152]{0:T(1024)S(1)}, s32[1152]{0:T(1024)}, u32[]{:S(2)}) copy-start(s32[1152]{0:T(1024)} %constant.107.clone) | copy-start | bytes 13828
  0.0 13.2 %copy-start.14 = (s32[1152]{0:T(1024)S(1)}, s32[1152]{0:T(1024)}, u32[]{:S(2)}) copy-start(s32[1152]{0:T(1024)} %constant.108.clone) | copy-start | bytes 13828
  0.0 13.2 %copy-start.4 = (s32[6,512]{1,0:T(8,128)S(1)}, s32[6,512]{1,0:T(8,128)}, u32[]{:S(2)}) copy-start(s32[6,512]{1,0:T(8,128)} %constant.102.clone.column_ref) | copy-start | bytes 36868
  0.0 13.2 %copy-start.5 = (f32[6,512]{1,0:T(8,128)S(1)}, f32[6,512]{1,0:T(8,128)}, u32[]{:S(2)}) copy-start(f32[6,512]{1,0:T(8,128)} %constant.103.clone.sign_ref) | copy-start | bytes 36868
  0.0 13.2 %copy-start.6 = (s32[6,512]{1,0:T(8,128)S(1)}, s32[6,512]{1,0:T(8,128)}, u32[]{:S(2)}) copy-start(s32[6,512]{1,0:T(8,128)} %constant.104.clone.more_ref) | copy-start | bytes 36868
  0.0 13.2 %copy-start.7 = (f32[6,512]{1,0:T(8,128)S(1)}, f32[6,512]{1,0:T(8,128)}, u32[]{:S(2)}) copy-start(f32[6,512]{1,0:T(8,128)} %constant.105.clone.moresign_ref) | copy-start | bytes 36868
  1.3 1.5 %copy-start = (f32[2,3,1,288,256]{4,3,2,1,0:T(8,128)S(1)}, f32[2,3,1,288,256]{4,3,2,1,0:T(8,128)}, u32[]{:S(2)}) copy-start(f32[2,3,1,288,256]{4,3,2,1,0:T(8,128)} %param.16) | copy-start | bytes 5308420
  3.5 13.8 %collective-permute-start = (f32[2,144,128]{2,1,0:T(8,128)S(1)}, f32[2,144,128]{2,1,0:T(8,128)S(1)}, u32[]{:S(2)}, u32[]{:S(2)}) collective-permute-start(f32[2,144,128]{2,1,0:T(8,128)S(1)} %get-tuple-element.41), channel_id=1, source_target_pairs={{0,4},{1,5},{2,6},{3,7},{4,8},{5,9},{6,10},{7,11},{8,12},{9,13},{1... | collective-permute-start | bytes 442376 | tf_op jit(solution)/shard_map/ppermute | solution.py:504
  6.6 10.7 %collective-permute-start.1 = (f32[2,144,128]{2,1,0:T(8,128)S(1)}, f32[2,144,128]{2,1,0:T(8,128)S(1)}, u32[]{:S(2)}, u32[]{:S(2)}) collective-permute-start(f32[2,144,128]{2,1,0:T(8,128)S(1)} %get-tuple-element.42), channel_id=1, source_target_pairs={{0,12},{1,13},{2,14},{3,15},{4,0},{5,1},{6,2},{7,3},{8,4},{9,5},{1... | collective-permute-start | bytes 442376 | tf_op jit(solution)/shard_map/ppermute | solution.py:504
  8.7 9.5 %collective-permute-start.2 = (f32[2,144,128]{2,1,0:T(8,128)S(1)}, f32[2,144,128]{2,1,0:T(8,128)S(1)}, u32[]{:S(2)}, u32[]{:S(2)}) collective-permute-start(f32[2,144,128]{2,1,0:T(8,128)S(1)} %get-tuple-element.43), channel_id=1, source_target_pairs={{0,1},{1,2},{2,3},{3,4},{4,5},{5,6},{6,7},{7,8},{8,9},{9,10},{10,1... | collective-permute-start | bytes 442376 | tf_op jit(solution)/shard_map/ppermute | solution.py:504
  8.7 9.5 %collective-permute-start.3 = (f32[2,144,128]{2,1,0:T(8,128)S(1)}, f32[2,144,128]{2,1,0:T(8,128)S(1)}, u32[]{:S(2)}, u32[]{:S(2)}) collective-permute-start(f32[2,144,128]{2,1,0:T(8,128)S(1)} %get-tuple-element.44), channel_id=1, source_target_pairs={{0,15},{1,0},{2,1},{3,2},{4,3},{5,4},{6,5},{7,6},{8,7},{9,8},{10,9... | collective-permute-start | bytes 442376 | tf_op jit(solution)/shard_map/ppermute | solution.py:504
  15.2 1.8 %copy-start.10 = (s32[4,3]{1,0:T(4,128)S(1)}, s32[4,3]{1,0:T(4,128)}, u32[]{:S(2)}) copy-start(s32[4,3]{1,0:T(4,128)} %param.18) | copy-start | bytes 148
  17.0 10.6 %copy-start.11 = (s32[1152]{0:T(1024)S(1)}, s32[1152]{0:T(1024)}, u32[]{:S(2)}) copy-start(s32[1152]{0:T(1024)} %constant.109.clone) | copy-start | bytes 13828
  17.2 12.4 %copy-start.2 = (s32[6,640]{1,0:T(8,128)S(1)}, s32[6,640]{1,0:T(8,128)}, u32[]{:S(2)}) copy-start(s32[6,640]{1,0:T(8,128)} %constant.110.clone.column_ref) | copy-start | bytes 46084
  17.2 12.4 %copy-start.3 = (f32[6,640]{1,0:T(8,128)S(1)}, f32[6,640]{1,0:T(8,128)}, u32[]{:S(2)}) copy-start(f32[6,640]{1,0:T(8,128)} %constant.111.clone.sign_ref) | copy-start | bytes 46084
  17.2 12.4 %copy-start.8 = (s32[6,256]{1,0:T(8,128)S(1)}, s32[6,256]{1,0:T(8,128)}, u32[]{:S(2)}) copy-start(s32[6,256]{1,0:T(8,128)} %constant.112.clone.more_ref) | copy-start | bytes 18436
  17.2 12.4 %copy-start.9 = (f32[6,256]{1,0:T(8,128)S(1)}, f32[6,256]{1,0:T(8,128)}, u32[]{:S(2)}) copy-start(f32[6,256]{1,0:T(8,128)} %constant.113.clone.moresign_ref) | copy-start | bytes 18436
  19.3 15.2 %collective-permute-start.4 = (f32[2,144,128]{2,1,0:T(8,128)S(1)}, f32[2,144,128]{2,1,0:T(8,128)S(1)}, u32[]{:S(2)}, u32[]{:S(2)}) collective-permute-start(f32[2,144,128]{2,1,0:T(8,128)S(1)} %get-tuple-element.51), channel_id=1, source_target_pairs={{0,4},{1,5},{2,6},{3,7},{4,8},{5,9},{6,10},{7,11},{8,12},{9,13},{1... | collective-permute-start | bytes 442376 | tf_op jit(solution)/shard_map/ppermute | solution.py:504
  19.4 15.1 %collective-permute-start.5 = (f32[2,144,128]{2,1,0:T(8,128)S(1)}, f32[2,144,128]{2,1,0:T(8,128)S(1)}, u32[]{:S(2)}, u32[]{:S(2)}) collective-permute-start(f32[2,144,128]{2,1,0:T(8,128)S(1)} %get-tuple-element.52), channel_id=1, source_target_pairs={{0,12},{1,13},{2,14},{3,15},{4,0},{5,1},{6,2},{7,3},{8,4},{9,5},{1... | collective-permute-start | bytes 442376 | tf_op jit(solution)/shard_map/ppermute | solution.py:504
  23.2 11.3 %collective-permute-start.6 = (f32[2,144,128]{2,1,0:T(8,128)S(1)}, f32[2,144,128]{2,1,0:T(8,128)S(1)}, u32[]{:S(2)}, u32[]{:S(2)}) collective-permute-start(f32[2,144,128]{2,1,0:T(8,128)S(1)} %get-tuple-element.53), channel_id=1, source_target_pairs={{0,1},{1,2},{2,3},{3,4},{4,5},{5,6},{6,7},{7,8},{8,9},{9,10},{10,1... | collective-permute-start | bytes 442376 | tf_op jit(solution)/shard_map/ppermute | solution.py:504
  23.2 11.3 %collective-permute-start.7 = (f32[2,144,128]{2,1,0:T(8,128)S(1)}, f32[2,144,128]{2,1,0:T(8,128)S(1)}, u32[]{:S(2)}, u32[]{:S(2)}) collective-permute-start(f32[2,144,128]{2,1,0:T(8,128)S(1)} %get-tuple-element.54), channel_id=1, source_target_pairs={{0,15},{1,0},{2,1},{3,2},{4,3},{5,4},{6,5},{7,6},{8,7},{9,8},{10,9... | collective-permute-start | bytes 442376 | tf_op jit(solution)/shard_map/ppermute | solution.py:504
  33.6 1.0 %copy-start.1 = (s32[256]{0:T(256)S(1)}, s32[256]{0:T(256)}, u32[]{:S(2)}) copy-start(s32[256]{0:T(256)} %param.19) | copy-start | bytes 3076
  41.8 2.7 %collective-permute-start.8 = (f32[8,16,2048]{2,1,0:T(8,128)S(1)}, f32[8,16,2048]{2,1,0:T(8,128)S(1)}, u32[]{:S(2)}, u32[]{:S(2)}) collective-permute-start(f32[8,16,2048]{2,1,0:T(8,128)S(1)} %shard_map.164), channel_id=1, source_target_pairs={{0,1},{1,0},{2,3},{3,2},{4,5},{5,4},{6,7},{7,6},{8,9},{9,8},{10,11... | collective-permute-start | bytes 3145736 | tf_op jit(solution)/shard_map/ppermute | solution.py:655
  44.6 9.2 %collective-permute-start.10 = (f32[2,16,2048]{2,1,0:T(8,128)S(1)}, f32[2,16,2048]{2,1,0:T(8,128)S(1)}, u32[]{:S(2)}, u32[]{:S(2)}) collective-permute-start(f32[2,16,2048]{2,1,0:T(8,128)S(1)} %get-tuple-element.61), channel_id=1, source_target_pairs={{0,2},{1,3},{2,0},{3,1},{4,6},{5,7},{6,4},{7,5},{8,10},{9,11},{10,... | collective-permute-start | bytes 786440 | tf_op jit(solution)/shard_map/ppermute | solution.py:667
  44.7 14.0 %collective-permute-start.9 = (f32[2,16,2048]{2,1,0:T(8,128)S(1)}, f32[2,16,2048]{2,1,0:T(8,128)S(1)}, u32[]{:S(2)}, u32[]{:S(2)}) collective-permute-start(f32[2,16,2048]{2,1,0:T(8,128)S(1)} %get-tuple-element.59), channel_id=1, source_target_pairs={{0,2},{1,3},{2,0},{3,1},{4,6},{5,7},{6,4},{7,5},{8,10},{9,11},{10,... | collective-permute-start | bytes 786440 | tf_op jit(solution)/shard_map/ppermute | solution.py:668
  53.9 8.3 %collective-permute-start.11 = (f32[1,16,2048]{2,1,0:T(8,128)S(1)}, f32[1,16,2048]{2,1,0:T(8,128)S(1)}, u32[]{:S(2)}, u32[]{:S(2)}) collective-permute-start(f32[1,16,2048]{2,1,0:T(8,128)S(1)} %get-tuple-element.62), channel_id=1, source_target_pairs={{0,4},{1,5},{2,6},{3,7},{4,8},{5,9},{6,10},{7,11},{8,12},{9,13},{1... | collective-permute-start | bytes 393224 | tf_op jit(solution)/shard_map/ppermute | solution.py:687
  54.0 11.4 %collective-permute-start.12 = (f32[1,16,2048]{2,1,0:T(8,128)S(1)}, f32[1,16,2048]{2,1,0:T(8,128)S(1)}, u32[]{:S(2)}, u32[]{:S(2)}) collective-permute-start(f32[1,16,2048]{2,1,0:T(8,128)S(1)} %get-tuple-element.63), channel_id=1, source_target_pairs={{0,8},{1,9},{2,10},{3,11},{4,12},{5,13},{6,14},{7,15},{8,0},{9,1},... | collective-permute-start | bytes 393224 | tf_op jit(solution)/shard_map/ppermute | solution.py:687
  58.7 7.1 %collective-permute-start.13 = (f32[1,16,2048]{2,1,0:T(8,128)S(1)}, f32[1,16,2048]{2,1,0:T(8,128)S(1)}, u32[]{:S(2)}, u32[]{:S(2)}) collective-permute-start(f32[1,16,2048]{2,1,0:T(8,128)S(1)} %get-tuple-element.64), channel_id=1, source_target_pairs={{0,12},{1,13},{2,14},{3,15},{4,0},{5,1},{6,2},{7,3},{8,4},{9,5},{1... | collective-permute-start | bytes 393224 | tf_op jit(solution)/shard_map/ppermute | solution.py:687

commit v5 on v4

--- a/solution.py
+++ b/solution.py
@@ -9,6 +9,7 @@
 from jax.experimental.pallas import tpu as pltpu
 from jax.sharding import PartitionSpec as P
 
+
 TLX = 12
 TLY = 12
 LZ = 2
@@ -21,7 +22,6 @@
 BOTH = 2 * XROWS
 PADDED = (TLX + 2) * BOTH
 WINDOW = 3 * BOTH
-SPLIT = 4 * BOTH
 EDGE = 4 * XROWS
 HEAD = MAIN // 128 * 128
 TAIL = MAIN - HEAD + EDGE
@@ -93,28 +93,32 @@
     return pl.ds(BOTH + part * XROWS + colour * LAYER + z * TLY + y, TLX, stride=BOTH)
 
 
-def send_layers(f_ref, wc_ref, xlo_ref, xhi_ref, ylo_ref, yhi_ref):
+def parity(tiles):
+    position = lax.axis_index("site")
+    return position // tiles % 2 == 0, position % 2 == 0
+
+
+def send_layers(f_ref, wc_ref, ax_ref, bx_ref, ay_ref, by_ref, tiles):
     last = TLX * BOTH
+    even_x, even_y = parity(tiles)
     for half in range(f_ref.shape[0]):
-        xlo_ref[half] = f_ref[half, BOTH : 2 * BOTH, :]
-        for part in range(2):
-            for colour in range(3):
-                for z in range(LZ):
-                    to = part * XROWS + colour * LAYER + z * TLX
-                    ylo_ref[half, to : to + TLX, :] = f_ref[half, y_rows(part, colour, z, 0), :]
         table = wc_ref[TLX * LAYER : (TLX + 1) * LAYER, :]
         hop = matvec(table, CX, grid2(lambda p, c: layer_rows(f_ref, p, half, last + c * LAYER)), adjoint=True)
         for part in range(2):
             for colour in range(3):
                 to = part * XROWS + colour * LAYER
-                xhi_ref[half, to : to + LAYER, :] = hop[part][colour]
+                low, high = f_ref[half, BOTH + to : BOTH + to + LAYER, :], hop[part][colour]
+                ax_ref[half, to : to + LAYER, :] = jnp.where(even_x, high, low)
+                bx_ref[half, to : to + LAYER, :] = jnp.where(even_x, low, high)
         for z in range(LZ):
             table = wc_ref[pl.ds(LAYER + z * TLY + TLY - 1, TLX, stride=LAYER), :]
             hop = matvec(table, CY, grid2(lambda p, c: f_ref[half, y_rows(p, c, z, TLY - 1), :]), adjoint=True)
             for part in range(2):
                 for colour in range(3):
                     to = part * XROWS + colour * LAYER + z * TLX
-                    yhi_ref[half, to : to + TLX, :] = hop[part][colour]
+                    low, high = f_ref[half, y_rows(part, colour, z, 0), :], hop[part][colour]
+                    ay_ref[half, to : to + TLX, :] = jnp.where(even_y, high, low)
+                    by_ref[half, to : to + TLX, :] = jnp.where(even_y, low, high)
 
 
 def clear_ends(ref):
@@ -123,7 +127,7 @@
         ref[half, PADDED - BOTH : PADDED, :] = jnp.zeros((BOTH, LANES), jnp.float32)
 
 
-def pack_kernel(v_ref, l_ref, fr_ref, wc_ref, xlo_ref, xhi_ref, ylo_ref, yhi_ref, la, lb, ta, tb):
+def pack_kernel(v_ref, l_ref, fr_ref, wc_ref, ax_ref, bx_ref, ay_ref, by_ref, la, lb, ta, tb, *, tiles):
     la[...] = jnp.zeros_like(la)
     lb[...] = jnp.zeros_like(lb)
     plane = SITES // LZ
@@ -167,7 +171,7 @@
                         fr_ref[half, dst : dst + TLY, :] = v_ref[
                             3 * part + colour, src : src + TLY, half * LANES : (half + 1) * LANES
                         ]
-    send_layers(fr_ref, wc_ref, xlo_ref, xhi_ref, ylo_ref, yhi_ref)
+    send_layers(fr_ref, wc_ref, ax_ref, bx_ref, ay_ref, by_ref, tiles)
 
 
 def split(value):
@@ -276,19 +280,29 @@
             out_ref[half, at, :] = (1.0 - 6.0 * KAPPA) * f_ref[half, at, :] + KAPPA * hops[:, lanes]
 
 
-def cross(once_ref, wc_ref, rxlo, rxhi, rylo, ryhi, save=None):
+def cross(once_ref, wc_ref, received, tiles, save=None):
     last = TLX * BOTH
+    even_x, even_y = parity(tiles)
+    ax, bx, ay, by = received
+
+    def arrived(above, half, part, first, size, along_y):
+        one, two, even = (ay, by, even_y) if along_y else (ax, bx, even_x)
+        values = (layer_rows(ref, part, half, first, size) for ref in ((one, two) if above else (two, one)))
+        return jnp.where(even, *values)
+
     for half in range(once_ref.shape[0]):
         table = wc_ref[TLX * LAYER : (TLX + 1) * LAYER, :]
-        hop_x = matvec(table, CX, grid2(lambda p, c: layer_rows(rxhi, p, half, c * LAYER)))
+        hop_x = matvec(table, CX, grid2(lambda p, c: arrived(True, half, p, c * LAYER, LAYER, False)))
         hop_y = []
         for z in range(LZ):
             table = wc_ref[pl.ds(LAYER + z * TLY + TLY - 1, TLX, stride=LAYER), :]
-            hop_y.append(matvec(table, CY, grid2(lambda p, c: layer_rows(ryhi, p, half, c * LAYER + z * TLX, TLX))))
+            hop_y.append(
+                matvec(table, CY, grid2(lambda p, c: arrived(True, half, p, c * LAYER + z * TLX, TLX, True)))
+            )
         for part in range(2):
             for colour in range(3):
                 at = colour * LAYER
-                low = layer_rows(rxlo, part, half, at)
+                low = arrived(False, half, part, at, LAYER, False)
                 to = part * XROWS + at
                 once_ref[half, BOTH + to : BOTH + to + LAYER, :] += KAPPA * low
                 once_ref[half, last + to : last + to + LAYER, :] += KAPPA * hop_x[part][colour]
@@ -296,7 +310,7 @@
                     save[part, half, at : at + LAYER, :] = low
                     save[part, half, XROWS + at : XROWS + at + LAYER, :] = hop_x[part][colour]
                 for z in range(LZ):
-                    low = layer_rows(rylo, part, half, at + z * TLX, TLX)
+                    low = arrived(False, half, part, at + z * TLX, TLX, True)
                     rows = y_rows(part, colour, z, 0)
                     once_ref[half, rows, :] = once_ref[half, rows, :] + KAPPA * low
                     rows = y_rows(part, colour, z, TLY - 1)
@@ -307,10 +321,11 @@
                         save[part, half, to + XROWS : to + XROWS + TLX, :] = hop_y[z][part][colour]
 
 
-def edge_kernel(part_ref, wc_ref, rxlo, rxhi, rylo, ryhi, once_ref, save, xlo_ref, xhi_ref, ylo_ref, yhi_ref):
+def edge_kernel(part_ref, wc_ref, rax, rbx, ray, rby, *refs, tiles):
+    once_ref, save, ax_ref, bx_ref, ay_ref, by_ref = refs[-6:]
     once_ref[...] = part_ref[...]
-    cross(once_ref, wc_ref, rxlo, rxhi, rylo, ryhi, save)
-    send_layers(once_ref, wc_ref, xlo_ref, xhi_ref, ylo_ref, yhi_ref)
+    cross(once_ref, wc_ref, (rax, rbx, ray, rby), tiles, save)
+    send_layers(once_ref, wc_ref, ax_ref, bx_ref, ay_ref, by_ref, tiles)
 
 
 def phased(real, imag, half, lane, at, size, cos_ref, sin_ref, ah_ref, al_ref):
@@ -354,9 +369,12 @@
             phased(real, imag, half, HEAD + at, at, TAIL, cos_ref, sin_ref, ah_ref, al_ref)
 
 
-def displace_kernel(part_ref, wc_ref, oh_ref, ol_ref, rxlo, rxhi, rylo, ryhi, dir_ref, sh_ref, sl_ref, th_ref, tl_ref, twice, shift, fh, fl, *, scale):
+def displace_kernel(
+    part_ref, wc_ref, oh_ref, ol_ref, rax, rbx, ray, rby, dir_ref, *refs, scale, tiles
+):
+    sh_ref, sl_ref, th_ref, tl_ref, twice, shift, fh, fl = refs[-8:]
     twice[...] = part_ref[...]
-    cross(twice, wc_ref, rxlo, rxhi, rylo, ryhi)
+    cross(twice, wc_ref, (rax, rbx, ray, rby), tiles)
     halves = range(twice.shape[0])
     width = len(halves) * LANES
 
@@ -365,12 +383,12 @@
 
     for half in halves:
         lanes = slice(half * LANES, (half + 1) * LANES)
+        masks = [jnp.where(along(which, lanes, BOTH), 1.0, 0.0).astype(jnp.bfloat16) for which in range(3)]
         for row in range(0, PADDED, BOTH):
-            value = scale * twice[half, row : row + BOTH, :]
+            high, low = split(scale * twice[half, row : row + BOTH, :])
             for which in range(3):
-                high, low = split(jnp.where(along(which, lanes, BOTH), value, 0.0))
-                fh[which, row : row + BOTH, lanes] = high
-                fl[which, row : row + BOTH, lanes] = low
+                fh[which, row : row + BOTH, lanes] = high * masks[which]
+                fl[which, row : row + BOTH, lanes] = low * masks[which]
     for x in range(TLX):
         rows = slice(x * BOTH, (x + 1) * BOTH)
         low, mid, top = (slice((x + k) * BOTH, (x + k + 1) * BOTH) for k in range(3))
@@ -449,24 +467,26 @@
             out_ref[k, :, lanes] = block
 
 
-def owners(groups, size, cores, turns):
+def owners(groups, size, cores, turn, steps):
     position = lax.axis_index("site")
     core, y, z = position % 2, position // 2 % 2, position // 4
-    core = (core + cores) % 2
-    return [((z + g) % groups * 4 + (y + turn) % 2 * 2 + core) * size for g in range(groups) for turn in turns]
-
-
-def piece_kernel(*refs, moments, groups, cores, turns):
+    return [((z + g) % groups * 4 + (y + turn) % 2 * 2 + (core + cores) % 2) * size for g in steps]
+
+
+def piece_kernel(*refs, moments, groups, cores, turn, steps):
     out_ref = refs[-1]
     size = out_ref.shape[1]
-    blocks = owners(groups, size, cores, turns)
-    put(out_ref, product((blocks, size), moments, refs[:-1]), len(blocks), moments)
-
-
-def merge_kernel(mine, theirs, *outs, picks):
-    for out_ref, pairs in zip(outs, picks):
-        for k, (a, b) in enumerate(pairs):
-            out_ref[k] = mine[a] + theirs[b]
+    blocks = owners(groups, size, cores, turn, steps)
+    put(out_ref, product((blocks, size), moments, refs[:8]), len(blocks), moments)
+
+
+def merge_kernel(*refs, sources, picks):
+    for out_ref, blocks in zip(refs[sources:], picks):
+        for k, places in enumerate(blocks):
+            total = refs[0][places[0]]
+            for ref, at in zip(refs[1:sources], places[1:]):
+                total = total + ref[at]
+            out_ref[k] = total
 
 
 def phases(momenta, position, devices, tiles):
@@ -500,18 +520,12 @@
     return jnp.cos(theta), jnp.sin(theta)
 
 
-def send(block, devices, distance):
-    return lax.ppermute(block, "site", [(i, (i + distance) % devices) for i in range(devices)])
-
-
 def halo(sends, devices, tiles):
-    xlo, xhi, ylo, yhi = sends
-    return (
-        send(xhi, devices, tiles),
-        send(xlo, devices, -tiles),
-        send(yhi, devices, 1),
-        send(ylo, devices, -1),
-    )
+    found = []
+    for block, stride, turn in zip(sends, (tiles, tiles, 1, 1), (1, -1, 1, -1)):
+        route = [(i, (i + (turn if i // stride % 2 == 0 else -turn) * stride) % devices) for i in range(devices)]
+        found.append(lax.ppermute(block, "site", route))
+    return found
 
 
 def stages(devices):
@@ -555,7 +569,7 @@
     layer = f32(halves, BOTH, LANES)
     padded = f32(halves, PADDED, LANES)
     fr, wc, *sends = call(
-        pack_kernel,
+        functools.partial(pack_kernel, tiles=tiles),
         (padded, f32((TLX + 1) * LAYER, LANES), layer, layer, layer, layer),
         [pltpu.VMEM((128, 384), jnp.float32)] * 2 + [pltpu.VMEM((384, 128), jnp.float32)] * 2,
         inputs=2,
@@ -584,14 +598,16 @@
         middle=2 * LANES,
     )
     edges = f32(2, halves, EDGE, LANES)
-    once, save, *sends = call(edge_kernel, (padded, edges, layer, layer, layer, layer), inputs=6)(once, wc, *received)
+    once, save, *sends = call(
+        functools.partial(edge_kernel, tiles=tiles), (padded, edges, layer, layer, layer, layer), inputs=7
+    )(once, wc, *received, ah)
     received = halo(sends, devices, tiles)
     twice = call(smear_kernel, padded, pair, flops, 3 << 20, 3)(once, *smear)
     rows = pltpu.VMEM((2, TAIL, LANES), jnp.float32)
     bh, bl = call(tail_kernel, (tail, tail), [rows], flops, 4 << 20, 4)(fr, save, cosine, sine)
     scale = 1.0 / math.sqrt(3.0 * TLX * tiles * TLY * tiles * LZ)
     operands = call(
-        functools.partial(displace_kernel, scale=scale),
+        functools.partial(displace_kernel, scale=scale, tiles=tiles),
         (bf16(2 * HEAD, 2 * nev), bf16(2 * HEAD, 2 * nev), bf16(2 * TAIL, 2 * nev), bf16(2 * TAIL, 2 * nev)),
         [
             pltpu.VMEM((halves, PADDED, LANES), jnp.float32),
@@ -603,7 +619,7 @@
     operands = (ah, al, bh, bl) + tuple(operands)
     size, columns = nev // devices, moments * 2 * nev
     if size % 16 == 0 and devices % 8 == 0:
-        total = pieces(operands, position, devices, moments, size, columns)
+        total = pieces(operands, devices, moments, size, columns)
     else:
         total = whole_product(operands, position, devices, moments, nev)
     return total.reshape(size, moments, 2, nev)
@@ -644,47 +660,59 @@
     return scatter_sum(partial.reshape(devices, nev // devices, moments * 2 * nev), position, devices)
 
 
-def pieces(operands, position, devices, moments, size, columns):
+def pieces(operands, devices, moments, size, columns):
     groups = devices // 4
-    shared = dict(moments=moments, groups=groups)
-    cost = dict(flops=2 * 3 * size * groups * moments * 4 * (HEAD + TAIL) * 256, moved=1 << 20)
     block = lambda count: f32(count, size, columns)
-    out = call(
-        functools.partial(piece_kernel, cores=1, turns=(0, 1), **shared), block(2 * groups), (), inputs=8, **cost
-    )(*operands)
-    swapped = lax.ppermute(out, "site", [(i, i ^ 1) for i in range(devices)])
-    far = call(
-        functools.partial(piece_kernel, cores=0, turns=(1,), **shared), block(groups), (), inputs=8, **cost
-    )(*operands)
-    early = list(range(1, groups // 2 + 1))
-    late = list(range(groups // 2 + 1, groups)) + [0]
-    first, second = call(
-        functools.partial(merge_kernel, picks=[[(g, 2 * g + 1) for g in early], [(g, 2 * g + 1) for g in late]]),
-        (block(len(early)), block(len(late))),
-        inputs=2,
-    )(far, swapped)
+    swap = [(i, i ^ 1) for i in range(devices)]
     flip = [(i, i ^ 2) for i in range(devices)]
-    first = lax.ppermute(first, "site", flip)
-    second = lax.ppermute(second, "site", flip)
-    near = call(
-        functools.partial(piece_kernel, cores=0, turns=(0,), **shared), block(groups), (), inputs=8, **cost
-    )(*operands)
-    near = call(
-        functools.partial(merge_kernel, picks=[[(g, 2 * g) for g in range(groups)]]), (block(groups),), inputs=2
-    )(near, swapped)[0]
-    total = None
-    arrived = []
-    for steps, got in ((early, first), (late, second)):
-        sums = call(
-            functools.partial(merge_kernel, picks=[[(g, k)] for k, g in enumerate(steps)]),
-            tuple(block(1) for _ in steps),
-            inputs=2,
-        )(near, got)
-        for step, value in zip(steps, sums):
-            if step == 0:
-                total = value
-            else:
-                arrived.append(lax.ppermute(value, "site", [(i, (i + 4 * step) % devices) for i in range(devices)]))
+
+    def piece(cores, turn, steps, *after):
+        kernel = functools.partial(
+            piece_kernel, moments=moments, groups=groups, cores=cores, turn=turn, steps=tuple(steps)
+        )
+        flops = 2 * 3 * size * len(steps) * moments * 4 * (HEAD + TAIL) * 256
+        return call(kernel, block(len(steps)), (), flops, 1 << 20, 8 + len(after))(*operands, *after)
+
+    def permute(value, route):
+        return lax.ppermute(value, "site", route)
+
+    def merge(arrays, picks):
+        kernel = functools.partial(merge_kernel, sources=len(arrays), picks=picks)
+        outs = tuple(block(len(p)) for p in picks)
+        return call(kernel, outs, inputs=len(arrays))(*arrays)
+
+    order = sorted(range(1, groups), key=lambda g: -min(g, groups - g)) + [0]
+    early, late = order[: groups // 2], order[groups // 2 :]
+    apart = [[[(k, k)] for k in range(len(early))], [[(k, k) for k in range(len(late))]]]
+    a1 = piece(1, 1, early)
+    got_a = permute(a1, swap)
+    a2 = piece(0, 1, early, a1)
+    b1 = piece(1, 1, late, a2)
+    got_b = permute(b1, swap)
+    out_a = merge((a2, got_a), apart[0])
+    crossed = [[permute(out, flip) for out in out_a]]
+    b2 = piece(0, 1, late, b1, out_a[0])
+    out_b = merge((b2, got_b), apart[1])
+    crossed.append([permute(out_b[0], flip)])
+    c1 = piece(1, 0, early, out_b[0])
+    got_c = permute(c1, swap)
+    c2 = piece(0, 0, early, c1)
+    d1 = piece(1, 0, late, c2)
+    got_d = permute(d1, swap)
+    d2 = piece(0, 0, late, d1)
+    kept = [(c2, got_c), (d2, got_d)]
+    total, arrived = None, []
+    for steps, got, (mine, swapped) in zip((early, late), crossed, kept):
+        for first, array in enumerate(got):
+            count = array.shape[0]
+            picks = [[(first + k, first + k, k)] for k in range(count)]
+            for k, value in enumerate(merge((mine, swapped, array), picks)):
+                step = steps[first + k]
+                if step == 0:
+                    total = value
+                else:
+                    route = [(i, (i + 4 * step) % devices) for i in range(devices)]
+                    arrived.append(lax.ppermute(value, "site", route))
     for value in arrived:
         total = total + value
     return total[0]

time: 66.8 us -> 67.6 us (1.012)
  starting transfers between devices: 20.3 us -> 21.8 us
  waiting for transfers between devices: 18.1 us -> 17.3 us
    ppermute x14 -> x18, starting transfers between devices: 20.3 us -> 21.8 us  [the longest x8 12.6 us: halo(): found.append(lax.ppermute(block, 'site', route))]
    ppermute x14 -> x18, waiting for transfers between devices: 18.1 us -> 17.3 us  [the longest x7 9.2 us: permute(): return lax.ppermute(value, 'site', route)]
    pallas_call x10 -> x16, Pallas kernels: 13.5 us -> 13.6 us  [the longest x8 8.61 us: piece(): call(kernel, block(len(steps)), (), flops, 1 << 20, 8 + len(after))]
  transfers between devices with their start and end apart: 14 -> 18, of which waited for: 7 -> 6; matrix products, arithmetic and copies ran while one was open for 1% -> 1% of each run, Pallas kernels for 22% -> 25%
where the time goes in v5:
time: 67.6 us; the launch traced here: 67.4 us
  Pallas kernels  24 us (36%)
  starting transfers between devices  21.8 us (32%)
  waiting for transfers between devices  17.3 us (26%)
  local copies, waits for them, and re-layouts  2.52 us (4%)
  other arithmetic  1.5 us (2%)
    ppermute x8, starting transfers between devices, halo(): found.append(lax.ppermute(block, 'site', route))  12.6 us
    ppermute x7, waiting for transfers between devices, permute(): return lax.ppermute(value, 'site', route)  9.2 us
    pallas_call x8, Pallas kernels, piece(): call(kernel, block(len(steps)), (), flops, 1 << 20, 8 + len(after))  8.61 us
    ppermute x3, waiting for transfers between devices, pieces(): arrived.append(lax.ppermute(value, 'site', route))  6.08 us
    ppermute x3, starting transfers between devices, pieces(): arrived.append(lax.ppermute(value, 'site', route))  5.57 us
    pallas_call x2, Pallas kernels, operator(): call(kernel, (out, out), (), 1 << 30, 4 << 20, 5)  4.17 us
    ppermute x7, starting transfers between devices, permute(): return lax.ppermute(value, 'site', route)  3.58 us
    pallas_call x1, Pallas kernels, on_device(): call(functools.partial(displace_kernel, scale=scale, tiles=tiles), (bf16(...  3.05 us
  transfers between devices with their start and end apart: 18, of which 6 were waited for; matrix products, arithmetic and copies ran while one was open for 1% of the time, Pallas kernels for 25%

profile of v5, /device:TPU:0, one launch (start us, length us, event | category | flops | bytes accessed | tf_op | source)
XLA Modules:
  0.0 67.4 jit_solution(1408202071205237819)
XLA Ops:
  0.0 1.2 %reduce = f32[3,2,3,3,288]{4,3,2,1,0:T(4,128)S(1)} reduce(f32[3,2,3,3,1,288]{5,4,3,2,1,0:T(1,128)} %param.17, f32[]{:T(128)} %constant.116), dimensions={4}, to_apply=%param.17.reduce_sub_computation | reduce | bytes 124420 | tf_op args[1]
  1.2 0.0 copy-start
  1.2 1.5 %copy-done = f32[2,3,1,288,256]{4,3,2,1,0:T(8,128)S(1)} copy-done((f32[2,3,1,288,256]{4,3,2,1,0:T(8,128)S(1)}, f32[2,3,1,288,256]{4,3,2,1,0:T(8,128)}, u32[]{:S(2)}) %copy-start) | copy-done | bytes 1769496
  2.7 0.7 %shard_map.154 = (f32[2,2016,128]{2,1,0:T(8,128)S(1)}, f32[312,128]{1,0:T(8,128)S(1)}, f32[2,144,128]{2,1,0:T(8,128)S(1)}, f32[2,144,128]{2,1,0:T(8,128)S(1)}, f...) custom-call(f32[6,288,256]{2,1,0:T(8,128)S(1)} %bitcast.2, f32[54,288]{1,0:T(8,128)S(1)} %reshape.10.l_ref), custom_call_target="tpu_custom_call" | custom-call | tf_op jit(solution)/shard_map/pallas_call | solution.py:571
  3.4 3.1 %collective-permute-start = (f32[2,144,128]{2,1,0:T(8,128)S(1)}, f32[2,144,128]{2,1,0:T(8,128)S(1)}, u32[]{:S(2)}, u32[]{:S(2)}) collective-permute-start(f32[2,144,128]{2,1,0:T(8,128)S(1)} %get-tuple-element.39), channel_id=1, source_target_pairs={{0,4},{1,5},{2,6},{3,7},{4,0},{5,1},{6,2},{7,3},{8,12},{9,13},{10,... | collective-permute-start | bytes 442376 | tf_op jit(solution)/shard_map/ppermute | solution.py:527
  6.5 2.5 %collective-permute-start.1 = (f32[2,144,128]{2,1,0:T(8,128)S(1)}, f32[2,144,128]{2,1,0:T(8,128)S(1)}, u32[]{:S(2)}, u32[]{:S(2)}) collective-permute-start(f32[2,144,128]{2,1,0:T(8,128)S(1)} %get-tuple-element.40), channel_id=1, source_target_pairs={{0,12},{1,13},{2,14},{3,15},{4,8},{5,9},{6,10},{7,11},{8,4},{9,5},... | collective-permute-start | bytes 442376 | tf_op jit(solution)/shard_map/ppermute | solution.py:527
  9.0 0.0 collective-permute-start.2
  9.0 2.4 %collective-permute-start.3 = (f32[2,144,128]{2,1,0:T(8,128)S(1)}, f32[2,144,128]{2,1,0:T(8,128)S(1)}, u32[]{:S(2)}, u32[]{:S(2)}) collective-permute-start(f32[2,144,128]{2,1,0:T(8,128)S(1)} %get-tuple-element.42), channel_id=1, source_target_pairs={{0,15},{1,2},{2,1},{3,4},{4,3},{5,6},{6,5},{7,8},{8,7},{9,10},{10,... | collective-permute-start | bytes 442376 | tf_op jit(solution)/shard_map/ppermute | solution.py:527
  11.4 0.0 copy-done.10
  11.4 0.2 slice_reduce_fusion.2
  11.6 0.0 copy-done.12
  11.7 0.0 copy-done.11
  11.7 0.3 fusion.21
  12.0 1.7 %shard_map.155 = (bf16[1024,1536]{1,0:T(8,128)(2,1)S(1)}, bf16[1024,1536]{1,0:T(8,128)(2,1)S(1)}) custom-call(f32[2,2016,128]{2,1,0:T(8,128)S(1)} %get-tuple-element.33.fr_ref.f_ref, f32[4,1152]{1,0:T(4,128)S(1)} %get-tuple-element.65.cos_ref, f32[4,1152]{1,0:T(4,128)S(1)} %get-tuple-element.64.sin_ref), custom_call_target="tpu_custom_call" | custom-call | flops 53084160 | bytes 8388608 | tf_op jit(solution)/shard_map/pallas_call | solution.py:592
  13.7 2.0 %shard_map.156 = (bf16[1728,432]{1,0:T(8,128)(2,1)S(1)}, bf16[1728,432]{1,0:T(8,128)(2,1)S(1)}) custom-call(f32[312,128]{1,0:T(8,128)S(1)} %get-tuple-element.36.wc_ref, s32[6,512]{1,0:T(8,128)S(1)} %copy-done.4, f32[6,512]{1,0:T(8,128)S(1)} %copy-done.5, s32[6,512]{1,0:T(8,128)S(1)} %copy-done.6, f32[6,512]{1,0:T(8,128)S(1)} %copy-done.7), custom_call_target="tpu_custom_call" | custom-call | flops 1073741824 | bytes 4194304 | tf_op jit(solution)/shard_map/pallas_call | solution.py:646
  15.8 1.7 %shard_map.157.part_ref = f32[2,2016,128]{2,1,0:T(8,128)S(1)} custom-call(f32[2,2016,128]{2,1,0:T(8,128)S(1)} %get-tuple-element.33.fr_ref.f_ref, bf16[1728,432]{1,0:T(8,128)(2,1)S(1)} %get-tuple-element.37.oh_ref, bf16[1728,432]{1,0:T(8,128)(2,1)S(1)} %get-tuple-element.38.ol_ref), custom_call_target="tpu_custom_call" | custom-call | flops 53084160 | bytes 3145728 | tf_op jit(solution)/shard_map/pallas_call | solution.py:587
  17.4 0.0 collective-permute-done.rax
  17.4 0.0 collective-permute-done.1.rbx
  17.4 0.0 collective-permute-done.2.ray
  17.5 0.9 %collective-permute-done.3.rby = f32[2,144,128]{2,1,0:T(8,128)S(1)} collective-permute-done((f32[2,144,128]{2,1,0:T(8,128)S(1)}, f32[2,144,128]{2,1,0:T(8,128)S(1)}, u32[]{:S(2)}, u32[]{:S(2)}) %collective-permute-start.3) | collective-permute-done | bytes 147488 | tf_op jit(solution)/shard_map/ppermute | solution.py:527
  18.4 1.1 %shard_map.158 = (f32[2,2016,128]{2,1,0:T(8,128)S(1)}, f32[2,2,288,128]{3,2,1,0:T(8,128)S(1)}, f32[2,144,128]{2,1,0:T(8,128)S(1)}, f32[2,144,128]{2,1,0:T(8,128)...) custom-call(f32[2,2016,128]{2,1,0:T(8,128)S(1)} %shard_map.157.part_ref, ...), custom_call_target="tpu_custom_call" | custom-call | tf_op jit(solution)/shard_map/pallas_call | solution.py:601
  19.5 0.1 collective-permute-start.4
  19.6 3.2 %collective-permute-start.5 = (f32[2,144,128]{2,1,0:T(8,128)S(1)}, f32[2,144,128]{2,1,0:T(8,128)S(1)}, u32[]{:S(2)}, u32[]{:S(2)}) collective-permute-start(f32[2,144,128]{2,1,0:T(8,128)S(1)} %get-tuple-element.50), channel_id=1, source_target_pairs={{0,12},{1,13},{2,14},{3,15},{4,8},{5,9},{6,10},{7,11},{8,4},{9,5},... | collective-permute-start | bytes 442376 | tf_op jit(solution)/shard_map/ppermute | solution.py:527
  22.8 0.0 collective-permute-start.6
  22.8 1.3 %collective-permute-start.7 = (f32[2,144,128]{2,1,0:T(8,128)S(1)}, f32[2,144,128]{2,1,0:T(8,128)S(1)}, u32[]{:S(2)}, u32[]{:S(2)}) collective-permute-start(f32[2,144,128]{2,1,0:T(8,128)S(1)} %get-tuple-element.52), channel_id=1, source_target_pairs={{0,15},{1,2},{2,1},{3,4},{4,3},{5,6},{6,5},{7,8},{8,7},{9,10},{10,... | collective-permute-start | bytes 442376 | tf_op jit(solution)/shard_map/ppermute | solution.py:527
  24.1 0.0 copy-done.3
  24.1 2.2 %shard_map.161 = (bf16[1728,576]{1,0:T(8,128)(2,1)S(1)}, bf16[1728,576]{1,0:T(8,128)(2,1)S(1)}) custom-call(f32[312,128]{1,0:T(8,128)S(1)} %get-tuple-element.36.wc_ref, s32[6,640]{1,0:T(8,128)S(1)} %copy-done.2, f32[6,640]{1,0:T(8,128)S(1)} %copy-done.3, s32[6,256]{1,0:T(8,128)S(1)} %copy-done.8, f32[6,256]{1,0:T(8,128)S(1)} %copy-done.9), custom_call_target="tpu_custom_call" | custom-call | flops 1073741824 | bytes 4194304 | tf_op jit(solution)/shard_map/pallas_call | solution.py:646
  26.3 1.8 %shard_map.160.part_ref = f32[2,2016,128]{2,1,0:T(8,128)S(1)} custom-call(f32[2,2016,128]{2,1,0:T(8,128)S(1)} %get-tuple-element.46.f_ref, bf16[1728,432]{1,0:T(8,128)(2,1)S(1)} %get-tuple-element.37.oh_ref, bf16[1728,432]{1,0:T(8,128)(2,1)S(1)} %get-tuple-element.38.ol_ref), custom_call_target="tpu_custom_call" | custom-call | flops 53084160 | bytes 3145728 | tf_op jit(solution)/shard_map/pallas_call | solution.py:605
  28.1 0.0 copy-start.1
  28.1 1.1 %shard_map.159 = (bf16[1024,768]{1,0:T(8,128)(2,1)S(1)}, bf16[1024,768]{1,0:T(8,128)(2,1)S(1)}) custom-call(f32[2,2016,128]{2,1,0:T(8,128)S(1)} %get-tuple-element.33.fr_ref.f_ref, f32[2,2,288,128]{3,2,1,0:T(8,128)S(1)} %get-tuple-element.43.save, f32[4,1152]{1,0:T(4,128)S(1)} %get-tuple-element.65.cos_ref, f32[4,1152]{1,0:T(4,128)S(1)} %get-tuple-element.64.sin_ref), custom_call_target="tpu_custom_call" | custom-call | flops 53084160 | bytes 4194304 | tf_op jit(solution)/shard_map/pallas_call | solution.py:607
  29.2 0.0 collective-permute-done.4.rax
  29.2 0.0 collective-permute-done.5.rbx
  29.2 0.0 collective-permute-done.6.ray
  29.2 1.1 %collective-permute-done.7.rby = f32[2,144,128]{2,1,0:T(8,128)S(1)} collective-permute-done((f32[2,144,128]{2,1,0:T(8,128)S(1)}, f32[2,144,128]{2,1,0:T(8,128)S(1)}, u32[]{:S(2)}, u32[]{:S(2)}) %collective-permute-start.7) | collective-permute-done | bytes 147488 | tf_op jit(solution)/shard_map/ppermute | solution.py:527
  30.3 3.0 %shard_map.162 = (bf16[1536,512]{1,0:T(8,128)(2,1)S(1)}, bf16[1536,512]{1,0:T(8,128)(2,1)S(1)}, bf16[768,512]{1,0:T(8,128)(2,1)S(1)}, bf16[768,512]{1,0:T(8,128)(2,1)S(1)}) custom-call(f32[2,2016,128]{2,1,0:T(8,128)S(1)} %shard_map.160.part_ref, f32[312,128]{1,0:T(8,128)S(1)} %get-tuple-element.36.wc_ref, bf16[1728,576]{1,0:T(8,128)(2,1)S(1)} %get-tuple-element.47.oh_ref, ...), custom_call_target="tpu_custom_call" | custom-call | tf_op jit(solution)/shard_map/pallas_call | solution.py:609
  33.3 1.1 %shard_map.163.refs_8_ = f32[2,16,2048]{2,1,0:T(8,128)S(1)} custom-call(bf16[1024,1536]{1,0:T(8,128)(2,1)S(1)} %get-tuple-element.34.refs_0_, bf16[1024,1536]{1,0:T(8,128)(2,1)S(1)} %get-tuple-element.35.refs_1_, bf16[1024,768]{1,0:T(8,128)(2,1)S(1)} %get-tuple-element.44.refs_2_, bf16[1024,768]{1,0:T(8,128)(2,1)S(1)} %get-tuple-element.45.refs_3_, ...), custom_call_target="tpu_custom_call" | custom-call | flops 905969664 | bytes 1048576 | tf_op jit(solution)/shard_map/pallas_call | solution.py:674
  34.4 0.1 collective-permute-start.8
  34.5 1.1 %shard_map.164.refs_8_.refs_0_ = f32[2,16,2048]{2,1,0:T(8,128)S(1)} custom-call(bf16[1024,1536]{1,0:T(8,128)(2,1)S(1)} %get-tuple-element.34.refs_0_, bf16[1024,1536]{1,0:T(8,128)(2,1)S(1)} %get-tuple-element.35.refs_1_, bf16[1024,768]{1,0:T(8,128)(2,1)S(1)} %get-tuple-element.44.refs_2_, bf16[1024,768]{1,0:T(8,128)(2,1)S(1)} %get-tuple-element.45.refs_3_, ...), custom_call_target="tpu_custom_call" | custom-call | flops 905969664 | bytes 1048576 | tf_op jit(solution)/shard_map/pallas_call | solution.py:674
  35.6 1.1 %shard_map.165.refs_8_ = f32[2,16,2048]{2,1,0:T(8,128)S(1)} custom-call(bf16[1024,1536]{1,0:T(8,128)(2,1)S(1)} %get-tuple-element.34.refs_0_, bf16[1024,1536]{1,0:T(8,128)(2,1)S(1)} %get-tuple-element.35.refs_1_, bf16[1024,768]{1,0:T(8,128)(2,1)S(1)} %get-tuple-element.44.refs_2_, bf16[1024,768]{1,0:T(8,128)(2,1)S(1)} %get-tuple-element.45.refs_3_, ...), custom_call_target="tpu_custom_call" | custom-call | flops 905969664 | bytes 1048576 | tf_op jit(solution)/shard_map/pallas_call | solution.py:674
  36.7 0.6 collective-permute-start.9
  37.2 0.0 collective-permute-done.8.refs_1_
  37.3 1.1 %shard_map.167.refs_0_ = f32[2,16,2048]{2,1,0:T(8,128)S(1)} custom-call(bf16[1024,1536]{1,0:T(8,128)(2,1)S(1)} %get-tuple-element.34.refs_0_, bf16[1024,1536]{1,0:T(8,128)(2,1)S(1)} %get-tuple-element.35.refs_1_, bf16[1024,768]{1,0:T(8,128)(2,1)S(1)} %get-tuple-element.44.refs_2_, bf16[1024,768]{1,0:T(8,128)(2,1)S(1)} %get-tuple-element.45.refs_3_, ...), custom_call_target="tpu_custom_call" | custom-call | flops 905969664 | bytes 1048576 | tf_op jit(solution)/shard_map/pallas_call | solution.py:674
  38.4 0.0 collective-permute-done.9.refs_1_
  38.4 1.1 %shard_map.169.refs_8_ = f32[2,16,2048]{2,1,0:T(8,128)S(1)} custom-call(bf16[1024,1536]{1,0:T(8,128)(2,1)S(1)} %get-tuple-element.34.refs_0_, bf16[1024,1536]{1,0:T(8,128)(2,1)S(1)} %get-tuple-element.35.refs_1_, bf16[1024,768]{1,0:T(8,128)(2,1)S(1)} %get-tuple-element.44.refs_2_, bf16[1024,768]{1,0:T(8,128)(2,1)S(1)} %get-tuple-element.45.refs_3_, ...), custom_call_target="tpu_custom_call" | custom-call | flops 905969664 | bytes 1048576 | tf_op jit(solution)/shard_map/pallas_call | solution.py:674
  39.5 0.4 collective-permute-start.12
  39.9 1.1 %shard_map.170.refs_8_.refs_0_ = f32[2,16,2048]{2,1,0:T(8,128)S(1)} custom-call(bf16[1024,1536]{1,0:T(8,128)(2,1)S(1)} %get-tuple-element.34.refs_0_, bf16[1024,1536]{1,0:T(8,128)(2,1)S(1)} %get-tuple-element.35.refs_1_, bf16[1024,768]{1,0:T(8,128)(2,1)S(1)} %get-tuple-element.44.refs_2_, bf16[1024,768]{1,0:T(8,128)(2,1)S(1)} %get-tuple-element.45.refs_3_, ...), custom_call_target="tpu_custom_call" | custom-call | flops 905969664 | bytes 1048576 | tf_op jit(solution)/shard_map/pallas_call | solution.py:674
  41.0 1.1 %shard_map.171.refs_8_ = f32[2,16,2048]{2,1,0:T(8,128)S(1)} custom-call(bf16[1024,1536]{1,0:T(8,128)(2,1)S(1)} %get-tuple-element.34.refs_0_, bf16[1024,1536]{1,0:T(8,128)(2,1)S(1)} %get-tuple-element.35.refs_1_, bf16[1024,768]{1,0:T(8,128)(2,1)S(1)} %get-tuple-element.44.refs_2_, bf16[1024,768]{1,0:T(8,128)(2,1)S(1)} %get-tuple-element.45.refs_3_, ...), custom_call_target="tpu_custom_call" | custom-call | flops 905969664 | bytes 1048576 | tf_op jit(solution)/shard_map/pallas_call | solution.py:674
  42.1 0.2 collective-permute-start.10
  42.3 0.3 collective-permute-start.11
  42.6 1.8 %collective-permute-start.13 = (f32[1,16,2048]{2,1,0:T(8,128)S(1)}, f32[1,16,2048]{2,1,0:T(8,128)S(1)}, u32[]{:S(2)}, u32[]{:S(2)}) collective-permute-start(f32[1,16,2048]{2,1,0:T(8,128)S(1)} %get-tuple-element.57.refs_9_), channel_id=1, source_target_pairs={{0,2},{1,3},{2,0},{3,1},{4,6},{5,7},{6,4},{7,5},{8,10},{9,11},{10,... | collective-permute-start | bytes 393224 | tf_op jit(solution)/shard_map/ppermute | solution.py:677
  44.3 0.3 collective-permute-start.15
  44.6 1.1 %shard_map.172.refs_0_ = f32[2,16,2048]{2,1,0:T(8,128)S(1)} custom-call(bf16[1024,1536]{1,0:T(8,128)(2,1)S(1)} %get-tuple-element.34.refs_0_, bf16[1024,1536]{1,0:T(8,128)(2,1)S(1)} %get-tuple-element.35.refs_1_, bf16[1024,768]{1,0:T(8,128)(2,1)S(1)} %get-tuple-element.44.refs_2_, bf16[1024,768]{1,0:T(8,128)(2,1)S(1)} %get-tuple-element.45.refs_3_, ...), custom_call_target="tpu_custom_call" | custom-call | flops 905969664 | bytes 1048576 | tf_op jit(solution)/shard_map/pallas_call | solution.py:674
  45.7 8.6 %collective-permute-done.13.refs_2_ = f32[1,16,2048]{2,1,0:T(8,128)S(1)} collective-permute-done((f32[1,16,2048]{2,1,0:T(8,128)S(1)}, f32[1,16,2048]{2,1,0:T(8,128)S(1)}, u32[]{:S(2)}, u32[]{:S(2)}) %collective-permute-start.13) | collective-permute-done | bytes 131104 | tf_op jit(solution)/shard_map/ppermute | solution.py:677
  54.3 0.0 collective-permute-done.12.refs_1_
  54.3 1.6 %collective-permute-start.14 = (f32[1,16,2048]{2,1,0:T(8,128)S(1)}, f32[1,16,2048]{2,1,0:T(8,128)S(1)}, u32[]{:S(2)}, u32[]{:S(2)}) collective-permute-start(f32[1,16,2048]{2,1,0:T(8,128)S(1)} %shard_map.174), channel_id=1, source_target_pairs={{0,8},{1,9},{2,10},{3,11},{4,12},{5,13},{6,14},{7,15},{8,0},{9,1},... | collective-permute-start | bytes 393224 | tf_op jit(solution)/shard_map/ppermute | solution.py:715
  56.0 0.5 collective-permute-done.15.refs_2_
  56.5 0.2 collective-permute-start.16
  56.7 0.0 collective-permute-done.10.refs_1_
  56.7 0.0 collective-permute-done.11.refs_2_
  56.7 3.8 %collective-permute-start.17 = (f32[1,16,2048]{2,1,0:T(8,128)S(1)}, f32[1,16,2048]{2,1,0:T(8,128)S(1)}, u32[]{:S(2)}, u32[]{:S(2)}) collective-permute-start(f32[1,16,2048]{2,1,0:T(8,128)S(1)} %get-tuple-element.60), channel_id=1, source_target_pairs={{0,12},{1,13},{2,14},{3,15},{4,0},{5,1},{6,2},{7,3},{8,4},{9,5},{1... | collective-permute-start | bytes 393224 | tf_op jit(solution)/shard_map/ppermute | solution.py:715
  60.5 5.0 %collective-permute-done.14 = f32[1,16,2048]{2,1,0:T(8,128)S(1)} collective-permute-done((f32[1,16,2048]{2,1,0:T(8,128)S(1)}, f32[1,16,2048]{2,1,0:T(8,128)S(1)}, u32[]{:S(2)}, u32[]{:S(2)}) %collective-permute-start.14) | collective-permute-done | bytes 131104 | tf_op jit(solution)/shard_map/ppermute | solution.py:715
  65.6 0.0 collective-permute-done.16
  65.6 1.0 %collective-permute-done.17 = f32[1,16,2048]{2,1,0:T(8,128)S(1)} collective-permute-done((f32[1,16,2048]{2,1,0:T(8,128)S(1)}, f32[1,16,2048]{2,1,0:T(8,128)S(1)}, u32[]{:S(2)}, u32[]{:S(2)}) %collective-permute-start.17) | collective-permute-done | bytes 131104 | tf_op jit(solution)/shard_map/ppermute | solution.py:715
  66.6 0.8 %reshape_squeeze.3 = f32[16,4,2,256]{3,2,1,0:T(2,128)} reshape(f32[1,16,2048]{2,1,0:T(8,128)S(1)} %add_add_fusion) | data formatting | bytes 262144 | tf_op jit(solution)/shard_map/reshape;squeeze | solution.py:625
  (31 shorter events, 0.3 us)
Async XLA Ops:
  0.0 11.6 %copy-start.12 = (s32[1152]{0:T(1024)S(1)}, s32[1152]{0:T(1024)}, u32[]{:S(2)}) copy-start(s32[1152]{0:T(1024)} %constant.106.clone) | copy-start | bytes 13828
  0.0 11.6 %copy-start.13 = (s32[1152]{0:T(1024)S(1)}, s32[1152]{0:T(1024)}, u32[]{:S(2)}) copy-start(s32[1152]{0:T(1024)} %constant.107.clone) | copy-start | bytes 13828
  0.0 11.6 %copy-start.14 = (s32[1152]{0:T(1024)S(1)}, s32[1152]{0:T(1024)}, u32[]{:S(2)}) copy-start(s32[1152]{0:T(1024)} %constant.108.clone) | copy-start | bytes 13828
  0.0 11.7 %copy-start.11 = (s32[1152]{0:T(1024)S(1)}, s32[1152]{0:T(1024)}, u32[]{:S(2)}) copy-start(s32[1152]{0:T(1024)} %constant.109.clone) | copy-start | bytes 13828
  0.0 11.4 %copy-start.10 = (s32[4,3]{1,0:T(4,128)S(1)}, s32[4,3]{1,0:T(4,128)}, u32[]{:S(2)}) copy-start(s32[4,3]{1,0:T(4,128)} %param.18) | copy-start | bytes 148
  1.2 1.5 %copy-start = (f32[2,3,1,288,256]{4,3,2,1,0:T(8,128)S(1)}, f32[2,3,1,288,256]{4,3,2,1,0:T(8,128)}, u32[]{:S(2)}) copy-start(f32[2,3,1,288,256]{4,3,2,1,0:T(8,128)} %param.16) | copy-start | bytes 5308420
  2.7 11.0 %copy-start.4 = (s32[6,512]{1,0:T(8,128)S(1)}, s32[6,512]{1,0:T(8,128)}, u32[]{:S(2)}) copy-start(s32[6,512]{1,0:T(8,128)} %constant.102.clone.column_ref) | copy-start | bytes 36868
  2.7 11.0 %copy-start.5 = (f32[6,512]{1,0:T(8,128)S(1)}, f32[6,512]{1,0:T(8,128)}, u32[]{:S(2)}) copy-start(f32[6,512]{1,0:T(8,128)} %constant.103.clone.sign_ref) | copy-start | bytes 36868
  2.7 11.0 %copy-start.6 = (s32[6,512]{1,0:T(8,128)S(1)}, s32[6,512]{1,0:T(8,128)}, u32[]{:S(2)}) copy-start(s32[6,512]{1,0:T(8,128)} %constant.104.clone.more_ref) | copy-start | bytes 36868
  2.7 11.0 %copy-start.7 = (f32[6,512]{1,0:T(8,128)S(1)}, f32[6,512]{1,0:T(8,128)}, u32[]{:S(2)}) copy-start(f32[6,512]{1,0:T(8,128)} %constant.105.clone.moresign_ref) | copy-start | bytes 36868
  3.4 14.0 %collective-permute-start = (f32[2,144,128]{2,1,0:T(8,128)S(1)}, f32[2,144,128]{2,1,0:T(8,128)S(1)}, u32[]{:S(2)}, u32[]{:S(2)}) collective-permute-start(f32[2,144,128]{2,1,0:T(8,128)S(1)} %get-tuple-element.39), channel_id=1, source_target_pairs={{0,4},{1,5},{2,6},{3,7},{4,0},{5,1},{6,2},{7,3},{8,12},{9,13},{10,... | collective-permute-start | bytes 442376 | tf_op jit(solution)/shard_map/ppermute | solution.py:527
  6.5 10.9 %collective-permute-start.1 = (f32[2,144,128]{2,1,0:T(8,128)S(1)}, f32[2,144,128]{2,1,0:T(8,128)S(1)}, u32[]{:S(2)}, u32[]{:S(2)}) collective-permute-start(f32[2,144,128]{2,1,0:T(8,128)S(1)} %get-tuple-element.40), channel_id=1, source_target_pairs={{0,12},{1,13},{2,14},{3,15},{4,8},{5,9},{6,10},{7,11},{8,4},{9,5},... | collective-permute-start | bytes 442376 | tf_op jit(solution)/shard_map/ppermute | solution.py:527
  9.0 8.4 %collective-permute-start.2 = (f32[2,144,128]{2,1,0:T(8,128)S(1)}, f32[2,144,128]{2,1,0:T(8,128)S(1)}, u32[]{:S(2)}, u32[]{:S(2)}) collective-permute-start(f32[2,144,128]{2,1,0:T(8,128)S(1)} %get-tuple-element.41), channel_id=1, source_target_pairs={{0,1},{1,0},{2,3},{3,2},{4,5},{5,4},{6,7},{7,6},{8,9},{9,8},{10,11... | collective-permute-start | bytes 442376 | tf_op jit(solution)/shard_map/ppermute | solution.py:527
  9.0 9.4 %collective-permute-start.3 = (f32[2,144,128]{2,1,0:T(8,128)S(1)}, f32[2,144,128]{2,1,0:T(8,128)S(1)}, u32[]{:S(2)}, u32[]{:S(2)}) collective-permute-start(f32[2,144,128]{2,1,0:T(8,128)S(1)} %get-tuple-element.42), channel_id=1, source_target_pairs={{0,15},{1,2},{2,1},{3,4},{4,3},{5,6},{6,5},{7,8},{8,7},{9,10},{10,... | collective-permute-start | bytes 442376 | tf_op jit(solution)/shard_map/ppermute | solution.py:527
  18.4 5.7 %copy-start.2 = (s32[6,640]{1,0:T(8,128)S(1)}, s32[6,640]{1,0:T(8,128)}, u32[]{:S(2)}) copy-start(s32[6,640]{1,0:T(8,128)} %constant.110.clone.column_ref) | copy-start | bytes 46084
  18.4 5.7 %copy-start.3 = (f32[6,640]{1,0:T(8,128)S(1)}, f32[6,640]{1,0:T(8,128)}, u32[]{:S(2)}) copy-start(f32[6,640]{1,0:T(8,128)} %constant.111.clone.sign_ref) | copy-start | bytes 46084
  18.4 5.7 %copy-start.8 = (s32[6,256]{1,0:T(8,128)S(1)}, s32[6,256]{1,0:T(8,128)}, u32[]{:S(2)}) copy-start(s32[6,256]{1,0:T(8,128)} %constant.112.clone.more_ref) | copy-start | bytes 18436
  18.4 5.7 %copy-start.9 = (f32[6,256]{1,0:T(8,128)S(1)}, f32[6,256]{1,0:T(8,128)}, u32[]{:S(2)}) copy-start(f32[6,256]{1,0:T(8,128)} %constant.113.clone.moresign_ref) | copy-start | bytes 18436
  19.5 9.7 %collective-permute-start.4 = (f32[2,144,128]{2,1,0:T(8,128)S(1)}, f32[2,144,128]{2,1,0:T(8,128)S(1)}, u32[]{:S(2)}, u32[]{:S(2)}) collective-permute-start(f32[2,144,128]{2,1,0:T(8,128)S(1)} %get-tuple-element.49), channel_id=1, source_target_pairs={{0,4},{1,5},{2,6},{3,7},{4,0},{5,1},{6,2},{7,3},{8,12},{9,13},{10,... | collective-permute-start | bytes 442376 | tf_op jit(solution)/shard_map/ppermute | solution.py:527
  19.6 9.6 %collective-permute-start.5 = (f32[2,144,128]{2,1,0:T(8,128)S(1)}, f32[2,144,128]{2,1,0:T(8,128)S(1)}, u32[]{:S(2)}, u32[]{:S(2)}) collective-permute-start(f32[2,144,128]{2,1,0:T(8,128)S(1)} %get-tuple-element.50), channel_id=1, source_target_pairs={{0,12},{1,13},{2,14},{3,15},{4,8},{5,9},{6,10},{7,11},{8,4},{9,5},... | collective-permute-start | bytes 442376 | tf_op jit(solution)/shard_map/ppermute | solution.py:527
  22.8 6.4 %collective-permute-start.6 = (f32[2,144,128]{2,1,0:T(8,128)S(1)}, f32[2,144,128]{2,1,0:T(8,128)S(1)}, u32[]{:S(2)}, u32[]{:S(2)}) collective-permute-start(f32[2,144,128]{2,1,0:T(8,128)S(1)} %get-tuple-element.51), channel_id=1, source_target_pairs={{0,1},{1,0},{2,3},{3,2},{4,5},{5,4},{6,7},{7,6},{8,9},{9,8},{10,11... | collective-permute-start | bytes 442376 | tf_op jit(solution)/shard_map/ppermute | solution.py:527
  22.8 7.5 %collective-permute-start.7 = (f32[2,144,128]{2,1,0:T(8,128)S(1)}, f32[2,144,128]{2,1,0:T(8,128)S(1)}, u32[]{:S(2)}, u32[]{:S(2)}) collective-permute-start(f32[2,144,128]{2,1,0:T(8,128)S(1)} %get-tuple-element.52), channel_id=1, source_target_pairs={{0,15},{1,2},{2,1},{3,4},{4,3},{5,6},{6,5},{7,8},{8,7},{9,10},{10,... | collective-permute-start | bytes 442376 | tf_op jit(solution)/shard_map/ppermute | solution.py:527
  28.1 2.2 %copy-start.1 = (s32[256]{0:T(256)S(1)}, s32[256]{0:T(256)}, u32[]{:S(2)}) copy-start(s32[256]{0:T(256)} %param.19) | copy-start | bytes 3076
  34.4 2.8 %collective-permute-start.8 = (f32[2,16,2048]{2,1,0:T(8,128)S(1)}, f32[2,16,2048]{2,1,0:T(8,128)S(1)}, u32[]{:S(2)}, u32[]{:S(2)}) collective-permute-start(f32[2,16,2048]{2,1,0:T(8,128)S(1)} %shard_map.163.refs_8_), channel_id=1, source_target_pairs={{0,1},{1,0},{2,3},{3,2},{4,5},{5,4},{6,7},{7,6},{8,9},{9,8},{10,11... | collective-permute-start | bytes 786440 | tf_op jit(solution)/shard_map/ppermute | solution.py:677
  36.7 1.7 %collective-permute-start.9 = (f32[2,16,2048]{2,1,0:T(8,128)S(1)}, f32[2,16,2048]{2,1,0:T(8,128)S(1)}, u32[]{:S(2)}, u32[]{:S(2)}) collective-permute-start(f32[2,16,2048]{2,1,0:T(8,128)S(1)} %shard_map.165.refs_8_), channel_id=1, source_target_pairs={{0,1},{1,0},{2,3},{3,2},{4,5},{5,4},{6,7},{7,6},{8,9},{9,8},{10,11... | collective-permute-start | bytes 786440 | tf_op jit(solution)/shard_map/ppermute | solution.py:677
  39.5 14.8 %collective-permute-start.12 = (f32[2,16,2048]{2,1,0:T(8,128)S(1)}, f32[2,16,2048]{2,1,0:T(8,128)S(1)}, u32[]{:S(2)}, u32[]{:S(2)}) collective-permute-start(f32[2,16,2048]{2,1,0:T(8,128)S(1)} %shard_map.169.refs_8_), channel_id=1, source_target_pairs={{0,1},{1,0},{2,3},{3,2},{4,5},{5,4},{6,7},{7,6},{8,9},{9,8},{10,11... | collective-permute-start | bytes 786440 | tf_op jit(solution)/shard_map/ppermute | solution.py:677
  42.1 14.6 %collective-permute-start.10 = (f32[2,16,2048]{2,1,0:T(8,128)S(1)}, f32[2,16,2048]{2,1,0:T(8,128)S(1)}, u32[]{:S(2)}, u32[]{:S(2)}) collective-permute-start(f32[2,16,2048]{2,1,0:T(8,128)S(1)} %shard_map.171.refs_8_), channel_id=1, source_target_pairs={{0,1},{1,0},{2,3},{3,2},{4,5},{5,4},{6,7},{7,6},{8,9},{9,8},{10,11... | collective-permute-start | bytes 786440 | tf_op jit(solution)/shard_map/ppermute | solution.py:677
  42.3 14.4 %collective-permute-start.11 = (f32[2,16,2048]{2,1,0:T(8,128)S(1)}, f32[2,16,2048]{2,1,0:T(8,128)S(1)}, u32[]{:S(2)}, u32[]{:S(2)}) collective-permute-start(f32[2,16,2048]{2,1,0:T(8,128)S(1)} %shard_map.168.refs_8_), channel_id=1, source_target_pairs={{0,2},{1,3},{2,0},{3,1},{4,6},{5,7},{6,4},{7,5},{8,10},{9,11},{10,... | collective-permute-start | bytes 786440 | tf_op jit(solution)/shard_map/ppermute | solution.py:677
  42.6 11.7 %collective-permute-start.13 = (f32[1,16,2048]{2,1,0:T(8,128)S(1)}, f32[1,16,2048]{2,1,0:T(8,128)S(1)}, u32[]{:S(2)}, u32[]{:S(2)}) collective-permute-start(f32[1,16,2048]{2,1,0:T(8,128)S(1)} %get-tuple-element.57.refs_9_), channel_id=1, source_target_pairs={{0,2},{1,3},{2,0},{3,1},{4,6},{5,7},{6,4},{7,5},{8,10},{9,11},{10,... | collective-permute-start | bytes 393224 | tf_op jit(solution)/shard_map/ppermute | solution.py:677
  44.3 12.2 %collective-permute-start.15 = (f32[1,16,2048]{2,1,0:T(8,128)S(1)}, f32[1,16,2048]{2,1,0:T(8,128)S(1)}, u32[]{:S(2)}, u32[]{:S(2)}) collective-permute-start(f32[1,16,2048]{2,1,0:T(8,128)S(1)} %get-tuple-element.59), channel_id=1, source_target_pairs={{0,2},{1,3},{2,0},{3,1},{4,6},{5,7},{6,4},{7,5},{8,10},{9,11},{10,... | collective-permute-start | bytes 393224 | tf_op jit(solution)/shard_map/ppermute | solution.py:677
  54.3 11.2 %collective-permute-start.14 = (f32[1,16,2048]{2,1,0:T(8,128)S(1)}, f32[1,16,2048]{2,1,0:T(8,128)S(1)}, u32[]{:S(2)}, u32[]{:S(2)}) collective-permute-start(f32[1,16,2048]{2,1,0:T(8,128)S(1)} %shard_map.174), channel_id=1, source_target_pairs={{0,8},{1,9},{2,10},{3,11},{4,12},{5,13},{6,14},{7,15},{8,0},{9,1},... | collective-permute-start | bytes 393224 | tf_op jit(solution)/shard_map/ppermute | solution.py:715
  56.5 9.0 %collective-permute-start.16 = (f32[1,16,2048]{2,1,0:T(8,128)S(1)}, f32[1,16,2048]{2,1,0:T(8,128)S(1)}, u32[]{:S(2)}, u32[]{:S(2)}) collective-permute-start(f32[1,16,2048]{2,1,0:T(8,128)S(1)} %shard_map.175), channel_id=1, source_target_pairs={{0,4},{1,5},{2,6},{3,7},{4,8},{5,9},{6,10},{7,11},{8,12},{9,13},{1... | collective-permute-start | bytes 393224 | tf_op jit(solution)/shard_map/ppermute | solution.py:715
  56.7 9.9 %collective-permute-start.17 = (f32[1,16,2048]{2,1,0:T(8,128)S(1)}, f32[1,16,2048]{2,1,0:T(8,128)S(1)}, u32[]{:S(2)}, u32[]{:S(2)}) collective-permute-start(f32[1,16,2048]{2,1,0:T(8,128)S(1)} %get-tuple-element.60), channel_id=1, source_target_pairs={{0,12},{1,13},{2,14},{3,15},{4,0},{5,1},{6,2},{7,3},{8,4},{9,5},{1... | collective-permute-start | bytes 393224 | tf_op jit(solution)/shard_map/ppermute | solution.py:715

commit v6 on v5

--- a/solution.py
+++ b/solution.py
@@ -487,6 +487,18 @@
             for ref, at in zip(refs[1:sources], places[1:]):
                 total = total + ref[at]
             out_ref[k] = total
+
+
+def final_kernel(*refs):
+    out_ref = refs[-1]
+    width = out_ref.shape[3]
+    for m in range(out_ref.shape[1]):
+        for part in range(2):
+            lanes = slice((2 * m + part) * width, (2 * m + part + 1) * width)
+            total = refs[0][0, :, lanes]
+            for ref in refs[1:-1]:
+                total = total + ref[0, :, lanes]
+            out_ref[:, m, part, :] = total
 
 
 def phases(momenta, position, devices, tiles):
@@ -683,39 +695,44 @@
 
     order = sorted(range(1, groups), key=lambda g: -min(g, groups - g)) + [0]
     early, late = order[: groups // 2], order[groups // 2 :]
-    apart = [[[(k, k)] for k in range(len(early))], [[(k, k) for k in range(len(late))]]]
+
+    def along_z(value, step):
+        return permute(value, [(i, (i + 4 * step) % devices) for i in range(devices)])
+
+    def split_sum(mine, swapped):
+        return merge((mine, swapped), [[(k, k)] for k in range(mine.shape[0])])
+
     a1 = piece(1, 1, early)
     got_a = permute(a1, swap)
     a2 = piece(0, 1, early, a1)
-    b1 = piece(1, 1, late, a2)
+    out_a = split_sum(a2, got_a)
+    crossed_a = [permute(out_a[0], flip)]
+    c1 = piece(1, 0, early, out_a[0])
+    got_c = permute(c1, swap)
+    crossed_a += [permute(out_a[k], flip) for k in range(1, len(early))]
+    c2 = piece(0, 0, early, c1)
+    b1 = piece(1, 1, late, c2)
     got_b = permute(b1, swap)
-    out_a = merge((a2, got_a), apart[0])
-    crossed = [[permute(out, flip) for out in out_a]]
-    b2 = piece(0, 1, late, b1, out_a[0])
-    out_b = merge((b2, got_b), apart[1])
-    crossed.append([permute(out_b[0], flip)])
-    c1 = piece(1, 0, early, out_b[0])
-    got_c = permute(c1, swap)
-    c2 = piece(0, 0, early, c1)
-    d1 = piece(1, 0, late, c2)
+    b2 = piece(0, 1, late, b1)
+    sums = list(merge((c2, got_c, crossed_a[0]), [[(0, 0, 0)]]))
+    arrived = [along_z(sums[0], early[0])]
+    out_b = split_sum(b2, got_b)
+    crossed_b = [permute(out, flip) for out in out_b]
+    for k in range(1, len(early)):
+        sums += merge((c2, got_c, crossed_a[k]), [[(k, k, 0)]])
+        arrived.append(along_z(sums[-1], early[k]))
+    d1 = piece(1, 0, late, out_b[0], sums[0])
     got_d = permute(d1, swap)
     d2 = piece(0, 0, late, d1)
-    kept = [(c2, got_c), (d2, got_d)]
-    total, arrived = None, []
-    for steps, got, (mine, swapped) in zip((early, late), crossed, kept):
-        for first, array in enumerate(got):
-            count = array.shape[0]
-            picks = [[(first + k, first + k, k)] for k in range(count)]
-            for k, value in enumerate(merge((mine, swapped, array), picks)):
-                step = steps[first + k]
-                if step == 0:
-                    total = value
-                else:
-                    route = [(i, (i + 4 * step) % devices) for i in range(devices)]
-                    arrived.append(lax.ppermute(value, "site", route))
-    for value in arrived:
-        total = total + value
-    return total[0]
+    total = None
+    for k, step in enumerate(late):
+        sums += merge((d2, got_d, crossed_b[k]), [[(k, k, 0)]])
+        if step == 0:
+            total = sums[-1]
+        else:
+            arrived.append(along_z(sums[-1], step))
+    parts = (total, *arrived)
+    return call(final_kernel, f32(size, moments, 2, columns // (2 * moments)), inputs=len(parts))(*parts)
 
 
 def solution(mesh):

time: 67.6 us -> 63.8 us (0.944)
  waiting for transfers between devices: 17.3 us -> 14 us
  local copies, waits for them, and re-layouts: 2.52 us -> 1.75 us
  Pallas kernels: 24 us -> 24.7 us
    ppermute x3 -> x0, waiting for transfers between devices: 6.08 us -> none  [pieces(): arrived.append(lax.ppermute(value, 'site', route))]
    ppermute x3 -> x0, starting transfers between devices: 5.57 us -> none  [pieces(): arrived.append(lax.ppermute(value, 'site', route))]
    ppermute x7 -> x11, starting transfers between devices: 3.58 us -> 8.76 us  [permute(): return lax.ppermute(value, 'site', route)]
    ppermute x7 -> x11, waiting for transfers between devices: 9.2 us -> 12 us  [permute(): return lax.ppermute(value, 'site', route)]
    another operation x1 -> x0, local copies, waits for them, and re-layouts: 0.77 us -> none  [on_device(): return total.reshape(size, moments, 2, nev)]
    pallas_call x0 -> x1, Pallas kernels: none -> 0.71 us  [pieces(): call(final_kernel, f32(size, moments, 2, columns // (2 * moments)), input...]
  transfers between devices with their start and end apart: 18 -> 19, of which waited for: 6 -> 8; matrix products, arithmetic and copies ran while one was open for 1% -> 1% of each run, Pallas kernels for 25% -> 25%
where the time goes in v6:
time: 63.8 us; the launch traced here: 63.7 us
  Pallas kernels  24.7 us (39%)
  starting transfers between devices  21.4 us (34%)
  waiting for transfers between devices  14 us (22%)
  local copies, waits for them, and re-layouts  1.75 us (3%)
  other arithmetic  1.47 us (2%)
    ppermute x8, starting transfers between devices, halo(): found.append(lax.ppermute(block, 'site', route))  12.6 us
    ppermute x11, waiting for transfers between devices, permute(): return lax.ppermute(value, 'site', route)  12 us
    ppermute x11, starting transfers between devices, permute(): return lax.ppermute(value, 'site', route)  8.76 us
    pallas_call x8, Pallas kernels, piece(): call(kernel, block(len(steps)), (), flops, 1 << 20, 8 + len(after))  8.61 us
    pallas_call x2, Pallas kernels, operator(): call(kernel, (out, out), (), 1 << 30, 4 << 20, 5)  4.17 us
    pallas_call x1, Pallas kernels, on_device(): call(functools.partial(displace_kernel, scale=scale, tiles=tiles), (bf16(...  3.05 us
    ppermute x8, waiting for transfers between devices, halo(): found.append(lax.ppermute(block, 'site', route))  2 us
    pallas_call x1, Pallas kernels, on_device(): twice = call(smear_kernel, padded, pair, flops, 3 << 20, 3)(once, *smear)  1.79 us
  transfers between devices with their start and end apart: 19, of which 8 were waited for; matrix products, arithmetic and copies ran while one was open for 1% of the time, Pallas kernels for 25%

profile of v6, /device:TPU:0, one launch (start us, length us, event | category | flops | bytes accessed | tf_op | source)
XLA Modules:
  0.0 63.7 jit_solution(13160829768606370953)
XLA Ops:
  0.0 1.2 %reduce = f32[3,2,3,3,288]{4,3,2,1,0:T(4,128)S(1)} reduce(f32[3,2,3,3,1,288]{5,4,3,2,1,0:T(1,128)} %param.17, f32[]{:T(128)} %constant.116), dimensions={4}, to_apply=%param.17.reduce_sub_computation | reduce | bytes 124420 | tf_op args[1]
  1.2 0.0 copy-start
  1.2 1.5 %copy-done = f32[2,3,1,288,256]{4,3,2,1,0:T(8,128)S(1)} copy-done((f32[2,3,1,288,256]{4,3,2,1,0:T(8,128)S(1)}, f32[2,3,1,288,256]{4,3,2,1,0:T(8,128)}, u32[]{:S(2)}) %copy-start) | copy-done | bytes 1769496
  2.7 0.7 %shard_map.154 = (f32[2,2016,128]{2,1,0:T(8,128)S(1)}, f32[312,128]{1,0:T(8,128)S(1)}, f32[2,144,128]{2,1,0:T(8,128)S(1)}, f32[2,144,128]{2,1,0:T(8,128)S(1)}, f...) custom-call(f32[6,288,256]{2,1,0:T(8,128)S(1)} %bitcast.2, f32[54,288]{1,0:T(8,128)S(1)} %reshape.10.l_ref), custom_call_target="tpu_custom_call" | custom-call | tf_op jit(solution)/shard_map/pallas_call | solution.py:583
  3.4 3.1 %collective-permute-start = (f32[2,144,128]{2,1,0:T(8,128)S(1)}, f32[2,144,128]{2,1,0:T(8,128)S(1)}, u32[]{:S(2)}, u32[]{:S(2)}) collective-permute-start(f32[2,144,128]{2,1,0:T(8,128)S(1)} %get-tuple-element.39), channel_id=1, source_target_pairs={{0,4},{1,5},{2,6},{3,7},{4,0},{5,1},{6,2},{7,3},{8,12},{9,13},{10,... | collective-permute-start | bytes 442376 | tf_op jit(solution)/shard_map/ppermute | solution.py:539
  6.5 2.5 %collective-permute-start.1 = (f32[2,144,128]{2,1,0:T(8,128)S(1)}, f32[2,144,128]{2,1,0:T(8,128)S(1)}, u32[]{:S(2)}, u32[]{:S(2)}) collective-permute-start(f32[2,144,128]{2,1,0:T(8,128)S(1)} %get-tuple-element.40), channel_id=1, source_target_pairs={{0,12},{1,13},{2,14},{3,15},{4,8},{5,9},{6,10},{7,11},{8,4},{9,5},... | collective-permute-start | bytes 442376 | tf_op jit(solution)/shard_map/ppermute | solution.py:539
  9.0 0.0 collective-permute-start.2
  9.0 2.4 %collective-permute-start.3 = (f32[2,144,128]{2,1,0:T(8,128)S(1)}, f32[2,144,128]{2,1,0:T(8,128)S(1)}, u32[]{:S(2)}, u32[]{:S(2)}) collective-permute-start(f32[2,144,128]{2,1,0:T(8,128)S(1)} %get-tuple-element.42), channel_id=1, source_target_pairs={{0,15},{1,2},{2,1},{3,4},{4,3},{5,6},{6,5},{7,8},{8,7},{9,10},{10,... | collective-permute-start | bytes 442376 | tf_op jit(solution)/shard_map/ppermute | solution.py:539
  11.4 0.2 slice_reduce_fusion.2
  11.7 0.0 copy-done.11
  11.7 0.3 fusion.21
  12.0 1.7 %shard_map.155 = (bf16[1024,1536]{1,0:T(8,128)(2,1)S(1)}, bf16[1024,1536]{1,0:T(8,128)(2,1)S(1)}) custom-call(f32[2,2016,128]{2,1,0:T(8,128)S(1)} %get-tuple-element.33.fr_ref.f_ref, f32[4,1152]{1,0:T(4,128)S(1)} %get-tuple-element.65.cos_ref, f32[4,1152]{1,0:T(4,128)S(1)} %get-tuple-element.64.sin_ref), custom_call_target="tpu_custom_call" | custom-call | flops 53084160 | bytes 8388608 | tf_op jit(solution)/shard_map/pallas_call | solution.py:604
  13.7 2.0 %shard_map.156 = (bf16[1728,432]{1,0:T(8,128)(2,1)S(1)}, bf16[1728,432]{1,0:T(8,128)(2,1)S(1)}) custom-call(f32[312,128]{1,0:T(8,128)S(1)} %get-tuple-element.36.wc_ref, s32[6,512]{1,0:T(8,128)S(1)} %copy-done.4, f32[6,512]{1,0:T(8,128)S(1)} %copy-done.5, s32[6,512]{1,0:T(8,128)S(1)} %copy-done.6, f32[6,512]{1,0:T(8,128)S(1)} %copy-done.7), custom_call_target="tpu_custom_call" | custom-call | flops 1073741824 | bytes 4194304 | tf_op jit(solution)/shard_map/pallas_call | solution.py:658
  15.8 1.7 %shard_map.157.part_ref = f32[2,2016,128]{2,1,0:T(8,128)S(1)} custom-call(f32[2,2016,128]{2,1,0:T(8,128)S(1)} %get-tuple-element.33.fr_ref.f_ref, bf16[1728,432]{1,0:T(8,128)(2,1)S(1)} %get-tuple-element.37.oh_ref, bf16[1728,432]{1,0:T(8,128)(2,1)S(1)} %get-tuple-element.38.ol_ref), custom_call_target="tpu_custom_call" | custom-call | flops 53084160 | bytes 3145728 | tf_op jit(solution)/shard_map/pallas_call | solution.py:599
  17.4 0.0 collective-permute-done.rax
  17.4 0.0 collective-permute-done.1.rbx
  17.4 0.0 collective-permute-done.2.ray
  17.5 0.9 %collective-permute-done.3.rby = f32[2,144,128]{2,1,0:T(8,128)S(1)} collective-permute-done((f32[2,144,128]{2,1,0:T(8,128)S(1)}, f32[2,144,128]{2,1,0:T(8,128)S(1)}, u32[]{:S(2)}, u32[]{:S(2)}) %collective-permute-start.3) | collective-permute-done | bytes 147488 | tf_op jit(solution)/shard_map/ppermute | solution.py:539
  18.4 1.1 %shard_map.158 = (f32[2,2016,128]{2,1,0:T(8,128)S(1)}, f32[2,2,288,128]{3,2,1,0:T(8,128)S(1)}, f32[2,144,128]{2,1,0:T(8,128)S(1)}, f32[2,144,128]{2,1,0:T(8,128)...) custom-call(f32[2,2016,128]{2,1,0:T(8,128)S(1)} %shard_map.157.part_ref, ...), custom_call_target="tpu_custom_call" | custom-call | tf_op jit(solution)/shard_map/pallas_call | solution.py:613
  19.5 0.1 collective-permute-start.4
  19.6 3.2 %collective-permute-start.5 = (f32[2,144,128]{2,1,0:T(8,128)S(1)}, f32[2,144,128]{2,1,0:T(8,128)S(1)}, u32[]{:S(2)}, u32[]{:S(2)}) collective-permute-start(f32[2,144,128]{2,1,0:T(8,128)S(1)} %get-tuple-element.50), channel_id=1, source_target_pairs={{0,12},{1,13},{2,14},{3,15},{4,8},{5,9},{6,10},{7,11},{8,4},{9,5},... | collective-permute-start | bytes 442376 | tf_op jit(solution)/shard_map/ppermute | solution.py:539
  22.8 0.0 collective-permute-start.6
  22.8 1.3 %collective-permute-start.7 = (f32[2,144,128]{2,1,0:T(8,128)S(1)}, f32[2,144,128]{2,1,0:T(8,128)S(1)}, u32[]{:S(2)}, u32[]{:S(2)}) collective-permute-start(f32[2,144,128]{2,1,0:T(8,128)S(1)} %get-tuple-element.52), channel_id=1, source_target_pairs={{0,15},{1,2},{2,1},{3,4},{4,3},{5,6},{6,5},{7,8},{8,7},{9,10},{10,... | collective-permute-start | bytes 442376 | tf_op jit(solution)/shard_map/ppermute | solution.py:539
  24.1 0.0 copy-done.3
  24.1 2.2 %shard_map.161 = (bf16[1728,576]{1,0:T(8,128)(2,1)S(1)}, bf16[1728,576]{1,0:T(8,128)(2,1)S(1)}) custom-call(f32[312,128]{1,0:T(8,128)S(1)} %get-tuple-element.36.wc_ref, s32[6,640]{1,0:T(8,128)S(1)} %copy-done.2, f32[6,640]{1,0:T(8,128)S(1)} %copy-done.3, s32[6,256]{1,0:T(8,128)S(1)} %copy-done.8, f32[6,256]{1,0:T(8,128)S(1)} %copy-done.9), custom_call_target="tpu_custom_call" | custom-call | flops 1073741824 | bytes 4194304 | tf_op jit(solution)/shard_map/pallas_call | solution.py:658
  26.3 1.8 %shard_map.160.part_ref = f32[2,2016,128]{2,1,0:T(8,128)S(1)} custom-call(f32[2,2016,128]{2,1,0:T(8,128)S(1)} %get-tuple-element.46.f_ref, bf16[1728,432]{1,0:T(8,128)(2,1)S(1)} %get-tuple-element.37.oh_ref, bf16[1728,432]{1,0:T(8,128)(2,1)S(1)} %get-tuple-element.38.ol_ref), custom_call_target="tpu_custom_call" | custom-call | flops 53084160 | bytes 3145728 | tf_op jit(solution)/shard_map/pallas_call | solution.py:617
  28.1 0.0 copy-start.1
  28.1 1.1 %shard_map.159 = (bf16[1024,768]{1,0:T(8,128)(2,1)S(1)}, bf16[1024,768]{1,0:T(8,128)(2,1)S(1)}) custom-call(f32[2,2016,128]{2,1,0:T(8,128)S(1)} %get-tuple-element.33.fr_ref.f_ref, f32[2,2,288,128]{3,2,1,0:T(8,128)S(1)} %get-tuple-element.43.save, f32[4,1152]{1,0:T(4,128)S(1)} %get-tuple-element.65.cos_ref, f32[4,1152]{1,0:T(4,128)S(1)} %get-tuple-element.64.sin_ref), custom_call_target="tpu_custom_call" | custom-call | flops 53084160 | bytes 4194304 | tf_op jit(solution)/shard_map/pallas_call | solution.py:619
  29.2 0.0 collective-permute-done.4.rax
  29.2 0.0 collective-permute-done.5.rbx
  29.2 0.0 collective-permute-done.6.ray
  29.2 1.1 %collective-permute-done.7.rby = f32[2,144,128]{2,1,0:T(8,128)S(1)} collective-permute-done((f32[2,144,128]{2,1,0:T(8,128)S(1)}, f32[2,144,128]{2,1,0:T(8,128)S(1)}, u32[]{:S(2)}, u32[]{:S(2)}) %collective-permute-start.7) | collective-permute-done | bytes 147488 | tf_op jit(solution)/shard_map/ppermute | solution.py:539
  30.3 3.0 %shard_map.162 = (bf16[1536,512]{1,0:T(8,128)(2,1)S(1)}, bf16[1536,512]{1,0:T(8,128)(2,1)S(1)}, bf16[768,512]{1,0:T(8,128)(2,1)S(1)}, bf16[768,512]{1,0:T(8,128)(2,1)S(1)}) custom-call(f32[2,2016,128]{2,1,0:T(8,128)S(1)} %shard_map.160.part_ref, f32[312,128]{1,0:T(8,128)S(1)} %get-tuple-element.36.wc_ref, bf16[1728,576]{1,0:T(8,128)(2,1)S(1)} %get-tuple-element.47.oh_ref, ...), custom_call_target="tpu_custom_call" | custom-call | tf_op jit(solution)/shard_map/pallas_call | solution.py:621
  33.3 1.1 %shard_map.163.refs_8_ = f32[2,16,2048]{2,1,0:T(8,128)S(1)} custom-call(bf16[1024,1536]{1,0:T(8,128)(2,1)S(1)} %get-tuple-element.34.refs_0_, bf16[1024,1536]{1,0:T(8,128)(2,1)S(1)} %get-tuple-element.35.refs_1_, bf16[1024,768]{1,0:T(8,128)(2,1)S(1)} %get-tuple-element.44.refs_2_, bf16[1024,768]{1,0:T(8,128)(2,1)S(1)} %get-tuple-element.45.refs_3_, ...), custom_call_target="tpu_custom_call" | custom-call | flops 905969664 | bytes 1048576 | tf_op jit(solution)/shard_map/pallas_call | solution.py:686
  34.4 0.1 collective-permute-start.8
  34.5 1.1 %shard_map.164.refs_0_ = f32[2,16,2048]{2,1,0:T(8,128)S(1)} custom-call(bf16[1024,1536]{1,0:T(8,128)(2,1)S(1)} %get-tuple-element.34.refs_0_, bf16[1024,1536]{1,0:T(8,128)(2,1)S(1)} %get-tuple-element.35.refs_1_, bf16[1024,768]{1,0:T(8,128)(2,1)S(1)} %get-tuple-element.44.refs_2_, bf16[1024,768]{1,0:T(8,128)(2,1)S(1)} %get-tuple-element.45.refs_3_, ...), custom_call_target="tpu_custom_call" | custom-call | flops 905969664 | bytes 1048576 | tf_op jit(solution)/shard_map/pallas_call | solution.py:686
  35.6 0.4 collective-permute-done.8.refs_1_
  36.1 1.1 %shard_map.166.refs_8_ = f32[2,16,2048]{2,1,0:T(8,128)S(1)} custom-call(bf16[1024,1536]{1,0:T(8,128)(2,1)S(1)} %get-tuple-element.34.refs_0_, bf16[1024,1536]{1,0:T(8,128)(2,1)S(1)} %get-tuple-element.35.refs_1_, bf16[1024,768]{1,0:T(8,128)(2,1)S(1)} %get-tuple-element.44.refs_2_, bf16[1024,768]{1,0:T(8,128)(2,1)S(1)} %get-tuple-element.45.refs_3_, ...), custom_call_target="tpu_custom_call" | custom-call | flops 905969664 | bytes 1048576 | tf_op jit(solution)/shard_map/pallas_call | solution.py:686
  37.1 0.2 collective-permute-start.10
  37.3 1.1 %shard_map.167.refs_8_.refs_0_ = f32[2,16,2048]{2,1,0:T(8,128)S(1)} custom-call(bf16[1024,1536]{1,0:T(8,128)(2,1)S(1)} %get-tuple-element.34.refs_0_, bf16[1024,1536]{1,0:T(8,128)(2,1)S(1)} %get-tuple-element.35.refs_1_, bf16[1024,768]{1,0:T(8,128)(2,1)S(1)} %get-tuple-element.44.refs_2_, bf16[1024,768]{1,0:T(8,128)(2,1)S(1)} %get-tuple-element.45.refs_3_, ...), custom_call_target="tpu_custom_call" | custom-call | flops 905969664 | bytes 1048576 | tf_op jit(solution)/shard_map/pallas_call | solution.py:686
  38.4 1.1 %shard_map.168.refs_8_ = f32[2,16,2048]{2,1,0:T(8,128)S(1)} custom-call(bf16[1024,1536]{1,0:T(8,128)(2,1)S(1)} %get-tuple-element.34.refs_0_, bf16[1024,1536]{1,0:T(8,128)(2,1)S(1)} %get-tuple-element.35.refs_1_, bf16[1024,768]{1,0:T(8,128)(2,1)S(1)} %get-tuple-element.44.refs_2_, bf16[1024,768]{1,0:T(8,128)(2,1)S(1)} %get-tuple-element.45.refs_3_, ...), custom_call_target="tpu_custom_call" | custom-call | flops 905969664 | bytes 1048576 | tf_op jit(solution)/shard_map/pallas_call | solution.py:686
  39.5 0.4 collective-permute-start.9
  39.9 0.0 collective-permute-start.11
  40.0 1.1 %shard_map.169.refs_0_ = f32[2,16,2048]{2,1,0:T(8,128)S(1)} custom-call(bf16[1024,1536]{1,0:T(8,128)(2,1)S(1)} %get-tuple-element.34.refs_0_, bf16[1024,1536]{1,0:T(8,128)(2,1)S(1)} %get-tuple-element.35.refs_1_, bf16[1024,768]{1,0:T(8,128)(2,1)S(1)} %get-tuple-element.44.refs_2_, bf16[1024,768]{1,0:T(8,128)(2,1)S(1)} %get-tuple-element.45.refs_3_, ...), custom_call_target="tpu_custom_call" | custom-call | flops 905969664 | bytes 1048576 | tf_op jit(solution)/shard_map/pallas_call | solution.py:686
  41.1 4.4 %collective-permute-done.11.refs_2_ = f32[1,16,2048]{2,1,0:T(8,128)S(1)} collective-permute-done((f32[1,16,2048]{2,1,0:T(8,128)S(1)}, f32[1,16,2048]{2,1,0:T(8,128)S(1)}, u32[]{:S(2)}, u32[]{:S(2)}) %collective-permute-start.11) | collective-permute-done | bytes 131104 | tf_op jit(solution)/shard_map/ppermute | solution.py:689
  45.5 0.0 collective-permute-done.10.refs_1_
  45.5 0.0 collective-permute-done.9.refs_1_
  45.6 1.1 %shard_map.172.refs_8_ = f32[2,16,2048]{2,1,0:T(8,128)S(1)} custom-call(bf16[1024,1536]{1,0:T(8,128)(2,1)S(1)} %get-tuple-element.34.refs_0_, bf16[1024,1536]{1,0:T(8,128)(2,1)S(1)} %get-tuple-element.35.refs_1_, bf16[1024,768]{1,0:T(8,128)(2,1)S(1)} %get-tuple-element.44.refs_2_, bf16[1024,768]{1,0:T(8,128)(2,1)S(1)} %get-tuple-element.45.refs_3_, ...), custom_call_target="tpu_custom_call" | custom-call | flops 905969664 | bytes 1048576 | tf_op jit(solution)/shard_map/pallas_call | solution.py:686
  46.6 0.1 collective-permute-start.12
  46.7 0.3 collective-permute-start.15
  47.1 1.7 %collective-permute-start.17 = (f32[1,16,2048]{2,1,0:T(8,128)S(1)}, f32[1,16,2048]{2,1,0:T(8,128)S(1)}, u32[]{:S(2)}, u32[]{:S(2)}) collective-permute-start(f32[1,16,2048]{2,1,0:T(8,128)S(1)} %get-tuple-element.58.refs_8_), channel_id=1, source_target_pairs={{0,2},{1,3},{2,0},{3,1},{4,6},{5,7},{6,4},{7,5},{8,10},{9,11},{10,... | collective-permute-start | bytes 393224 | tf_op jit(solution)/shard_map/ppermute | solution.py:689
  48.8 1.6 %collective-permute-start.14 = (f32[1,16,2048]{2,1,0:T(8,128)S(1)}, f32[1,16,2048]{2,1,0:T(8,128)S(1)}, u32[]{:S(2)}, u32[]{:S(2)}) collective-permute-start(f32[1,16,2048]{2,1,0:T(8,128)S(1)} %shard_map.171.refs_9_), channel_id=1, source_target_pairs={{0,8},{1,9},{2,10},{3,11},{4,12},{5,13},{6,14},{7,15},{8,0},{9,1},... | collective-permute-start | bytes 393224 | tf_op jit(solution)/shard_map/ppermute | solution.py:689
  50.4 2.8 %collective-permute-done.15.refs_2_ = f32[1,16,2048]{2,1,0:T(8,128)S(1)} collective-permute-done((f32[1,16,2048]{2,1,0:T(8,128)S(1)}, f32[1,16,2048]{2,1,0:T(8,128)S(1)}, u32[]{:S(2)}, u32[]{:S(2)}) %collective-permute-start.15) | collective-permute-done | bytes 131104 | tf_op jit(solution)/shard_map/ppermute | solution.py:689
  53.2 0.1 collective-permute-start.16
  53.3 1.1 %shard_map.173.refs_0_ = f32[2,16,2048]{2,1,0:T(8,128)S(1)} custom-call(bf16[1024,1536]{1,0:T(8,128)(2,1)S(1)} %get-tuple-element.34.refs_0_, bf16[1024,1536]{1,0:T(8,128)(2,1)S(1)} %get-tuple-element.35.refs_1_, bf16[1024,768]{1,0:T(8,128)(2,1)S(1)} %get-tuple-element.44.refs_2_, bf16[1024,768]{1,0:T(8,128)(2,1)S(1)} %get-tuple-element.45.refs_3_, ...), custom_call_target="tpu_custom_call" | custom-call | flops 905969664 | bytes 1048576 | tf_op jit(solution)/shard_map/pallas_call | solution.py:686
  54.4 1.7 %collective-permute-start.13 = (f32[1,16,2048]{2,1,0:T(8,128)S(1)}, f32[1,16,2048]{2,1,0:T(8,128)S(1)}, u32[]{:S(2)}, u32[]{:S(2)}) collective-permute-start(f32[1,16,2048]{2,1,0:T(8,128)S(1)} %get-tuple-element.59), channel_id=1, source_target_pairs={{0,2},{1,3},{2,0},{3,1},{4,6},{5,7},{6,4},{7,5},{8,10},{9,11},{10,... | collective-permute-start | bytes 393224 | tf_op jit(solution)/shard_map/ppermute | solution.py:689
  56.1 0.0 collective-permute-done.17.refs_2_
  56.1 0.0 collective-permute-done.12.refs_1_
  56.1 2.4 %collective-permute-start.18 = (f32[1,16,2048]{2,1,0:T(8,128)S(1)}, f32[1,16,2048]{2,1,0:T(8,128)S(1)}, u32[]{:S(2)}, u32[]{:S(2)}) collective-permute-start(f32[1,16,2048]{2,1,0:T(8,128)S(1)} %shard_map.176), channel_id=1, source_target_pairs={{0,12},{1,13},{2,14},{3,15},{4,0},{5,1},{6,2},{7,3},{8,4},{9,5},{1... | collective-permute-start | bytes 393224 | tf_op jit(solution)/shard_map/ppermute | solution.py:689
  58.6 0.9 %collective-permute-done.13.refs_2_ = f32[1,16,2048]{2,1,0:T(8,128)S(1)} collective-permute-done((f32[1,16,2048]{2,1,0:T(8,128)S(1)}, f32[1,16,2048]{2,1,0:T(8,128)S(1)}, u32[]{:S(2)}, u32[]{:S(2)}) %collective-permute-start.13) | collective-permute-done | bytes 131104 | tf_op jit(solution)/shard_map/ppermute | solution.py:689
  59.5 1.8 %collective-permute-done.16.refs_2_ = f32[1,16,2048]{2,1,0:T(8,128)S(1)} collective-permute-done((f32[1,16,2048]{2,1,0:T(8,128)S(1)}, f32[1,16,2048]{2,1,0:T(8,128)S(1)}, u32[]{:S(2)}, u32[]{:S(2)}) %collective-permute-start.16) | collective-permute-done | bytes 131104 | tf_op jit(solution)/shard_map/ppermute | solution.py:689
  61.3 0.0 collective-permute-done.14.refs_1_
  61.3 1.6 %collective-permute-done.18.refs_3_ = f32[1,16,2048]{2,1,0:T(8,128)S(1)} collective-permute-done((f32[1,16,2048]{2,1,0:T(8,128)S(1)}, f32[1,16,2048]{2,1,0:T(8,128)S(1)}, u32[]{:S(2)}, u32[]{:S(2)}) %collective-permute-start.18) | collective-permute-done | bytes 131104 | tf_op jit(solution)/shard_map/ppermute | solution.py:689
  63.0 0.7 %shard_map.177 = f32[16,4,2,256]{3,2,1,0:T(2,128)} custom-call(f32[1,16,2048]{2,1,0:T(8,128)S(1)} %shard_map.174.refs_0_, f32[1,16,2048]{2,1,0:T(8,128)S(1)} %collective-permute-done.14.refs_1_, f32[1,16,2048]{2,1,0:T(8,128)S(1)} %collective-permute-done.16.refs_2_, f32[1,16,2048]{2,1,0:T(8,128)S(1)} %collective-permute-done.18.refs_3_), custom_call_target="tpu_custom_call" | custom-call | tf_op jit(solution)/shard_map/pallas_call | solution.py:735
  (33 shorter events, 0.3 us)
Async XLA Ops:
  0.0 11.6 %copy-start.12 = (s32[1152]{0:T(1024)S(1)}, s32[1152]{0:T(1024)}, u32[]{:S(2)}) copy-start(s32[1152]{0:T(1024)} %constant.106.clone) | copy-start | bytes 13828
  0.0 11.6 %copy-start.13 = (s32[1152]{0:T(1024)S(1)}, s32[1152]{0:T(1024)}, u32[]{:S(2)}) copy-start(s32[1152]{0:T(1024)} %constant.107.clone) | copy-start | bytes 13828
  0.0 11.6 %copy-start.14 = (s32[1152]{0:T(1024)S(1)}, s32[1152]{0:T(1024)}, u32[]{:S(2)}) copy-start(s32[1152]{0:T(1024)} %constant.108.clone) | copy-start | bytes 13828
  0.0 11.7 %copy-start.11 = (s32[1152]{0:T(1024)S(1)}, s32[1152]{0:T(1024)}, u32[]{:S(2)}) copy-start(s32[1152]{0:T(1024)} %constant.109.clone) | copy-start | bytes 13828
  0.0 11.4 %copy-start.10 = (s32[4,3]{1,0:T(4,128)S(1)}, s32[4,3]{1,0:T(4,128)}, u32[]{:S(2)}) copy-start(s32[4,3]{1,0:T(4,128)} %param.18) | copy-start | bytes 148
  1.2 1.5 %copy-start = (f32[2,3,1,288,256]{4,3,2,1,0:T(8,128)S(1)}, f32[2,3,1,288,256]{4,3,2,1,0:T(8,128)}, u32[]{:S(2)}) copy-start(f32[2,3,1,288,256]{4,3,2,1,0:T(8,128)} %param.16) | copy-start | bytes 5308420
  2.7 11.0 %copy-start.4 = (s32[6,512]{1,0:T(8,128)S(1)}, s32[6,512]{1,0:T(8,128)}, u32[]{:S(2)}) copy-start(s32[6,512]{1,0:T(8,128)} %constant.102.clone.column_ref) | copy-start | bytes 36868
  2.7 11.0 %copy-start.5 = (f32[6,512]{1,0:T(8,128)S(1)}, f32[6,512]{1,0:T(8,128)}, u32[]{:S(2)}) copy-start(f32[6,512]{1,0:T(8,128)} %constant.103.clone.sign_ref) | copy-start | bytes 36868
  2.7 11.0 %copy-start.6 = (s32[6,512]{1,0:T(8,128)S(1)}, s32[6,512]{1,0:T(8,128)}, u32[]{:S(2)}) copy-start(s32[6,512]{1,0:T(8,128)} %constant.104.clone.more_ref) | copy-start | bytes 36868
  2.7 11.0 %copy-start.7 = (f32[6,512]{1,0:T(8,128)S(1)}, f32[6,512]{1,0:T(8,128)}, u32[]{:S(2)}) copy-start(f32[6,512]{1,0:T(8,128)} %constant.105.clone.moresign_ref) | copy-start | bytes 36868
  3.4 14.0 %collective-permute-start = (f32[2,144,128]{2,1,0:T(8,128)S(1)}, f32[2,144,128]{2,1,0:T(8,128)S(1)}, u32[]{:S(2)}, u32[]{:S(2)}) collective-permute-start(f32[2,144,128]{2,1,0:T(8,128)S(1)} %get-tuple-element.39), channel_id=1, source_target_pairs={{0,4},{1,5},{2,6},{3,7},{4,0},{5,1},{6,2},{7,3},{8,12},{9,13},{10,... | collective-permute-start | bytes 442376 | tf_op jit(solution)/shard_map/ppermute | solution.py:539
  6.5 10.9 %collective-permute-start.1 = (f32[2,144,128]{2,1,0:T(8,128)S(1)}, f32[2,144,128]{2,1,0:T(8,128)S(1)}, u32[]{:S(2)}, u32[]{:S(2)}) collective-permute-start(f32[2,144,128]{2,1,0:T(8,128)S(1)} %get-tuple-element.40), channel_id=1, source_target_pairs={{0,12},{1,13},{2,14},{3,15},{4,8},{5,9},{6,10},{7,11},{8,4},{9,5},... | collective-permute-start | bytes 442376 | tf_op jit(solution)/shard_map/ppermute | solution.py:539
  9.0 8.4 %collective-permute-start.2 = (f32[2,144,128]{2,1,0:T(8,128)S(1)}, f32[2,144,128]{2,1,0:T(8,128)S(1)}, u32[]{:S(2)}, u32[]{:S(2)}) collective-permute-start(f32[2,144,128]{2,1,0:T(8,128)S(1)} %get-tuple-element.41), channel_id=1, source_target_pairs={{0,1},{1,0},{2,3},{3,2},{4,5},{5,4},{6,7},{7,6},{8,9},{9,8},{10,11... | collective-permute-start | bytes 442376 | tf_op jit(solution)/shard_map/ppermute | solution.py:539
  9.0 9.4 %collective-permute-start.3 = (f32[2,144,128]{2,1,0:T(8,128)S(1)}, f32[2,144,128]{2,1,0:T(8,128)S(1)}, u32[]{:S(2)}, u32[]{:S(2)}) collective-permute-start(f32[2,144,128]{2,1,0:T(8,128)S(1)} %get-tuple-element.42), channel_id=1, source_target_pairs={{0,15},{1,2},{2,1},{3,4},{4,3},{5,6},{6,5},{7,8},{8,7},{9,10},{10,... | collective-permute-start | bytes 442376 | tf_op jit(solution)/shard_map/ppermute | solution.py:539
  18.4 5.7 %copy-start.2 = (s32[6,640]{1,0:T(8,128)S(1)}, s32[6,640]{1,0:T(8,128)}, u32[]{:S(2)}) copy-start(s32[6,640]{1,0:T(8,128)} %constant.110.clone.column_ref) | copy-start | bytes 46084
  18.4 5.7 %copy-start.3 = (f32[6,640]{1,0:T(8,128)S(1)}, f32[6,640]{1,0:T(8,128)}, u32[]{:S(2)}) copy-start(f32[6,640]{1,0:T(8,128)} %constant.111.clone.sign_ref) | copy-start | bytes 46084
  18.4 5.7 %copy-start.8 = (s32[6,256]{1,0:T(8,128)S(1)}, s32[6,256]{1,0:T(8,128)}, u32[]{:S(2)}) copy-start(s32[6,256]{1,0:T(8,128)} %constant.112.clone.more_ref) | copy-start | bytes 18436
  18.4 5.7 %copy-start.9 = (f32[6,256]{1,0:T(8,128)S(1)}, f32[6,256]{1,0:T(8,128)}, u32[]{:S(2)}) copy-start(f32[6,256]{1,0:T(8,128)} %constant.113.clone.moresign_ref) | copy-start | bytes 18436
  19.5 9.7 %collective-permute-start.4 = (f32[2,144,128]{2,1,0:T(8,128)S(1)}, f32[2,144,128]{2,1,0:T(8,128)S(1)}, u32[]{:S(2)}, u32[]{:S(2)}) collective-permute-start(f32[2,144,128]{2,1,0:T(8,128)S(1)} %get-tuple-element.49), channel_id=1, source_target_pairs={{0,4},{1,5},{2,6},{3,7},{4,0},{5,1},{6,2},{7,3},{8,12},{9,13},{10,... | collective-permute-start | bytes 442376 | tf_op jit(solution)/shard_map/ppermute | solution.py:539
  19.6 9.6 %collective-permute-start.5 = (f32[2,144,128]{2,1,0:T(8,128)S(1)}, f32[2,144,128]{2,1,0:T(8,128)S(1)}, u32[]{:S(2)}, u32[]{:S(2)}) collective-permute-start(f32[2,144,128]{2,1,0:T(8,128)S(1)} %get-tuple-element.50), channel_id=1, source_target_pairs={{0,12},{1,13},{2,14},{3,15},{4,8},{5,9},{6,10},{7,11},{8,4},{9,5},... | collective-permute-start | bytes 442376 | tf_op jit(solution)/shard_map/ppermute | solution.py:539
  22.8 6.4 %collective-permute-start.6 = (f32[2,144,128]{2,1,0:T(8,128)S(1)}, f32[2,144,128]{2,1,0:T(8,128)S(1)}, u32[]{:S(2)}, u32[]{:S(2)}) collective-permute-start(f32[2,144,128]{2,1,0:T(8,128)S(1)} %get-tuple-element.51), channel_id=1, source_target_pairs={{0,1},{1,0},{2,3},{3,2},{4,5},{5,4},{6,7},{7,6},{8,9},{9,8},{10,11... | collective-permute-start | bytes 442376 | tf_op jit(solution)/shard_map/ppermute | solution.py:539
  22.8 7.5 %collective-permute-start.7 = (f32[2,144,128]{2,1,0:T(8,128)S(1)}, f32[2,144,128]{2,1,0:T(8,128)S(1)}, u32[]{:S(2)}, u32[]{:S(2)}) collective-permute-start(f32[2,144,128]{2,1,0:T(8,128)S(1)} %get-tuple-element.52), channel_id=1, source_target_pairs={{0,15},{1,2},{2,1},{3,4},{4,3},{5,6},{6,5},{7,8},{8,7},{9,10},{10,... | collective-permute-start | bytes 442376 | tf_op jit(solution)/shard_map/ppermute | solution.py:539
  28.1 2.2 %copy-start.1 = (s32[256]{0:T(256)S(1)}, s32[256]{0:T(256)}, u32[]{:S(2)}) copy-start(s32[256]{0:T(256)} %param.19) | copy-start | bytes 3076
  34.4 1.6 %collective-permute-start.8 = (f32[2,16,2048]{2,1,0:T(8,128)S(1)}, f32[2,16,2048]{2,1,0:T(8,128)S(1)}, u32[]{:S(2)}, u32[]{:S(2)}) collective-permute-start(f32[2,16,2048]{2,1,0:T(8,128)S(1)} %shard_map.163.refs_8_), channel_id=1, source_target_pairs={{0,1},{1,0},{2,3},{3,2},{4,5},{5,4},{6,7},{7,6},{8,9},{9,8},{10,11... | collective-permute-start | bytes 786440 | tf_op jit(solution)/shard_map/ppermute | solution.py:689
  37.1 8.3 %collective-permute-start.10 = (f32[2,16,2048]{2,1,0:T(8,128)S(1)}, f32[2,16,2048]{2,1,0:T(8,128)S(1)}, u32[]{:S(2)}, u32[]{:S(2)}) collective-permute-start(f32[2,16,2048]{2,1,0:T(8,128)S(1)} %shard_map.166.refs_8_), channel_id=1, source_target_pairs={{0,1},{1,0},{2,3},{3,2},{4,5},{5,4},{6,7},{7,6},{8,9},{9,8},{10,11... | collective-permute-start | bytes 786440 | tf_op jit(solution)/shard_map/ppermute | solution.py:689
  39.5 6.0 %collective-permute-start.9 = (f32[2,16,2048]{2,1,0:T(8,128)S(1)}, f32[2,16,2048]{2,1,0:T(8,128)S(1)}, u32[]{:S(2)}, u32[]{:S(2)}) collective-permute-start(f32[2,16,2048]{2,1,0:T(8,128)S(1)} %shard_map.168.refs_8_), channel_id=1, source_target_pairs={{0,1},{1,0},{2,3},{3,2},{4,5},{5,4},{6,7},{7,6},{8,9},{9,8},{10,11... | collective-permute-start | bytes 786440 | tf_op jit(solution)/shard_map/ppermute | solution.py:689
  39.9 5.5 %collective-permute-start.11 = (f32[1,16,2048]{2,1,0:T(8,128)S(1)}, f32[1,16,2048]{2,1,0:T(8,128)S(1)}, u32[]{:S(2)}, u32[]{:S(2)}) collective-permute-start(f32[1,16,2048]{2,1,0:T(8,128)S(1)} %get-tuple-element.57.refs_8_), channel_id=1, source_target_pairs={{0,2},{1,3},{2,0},{3,1},{4,6},{5,7},{6,4},{7,5},{8,10},{9,11},{10,... | collective-permute-start | bytes 393224 | tf_op jit(solution)/shard_map/ppermute | solution.py:689
  46.6 9.5 %collective-permute-start.12 = (f32[2,16,2048]{2,1,0:T(8,128)S(1)}, f32[2,16,2048]{2,1,0:T(8,128)S(1)}, u32[]{:S(2)}, u32[]{:S(2)}) collective-permute-start(f32[2,16,2048]{2,1,0:T(8,128)S(1)} %shard_map.172.refs_8_), channel_id=1, source_target_pairs={{0,1},{1,0},{2,3},{3,2},{4,5},{5,4},{6,7},{7,6},{8,9},{9,8},{10,11... | collective-permute-start | bytes 786440 | tf_op jit(solution)/shard_map/ppermute | solution.py:689
  46.7 6.4 %collective-permute-start.15 = (f32[1,16,2048]{2,1,0:T(8,128)S(1)}, f32[1,16,2048]{2,1,0:T(8,128)S(1)}, u32[]{:S(2)}, u32[]{:S(2)}) collective-permute-start(f32[1,16,2048]{2,1,0:T(8,128)S(1)} %get-tuple-element.60), channel_id=1, source_target_pairs={{0,2},{1,3},{2,0},{3,1},{4,6},{5,7},{6,4},{7,5},{8,10},{9,11},{10,... | collective-permute-start | bytes 393224 | tf_op jit(solution)/shard_map/ppermute | solution.py:689
  47.1 9.0 %collective-permute-start.17 = (f32[1,16,2048]{2,1,0:T(8,128)S(1)}, f32[1,16,2048]{2,1,0:T(8,128)S(1)}, u32[]{:S(2)}, u32[]{:S(2)}) collective-permute-start(f32[1,16,2048]{2,1,0:T(8,128)S(1)} %get-tuple-element.58.refs_8_), channel_id=1, source_target_pairs={{0,2},{1,3},{2,0},{3,1},{4,6},{5,7},{6,4},{7,5},{8,10},{9,11},{10,... | collective-permute-start | bytes 393224 | tf_op jit(solution)/shard_map/ppermute | solution.py:689
  48.8 12.5 %collective-permute-start.14 = (f32[1,16,2048]{2,1,0:T(8,128)S(1)}, f32[1,16,2048]{2,1,0:T(8,128)S(1)}, u32[]{:S(2)}, u32[]{:S(2)}) collective-permute-start(f32[1,16,2048]{2,1,0:T(8,128)S(1)} %shard_map.171.refs_9_), channel_id=1, source_target_pairs={{0,8},{1,9},{2,10},{3,11},{4,12},{5,13},{6,14},{7,15},{8,0},{9,1},... | collective-permute-start | bytes 393224 | tf_op jit(solution)/shard_map/ppermute | solution.py:689
  53.2 8.1 %collective-permute-start.16 = (f32[1,16,2048]{2,1,0:T(8,128)S(1)}, f32[1,16,2048]{2,1,0:T(8,128)S(1)}, u32[]{:S(2)}, u32[]{:S(2)}) collective-permute-start(f32[1,16,2048]{2,1,0:T(8,128)S(1)} %shard_map.175), channel_id=1, source_target_pairs={{0,4},{1,5},{2,6},{3,7},{4,8},{5,9},{6,10},{7,11},{8,12},{9,13},{1... | collective-permute-start | bytes 393224 | tf_op jit(solution)/shard_map/ppermute | solution.py:689
  54.4 5.0 %collective-permute-start.13 = (f32[1,16,2048]{2,1,0:T(8,128)S(1)}, f32[1,16,2048]{2,1,0:T(8,128)S(1)}, u32[]{:S(2)}, u32[]{:S(2)}) collective-permute-start(f32[1,16,2048]{2,1,0:T(8,128)S(1)} %get-tuple-element.59), channel_id=1, source_target_pairs={{0,2},{1,3},{2,0},{3,1},{4,6},{5,7},{6,4},{7,5},{8,10},{9,11},{10,... | collective-permute-start | bytes 393224 | tf_op jit(solution)/shard_map/ppermute | solution.py:689
  56.1 6.8 %collective-permute-start.18 = (f32[1,16,2048]{2,1,0:T(8,128)S(1)}, f32[1,16,2048]{2,1,0:T(8,128)S(1)}, u32[]{:S(2)}, u32[]{:S(2)}) collective-permute-start(f32[1,16,2048]{2,1,0:T(8,128)S(1)} %shard_map.176), channel_id=1, source_target_pairs={{0,12},{1,13},{2,14},{3,15},{4,0},{5,1},{6,2},{7,3},{8,4},{9,5},{1... | collective-permute-start | bytes 393224 | tf_op jit(solution)/shard_map/ppermute | solution.py:689

commit v7 on v6

--- a/solution.py
+++ b/solution.py
@@ -323,7 +323,6 @@
 
 def edge_kernel(part_ref, wc_ref, rax, rbx, ray, rby, *refs, tiles):
     once_ref, save, ax_ref, bx_ref, ay_ref, by_ref = refs[-6:]
-    once_ref[...] = part_ref[...]
     cross(once_ref, wc_ref, (rax, rbx, ray, rby), tiles, save)
     send_layers(once_ref, wc_ref, ax_ref, bx_ref, ay_ref, by_ref, tiles)
 
@@ -611,7 +610,8 @@
     )
     edges = f32(2, halves, EDGE, LANES)
     once, save, *sends = call(
-        functools.partial(edge_kernel, tiles=tiles), (padded, edges, layer, layer, layer, layer), inputs=7
+        functools.partial(edge_kernel, tiles=tiles), (padded, edges, layer, layer, layer, layer), inputs=7,
+        input_output_aliases={0: 0},
     )(once, wc, *received, ah)
     received = halo(sends, devices, tiles)
     twice = call(smear_kernel, padded, pair, flops, 3 << 20, 3)(once, *smear)
@@ -693,7 +693,7 @@
         outs = tuple(block(len(p)) for p in picks)
         return call(kernel, outs, inputs=len(arrays))(*arrays)
 
-    order = sorted(range(1, groups), key=lambda g: -min(g, groups - g)) + [0]
+    order = [*range(1, groups), 0]
     early, late = order[: groups // 2], order[groups // 2 :]
 
     def along_z(value, step):

time: 63.8 us -> 64.1 us (level)
  waiting for transfers between devices: 14 us -> 15.9 us
  starting transfers between devices: 21.4 us -> 19.9 us
    ppermute x11, waiting for transfers between devices: 12 us -> 13.7 us  [permute(): return lax.ppermute(value, 'site', route)]
    ppermute x11, starting transfers between devices: 8.76 us -> 7.25 us  [permute(): return lax.ppermute(value, 'site', route)]
where the time goes in v7:
time: 64.1 us; the launch traced here: 63.9 us
  Pallas kernels  24.6 us (38%)
  starting transfers between devices  19.9 us (31%)
  waiting for transfers between devices  15.9 us (25%)
  local copies, waits for them, and re-layouts  1.75 us (3%)
  other arithmetic  1.47 us (2%)
    ppermute x11, waiting for transfers between devices, permute(): return lax.ppermute(value, 'site', route)  13.7 us
    ppermute x8, starting transfers between devices, halo(): found.append(lax.ppermute(block, 'site', route))  12.6 us
    pallas_call x8, Pallas kernels, piece(): call(kernel, block(len(steps)), (), flops, 1 << 20, 8 + len(after))  8.62 us
    ppermute x11, starting transfers between devices, permute(): return lax.ppermute(value, 'site', route)  7.25 us
    pallas_call x2, Pallas kernels, operator(): call(kernel, (out, out), (), 1 << 30, 4 << 20, 5)  4.17 us
    pallas_call x1, Pallas kernels, on_device(): call(functools.partial(displace_kernel, scale=scale, tiles=tiles), (bf16(...  3.12 us
    ppermute x8, waiting for transfers between devices, halo(): found.append(lax.ppermute(block, 'site', route))  2.13 us
    pallas_call x1, Pallas kernels, on_device(): call(head_kernel, (head, head), [rows], flops, 8 << 20, 3)(fr, cosine, sine)  1.72 us
  transfers between devices with their start and end apart: 19, of which 8 were waited for; matrix products, arithmetic and copies ran while one was open for 1% of the time, Pallas kernels for 25%

profile of v7, /device:TPU:0, one launch (start us, length us, event | category | flops | bytes accessed | tf_op | source)
XLA Modules:
  0.0 63.9 jit_solution(6590371092770853449)
XLA Ops:
  0.0 1.2 %reduce = f32[3,2,3,3,288]{4,3,2,1,0:T(4,128)S(1)} reduce(f32[3,2,3,3,1,288]{5,4,3,2,1,0:T(1,128)} %param.17, f32[]{:T(128)} %constant.116), dimensions={4}, to_apply=%param.17.reduce_sub_computation | reduce | bytes 124420 | tf_op args[1]
  1.2 0.0 copy-start
  1.2 1.5 %copy-done = f32[2,3,1,288,256]{4,3,2,1,0:T(8,128)S(1)} copy-done((f32[2,3,1,288,256]{4,3,2,1,0:T(8,128)S(1)}, f32[2,3,1,288,256]{4,3,2,1,0:T(8,128)}, u32[]{:S(2)}) %copy-start) | copy-done | bytes 1769496
  2.7 0.7 %shard_map.154 = (f32[2,2016,128]{2,1,0:T(8,128)S(1)}, f32[312,128]{1,0:T(8,128)S(1)}, f32[2,144,128]{2,1,0:T(8,128)S(1)}, f32[2,144,128]{2,1,0:T(8,128)S(1)}, f...) custom-call(f32[6,288,256]{2,1,0:T(8,128)S(1)} %bitcast.2, f32[54,288]{1,0:T(8,128)S(1)} %reshape.10.l_ref), custom_call_target="tpu_custom_call" | custom-call | tf_op jit(solution)/shard_map/pallas_call | solution.py:582
  3.4 3.1 %collective-permute-start = (f32[2,144,128]{2,1,0:T(8,128)S(1)}, f32[2,144,128]{2,1,0:T(8,128)S(1)}, u32[]{:S(2)}, u32[]{:S(2)}) collective-permute-start(f32[2,144,128]{2,1,0:T(8,128)S(1)} %get-tuple-element.39), channel_id=1, source_target_pairs={{0,4},{1,5},{2,6},{3,7},{4,0},{5,1},{6,2},{7,3},{8,12},{9,13},{10,... | collective-permute-start | bytes 442376 | tf_op jit(solution)/shard_map/ppermute | solution.py:538
  6.5 2.5 %collective-permute-start.1 = (f32[2,144,128]{2,1,0:T(8,128)S(1)}, f32[2,144,128]{2,1,0:T(8,128)S(1)}, u32[]{:S(2)}, u32[]{:S(2)}) collective-permute-start(f32[2,144,128]{2,1,0:T(8,128)S(1)} %get-tuple-element.40), channel_id=1, source_target_pairs={{0,12},{1,13},{2,14},{3,15},{4,8},{5,9},{6,10},{7,11},{8,4},{9,5},... | collective-permute-start | bytes 442376 | tf_op jit(solution)/shard_map/ppermute | solution.py:538
  9.0 0.0 collective-permute-start.2
  9.0 2.4 %collective-permute-start.3 = (f32[2,144,128]{2,1,0:T(8,128)S(1)}, f32[2,144,128]{2,1,0:T(8,128)S(1)}, u32[]{:S(2)}, u32[]{:S(2)}) collective-permute-start(f32[2,144,128]{2,1,0:T(8,128)S(1)} %get-tuple-element.42), channel_id=1, source_target_pairs={{0,15},{1,2},{2,1},{3,4},{4,3},{5,6},{6,5},{7,8},{8,7},{9,10},{10,... | collective-permute-start | bytes 442376 | tf_op jit(solution)/shard_map/ppermute | solution.py:538
  11.4 0.2 slice_reduce_fusion.2
  11.7 0.0 copy-done.11
  11.7 0.3 fusion.21
  12.0 1.7 %shard_map.155 = (bf16[1024,1536]{1,0:T(8,128)(2,1)S(1)}, bf16[1024,1536]{1,0:T(8,128)(2,1)S(1)}) custom-call(f32[2,2016,128]{2,1,0:T(8,128)S(1)} %get-tuple-element.33.fr_ref.f_ref, f32[4,1152]{1,0:T(4,128)S(1)} %get-tuple-element.65.cos_ref, f32[4,1152]{1,0:T(4,128)S(1)} %get-tuple-element.64.sin_ref), custom_call_target="tpu_custom_call" | custom-call | flops 53084160 | bytes 8388608 | tf_op jit(solution)/shard_map/pallas_call | solution.py:603
  13.7 2.0 %shard_map.156 = (bf16[1728,432]{1,0:T(8,128)(2,1)S(1)}, bf16[1728,432]{1,0:T(8,128)(2,1)S(1)}) custom-call(f32[312,128]{1,0:T(8,128)S(1)} %get-tuple-element.36.wc_ref, s32[6,512]{1,0:T(8,128)S(1)} %copy-done.4, f32[6,512]{1,0:T(8,128)S(1)} %copy-done.5, s32[6,512]{1,0:T(8,128)S(1)} %copy-done.6, f32[6,512]{1,0:T(8,128)S(1)} %copy-done.7), custom_call_target="tpu_custom_call" | custom-call | flops 1073741824 | bytes 4194304 | tf_op jit(solution)/shard_map/pallas_call | solution.py:658
  15.8 1.7 %shard_map.157.part_ref = f32[2,2016,128]{2,1,0:T(8,128)S(1)} custom-call(f32[2,2016,128]{2,1,0:T(8,128)S(1)} %get-tuple-element.33.fr_ref.f_ref, bf16[1728,432]{1,0:T(8,128)(2,1)S(1)} %get-tuple-element.37.oh_ref, bf16[1728,432]{1,0:T(8,128)(2,1)S(1)} %get-tuple-element.38.ol_ref), custom_call_target="tpu_custom_call" | custom-call | flops 53084160 | bytes 3145728 | tf_op jit(solution)/shard_map/pallas_call | solution.py:598
  17.4 0.0 collective-permute-done.rax
  17.4 0.0 collective-permute-done.1.rbx
  17.4 0.0 collective-permute-done.2.ray
  17.5 0.9 %collective-permute-done.3.rby = f32[2,144,128]{2,1,0:T(8,128)S(1)} collective-permute-done((f32[2,144,128]{2,1,0:T(8,128)S(1)}, f32[2,144,128]{2,1,0:T(8,128)S(1)}, u32[]{:S(2)}, u32[]{:S(2)}) %collective-permute-start.3) | collective-permute-done | bytes 147488 | tf_op jit(solution)/shard_map/ppermute | solution.py:538
  18.4 1.0 %shard_map.158 = (f32[2,2016,128]{2,1,0:T(8,128)S(1)}, f32[2,2,288,128]{3,2,1,0:T(8,128)S(1)}, f32[2,144,128]{2,1,0:T(8,128)S(1)}, f32[2,144,128]{2,1,0:T(8,128)...) custom-call(f32[2,2016,128]{2,1,0:T(8,128)S(1)} %shard_map.157.part_ref, ...), custom_call_target="tpu_custom_call", output_to_operand_aliasing={{0}: (0, {})} | custom-call | tf_op jit(solution)/shard_map/pallas_call | solution.py:612
  19.4 0.1 collective-permute-start.4
  19.5 3.2 %collective-permute-start.5 = (f32[2,144,128]{2,1,0:T(8,128)S(1)}, f32[2,144,128]{2,1,0:T(8,128)S(1)}, u32[]{:S(2)}, u32[]{:S(2)}) collective-permute-start(f32[2,144,128]{2,1,0:T(8,128)S(1)} %get-tuple-element.50), channel_id=1, source_target_pairs={{0,12},{1,13},{2,14},{3,15},{4,8},{5,9},{6,10},{7,11},{8,4},{9,5},... | collective-permute-start | bytes 442376 | tf_op jit(solution)/shard_map/ppermute | solution.py:538
  22.7 0.0 collective-permute-start.6
  22.7 1.3 %collective-permute-start.7 = (f32[2,144,128]{2,1,0:T(8,128)S(1)}, f32[2,144,128]{2,1,0:T(8,128)S(1)}, u32[]{:S(2)}, u32[]{:S(2)}) collective-permute-start(f32[2,144,128]{2,1,0:T(8,128)S(1)} %get-tuple-element.52), channel_id=1, source_target_pairs={{0,15},{1,2},{2,1},{3,4},{4,3},{5,6},{6,5},{7,8},{8,7},{9,10},{10,... | collective-permute-start | bytes 442376 | tf_op jit(solution)/shard_map/ppermute | solution.py:538
  24.1 0.0 copy-done.9
  24.1 2.2 %shard_map.161 = (bf16[1728,576]{1,0:T(8,128)(2,1)S(1)}, bf16[1728,576]{1,0:T(8,128)(2,1)S(1)}) custom-call(f32[312,128]{1,0:T(8,128)S(1)} %get-tuple-element.36.wc_ref, s32[6,640]{1,0:T(8,128)S(1)} %copy-done.2, f32[6,640]{1,0:T(8,128)S(1)} %copy-done.3, s32[6,256]{1,0:T(8,128)S(1)} %copy-done.8, f32[6,256]{1,0:T(8,128)S(1)} %copy-done.9), custom_call_target="tpu_custom_call" | custom-call | flops 1073741824 | bytes 4194304 | tf_op jit(solution)/shard_map/pallas_call | solution.py:658
  26.2 1.7 %shard_map.160.part_ref = f32[2,2016,128]{2,1,0:T(8,128)S(1)} custom-call(f32[2,2016,128]{2,1,0:T(8,128)S(1)} %get-tuple-element.46.f_ref, bf16[1728,432]{1,0:T(8,128)(2,1)S(1)} %get-tuple-element.37.oh_ref, bf16[1728,432]{1,0:T(8,128)(2,1)S(1)} %get-tuple-element.38.ol_ref), custom_call_target="tpu_custom_call" | custom-call | flops 53084160 | bytes 3145728 | tf_op jit(solution)/shard_map/pallas_call | solution.py:617
  27.9 0.0 copy-start.1
  27.9 1.1 %shard_map.159 = (bf16[1024,768]{1,0:T(8,128)(2,1)S(1)}, bf16[1024,768]{1,0:T(8,128)(2,1)S(1)}) custom-call(f32[2,2016,128]{2,1,0:T(8,128)S(1)} %get-tuple-element.33.fr_ref.f_ref, f32[2,2,288,128]{3,2,1,0:T(8,128)S(1)} %get-tuple-element.43.save, f32[4,1152]{1,0:T(4,128)S(1)} %get-tuple-element.65.cos_ref, f32[4,1152]{1,0:T(4,128)S(1)} %get-tuple-element.64.sin_ref), custom_call_target="tpu_custom_call" | custom-call | flops 53084160 | bytes 4194304 | tf_op jit(solution)/shard_map/pallas_call | solution.py:619
  29.0 0.0 collective-permute-done.4.rax
  29.0 0.0 collective-permute-done.5.rbx
  29.0 0.0 collective-permute-done.6.ray
  29.0 1.2 %collective-permute-done.7.rby = f32[2,144,128]{2,1,0:T(8,128)S(1)} collective-permute-done((f32[2,144,128]{2,1,0:T(8,128)S(1)}, f32[2,144,128]{2,1,0:T(8,128)S(1)}, u32[]{:S(2)}, u32[]{:S(2)}) %collective-permute-start.7) | collective-permute-done | bytes 147488 | tf_op jit(solution)/shard_map/ppermute | solution.py:538
  30.2 3.1 %shard_map.162 = (bf16[1536,512]{1,0:T(8,128)(2,1)S(1)}, bf16[1536,512]{1,0:T(8,128)(2,1)S(1)}, bf16[768,512]{1,0:T(8,128)(2,1)S(1)}, bf16[768,512]{1,0:T(8,128)(2,1)S(1)}) custom-call(f32[2,2016,128]{2,1,0:T(8,128)S(1)} %shard_map.160.part_ref, f32[312,128]{1,0:T(8,128)S(1)} %get-tuple-element.36.wc_ref, bf16[1728,576]{1,0:T(8,128)(2,1)S(1)} %get-tuple-element.47.oh_ref, ...), custom_call_target="tpu_custom_call" | custom-call | tf_op jit(solution)/shard_map/pallas_call | solution.py:621
  33.4 1.1 %shard_map.163.refs_8_ = f32[2,16,2048]{2,1,0:T(8,128)S(1)} custom-call(bf16[1024,1536]{1,0:T(8,128)(2,1)S(1)} %get-tuple-element.34.refs_0_, bf16[1024,1536]{1,0:T(8,128)(2,1)S(1)} %get-tuple-element.35.refs_1_, bf16[1024,768]{1,0:T(8,128)(2,1)S(1)} %get-tuple-element.44.refs_2_, bf16[1024,768]{1,0:T(8,128)(2,1)S(1)} %get-tuple-element.45.refs_3_, ...), custom_call_target="tpu_custom_call" | custom-call | flops 905969664 | bytes 1048576 | tf_op jit(solution)/shard_map/pallas_call | solution.py:686
  34.4 0.1 collective-permute-start.8
  34.5 1.1 %shard_map.164.refs_0_ = f32[2,16,2048]{2,1,0:T(8,128)S(1)} custom-call(bf16[1024,1536]{1,0:T(8,128)(2,1)S(1)} %get-tuple-element.34.refs_0_, bf16[1024,1536]{1,0:T(8,128)(2,1)S(1)} %get-tuple-element.35.refs_1_, bf16[1024,768]{1,0:T(8,128)(2,1)S(1)} %get-tuple-element.44.refs_2_, bf16[1024,768]{1,0:T(8,128)(2,1)S(1)} %get-tuple-element.45.refs_3_, ...), custom_call_target="tpu_custom_call" | custom-call | flops 905969664 | bytes 1048576 | tf_op jit(solution)/shard_map/pallas_call | solution.py:686
  35.6 0.4 collective-permute-done.8.refs_1_
  36.1 1.1 %shard_map.166.refs_8_ = f32[2,16,2048]{2,1,0:T(8,128)S(1)} custom-call(bf16[1024,1536]{1,0:T(8,128)(2,1)S(1)} %get-tuple-element.34.refs_0_, bf16[1024,1536]{1,0:T(8,128)(2,1)S(1)} %get-tuple-element.35.refs_1_, bf16[1024,768]{1,0:T(8,128)(2,1)S(1)} %get-tuple-element.44.refs_2_, bf16[1024,768]{1,0:T(8,128)(2,1)S(1)} %get-tuple-element.45.refs_3_, ...), custom_call_target="tpu_custom_call" | custom-call | flops 905969664 | bytes 1048576 | tf_op jit(solution)/shard_map/pallas_call | solution.py:686
  37.2 0.2 collective-permute-start.10
  37.4 1.1 %shard_map.167.refs_8_.refs_0_ = f32[2,16,2048]{2,1,0:T(8,128)S(1)} custom-call(bf16[1024,1536]{1,0:T(8,128)(2,1)S(1)} %get-tuple-element.34.refs_0_, bf16[1024,1536]{1,0:T(8,128)(2,1)S(1)} %get-tuple-element.35.refs_1_, bf16[1024,768]{1,0:T(8,128)(2,1)S(1)} %get-tuple-element.44.refs_2_, bf16[1024,768]{1,0:T(8,128)(2,1)S(1)} %get-tuple-element.45.refs_3_, ...), custom_call_target="tpu_custom_call" | custom-call | flops 905969664 | bytes 1048576 | tf_op jit(solution)/shard_map/pallas_call | solution.py:686
  38.5 1.1 %shard_map.168.refs_8_ = f32[2,16,2048]{2,1,0:T(8,128)S(1)} custom-call(bf16[1024,1536]{1,0:T(8,128)(2,1)S(1)} %get-tuple-element.34.refs_0_, bf16[1024,1536]{1,0:T(8,128)(2,1)S(1)} %get-tuple-element.35.refs_1_, bf16[1024,768]{1,0:T(8,128)(2,1)S(1)} %get-tuple-element.44.refs_2_, bf16[1024,768]{1,0:T(8,128)(2,1)S(1)} %get-tuple-element.45.refs_3_, ...), custom_call_target="tpu_custom_call" | custom-call | flops 905969664 | bytes 1048576 | tf_op jit(solution)/shard_map/pallas_call | solution.py:686
  39.5 0.4 collective-permute-start.9
  40.0 0.0 collective-permute-start.11
  40.0 1.1 %shard_map.169.refs_0_ = f32[2,16,2048]{2,1,0:T(8,128)S(1)} custom-call(bf16[1024,1536]{1,0:T(8,128)(2,1)S(1)} %get-tuple-element.34.refs_0_, bf16[1024,1536]{1,0:T(8,128)(2,1)S(1)} %get-tuple-element.35.refs_1_, bf16[1024,768]{1,0:T(8,128)(2,1)S(1)} %get-tuple-element.44.refs_2_, bf16[1024,768]{1,0:T(8,128)(2,1)S(1)} %get-tuple-element.45.refs_3_, ...), custom_call_target="tpu_custom_call" | custom-call | flops 905969664 | bytes 1048576 | tf_op jit(solution)/shard_map/pallas_call | solution.py:686
  41.1 4.4 %collective-permute-done.11.refs_2_ = f32[1,16,2048]{2,1,0:T(8,128)S(1)} collective-permute-done((f32[1,16,2048]{2,1,0:T(8,128)S(1)}, f32[1,16,2048]{2,1,0:T(8,128)S(1)}, u32[]{:S(2)}, u32[]{:S(2)}) %collective-permute-start.11) | collective-permute-done | bytes 131104 | tf_op jit(solution)/shard_map/ppermute | solution.py:689
  45.5 0.0 collective-permute-done.10.refs_1_
  45.5 0.0 collective-permute-done.9.refs_1_
  45.6 1.1 %shard_map.172.refs_8_ = f32[2,16,2048]{2,1,0:T(8,128)S(1)} custom-call(bf16[1024,1536]{1,0:T(8,128)(2,1)S(1)} %get-tuple-element.34.refs_0_, bf16[1024,1536]{1,0:T(8,128)(2,1)S(1)} %get-tuple-element.35.refs_1_, bf16[1024,768]{1,0:T(8,128)(2,1)S(1)} %get-tuple-element.44.refs_2_, bf16[1024,768]{1,0:T(8,128)(2,1)S(1)} %get-tuple-element.45.refs_3_, ...), custom_call_target="tpu_custom_call" | custom-call | flops 905969664 | bytes 1048576 | tf_op jit(solution)/shard_map/pallas_call | solution.py:686
  46.7 0.1 collective-permute-start.12
  46.8 0.3 collective-permute-start.15
  47.1 1.7 %collective-permute-start.17 = (f32[1,16,2048]{2,1,0:T(8,128)S(1)}, f32[1,16,2048]{2,1,0:T(8,128)S(1)}, u32[]{:S(2)}, u32[]{:S(2)}) collective-permute-start(f32[1,16,2048]{2,1,0:T(8,128)S(1)} %get-tuple-element.58.refs_8_), channel_id=1, source_target_pairs={{0,2},{1,3},{2,0},{3,1},{4,6},{5,7},{6,4},{7,5},{8,10},{9,11},{10,... | collective-permute-start | bytes 393224 | tf_op jit(solution)/shard_map/ppermute | solution.py:689
  48.8 0.1 collective-permute-start.14
  48.9 4.2 %collective-permute-done.15.refs_2_ = f32[1,16,2048]{2,1,0:T(8,128)S(1)} collective-permute-done((f32[1,16,2048]{2,1,0:T(8,128)S(1)}, f32[1,16,2048]{2,1,0:T(8,128)S(1)}, u32[]{:S(2)}, u32[]{:S(2)}) %collective-permute-start.15) | collective-permute-done | bytes 131104 | tf_op jit(solution)/shard_map/ppermute | solution.py:689
  53.2 1.6 %collective-permute-start.16 = (f32[1,16,2048]{2,1,0:T(8,128)S(1)}, f32[1,16,2048]{2,1,0:T(8,128)S(1)}, u32[]{:S(2)}, u32[]{:S(2)}) collective-permute-start(f32[1,16,2048]{2,1,0:T(8,128)S(1)} %shard_map.175), channel_id=1, source_target_pairs={{0,8},{1,9},{2,10},{3,11},{4,12},{5,13},{6,14},{7,15},{8,0},{9,1},... | collective-permute-start | bytes 393224 | tf_op jit(solution)/shard_map/ppermute | solution.py:689
  54.8 1.1 %shard_map.173.refs_0_ = f32[2,16,2048]{2,1,0:T(8,128)S(1)} custom-call(bf16[1024,1536]{1,0:T(8,128)(2,1)S(1)} %get-tuple-element.34.refs_0_, bf16[1024,1536]{1,0:T(8,128)(2,1)S(1)} %get-tuple-element.35.refs_1_, bf16[1024,768]{1,0:T(8,128)(2,1)S(1)} %get-tuple-element.44.refs_2_, bf16[1024,768]{1,0:T(8,128)(2,1)S(1)} %get-tuple-element.45.refs_3_, ...), custom_call_target="tpu_custom_call" | custom-call | flops 905969664 | bytes 1048576 | tf_op jit(solution)/shard_map/pallas_call | solution.py:686
  55.9 0.3 collective-permute-start.13
  56.3 0.0 collective-permute-done.17.refs_2_
  56.3 0.0 collective-permute-done.12.refs_1_
  56.3 2.3 %collective-permute-start.18 = (f32[1,16,2048]{2,1,0:T(8,128)S(1)}, f32[1,16,2048]{2,1,0:T(8,128)S(1)}, u32[]{:S(2)}, u32[]{:S(2)}) collective-permute-start(f32[1,16,2048]{2,1,0:T(8,128)S(1)} %shard_map.176), channel_id=1, source_target_pairs={{0,12},{1,13},{2,14},{3,15},{4,0},{5,1},{6,2},{7,3},{8,4},{9,5},{1... | collective-permute-start | bytes 393224 | tf_op jit(solution)/shard_map/ppermute | solution.py:689
  58.6 2.4 %collective-permute-done.13.refs_2_ = f32[1,16,2048]{2,1,0:T(8,128)S(1)} collective-permute-done((f32[1,16,2048]{2,1,0:T(8,128)S(1)}, f32[1,16,2048]{2,1,0:T(8,128)S(1)}, u32[]{:S(2)}, u32[]{:S(2)}) %collective-permute-start.13) | collective-permute-done | bytes 131104 | tf_op jit(solution)/shard_map/ppermute | solution.py:689
  61.0 0.7 %collective-permute-done.16.refs_2_ = f32[1,16,2048]{2,1,0:T(8,128)S(1)} collective-permute-done((f32[1,16,2048]{2,1,0:T(8,128)S(1)}, f32[1,16,2048]{2,1,0:T(8,128)S(1)}, u32[]{:S(2)}, u32[]{:S(2)}) %collective-permute-start.16) | collective-permute-done | bytes 131104 | tf_op jit(solution)/shard_map/ppermute | solution.py:689
  61.7 0.0 collective-permute-done.14.refs_1_
  61.7 1.5 %collective-permute-done.18.refs_3_ = f32[1,16,2048]{2,1,0:T(8,128)S(1)} collective-permute-done((f32[1,16,2048]{2,1,0:T(8,128)S(1)}, f32[1,16,2048]{2,1,0:T(8,128)S(1)}, u32[]{:S(2)}, u32[]{:S(2)}) %collective-permute-start.18) | collective-permute-done | bytes 131104 | tf_op jit(solution)/shard_map/ppermute | solution.py:689
  63.2 0.7 %shard_map.177 = f32[16,4,2,256]{3,2,1,0:T(2,128)} custom-call(f32[1,16,2048]{2,1,0:T(8,128)S(1)} %shard_map.174.refs_0_, f32[1,16,2048]{2,1,0:T(8,128)S(1)} %collective-permute-done.14.refs_1_, f32[1,16,2048]{2,1,0:T(8,128)S(1)} %collective-permute-done.16.refs_2_, f32[1,16,2048]{2,1,0:T(8,128)S(1)} %collective-permute-done.18.refs_3_), custom_call_target="tpu_custom_call" | custom-call | tf_op jit(solution)/shard_map/pallas_call | solution.py:735
  (33 shorter events, 0.3 us)
Async XLA Ops:
  0.0 11.6 %copy-start.12 = (s32[1152]{0:T(1024)S(1)}, s32[1152]{0:T(1024)}, u32[]{:S(2)}) copy-start(s32[1152]{0:T(1024)} %constant.106.clone) | copy-start | bytes 13828
  0.0 11.6 %copy-start.13 = (s32[1152]{0:T(1024)S(1)}, s32[1152]{0:T(1024)}, u32[]{:S(2)}) copy-start(s32[1152]{0:T(1024)} %constant.107.clone) | copy-start | bytes 13828
  0.0 11.6 %copy-start.14 = (s32[1152]{0:T(1024)S(1)}, s32[1152]{0:T(1024)}, u32[]{:S(2)}) copy-start(s32[1152]{0:T(1024)} %constant.108.clone) | copy-start | bytes 13828
  0.0 11.7 %copy-start.11 = (s32[1152]{0:T(1024)S(1)}, s32[1152]{0:T(1024)}, u32[]{:S(2)}) copy-start(s32[1152]{0:T(1024)} %constant.109.clone) | copy-start | bytes 13828
  0.0 11.4 %copy-start.10 = (s32[4,3]{1,0:T(4,128)S(1)}, s32[4,3]{1,0:T(4,128)}, u32[]{:S(2)}) copy-start(s32[4,3]{1,0:T(4,128)} %param.18) | copy-start | bytes 148
  1.2 1.5 %copy-start = (f32[2,3,1,288,256]{4,3,2,1,0:T(8,128)S(1)}, f32[2,3,1,288,256]{4,3,2,1,0:T(8,128)}, u32[]{:S(2)}) copy-start(f32[2,3,1,288,256]{4,3,2,1,0:T(8,128)} %param.16) | copy-start | bytes 5308420
  2.7 11.0 %copy-start.4 = (s32[6,512]{1,0:T(8,128)S(1)}, s32[6,512]{1,0:T(8,128)}, u32[]{:S(2)}) copy-start(s32[6,512]{1,0:T(8,128)} %constant.102.clone.column_ref) | copy-start | bytes 36868
  2.7 11.0 %copy-start.5 = (f32[6,512]{1,0:T(8,128)S(1)}, f32[6,512]{1,0:T(8,128)}, u32[]{:S(2)}) copy-start(f32[6,512]{1,0:T(8,128)} %constant.103.clone.sign_ref) | copy-start | bytes 36868
  2.7 11.0 %copy-start.6 = (s32[6,512]{1,0:T(8,128)S(1)}, s32[6,512]{1,0:T(8,128)}, u32[]{:S(2)}) copy-start(s32[6,512]{1,0:T(8,128)} %constant.104.clone.more_ref) | copy-start | bytes 36868
  2.7 11.0 %copy-start.7 = (f32[6,512]{1,0:T(8,128)S(1)}, f32[6,512]{1,0:T(8,128)}, u32[]{:S(2)}) copy-start(f32[6,512]{1,0:T(8,128)} %constant.105.clone.moresign_ref) | copy-start | bytes 36868
  3.4 14.0 %collective-permute-start = (f32[2,144,128]{2,1,0:T(8,128)S(1)}, f32[2,144,128]{2,1,0:T(8,128)S(1)}, u32[]{:S(2)}, u32[]{:S(2)}) collective-permute-start(f32[2,144,128]{2,1,0:T(8,128)S(1)} %get-tuple-element.39), channel_id=1, source_target_pairs={{0,4},{1,5},{2,6},{3,7},{4,0},{5,1},{6,2},{7,3},{8,12},{9,13},{10,... | collective-permute-start | bytes 442376 | tf_op jit(solution)/shard_map/ppermute | solution.py:538
  6.5 10.9 %collective-permute-start.1 = (f32[2,144,128]{2,1,0:T(8,128)S(1)}, f32[2,144,128]{2,1,0:T(8,128)S(1)}, u32[]{:S(2)}, u32[]{:S(2)}) collective-permute-start(f32[2,144,128]{2,1,0:T(8,128)S(1)} %get-tuple-element.40), channel_id=1, source_target_pairs={{0,12},{1,13},{2,14},{3,15},{4,8},{5,9},{6,10},{7,11},{8,4},{9,5},... | collective-permute-start | bytes 442376 | tf_op jit(solution)/shard_map/ppermute | solution.py:538
  9.0 8.4 %collective-permute-start.2 = (f32[2,144,128]{2,1,0:T(8,128)S(1)}, f32[2,144,128]{2,1,0:T(8,128)S(1)}, u32[]{:S(2)}, u32[]{:S(2)}) collective-permute-start(f32[2,144,128]{2,1,0:T(8,128)S(1)} %get-tuple-element.41), channel_id=1, source_target_pairs={{0,1},{1,0},{2,3},{3,2},{4,5},{5,4},{6,7},{7,6},{8,9},{9,8},{10,11... | collective-permute-start | bytes 442376 | tf_op jit(solution)/shard_map/ppermute | solution.py:538
  9.0 9.4 %collective-permute-start.3 = (f32[2,144,128]{2,1,0:T(8,128)S(1)}, f32[2,144,128]{2,1,0:T(8,128)S(1)}, u32[]{:S(2)}, u32[]{:S(2)}) collective-permute-start(f32[2,144,128]{2,1,0:T(8,128)S(1)} %get-tuple-element.42), channel_id=1, source_target_pairs={{0,15},{1,2},{2,1},{3,4},{4,3},{5,6},{6,5},{7,8},{8,7},{9,10},{10,... | collective-permute-start | bytes 442376 | tf_op jit(solution)/shard_map/ppermute | solution.py:538
  18.4 5.7 %copy-start.2 = (s32[6,640]{1,0:T(8,128)S(1)}, s32[6,640]{1,0:T(8,128)}, u32[]{:S(2)}) copy-start(s32[6,640]{1,0:T(8,128)} %constant.110.clone.column_ref) | copy-start | bytes 46084
  18.4 5.7 %copy-start.3 = (f32[6,640]{1,0:T(8,128)S(1)}, f32[6,640]{1,0:T(8,128)}, u32[]{:S(2)}) copy-start(f32[6,640]{1,0:T(8,128)} %constant.111.clone.sign_ref) | copy-start | bytes 46084
  18.4 5.7 %copy-start.8 = (s32[6,256]{1,0:T(8,128)S(1)}, s32[6,256]{1,0:T(8,128)}, u32[]{:S(2)}) copy-start(s32[6,256]{1,0:T(8,128)} %constant.112.clone.more_ref) | copy-start | bytes 18436
  18.4 5.7 %copy-start.9 = (f32[6,256]{1,0:T(8,128)S(1)}, f32[6,256]{1,0:T(8,128)}, u32[]{:S(2)}) copy-start(f32[6,256]{1,0:T(8,128)} %constant.113.clone.moresign_ref) | copy-start | bytes 18436
  19.4 9.6 %collective-permute-start.4 = (f32[2,144,128]{2,1,0:T(8,128)S(1)}, f32[2,144,128]{2,1,0:T(8,128)S(1)}, u32[]{:S(2)}, u32[]{:S(2)}) collective-permute-start(f32[2,144,128]{2,1,0:T(8,128)S(1)} %get-tuple-element.49), channel_id=1, source_target_pairs={{0,4},{1,5},{2,6},{3,7},{4,0},{5,1},{6,2},{7,3},{8,12},{9,13},{10,... | collective-permute-start | bytes 442376 | tf_op jit(solution)/shard_map/ppermute | solution.py:538
  19.5 9.5 %collective-permute-start.5 = (f32[2,144,128]{2,1,0:T(8,128)S(1)}, f32[2,144,128]{2,1,0:T(8,128)S(1)}, u32[]{:S(2)}, u32[]{:S(2)}) collective-permute-start(f32[2,144,128]{2,1,0:T(8,128)S(1)} %get-tuple-element.50), channel_id=1, source_target_pairs={{0,12},{1,13},{2,14},{3,15},{4,8},{5,9},{6,10},{7,11},{8,4},{9,5},... | collective-permute-start | bytes 442376 | tf_op jit(solution)/shard_map/ppermute | solution.py:538
  22.7 6.3 %collective-permute-start.6 = (f32[2,144,128]{2,1,0:T(8,128)S(1)}, f32[2,144,128]{2,1,0:T(8,128)S(1)}, u32[]{:S(2)}, u32[]{:S(2)}) collective-permute-start(f32[2,144,128]{2,1,0:T(8,128)S(1)} %get-tuple-element.51), channel_id=1, source_target_pairs={{0,1},{1,0},{2,3},{3,2},{4,5},{5,4},{6,7},{7,6},{8,9},{9,8},{10,11... | collective-permute-start | bytes 442376 | tf_op jit(solution)/shard_map/ppermute | solution.py:538
  22.7 7.5 %collective-permute-start.7 = (f32[2,144,128]{2,1,0:T(8,128)S(1)}, f32[2,144,128]{2,1,0:T(8,128)S(1)}, u32[]{:S(2)}, u32[]{:S(2)}) collective-permute-start(f32[2,144,128]{2,1,0:T(8,128)S(1)} %get-tuple-element.52), channel_id=1, source_target_pairs={{0,15},{1,2},{2,1},{3,4},{4,3},{5,6},{6,5},{7,8},{8,7},{9,10},{10,... | collective-permute-start | bytes 442376 | tf_op jit(solution)/shard_map/ppermute | solution.py:538
  27.9 2.3 %copy-start.1 = (s32[256]{0:T(256)S(1)}, s32[256]{0:T(256)}, u32[]{:S(2)}) copy-start(s32[256]{0:T(256)} %param.19) | copy-start | bytes 3076
  34.4 1.6 %collective-permute-start.8 = (f32[2,16,2048]{2,1,0:T(8,128)S(1)}, f32[2,16,2048]{2,1,0:T(8,128)S(1)}, u32[]{:S(2)}, u32[]{:S(2)}) collective-permute-start(f32[2,16,2048]{2,1,0:T(8,128)S(1)} %shard_map.163.refs_8_), channel_id=1, source_target_pairs={{0,1},{1,0},{2,3},{3,2},{4,5},{5,4},{6,7},{7,6},{8,9},{9,8},{10,11... | collective-permute-start | bytes 786440 | tf_op jit(solution)/shard_map/ppermute | solution.py:689
  37.2 8.4 %collective-permute-start.10 = (f32[2,16,2048]{2,1,0:T(8,128)S(1)}, f32[2,16,2048]{2,1,0:T(8,128)S(1)}, u32[]{:S(2)}, u32[]{:S(2)}) collective-permute-start(f32[2,16,2048]{2,1,0:T(8,128)S(1)} %shard_map.166.refs_8_), channel_id=1, source_target_pairs={{0,1},{1,0},{2,3},{3,2},{4,5},{5,4},{6,7},{7,6},{8,9},{9,8},{10,11... | collective-permute-start | bytes 786440 | tf_op jit(solution)/shard_map/ppermute | solution.py:689
  39.5 6.0 %collective-permute-start.9 = (f32[2,16,2048]{2,1,0:T(8,128)S(1)}, f32[2,16,2048]{2,1,0:T(8,128)S(1)}, u32[]{:S(2)}, u32[]{:S(2)}) collective-permute-start(f32[2,16,2048]{2,1,0:T(8,128)S(1)} %shard_map.168.refs_8_), channel_id=1, source_target_pairs={{0,1},{1,0},{2,3},{3,2},{4,5},{5,4},{6,7},{7,6},{8,9},{9,8},{10,11... | collective-permute-start | bytes 786440 | tf_op jit(solution)/shard_map/ppermute | solution.py:689
  40.0 5.5 %collective-permute-start.11 = (f32[1,16,2048]{2,1,0:T(8,128)S(1)}, f32[1,16,2048]{2,1,0:T(8,128)S(1)}, u32[]{:S(2)}, u32[]{:S(2)}) collective-permute-start(f32[1,16,2048]{2,1,0:T(8,128)S(1)} %get-tuple-element.57.refs_8_), channel_id=1, source_target_pairs={{0,2},{1,3},{2,0},{3,1},{4,6},{5,7},{6,4},{7,5},{8,10},{9,11},{10,... | collective-permute-start | bytes 393224 | tf_op jit(solution)/shard_map/ppermute | solution.py:689
  46.7 9.6 %collective-permute-start.12 = (f32[2,16,2048]{2,1,0:T(8,128)S(1)}, f32[2,16,2048]{2,1,0:T(8,128)S(1)}, u32[]{:S(2)}, u32[]{:S(2)}) collective-permute-start(f32[2,16,2048]{2,1,0:T(8,128)S(1)} %shard_map.172.refs_8_), channel_id=1, source_target_pairs={{0,1},{1,0},{2,3},{3,2},{4,5},{5,4},{6,7},{7,6},{8,9},{9,8},{10,11... | collective-permute-start | bytes 786440 | tf_op jit(solution)/shard_map/ppermute | solution.py:689
  46.8 6.4 %collective-permute-start.15 = (f32[1,16,2048]{2,1,0:T(8,128)S(1)}, f32[1,16,2048]{2,1,0:T(8,128)S(1)}, u32[]{:S(2)}, u32[]{:S(2)}) collective-permute-start(f32[1,16,2048]{2,1,0:T(8,128)S(1)} %get-tuple-element.60), channel_id=1, source_target_pairs={{0,2},{1,3},{2,0},{3,1},{4,6},{5,7},{6,4},{7,5},{8,10},{9,11},{10,... | collective-permute-start | bytes 393224 | tf_op jit(solution)/shard_map/ppermute | solution.py:689
  47.1 9.2 %collective-permute-start.17 = (f32[1,16,2048]{2,1,0:T(8,128)S(1)}, f32[1,16,2048]{2,1,0:T(8,128)S(1)}, u32[]{:S(2)}, u32[]{:S(2)}) collective-permute-start(f32[1,16,2048]{2,1,0:T(8,128)S(1)} %get-tuple-element.58.refs_8_), channel_id=1, source_target_pairs={{0,2},{1,3},{2,0},{3,1},{4,6},{5,7},{6,4},{7,5},{8,10},{9,11},{10,... | collective-permute-start | bytes 393224 | tf_op jit(solution)/shard_map/ppermute | solution.py:689
  48.8 12.8 %collective-permute-start.14 = (f32[1,16,2048]{2,1,0:T(8,128)S(1)}, f32[1,16,2048]{2,1,0:T(8,128)S(1)}, u32[]{:S(2)}, u32[]{:S(2)}) collective-permute-start(f32[1,16,2048]{2,1,0:T(8,128)S(1)} %shard_map.171.refs_9_), channel_id=1, source_target_pairs={{0,4},{1,5},{2,6},{3,7},{4,8},{5,9},{6,10},{7,11},{8,12},{9,13},{1... | collective-permute-start | bytes 393224 | tf_op jit(solution)/shard_map/ppermute | solution.py:689
  53.2 8.5 %collective-permute-start.16 = (f32[1,16,2048]{2,1,0:T(8,128)S(1)}, f32[1,16,2048]{2,1,0:T(8,128)S(1)}, u32[]{:S(2)}, u32[]{:S(2)}) collective-permute-start(f32[1,16,2048]{2,1,0:T(8,128)S(1)} %shard_map.175), channel_id=1, source_target_pairs={{0,8},{1,9},{2,10},{3,11},{4,12},{5,13},{6,14},{7,15},{8,0},{9,1},... | collective-permute-start | bytes 393224 | tf_op jit(solution)/shard_map/ppermute | solution.py:689
  55.9 5.0 %collective-permute-start.13 = (f32[1,16,2048]{2,1,0:T(8,128)S(1)}, f32[1,16,2048]{2,1,0:T(8,128)S(1)}, u32[]{:S(2)}, u32[]{:S(2)}) collective-permute-start(f32[1,16,2048]{2,1,0:T(8,128)S(1)} %get-tuple-element.59), channel_id=1, source_target_pairs={{0,2},{1,3},{2,0},{3,1},{4,6},{5,7},{6,4},{7,5},{8,10},{9,11},{10,... | collective-permute-start | bytes 393224 | tf_op jit(solution)/shard_map/ppermute | solution.py:689
  56.3 6.9 %collective-permute-start.18 = (f32[1,16,2048]{2,1,0:T(8,128)S(1)}, f32[1,16,2048]{2,1,0:T(8,128)S(1)}, u32[]{:S(2)}, u32[]{:S(2)}) collective-permute-start(f32[1,16,2048]{2,1,0:T(8,128)S(1)} %shard_map.176), channel_id=1, source_target_pairs={{0,12},{1,13},{2,14},{3,15},{4,0},{5,1},{6,2},{7,3},{8,4},{9,5},{1... | collective-permute-start | bytes 393224 | tf_op jit(solution)/shard_map/ppermute | solution.py:689
